TPU v7x, 32 devices: a whole 2x2x4 slice. The times are simulated.
32 devices in a mesh: tile: 4 (over y, x), phi: 8 (over z, core).
Axes of the slice: x: 2, y: 2, z: 4, core: 2. Of those that a mesh axis runs over, the one named last changes fastest.
Arguments:
- conserved: float32 [256, 5, 4096], P(('tile', 'phi')), may hold values from -6 to 6
- face_field: float32 [256, 3, 4096], P(('tile', 'phi')), may hold values from -1.5 to 1.5
- block_ids: int32 [256], P(('tile', 'phi')), may hold values from 0 to 63, as said below
- int_shift: int32 [64], P('tile'), may hold values from 0 to 511
- frac_shift: float32 [64], P('tile'), may hold values from 0 to 1, as said below
Outputs:
- conserved_out: float32 [256, 5, 4096], P(('tile', 'phi'))
- field_out: float32 [256, 3, 4096], P(('tile', 'phi'))
Inputs may be any that keep to these rules, and one draw needn't show every extreme that they name: `block_ids`: within each slab (aligned runs of 64 entries, one slab per index of tile) every number from 0 to 63 appears once. Number v belongs to the owner v // 8. The slots of one device hold at most 2 blocks of any one owner, and in every slab some device holds exactly 2 blocks of some owner. `frac_shift`: multiples of 1/256, below 1.
All inputs are finite; a program needn't handle non-finite values.
Results may differ from a plain program's by a relative error of at most 0.0003.
Values sent between devices are 32-bit elements; how exact they have to be, the bound alone decides.
No kernel may reach another device: no remote copies, remote signals or barrier semaphores. Data moves between devices by JAX's collectives and lax.ppermute only.
A program may use at most 64 MiB of HBM per device.

v0:
```python
import jax
import jax.numpy as jnp
from jax import lax
from jax.sharding import PartitionSpec as P

BS = 16
TB = 2
PB = 4


NODES = (-3, -2, -1, 0, 1, 2, 3)


def shifted_2(value, axis, steps):
    count = lax.axis_size(axis)
    initial, last = (max(0, -steps), min(count, count - steps))
    return lax.ppermute(value, axis, [(source, source + steps) for source in range(initial, last)])


def flux_weights(fraction):
    position = -fraction
    lagrange = []
    for a in NODES:
        product = jnp.ones_like(fraction)
        for b in NODES:
            if b != a:
                product = product * (position - float(b)) / float(a - b)
        lagrange.append(product)
    weights = []
    for m in range(-3, 3):
        weight_sum = jnp.zeros_like(fraction)
        if m >= 0:
            for a in range(m + 1, 4):
                weight_sum = weight_sum - lagrange[a + 3]
        else:
            for a in range(-3, m + 1):
                weight_sum = weight_sum + lagrange[a + 3]
        weights.append(weight_sum)
    return weights


def row_rotate(fields, whole_shift):
    length = fields.shape[2]
    result = fields
    for bit_index in range(max(1, length.bit_length())):
        step_size = (1 << bit_index) % length
        taken = whole_shift >> bit_index & 1 == 1
        result = jnp.where(taken[None, :, None], jnp.roll(result, step_size, axis=2), result)
    return result


def exclusive_prefix(values):
    length = values.shape[2]
    block_len = 128
    block_count = length // block_len
    shaped = values.reshape(values.shape[0], values.shape[1], block_count, block_len)
    positions = jnp.arange(block_len, dtype=jnp.int32)
    lower_table = (positions[:, None] < positions[None, :]).astype(jnp.float32)
    inside = jnp.einsum("abcj,jk->abck", shaped, lower_table, precision=lax.Precision.HIGHEST)
    block_sums = jnp.sum(shaped, axis=3)
    offsets = jnp.cumsum(block_sums, axis=2) - block_sums
    return (
        (inside + offsets[..., None]).reshape(values.shape),
        jnp.sum(block_sums, axis=2, keepdims=True),
    )


def remap_rows(fields, whole_shift, part_shift):
    length = fields.shape[2]
    cells_phi = jnp.arange(length, dtype=jnp.int32)
    shifted = row_rotate(fields, whole_shift)
    weights = flux_weights(part_shift)
    face_flux = jnp.zeros_like(shifted)
    for term_index in range(6):
        face_flux = face_flux + weights[term_index][None, :, None] * jnp.roll(
            shifted, 3 - term_index, axis=2
        )
    updated = shifted - (jnp.roll(face_flux, -1, axis=2) - face_flux)
    magnetic = fields[5:7]
    prefix, row_total = exclusive_prefix(magnetic)
    behind = row_rotate(prefix, whole_shift)
    wrapped = (cells_phi[None, :] < whole_shift[:, None]).astype(jnp.float32)
    whole_flux = prefix - behind + wrapped[None] * row_total
    return (updated, whole_flux + face_flux[5:7])


def shards(conserved, face_field, block_ids, int_shift, frac_shift):
    peer_count = lax.axis_size("phi")
    own_index = lax.axis_index("phi")
    slot_count = conserved.shape[0]
    cube_cells = conserved.shape[2]
    group_rows = BS * BS // peer_count
    stacked = jnp.concatenate([conserved, face_field], axis=1)
    extra_parts = []
    azimuthal = stacked[:, 7]
    capacity = 2 * max(1, slot_count // peer_count)
    targets = block_ids // slot_count
    onehot = (targets[:, None] == jnp.arange(peer_count, dtype=jnp.int32)[None, :]).astype(
        jnp.int32
    )
    slot_ranks = jnp.sum(jnp.cumsum(onehot, axis=0) * onehot, axis=1) - 1
    buffer_slot = targets * capacity + slot_ranks
    packed = (
        jnp.zeros((peer_count * capacity, 8, cube_cells), jnp.float32).at[buffer_slot].set(stacked)
    )
    packed_ids = (
        jnp.full((peer_count * capacity,), -1.0, jnp.float32)
        .at[buffer_slot]
        .set(block_ids.astype(jnp.float32))
    )
    arrived, arrived_ids = (
        lax.all_to_all(
            packed.reshape(peer_count, capacity, 8, cube_cells),
            "phi",
            split_axis=0,
            concat_axis=0,
            tiled=True,
        ),
        lax.all_to_all(
            packed_ids.reshape(peer_count, capacity), "phi", split_axis=0, concat_axis=0, tiled=True
        ),
    )
    number = arrived_ids.reshape(-1).astype(jnp.int32)
    placing = jnp.where(number >= 0, number - own_index * slot_count, slot_count)
    owned_blocks = (
        jnp.zeros((slot_count + 1, 8, cube_cells), jnp.float32)
        .at[placing]
        .set(arrived.reshape(peer_count * capacity, 8, cube_cells))[:slot_count]
    )
    outgoing = (
        owned_blocks[:, :7]
        .reshape(slot_count, 7, peer_count, group_rows * BS)
        .transpose(2, 0, 1, 3)
    )
    incoming = lax.all_to_all(outgoing, "phi", split_axis=0, concat_axis=0, tiled=True)
    fields = (
        incoming.reshape(peer_count, TB, PB, 7, group_rows, BS)
        .transpose(3, 1, 4, 0, 2, 5)
        .reshape(7, TB * group_rows, peer_count * PB * BS)
    )
    azimuthal = owned_blocks[:, 7]
    radius_rows = (own_index * group_rows + jnp.arange(group_rows, dtype=jnp.int32)) // BS
    row_shift = jnp.tile(int_shift[radius_rows], TB)
    row_frac = jnp.tile(frac_shift[radius_rows], TB)
    updated, fluxes = remap_rows(fields, row_shift, row_frac)
    payload = jnp.concatenate([updated, fluxes] + extra_parts, axis=0)
    parts_count = payload.shape[0]
    sending = (
        payload.reshape(parts_count, TB, group_rows, peer_count, PB, BS)
        .transpose(3, 1, 4, 0, 2, 5)
        .reshape(peer_count, slot_count, parts_count, group_rows * BS)
    )
    returned = lax.all_to_all(sending, "phi", split_axis=0, concat_axis=0, tiled=True)
    returned = returned.transpose(1, 2, 0, 3).reshape(slot_count, parts_count, cube_cells)
    block_shape = (TB, PB, BS, BS, BS)
    radial_flux = returned[:, 7].reshape(block_shape)
    polar_flux = returned[:, 8].reshape(block_shape)
    outer_rim = shifted_2(radial_flux[:, :, 0], "tile", -1)
    radial_next = jnp.concatenate([radial_flux[:, :, 1:], outer_rim[:, :, None]], axis=2)
    polar_first = jnp.concatenate(
        [polar_flux[1:, :, :, 0:1, :], jnp.zeros_like(polar_flux[:1, :, :, 0:1, :])], axis=0
    )
    polar_next = jnp.concatenate([polar_flux[:, :, :, 1:, :], polar_first], axis=3)
    new_azimuthal = (
        azimuthal.reshape(block_shape) + (radial_next - radial_flux) + (polar_next - polar_flux)
    )
    field_out = jnp.concatenate(
        [returned[:, 5:7], new_azimuthal.reshape(slot_count, 1, cube_cells)], axis=1
    )
    return (returned[:, :5], field_out)


def solution(mesh):
    return jax.shard_map(
        shards,
        mesh=mesh,
        in_specs=(
            P(("tile", "phi"), None, None),
            P(("tile", "phi"), None, None),
            P(("tile", "phi")),
            P("tile"),
            P("tile"),
        ),
        out_specs=(P(("tile", "phi"), None, None), P(("tile", "phi"), None, None)),
        check_vma=False,
    )
```

profile of v0, /device:TPU:13, one launch (start us, length us, event | category | flops | bytes accessed | tf_op | source)
XLA Modules:
  0.0 212.1 jit_solution(6775254225873682218)
XLA Ops:
  3.0 5.6 %all-to-all-start = ((f32[8,1,2]{2,1,0:T(1,128)}), f32[8,1,2]{2,1,0:T(1,128)S(1)}, u32[]{:S(2)}, u32[]{:S(2)}) async-start(f32[8,1,2]{2,1,0:T(1,128)} %bitcast.1), calls=%async_computation | async-start | bytes 8192 | tf_op jit(solution)/shard_map/all_to_all | solution.py:119
  10.5 1.6 broadcast_in_dim.169
  12.1 3.0 %scatter_fusion = f32[16,8,4096]{2,1,0:T(8,128)} fusion(f32[16,8,4096]{2,1,0:T(8,128)} %broadcast_in_dim.169, s32[8]{0:T(128)S(1)} %compare_select_fusion.2, f32[8,8,4096]{2,1,0:T(8,128)S(1)} %copy.60), kind=kCustom, calls=%fused_computation.3 | custom fusion | bytes 3145760 | tf_op jit(solution)/shard_map/scatter | solution.py:104
  15.0 5.0 %all-to-all-start.1 = ((f32[8,2,8,4096]{3,2,1,0:T(8,128)}), f32[8,2,8,4096]{3,2,1,0:T(8,128)S(1)}, u32[]{:S(2)}, u32[]{:S(2)}) async-start(f32[8,2,8,4096]{3,2,1,0:T(8,128)} %bitcast.3), calls=%async_computation.1 | async-start | bytes 4194304 | tf_op jit(solution)/shard_map/all_to_all | solution.py:112
  20.2 45.4 %all-to-all-done.1 = f32[8,2,8,4096]{3,2,1,0:T(8,128)S(1)} async-done(((f32[8,2,8,4096]{3,2,1,0:T(8,128)}), f32[8,2,8,4096]{3,2,1,0:T(8,128)S(1)}, u32[]{:S(2)}, u32[]{:S(2)}) %all-to-all-start.1) | async-done | bytes 2097184 | tf_op jit(solution)/shard_map/all_to_all | solution.py:112
  67.5 1.5 copy.62
  68.9 7.0 %all-to-all-start.2 = ((f32[8,8,7,512]{3,1,2,0:T(8,128)}), f32[8,8,7,512]{3,1,2,0:T(8,128)S(1)}, u32[]{:S(2)}, u32[]{:S(2)}) async-start(f32[8,8,7,512]{3,1,2,0:T(8,128)} %copy.62), calls=%async_computation.2 | async-start | bytes 1835008 | tf_op jit(solution)/shard_map/all_to_all | solution.py:135
  80.1 16.0 %all-to-all-done.2 = f32[8,8,7,512]{3,1,2,0:T(8,128)S(1)} async-done(((f32[8,8,7,512]{3,1,2,0:T(8,128)}), f32[8,8,7,512]{3,1,2,0:T(8,128)S(1)}, u32[]{:S(2)}, u32[]{:S(2)}) %all-to-all-start.2) | async-done | bytes 917536 | tf_op jit(solution)/shard_map/all_to_all | solution.py:135
  96.2 4.3 %reshape.341 = f32[8,2,4,7,32,16]{5,4,2,1,3,0:T(8,128)} reshape(f32[8,8,7,512]{3,1,2,0:T(8,128)S(1)} %all-to-all-done.2) | data formatting | bytes 1835008 | tf_op jit(solution)/shard_map/reshape | solution.py:137
  100.5 2.2 %slice_reduce_fusion = (f32[2,2,32]{2,1,0:T(2,128)S(1)}, f32[2,2,32,8]{2,1,0,3:T(2,128)S(1)}, f32[2,2,32,8,4,16]{5,2,4,1,0,3:T(8,128)S(1)}) fusion(f32[7,2,32,8,4,16]{5,2,4,1,0,3:T(8,128)} %bitcast.63), kind=kLoop, calls=%fused_computation.99 | loop fusion | flops 129920 | bytes 528896 | tf_op jit(solution)/shard_map/reduce_sum | solution.py:64
  102.7 7.9 %copy.63 = f32[7,2,32,8,4,16]{2,1,5,4,3,0:T(2,128)} copy(f32[7,2,32,8,4,16]{5,2,4,1,0,3:T(8,128)} %bitcast.64) | data formatting | bytes 1835008 | tf_op jit(solution)/shard_map/transpose | solution.py:138
  110.8 1.6 copy.64
  112.4 1.8 reshape.343
  118.6 3.8 %reshape.342 = f32[7,64,512]{1,2,0:T(8,128)S(1)} reshape(f32[7,2,32,8,4,16]{2,1,5,4,3,0:T(2,128)} %copy.63) | data formatting | bytes 1835008 | tf_op jit(solution)/shard_map/reshape | solution.py:139
  129.6 2.6 %fusion.4 = f32[7,64,512]{1,2,0:T(8,128)S(1)} fusion(f32[7,64,509]{1,2,0:T(8,128)S(1)} %bitcast.62, f32[7,64,3]{1,2,0:T(4,128)S(1)} %slice.309, f32[7,64,510]{1,2,0:T(8,128)S(1)} %get-tuple-element.14, f32[7,64,2]{1,2,0:T(2,128)S(1)} %get-tuple-element.16, f32[7,64,511]{1,2,0:T(8,128)S(1)} %get-tuple-element.18, f32[7,64,1]{1,2,0:T(1,128)S(1)} %get-tuple-element.20, ...), kind=kLoop, calls=%fused_computation.20 | loop fusion | flops 3670016 | bytes 6424064 | tf_op jit(solution)/shard_map/add | solution.py:75
  132.2 1.5 slice.319
  136.5 2.0 fusion.5
  138.9 4.4 %reshape.345 = f32[9,2,32,8,4,16]{2,1,5,4,3,0:T(2,128)} reshape(f32[9,64,512]{1,2,0:T(8,128)S(1)} %pad_maximum_fusion) | data formatting | bytes 2359296 | tf_op jit(solution)/shard_map/reshape | solution.py:149
  143.2 9.6 %copy.72 = f32[8,2,4,9,32,16]{5,4,2,1,3,0:T(8,128)} copy(f32[8,2,4,9,32,16]{4,1,5,2,0,3:T(2,128)} %bitcast.65) | data formatting | bytes 2359296 | tf_op jit(solution)/shard_map/transpose | solution.py:150
  152.8 8.4 %reshape.346 = f32[8,8,9,512]{3,1,2,0:T(8,128)S(1)} reshape(f32[8,2,4,9,32,16]{5,4,2,1,3,0:T(8,128)} %copy.72) | data formatting | bytes 2359296 | tf_op jit(solution)/shard_map/reshape | solution.py:151
  161.2 33.1 %all_to_all.24 = f32[8,8,9,512]{3,1,2,0:T(8,128)S(1)} all-to-all(f32[8,8,9,512]{3,1,2,0:T(8,128)S(1)} %reshape.346), channel_id=1, replica_groups=mesh['tile'=4,'phi'=8] {'phi'}, dimensions={0} | all-to-all | bytes 2359296 | tf_op jit(solution)/shard_map/all_to_all | solution.py:153
  199.0 3.1 %collective-permute-start = (f32[2,4,16,16]{3,2,1,0:T(8,128)}, f32[2,4,16,16]{3,2,1,0:T(8,128)}, u32[]{:S(2)}, u32[]{:S(2)}) collective-permute-start(f32[2,4,16,16]{3,2,1,0:T(8,128)} %slice_bitcast_fusion), channel_id=1, source_target_pairs={{8,0},{16,8},{24,16},{9,1},{17,9},{25,17},{10,2},{18,10},{26,18},{... | collective-permute-start | bytes 24584 | tf_op jit(solution)/shard_map/ppermute | solution.py:17
  202.1 2.4 %select_maximum_fusion = f32[2,4,16,16,16]{4,3,2,1,0:T(8,128)} fusion(f32[1,4,16,1,16]{4,3,2,1,0:T(1,128)} %slice.349, f32[2,4,16,15,16]{4,3,2,1,0:T(8,128)} %slice.348), kind=kLoop, calls=%fused_computation.28 | loop fusion | flops 98304 | bytes 258048 | tf_op jit(solution)/shard_map/concatenate | solution.py:163
  206.1 2.4 %concatenate.145 = f32[8,1,4096]{2,1,0:T(1,128)} reshape(f32[2,4,16,16,16]{4,3,2,1,0:T(8,128)} %select_maximum_fusion) | data formatting | bytes 262144 | tf_op jit(solution)/shard_map/concatenate | solution.py:163
  (168 shorter events, 34.6 us)
Async XLA Ops:
  0.6 75.4 %copy-start = (f32[16]{0:T(128)S(1)}, f32[16]{0:T(128)}, u32[]{:S(2)}) copy-start(f32[16]{0:T(128)} %param.9) | copy-start | bytes 196
  3.0 12.1 %all-to-all-start = ((f32[8,1,2]{2,1,0:T(1,128)}), f32[8,1,2]{2,1,0:T(1,128)S(1)}, u32[]{:S(2)}, u32[]{:S(2)}) async-start(f32[8,1,2]{2,1,0:T(1,128)} %bitcast.1), calls=%async_computation | async-start | bytes 8192 | tf_op jit(solution)/shard_map/all_to_all | solution.py:119
  15.0 50.5 %all-to-all-start.1 = ((f32[8,2,8,4096]{3,2,1,0:T(8,128)}), f32[8,2,8,4096]{3,2,1,0:T(8,128)S(1)}, u32[]{:S(2)}, u32[]{:S(2)}) async-start(f32[8,2,8,4096]{3,2,1,0:T(8,128)} %bitcast.3), calls=%async_computation.1 | async-start | bytes 4194304 | tf_op jit(solution)/shard_map/all_to_all | solution.py:112
  67.4 9.2 %copy-start.2 = (s32[16]{0:T(128)S(1)}, s32[16]{0:T(128)}, u32[]{:S(2)}) copy-start(s32[16]{0:T(128)} %param.8) | copy-start | bytes 196
  68.9 27.2 %all-to-all-start.2 = ((f32[8,8,7,512]{3,1,2,0:T(8,128)}), f32[8,8,7,512]{3,1,2,0:T(8,128)S(1)}, u32[]{:S(2)}, u32[]{:S(2)}) async-start(f32[8,8,7,512]{3,1,2,0:T(8,128)} %copy.62), calls=%async_computation.2 | async-start | bytes 1835008 | tf_op jit(solution)/shard_map/all_to_all | solution.py:135
  114.2 0.9 copy-start.21
  117.0 0.8 copy-start.5
  122.4 0.7 copy-start.22
  128.8 0.7 copy-start.24
  128.8 0.7 copy-start.25
  128.9 0.7 copy-start.26
  128.9 0.7 copy-start.27
  128.9 0.7 copy-start.28
  128.9 0.7 copy-start.29
  132.2 1.8 copy-start.3
  134.6 1.8 copy-start.4
  136.5 2.0 copy-start.8
  136.5 2.0 copy-start.23
  198.4 7.8 %copy-start.6 = (f32[2,4,16,16,16]{4,3,2,1,0:T(8,128)}, f32[2,4,16,16,16]{4,3,2,1,0:T(8,128)S(1)}, u32[]{:S(2)}) copy-start(f32[2,4,16,16,16]{4,3,2,1,0:T(8,128)S(1)} %reshape_squeeze.7) | copy-start | bytes 393220
  199.0 9.5 %collective-permute-start = (f32[2,4,16,16]{3,2,1,0:T(8,128)}, f32[2,4,16,16]{3,2,1,0:T(8,128)}, u32[]{:S(2)}, u32[]{:S(2)}) collective-permute-start(f32[2,4,16,16]{3,2,1,0:T(8,128)} %slice_bitcast_fusion), channel_id=1, source_target_pairs={{8,0},{16,8},{24,16},{9,1},{17,9},{25,17},{10,2},{18,10},{26,18},{... | collective-permute-start | bytes 24584 | tf_op jit(solution)/shard_map/ppermute | solution.py:17
  206.1 2.4 %slice-start = ((f32[2,4,16,16,16]{4,3,2,1,0:T(8,128)}), f32[2,4,15,16,16]{4,3,2,1,0:T(8,128)S(1)}, s32[]{:S(2)}) async-start(f32[2,4,16,16,16]{4,3,2,1,0:T(8,128)} %copy-done.6), calls=%async_computation.4 | async-start | bytes 1966080 | tf_op jit(solution)/shard_map/slice | solution.py:159
  208.5 1.4 copy-start.7
  208.5 3.6 %copy-start.1 = (f32[16]{0:T(128)S(1)}, f32[16]{0:T(128)}, u32[]{:S(2)}) copy-start(f32[16]{0:T(128)} %param.9) | copy-start | bytes 196
  209.5 1.8 copy-start.9
  (11 other events, 6.9 us)
where the time goes:
time: 215 us; the launch traced here: 212 us
  local copies, waits for them, and re-layouts  73.4 us (34%)
  waiting for transfers between devices  61.5 us (29%)
  blocking collectives  33.1 us (15%)
  other arithmetic  21.5 us (10%)
  starting transfers between devices  20.8 us (10%)
    all_to_all x1, waiting for transfers between devices, shards(): lax.all_to_all(packed.reshape(peer_count, capacity, 8, cube_cells), 'phi'...  45.4 us
    all_to_all x1, blocking collectives, shards(): lax.all_to_all(sending, 'phi', split_axis=0, concat_axis=0, tiled=True)  33.1 us
    all_to_all x1, waiting for transfers between devices, shards(): lax.all_to_all(outgoing, 'phi', split_axis=0, concat_axis=0, tiled=True)  16 us
    transpose x1, local copies, waits for them, and re-layouts, shards(): sending = payload.reshape(parts_count, TB, group_rows, peer_count, PB, BS...  9.57 us
    reshape x1, local copies, waits for them, and re-layouts, shards(): sending = payload.reshape(parts_count, TB, group_rows, peer_count, PB, BS...  8.38 us
    transpose x1, local copies, waits for them, and re-layouts, shards(): fields = incoming.reshape(peer_count, TB, PB, 7, group_rows, BS).transpos...  7.92 us
    all_to_all x1, starting transfers between devices, shards(): lax.all_to_all(outgoing, 'phi', split_axis=0, concat_axis=0, tiled=True)  7.02 us
    all_to_all x1, starting transfers between devices, shards(): lax.all_to_all(packed_ids.reshape(peer_count, capacity), 'phi', split_axi...  5.64 us
  transfers between devices with their start and end apart: 4, of which 2 were waited for; matrix products, arithmetic and copies ran while one was open for 8% of the time, Pallas kernels for 0%

commit v1 on v0

v1 whole, which is shorter than its diff:
```python
import functools

import jax
import jax.numpy as jnp
from jax import lax
from jax.experimental import pallas as pl
from jax.experimental.pallas import tpu as pltpu
from jax.sharding import PartitionSpec as P

BS = 16
TB = 2
PB = 4
LANES = 128
SUB = 8
NODES = (-3, -2, -1, 0, 1, 2, 3)
F32 = jnp.float32
BF16 = jnp.bfloat16


def halves(x):
    hi = x.astype(BF16)
    return hi, (x - hi.astype(F32)).astype(BF16)


def thirds(x):
    hi = x.astype(BF16)
    rest = x - hi.astype(F32)
    mid = rest.astype(BF16)
    return hi, mid, (rest - mid.astype(F32)).astype(BF16)


def dot(a, b):
    return jnp.dot(a, b, preferred_element_type=F32)


def nearest_blocks(shift):
    whole = (shift + BS // 2) // BS
    return whole, shift - whole * BS


def pack_fields_kernel(cfg, me_ref, ids_ref, face_ref, *refs):
    outs, tile_ref, sem, id_sem = refs[: cfg.n], refs[cfg.n], refs[cfg.n + 1], refs[cfg.n + 2]
    me = me_ref[0]
    rows = lax.broadcasted_iota(jnp.int32, (SUB, LANES), 0)
    ids = jnp.zeros((SUB, LANES), jnp.int32)
    for slot in range(SUB):
        ids = jnp.where(rows == slot, ids_ref[slot], ids)
    tile_ref[...] = ids.astype(F32)[None]
    copies = []
    for k in range(cfg.n):
        dest = jnp.bitwise_xor(me, k)
        for c in range(3):
            copies.append(
                pltpu.make_async_copy(
                    face_ref.at[c, pl.ds(dest * cfg.tiles, cfg.tiles)],
                    outs[k].at[pl.ds(c * cfg.tiles, cfg.tiles)],
                    sem.at[k * 3 + c],
                )
            )
        copies.append(
            pltpu.make_async_copy(tile_ref, outs[k].at[pl.ds(3 * cfg.tiles, 1)], id_sem.at[k])
        )
    for copy in copies:
        copy.start()
    for copy in copies:
        copy.wait()


def pack_conserved_kernel(cfg, me_ref, conserved_ref, *refs):
    outs, sem = refs[: cfg.n], refs[cfg.n]
    me = me_ref[0]
    copies = []
    for k in range(cfg.n):
        dest = jnp.bitwise_xor(me, k)
        copies.append(
            pltpu.make_async_copy(
                conserved_ref.at[:, pl.ds(dest * cfg.tiles, cfg.tiles)], outs[k], sem.at[k]
            )
        )
    for copy in copies:
        copy.start()
    for copy in copies:
        copy.wait()


def unpack_kernel(cfg, me_ref, *refs):
    first, second = refs[: cfg.n], refs[cfg.n : 2 * cfg.n]
    conserved_ref, field_ref, sem = refs[2 * cfg.n :]
    me = me_ref[0]
    copies = []
    for k in range(cfg.n):
        at = pl.ds(jnp.bitwise_xor(me, k) * cfg.tiles, cfg.tiles)
        copies.append(
            pltpu.make_async_copy(second[k].at[pl.ds(0, 5)], conserved_ref.at[:, at], sem.at[k, 0])
        )
        copies.append(
            pltpu.make_async_copy(first[k], field_ref.at[pl.ds(0, 2), at], sem.at[k, 1])
        )
        copies.append(
            pltpu.make_async_copy(
                second[k].at[pl.ds(5, 1)], field_ref.at[pl.ds(2, 1), at], sem.at[k, 2]
            )
        )
    for copy in copies:
        copy.start()
    for copy in copies:
        copy.wait()


def operators_kernel(cfg, me_ref, shift_ref, frac_ref, mh_ref, ml_ref, gh_ref, gl_ref, tj_ref):
    size = cfg.lanes
    first = (me_ref[0] * cfg.rows) // BS
    row = lax.broadcasted_iota(jnp.int32, (size, size), 0)
    col = lax.broadcasted_iota(jnp.int32, (size, size), 1)
    same = (row // BS) == (col // BS)
    e_in, e_out = row % BS, col % BS
    zero = jnp.zeros((size, size), F32)
    tj_ref[0] = jnp.where(same & (e_in < e_out), 1.0, zero).astype(BF16)
    tj_ref[1] = jnp.where(same, 1.0, zero).astype(BF16)
    for al in range(cfg.radii):
        _, rest = nearest_blocks(shift_ref[first + al])
        position = -jnp.full((1, size), frac_ref[first + al], F32)
        lagrange = []
        for a in NODES:
            product = jnp.ones_like(position)
            for b in NODES:
                if b != a:
                    product = product * ((position - float(b)) * (1.0 / float(a - b)))
            lagrange.append(product)
        weights = []
        for m in range(-3, 3):
            total = jnp.zeros_like(position)
            if m >= 0:
                for a in range(m + 1, 4):
                    total = total - lagrange[a + 3]
            else:
                for a in range(-3, m + 1):
                    total = total + lagrange[a + 3]
            weights.append(total)
        for d in range(3):
            at = e_in + BS * (d - 1)
            tap = jnp.where(same, at - e_out + rest, 100)
            remap, flux = zero, zero
            for a in NODES:
                hit = tap == a
                remap = jnp.where(hit, lagrange[a + 3], remap)
                if a < 3:
                    flux = jnp.where(hit, weights[a + 3], flux)
            flux = flux - jnp.where(same & (at < e_out - rest), 1.0, zero)
            mh_ref[al, d], ml_ref[al, d] = halves(remap)
            gh_ref[al, d], gl_ref[al, d] = halves(flux)


def gather_matrix(cfg, me, ids, whole):
    shape = (cfg.slots, 3 * cfg.slots)
    target = lax.broadcasted_iota(jnp.int32, shape, 0)
    owner = jnp.bitwise_xor(target >> 3, me)
    q_out, b_out = owner * PB + (target & 3), (target >> 2) & 1
    v = jnp.broadcast_to(ids, shape)
    q_in, b_in = (v >> 3) * PB + (v & 3), (v >> 2) & 1
    same = b_in == b_out
    cells = cfg.n * PB
    rows = []
    for d in (-1, 0, 1):
        hit = same & (((q_out - whole + d - q_in + 2 * cells) & (cells - 1)) == 0)
        rows.append(jnp.where(hit, 1.0, 0.0))
    rows.append(jnp.where(same & (q_in == q_out), 1.0, 0.0))
    back = (q_out - 1 - q_in + cells) & (cells - 1)
    count = jnp.where(back <= whole, 1.0, 0.0) + jnp.where(back + cells <= whole, 1.0, 0.0)
    rows.append(jnp.where(same, count, 0.0))
    return rows


def three_dots(high, low, mh, ml):
    rows = high.shape[0]
    both = dot(jnp.concatenate([high, low], axis=0), mh)
    return both[:rows] + both[rows:] + dot(high, ml)


def fields_kernel(cfg, me_ref, shift_ref, *refs):
    n, slots, tiles, wide = cfg.n, cfg.slots, cfg.tiles, cfg.lanes
    pieces = refs[:n]
    mh_ref, ml_ref, gh_ref, gl_ref, tj_ref = refs[n : n + 5]
    outs = refs[n + 5 : 2 * n + 5]
    bp_ref, halo_ref, polar_ref, rows_ref = refs[2 * n + 5 :]
    me = me_ref[0]
    first = (me * cfg.rows) // BS
    per = wide // LANES
    ids = jnp.concatenate([p[3 * tiles] for p in pieces] * 3, axis=0)
    ids = jnp.transpose(ids)[0:1].astype(jnp.int32)

    def source(c, al):
        x = jnp.concatenate(
            [
                jnp.concatenate([p[c * tiles + al * per + t] for p in pieces], axis=0)
                for t in range(per)
            ],
            axis=1,
        )
        return jnp.concatenate(thirds(x), axis=0)

    lane = lax.broadcasted_iota(jnp.int32, (slots, wide), 1)
    lower = (lax.broadcasted_iota(jnp.int32, (slots, wide), 0) >> 2) & 1 == 0
    total = []
    for al in range(cfg.radii):
        whole, _ = nearest_blocks(shift_ref[first + al])
        rows = gather_matrix(cfg, me, ids, whole)
        taken = jnp.concatenate(rows, axis=0).astype(BF16)
        rows_ref[al] = taken[: 3 * slots]
        own = taken[3 * slots : 4 * slots]
        y = [dot(taken, source(c, al)) for c in range(2)]
        part = [
            halves(jnp.concatenate([y[c][j * slots : (j + 1) * slots] for c in range(2)], axis=0))
            for j in range(5)
        ]
        remap = jnp.zeros((2 * slots, wide), F32)
        flux = jnp.zeros((2 * slots, wide), F32)
        for d in range(3):
            remap = remap + three_dots(*part[d], mh_ref[al, d], ml_ref[al, d])
            flux = flux + three_dots(*part[d], gh_ref[al, d], gl_ref[al, d])
        for j in range(2):
            both = dot(jnp.concatenate(part[3 + j], axis=0), tj_ref[j])
            flux = flux + (both[: 2 * slots] + both[2 * slots :])
        for c in range(2):
            for k in range(n):
                for t in range(per):
                    outs[k][c, al * per + t] = remap[
                        c * slots + k * SUB : c * slots + (k + 1) * SUB,
                        t * LANES : (t + 1) * LANES,
                    ]
        radial, polar = flux[:slots], flux[slots:]
        if cfg.split == 1:
            up = jnp.where(lower, jnp.concatenate([polar[4:], polar[:4]], axis=0), 0.0)
            after = pltpu.roll(jnp.where(lane < BS, up, polar), wide - BS, 1)
        else:
            after = jnp.where(lane < wide - BS, pltpu.roll(polar, wide - BS, 1), 0.0)
        azimuthal = dot(own, source(2, al))
        total.append((azimuthal + (after - polar) - radial, radial))
        if al == 0:
            for k in range(n):
                at = pl.ds(pl.multiple_of(jnp.bitwise_xor(me, k) * SUB, SUB), SUB)
                for t in range(per):
                    cut = (slice(k * SUB, (k + 1) * SUB), slice(t * LANES, (t + 1) * LANES))
                    halo_ref[t, at, :] = radial[cut]
                    if cfg.split > 1:
                        polar_ref[t, at, :] = polar[cut]
            if cfg.split == 1:
                polar_ref[...] = jnp.zeros_like(polar_ref)
    for al in range(cfg.radii):
        bp = total[al][0]
        if al + 1 < cfg.radii:
            bp = bp + total[al + 1][1]
        for t in range(per):
            bp_ref[al * per + t] = bp[:, t * LANES : (t + 1) * LANES]


def conserved_kernel(cfg, me_ref, *refs):
    n, slots, wide = cfg.n, cfg.slots, cfg.lanes
    pieces = refs[:n]
    mh_ref, ml_ref, rows_ref, bp_ref, halo_ref, polar_ref = refs[n : n + 6]
    outs = refs[n + 6 :]
    me = me_ref[0]
    per = wide // LANES
    for al in range(cfg.radii):
        taken = rows_ref[al]
        ys = []
        for c in range(5):
            x = jnp.concatenate(
                [
                    jnp.concatenate([p[c, al * per + t] for p in pieces], axis=0)
                    for t in range(per)
                ],
                axis=1,
            )
            ys.append(dot(taken, jnp.concatenate(thirds(x), axis=0)))
        out = jnp.zeros((5 * slots, wide), F32)
        for d in range(3):
            part = halves(
                jnp.concatenate([y[d * slots : (d + 1) * slots] for y in ys], axis=0)
            )
            out = out + three_dots(*part, mh_ref[al, d], ml_ref[al, d])
        for c in range(5):
            for k in range(n):
                for t in range(per):
                    outs[k][c, al * per + t] = out[
                        c * slots + k * SUB : c * slots + (k + 1) * SUB,
                        t * LANES : (t + 1) * LANES,
                    ]
    for k in range(n):
        at = pl.ds(pl.multiple_of(jnp.bitwise_xor(me, k) * SUB, SUB), SUB)
        for t in range(cfg.tiles):
            bp = bp_ref[t, k * SUB : (k + 1) * SUB, :]
            if t >= cfg.tiles - per:
                bp = bp + halo_ref[t - (cfg.tiles - per), at, :]
                if cfg.split > 1 and t == cfg.tiles - 1:
                    after = polar_ref[0, at, :]
                    low = (lax.broadcasted_iota(jnp.int32, after.shape, 0) >> 2) == 0
                    up = jnp.where(low, jnp.concatenate([after[4:], after[:4]], axis=0), 0.0)
                    here = lax.rem(me, cfg.split)
                    after = jnp.where(here == cfg.split - 1, up, after)
                    lane = lax.broadcasted_iota(jnp.int32, after.shape, 1)
                    after = jnp.where(lane < BS, after, 0.0)
                    bp = bp + pltpu.roll(after, LANES - BS, 1)
            outs[k][5, t] = bp


class Sizes:
    def __init__(self, n):
        self.n = n
        self.rows = BS * BS // n
        self.tiles = self.rows * BS // LANES
        self.lanes = min(self.rows, BS) * BS
        self.radii = max(1, self.rows // BS)
        self.split = max(1, BS // self.rows)
        self.slots = n * SUB


def shape(*dims, dtype=F32):
    return jax.ShapeDtypeStruct(dims, dtype)


def shards(conserved, face_field, block_ids, int_shift, frac_shift):
    n = lax.axis_size("phi")
    cfg = Sizes(n)
    count = lax.axis_size("tile") * n
    tiles, slots = cfg.tiles, cfg.slots
    per = cfg.lanes // LANES
    smem = pl.BlockSpec(memory_space=pltpu.SMEM)
    vmem = pl.BlockSpec(memory_space=pltpu.VMEM)
    anywhere = pl.BlockSpec(memory_space=pl.ANY)
    params = pltpu.CompilerParams(vmem_limit_bytes=48 * 2**20)
    me = lax.axis_index("phi").astype(jnp.int32).reshape(1)

    def tiled(x):
        return x.reshape(SUB, x.shape[1], n * tiles, LANES).transpose(1, 2, 0, 3)

    def untiled(x):
        return x.transpose(2, 0, 1, 3).reshape(SUB, x.shape[0], n * tiles * LANES)

    def exchange(pieces):
        return [pieces[0]] + [
            lax.ppermute(pieces[k], "phi", [(s, s ^ k) for s in range(n)]) for k in range(1, n)
        ]

    sent = pl.pallas_call(
        functools.partial(pack_fields_kernel, cfg),
        out_shape=[shape(3 * tiles + 1, SUB, LANES)] * n,
        in_specs=[smem, smem, anywhere],
        out_specs=[anywhere] * n,
        scratch_shapes=[
            pltpu.VMEM((1, SUB, LANES), F32),
            pltpu.SemaphoreType.DMA((3 * n,)),
            pltpu.SemaphoreType.DMA((n,)),
        ],
        name="pack_fields",
    )(me, block_ids, tiled(face_field))
    fields = exchange(sent)
    sent = pl.pallas_call(
        functools.partial(pack_conserved_kernel, cfg),
        out_shape=[shape(5, tiles, SUB, LANES)] * n,
        in_specs=[smem, anywhere],
        out_specs=[anywhere] * n,
        scratch_shapes=[pltpu.SemaphoreType.DMA((n,))],
        name="pack_conserved",
    )(me, tiled(conserved))
    fluid = exchange(sent)

    square = shape(cfg.radii, 3, cfg.lanes, cfg.lanes, dtype=BF16)
    mh, ml, gh, gl, tj = pl.pallas_call(
        functools.partial(operators_kernel, cfg),
        out_shape=[square] * 4 + [shape(2, cfg.lanes, cfg.lanes, dtype=BF16)],
        in_specs=[smem] * 3,
        out_specs=[vmem] * 5,
        compiler_params=params,
        name="operators",
    )(me, int_shift, frac_shift)

    *first, bp, halo, polar, taken = pl.pallas_call(
        functools.partial(fields_kernel, cfg),
        out_shape=[shape(2, tiles, SUB, LANES)] * n
        + [
            shape(tiles, slots, LANES),
            shape(per, slots, LANES),
            shape(per, slots, LANES) if cfg.split > 1 else shape(1, SUB, LANES),
            shape(cfg.radii, 3 * slots, 3 * slots, dtype=BF16),
        ],
        in_specs=[smem] * 2 + [vmem] * (n + 5),
        out_specs=[vmem] * (n + 4),
        compiler_params=params,
        name="fields",
    )(me, int_shift, *fields, mh, ml, gh, gl, tj)
    halo = lax.ppermute(
        halo, ("tile", "phi"), [(s, s - cfg.split) for s in range(cfg.split, count)]
    )
    if cfg.split > 1:
        polar = lax.ppermute(
            polar,
            "phi",
            [(s, s - 1 if s % cfg.split else s + cfg.split - 1) for s in range(n)],
        )
    first = exchange(first)
    second = pl.pallas_call(
        functools.partial(conserved_kernel, cfg),
        out_shape=[shape(6, tiles, SUB, LANES)] * n,
        in_specs=[smem] + [vmem] * (n + 6),
        out_specs=[vmem] * n,
        compiler_params=params,
        name="conserved",
    )(me, *fluid, mh, ml, taken, bp, halo, polar)
    second = exchange(second)
    conserved_out, field_out = pl.pallas_call(
        functools.partial(unpack_kernel, cfg),
        out_shape=[shape(5, n * tiles, SUB, LANES), shape(3, n * tiles, SUB, LANES)],
        in_specs=[smem] + [anywhere] * (2 * n),
        out_specs=[anywhere] * 2,
        scratch_shapes=[pltpu.SemaphoreType.DMA((n, 3))],
        name="unpack",
    )(me, *first, *second)
    return untiled(conserved_out), untiled(field_out)


def solution(mesh):
    return jax.shard_map(
        shards,
        mesh=mesh,
        in_specs=(
            P(("tile", "phi"), None, None),
            P(("tile", "phi"), None, None),
            P(("tile", "phi")),
            P("tile"),
            P("tile"),
        ),
        out_specs=(P(("tile", "phi"), None, None), P(("tile", "phi"), None, None)),
        check_vma=False,
    )
```

time: 215 us -> 136 us (0.63); the launches traced: 212 us -> 135 us
  Pallas kernels: 0 us -> 73.7 us
  local copies, waits for them, and re-layouts: 73.4 us -> 1.24 us
  waiting for transfers between devices: 61.5 us -> 23.2 us
  blocking collectives: 33.1 us -> 0 us
  other arithmetic: 21.5 us -> 0 us
  starting transfers between devices: 20.8 us -> 36.4 us
    pallas_call x0 -> x6, Pallas kernels: none -> 73.7 us  [the longest x1 33.1 us: shards(): pl.pallas_call(functools.partial(unpack_kernel, cfg), out_shape=[shape(5,...]
    all_to_all x3 -> x0, waiting for transfers between devices: 61.5 us -> none  [the longest x1 45.4 us: shards(): lax.all_to_all(packed.reshape(peer_count, capacity, 8, cube_cells), 'phi'...]
    ppermute x1 -> x29, starting transfers between devices: 3.1 us -> 36.4 us  [the longest x28 34.4 us: exchange(): lax.ppermute(pieces[k], 'phi', [(s, s ^ k) for s in range(n)])]
    all_to_all x1 -> x0, blocking collectives: 33.1 us -> none  [shards(): lax.all_to_all(sending, 'phi', split_axis=0, concat_axis=0, tiled=True)]
    reshape x8 -> x0, local copies, waits for them, and re-layouts: 23.5 us -> none  [the longest x1 8.38 us: shards(): sending = payload.reshape(parts_count, TB, group_rows, peer_count, PB, BS...]
    ppermute x1 -> x29, waiting for transfers between devices: 0.01 us -> 23.2 us  [the longest x28 22 us: exchange(): lax.ppermute(pieces[k], 'phi', [(s, s ^ k) for s in range(n)])]
    transpose x3 -> x0, local copies, waits for them, and re-layouts: 19 us -> none  [the longest x1 9.57 us: shards(): sending = payload.reshape(parts_count, TB, group_rows, peer_count, PB, BS...]
    all_to_all x3 -> x0, starting transfers between devices: 17.7 us -> none  [the longest x1 7.02 us: shards(): lax.all_to_all(outgoing, 'phi', split_axis=0, concat_axis=0, tiled=True)]
  transfers between devices with their start and end apart: 4 -> 29, of which waited for: 2 -> 10; matrix products, arithmetic and copies ran while one was open for 8% -> 0% of each run, Pallas kernels for 0% -> 20%
where the time goes in v1:
time: 136 us; the launch traced here: 135 us
  Pallas kernels  73.7 us (54%)
  starting transfers between devices  36.4 us (27%)
  waiting for transfers between devices  23.2 us (17%)
    ppermute x28, starting transfers between devices, exchange(): lax.ppermute(pieces[k], 'phi', [(s, s ^ k) for s in range(n)])  34.4 us
    pallas_call x1, Pallas kernels, shards(): pl.pallas_call(functools.partial(unpack_kernel, cfg), out_shape=[shape(5,...  33.1 us
    ppermute x28, waiting for transfers between devices, exchange(): lax.ppermute(pieces[k], 'phi', [(s, s ^ k) for s in range(n)])  22 us
    pallas_call x1, Pallas kernels, shards(): pl.pallas_call(functools.partial(pack_conserved_kernel, cfg), out_shape=[...  21 us
    pallas_call x1, Pallas kernels, shards(): pl.pallas_call(functools.partial(pack_fields_kernel, cfg), out_shape=[sha...  14 us
  transfers between devices with their start and end apart: 29, of which 10 were waited for; matrix products, arithmetic and copies ran while one was open for 0% of the time, Pallas kernels for 20%

profile of v1, /device:TPU:13, one launch (start us, length us, event | category | flops | bytes accessed | tf_op | source)
XLA Modules:
  0.0 135.4 jit_solution(16706371808436607187)
XLA Ops:
  0.6 14.0 %pack_fields.1 = (f32[13,8,128]{2,1,0:T(8,128)}, f32[13,8,128]{2,1,0:T(8,128)}, f32[13,8,128]{2,1,0:T(8,128)}, f32[13,8,128]{2,1,0:T(8,128)}, f32[13,8,128]{2,1,...) custom-call(s32[1]{0:T(128)} %bitcast.me_ref, s32[8]{0:T(128)} %ids_ref.1, ...), custom_call_target="tpu_custom_call" | custom-call | tf_op jit(solution)/shard_map/pack_fields/pallas_call | solution.py:345
  15.5 1.5 %collective-permute-start.2 = (f32[13,8,128]{2,1,0:T(8,128)}, f32[13,8,128]{2,1,0:T(8,128)S(1)}, u32[]{:S(2)}, u32[]{:S(2)}) collective-permute-start(f32[13,8,128]{2,1,0:T(8,128)} %get-tuple-element.48), channel_id=1, source_target_pairs={{0,3},{1,2},{2,1},{3,0},{4,7},{5,6},{6,5},{7,4},{8,11},{9,10},{10,... | collective-permute-start | bytes 159752 | tf_op jit(solution)/shard_map/ppermute | solution.py:342
  17.1 2.3 %collective-permute-start.3 = (f32[13,8,128]{2,1,0:T(8,128)}, f32[13,8,128]{2,1,0:T(8,128)S(1)}, u32[]{:S(2)}, u32[]{:S(2)}) collective-permute-start(f32[13,8,128]{2,1,0:T(8,128)} %get-tuple-element.49), channel_id=1, source_target_pairs={{0,4},{1,5},{2,6},{3,7},{4,0},{5,1},{6,2},{7,3},{8,12},{9,13},{10,... | collective-permute-start | bytes 159752 | tf_op jit(solution)/shard_map/ppermute | solution.py:342
  19.8 21.0 %pack_conserved.1 = (f32[5,4,8,128]{3,2,1,0:T(8,128)}, f32[5,4,8,128]{3,2,1,0:T(8,128)}, f32[5,4,8,128]{3,2,1,0:T(8,128)}, f32[5,4,8,128]{3,2,1,0:T(8,128)}, f32...) custom-call(s32[1]{0:T(128)} %bitcast.me_ref, ...), custom_call_target="tpu_custom_call" | custom-call | tf_op jit(solution)/shard_map/pack_conserved/pallas_call | solution.py:358
  41.1 1.9 %collective-permute-start.16 = (f32[5,4,8,128]{3,2,1,0:T(8,128)}, f32[5,4,8,128]{3,2,1,0:T(8,128)S(1)}, u32[]{:S(2)}, u32[]{:S(2)}) collective-permute-start(f32[5,4,8,128]{3,2,1,0:T(8,128)} %get-tuple-element.69), channel_id=1, source_target_pairs={{0,3},{1,2},{2,1},{3,0},{4,7},{5,6},{6,5},{7,4},{8,11},{9,10},{10,... | collective-permute-start | bytes 245768 | tf_op jit(solution)/shard_map/ppermute | solution.py:342
  44.5 2.1 %collective-permute-done.5.refs_6_ = f32[13,8,128]{2,1,0:T(8,128)S(1)} collective-permute-done((f32[13,8,128]{2,1,0:T(8,128)S(1)}, f32[13,8,128]{2,1,0:T(8,128)S(1)}, u32[]{:S(2)}, u32[]{:S(2)}) %collective-permute-start.5) | collective-permute-done | bytes 53280 | tf_op jit(solution)/shard_map/ppermute | solution.py:342
  46.6 4.1 %collective-permute-start.17 = (f32[5,4,8,128]{3,2,1,0:T(8,128)}, f32[5,4,8,128]{3,2,1,0:T(8,128)S(1)}, u32[]{:S(2)}, u32[]{:S(2)}) collective-permute-start(f32[5,4,8,128]{3,2,1,0:T(8,128)} %get-tuple-element.70), channel_id=1, source_target_pairs={{0,4},{1,5},{2,6},{3,7},{4,0},{5,1},{6,2},{7,3},{8,12},{9,13},{10,... | collective-permute-start | bytes 245768 | tf_op jit(solution)/shard_map/ppermute | solution.py:342
  50.7 1.5 %collective-permute-start.18 = (f32[5,4,8,128]{3,2,1,0:T(8,128)}, f32[5,4,8,128]{3,2,1,0:T(8,128)S(1)}, u32[]{:S(2)}, u32[]{:S(2)}) collective-permute-start(f32[5,4,8,128]{3,2,1,0:T(8,128)} %get-tuple-element.71), channel_id=1, source_target_pairs={{0,5},{1,4},{2,7},{3,6},{4,1},{5,0},{6,3},{7,2},{8,13},{9,12},{10,... | collective-permute-start | bytes 245768 | tf_op jit(solution)/shard_map/ppermute | solution.py:342
  54.0 2.2 %operators.1 = (bf16[2,3,256,256]{3,2,1,0:T(8,128)(2,1)S(1)}, bf16[2,3,256,256]{3,2,1,0:T(8,128)(2,1)S(1)}, bf16[2,3,256,256]{3,2,1,0:T(8,128)(2,1)S(1)}, bf16[2...) custom-call(s32[1]{0:T(128)} %bitcast.me_ref, s32[16]{0:T(128)S(1)} %copy-done.4, f32[16]{0:T(128)S(1)} %copy-done.5), custom_call_target="tpu_custom_call" | custom-call | tf_op jit(solution)/shard_map/operators/pallas_call | solution.py:369
  56.3 2.1 %fields.1 = (f32[2,4,8,128]{3,2,1,0:T(8,128)S(1)}, f32[2,4,8,128]{3,2,1,0:T(8,128)S(1)}, f32[2,4,8,128]{3,2,1,0:T(8,128)S(1)}, f32[2,4,8,128]{3,2,1,0:T(8,128)S(...) custom-call(s32[1]{0:T(128)} %bitcast.me_ref, ...), custom_call_target="tpu_custom_call" | custom-call | tf_op jit(solution)/shard_map/fields/pallas_call | solution.py:378
  58.4 2.1 %collective-permute-start.21 = (f32[2,64,128]{2,1,0:T(8,128)S(1)}, f32[2,64,128]{2,1,0:T(8,128)S(1)}, u32[]{:S(2)}, u32[]{:S(2)}) collective-permute-start(f32[2,64,128]{2,1,0:T(8,128)S(1)} %get-tuple-element.76), channel_id=1, source_target_pairs={{1,0},{2,1},{3,2},{4,3},{5,4},{6,5},{7,6},{8,7},{9,8},{10,9},{11,1... | collective-permute-start | bytes 196616 | tf_op jit(solution)/shard_map/ppermute | solution.py:392
  60.4 3.9 %collective-permute-start.10 = (f32[2,4,8,128]{3,2,1,0:T(8,128)S(1)}, f32[2,4,8,128]{3,2,1,0:T(8,128)S(1)}, u32[]{:S(2)}, u32[]{:S(2)}) collective-permute-start(f32[2,4,8,128]{3,2,1,0:T(8,128)S(1)} %get-tuple-element.62), channel_id=1, source_target_pairs={{0,4},{1,5},{2,6},{3,7},{4,0},{5,1},{6,2},{7,3},{8,12},{9,13},{10,... | collective-permute-start | bytes 98312 | tf_op jit(solution)/shard_map/ppermute | solution.py:342
  64.7 2.1 %collective-permute-done.20.refs_7_ = f32[5,4,8,128]{3,2,1,0:T(8,128)S(1)} collective-permute-done((f32[5,4,8,128]{3,2,1,0:T(8,128)}, f32[5,4,8,128]{3,2,1,0:T(8,128)S(1)}, u32[]{:S(2)}, u32[]{:S(2)}) %collective-permute-start.20) | collective-permute-done | bytes 81952 | tf_op jit(solution)/shard_map/ppermute | solution.py:342
  69.9 2.1 %collective-permute-start.11 = (f32[2,4,8,128]{3,2,1,0:T(8,128)S(1)}, f32[2,4,8,128]{3,2,1,0:T(8,128)S(1)}, u32[]{:S(2)}, u32[]{:S(2)}) collective-permute-start(f32[2,4,8,128]{3,2,1,0:T(8,128)S(1)} %get-tuple-element.63), channel_id=1, source_target_pairs={{0,5},{1,4},{2,7},{3,6},{4,1},{5,0},{6,3},{7,2},{8,13},{9,12},{10,... | collective-permute-start | bytes 98312 | tf_op jit(solution)/shard_map/ppermute | solution.py:342
  73.7 1.8 %collective-permute-done.11.refs_5_ = f32[2,4,8,128]{3,2,1,0:T(8,128)S(1)} collective-permute-done((f32[2,4,8,128]{3,2,1,0:T(8,128)S(1)}, f32[2,4,8,128]{3,2,1,0:T(8,128)S(1)}, u32[]{:S(2)}, u32[]{:S(2)}) %collective-permute-start.11) | collective-permute-done | bytes 32800 | tf_op jit(solution)/shard_map/ppermute | solution.py:342
  76.5 2.4 %collective-permute-start.8 = (f32[2,4,8,128]{3,2,1,0:T(8,128)S(1)}, f32[2,4,8,128]{3,2,1,0:T(8,128)S(1)}, u32[]{:S(2)}, u32[]{:S(2)}) collective-permute-start(f32[2,4,8,128]{3,2,1,0:T(8,128)S(1)} %get-tuple-element.60), channel_id=1, source_target_pairs={{0,2},{1,3},{2,0},{3,1},{4,6},{5,7},{6,4},{7,5},{8,10},{9,11},{10,... | collective-permute-start | bytes 98312 | tf_op jit(solution)/shard_map/ppermute | solution.py:342
  80.6 2.2 %collective-permute-start.25 = (f32[6,4,8,128]{3,2,1,0:T(8,128)S(1)}, f32[6,4,8,128]{3,2,1,0:T(8,128)S(1)}, u32[]{:S(2)}, u32[]{:S(2)}) collective-permute-start(f32[6,4,8,128]{3,2,1,0:T(8,128)S(1)} %get-tuple-element.82), channel_id=1, source_target_pairs={{0,4},{1,5},{2,6},{3,7},{4,0},{5,1},{6,2},{7,3},{8,12},{9,13},{10,... | collective-permute-start | bytes 294920 | tf_op jit(solution)/shard_map/ppermute | solution.py:342
  82.8 1.6 %collective-permute-start.26 = (f32[6,4,8,128]{3,2,1,0:T(8,128)S(1)}, f32[6,4,8,128]{3,2,1,0:T(8,128)S(1)}, u32[]{:S(2)}, u32[]{:S(2)}) collective-permute-start(f32[6,4,8,128]{3,2,1,0:T(8,128)S(1)} %get-tuple-element.83), channel_id=1, source_target_pairs={{0,5},{1,4},{2,7},{3,6},{4,1},{5,0},{6,3},{7,2},{8,13},{9,12},{10,... | collective-permute-start | bytes 294920 | tf_op jit(solution)/shard_map/ppermute | solution.py:342
  85.1 1.9 %collective-permute-start.28 = (f32[6,4,8,128]{3,2,1,0:T(8,128)S(1)}, f32[6,4,8,128]{3,2,1,0:T(8,128)S(1)}, u32[]{:S(2)}, u32[]{:S(2)}) collective-permute-start(f32[6,4,8,128]{3,2,1,0:T(8,128)S(1)} %get-tuple-element.85), channel_id=1, source_target_pairs={{0,7},{1,6},{2,5},{3,4},{4,3},{5,2},{6,1},{7,0},{8,15},{9,14},{10,... | collective-permute-start | bytes 294920 | tf_op jit(solution)/shard_map/ppermute | solution.py:342
  87.0 6.4 %collective-permute-done.25.refs_12_ = f32[6,4,8,128]{3,2,1,0:T(8,128)S(1)} collective-permute-done((f32[6,4,8,128]{3,2,1,0:T(8,128)S(1)}, f32[6,4,8,128]{3,2,1,0:T(8,128)S(1)}, u32[]{:S(2)}, u32[]{:S(2)}) %collective-permute-start.25) | collective-permute-done | bytes 98336 | tf_op jit(solution)/shard_map/ppermute | solution.py:342
  93.5 2.1 %collective-permute-done.26.refs_13_ = f32[6,4,8,128]{3,2,1,0:T(8,128)S(1)} collective-permute-done((f32[6,4,8,128]{3,2,1,0:T(8,128)S(1)}, f32[6,4,8,128]{3,2,1,0:T(8,128)S(1)}, u32[]{:S(2)}, u32[]{:S(2)}) %collective-permute-start.26) | collective-permute-done | bytes 98336 | tf_op jit(solution)/shard_map/ppermute | solution.py:342
  95.6 2.9 %collective-permute-done.27.refs_14_ = f32[6,4,8,128]{3,2,1,0:T(8,128)S(1)} collective-permute-done((f32[6,4,8,128]{3,2,1,0:T(8,128)S(1)}, f32[6,4,8,128]{3,2,1,0:T(8,128)S(1)}, u32[]{:S(2)}, u32[]{:S(2)}) %collective-permute-start.27) | collective-permute-done | bytes 98336 | tf_op jit(solution)/shard_map/ppermute | solution.py:342
  98.5 3.2 %collective-permute-done.28.refs_15_ = f32[6,4,8,128]{3,2,1,0:T(8,128)S(1)} collective-permute-done((f32[6,4,8,128]{3,2,1,0:T(8,128)S(1)}, f32[6,4,8,128]{3,2,1,0:T(8,128)S(1)}, u32[]{:S(2)}, u32[]{:S(2)}) %collective-permute-start.28) | collective-permute-done | bytes 98336 | tf_op jit(solution)/shard_map/ppermute | solution.py:342
  102.3 33.1 %unpack.1 = (f32[5,32,8,128]{3,2,1,0:T(8,128)}, f32[3,32,8,128]{3,2,1,0:T(8,128)}) custom-call(s32[1]{0:T(128)} %bitcast.me_ref, f32[2,4,8,128]{3,2,1,0:T(8,128)} %copy-done.3, f32[2,4,8,128]{3,2,1,0:T(8,128)} %copy-done.17, f32[2,4,8,128]{3,2,1,0:T(8,128)} %copy-done.18, f32[2,4,8,128]{3,2,1,0:T(8,128)} %copy-done.19, f32[2,4,8,128]{3,2,1,0:T(8,128)} %copy-done.13, ...), custom_call_target="tpu_custom_call" | custom-call | tf_op jit(solution)/shard_map/unpack/pallas_call | solution.py:411
  (84 shorter events, 14.0 us)
Async XLA Ops:
  14.6 26.2 %collective-permute-start = (f32[13,8,128]{2,1,0:T(8,128)}, f32[13,8,128]{2,1,0:T(8,128)S(1)}, u32[]{:S(2)}, u32[]{:S(2)}) collective-permute-start(f32[13,8,128]{2,1,0:T(8,128)} %get-tuple-element.46), channel_id=1, source_target_pairs={{0,1},{1,0},{2,3},{3,2},{4,5},{5,4},{6,7},{7,6},{8,9},{9,8},{10,11... | collective-permute-start | bytes 159752 | tf_op jit(solution)/shard_map/ppermute | solution.py:342
  15.4 25.6 %collective-permute-start.1 = (f32[13,8,128]{2,1,0:T(8,128)}, f32[13,8,128]{2,1,0:T(8,128)S(1)}, u32[]{:S(2)}, u32[]{:S(2)}) collective-permute-start(f32[13,8,128]{2,1,0:T(8,128)} %get-tuple-element.47), channel_id=1, source_target_pairs={{0,2},{1,3},{2,0},{3,1},{4,6},{5,7},{6,4},{7,5},{8,10},{9,11},{10,... | collective-permute-start | bytes 159752 | tf_op jit(solution)/shard_map/ppermute | solution.py:342
  15.5 25.6 %collective-permute-start.2 = (f32[13,8,128]{2,1,0:T(8,128)}, f32[13,8,128]{2,1,0:T(8,128)S(1)}, u32[]{:S(2)}, u32[]{:S(2)}) collective-permute-start(f32[13,8,128]{2,1,0:T(8,128)} %get-tuple-element.48), channel_id=1, source_target_pairs={{0,3},{1,2},{2,1},{3,0},{4,7},{5,6},{6,5},{7,4},{8,11},{9,10},{10,... | collective-permute-start | bytes 159752 | tf_op jit(solution)/shard_map/ppermute | solution.py:342
  17.1 26.0 %collective-permute-start.3 = (f32[13,8,128]{2,1,0:T(8,128)}, f32[13,8,128]{2,1,0:T(8,128)S(1)}, u32[]{:S(2)}, u32[]{:S(2)}) collective-permute-start(f32[13,8,128]{2,1,0:T(8,128)} %get-tuple-element.49), channel_id=1, source_target_pairs={{0,4},{1,5},{2,6},{3,7},{4,0},{5,1},{6,2},{7,3},{8,12},{9,13},{10,... | collective-permute-start | bytes 159752 | tf_op jit(solution)/shard_map/ppermute | solution.py:342
  19.4 25.0 %collective-permute-start.4 = (f32[13,8,128]{2,1,0:T(8,128)}, f32[13,8,128]{2,1,0:T(8,128)S(1)}, u32[]{:S(2)}, u32[]{:S(2)}) collective-permute-start(f32[13,8,128]{2,1,0:T(8,128)} %get-tuple-element.50), channel_id=1, source_target_pairs={{0,5},{1,4},{2,7},{3,6},{4,1},{5,0},{6,3},{7,2},{8,13},{9,12},{10,... | collective-permute-start | bytes 159752 | tf_op jit(solution)/shard_map/ppermute | solution.py:342
  40.8 11.4 %collective-permute-start.14 = (f32[5,4,8,128]{3,2,1,0:T(8,128)}, f32[5,4,8,128]{3,2,1,0:T(8,128)S(1)}, u32[]{:S(2)}, u32[]{:S(2)}) collective-permute-start(f32[5,4,8,128]{3,2,1,0:T(8,128)} %get-tuple-element.67), channel_id=1, source_target_pairs={{0,1},{1,0},{2,3},{3,2},{4,5},{5,4},{6,7},{7,6},{8,9},{9,8},{10,11... | collective-permute-start | bytes 245768 | tf_op jit(solution)/shard_map/ppermute | solution.py:342
  41.0 12.1 %collective-permute-start.15 = (f32[5,4,8,128]{3,2,1,0:T(8,128)}, f32[5,4,8,128]{3,2,1,0:T(8,128)S(1)}, u32[]{:S(2)}, u32[]{:S(2)}) collective-permute-start(f32[5,4,8,128]{3,2,1,0:T(8,128)} %get-tuple-element.68), channel_id=1, source_target_pairs={{0,2},{1,3},{2,0},{3,1},{4,6},{5,7},{6,4},{7,5},{8,10},{9,11},{10,... | collective-permute-start | bytes 245768 | tf_op jit(solution)/shard_map/ppermute | solution.py:342
  41.1 17.2 %collective-permute-start.16 = (f32[5,4,8,128]{3,2,1,0:T(8,128)}, f32[5,4,8,128]{3,2,1,0:T(8,128)S(1)}, u32[]{:S(2)}, u32[]{:S(2)}) collective-permute-start(f32[5,4,8,128]{3,2,1,0:T(8,128)} %get-tuple-element.69), channel_id=1, source_target_pairs={{0,3},{1,2},{2,1},{3,0},{4,7},{5,6},{6,5},{7,4},{8,11},{9,10},{10,... | collective-permute-start | bytes 245768 | tf_op jit(solution)/shard_map/ppermute | solution.py:342
  44.3 6.4 %collective-permute-start.6 = (f32[13,8,128]{2,1,0:T(8,128)S(1)}, f32[13,8,128]{2,1,0:T(8,128)S(1)}, u32[]{:S(2)}, u32[]{:S(2)}) collective-permute-start(f32[13,8,128]{2,1,0:T(8,128)S(1)} %copy-done.20), channel_id=1, source_target_pairs={{0,7},{1,6},{2,5},{3,4},{4,3},{5,2},{6,1},{7,0},{8,15},{9,14},{10,... | collective-permute-start | bytes 159752 | tf_op jit(solution)/shard_map/ppermute | solution.py:342
  46.6 13.8 %collective-permute-start.17 = (f32[5,4,8,128]{3,2,1,0:T(8,128)}, f32[5,4,8,128]{3,2,1,0:T(8,128)S(1)}, u32[]{:S(2)}, u32[]{:S(2)}) collective-permute-start(f32[5,4,8,128]{3,2,1,0:T(8,128)} %get-tuple-element.70), channel_id=1, source_target_pairs={{0,4},{1,5},{2,6},{3,7},{4,0},{5,1},{6,2},{7,3},{8,12},{9,13},{10,... | collective-permute-start | bytes 245768 | tf_op jit(solution)/shard_map/ppermute | solution.py:342
  50.7 13.6 %collective-permute-start.18 = (f32[5,4,8,128]{3,2,1,0:T(8,128)}, f32[5,4,8,128]{3,2,1,0:T(8,128)S(1)}, u32[]{:S(2)}, u32[]{:S(2)}) collective-permute-start(f32[5,4,8,128]{3,2,1,0:T(8,128)} %get-tuple-element.71), channel_id=1, source_target_pairs={{0,5},{1,4},{2,7},{3,6},{4,1},{5,0},{6,3},{7,2},{8,13},{9,12},{10,... | collective-permute-start | bytes 245768 | tf_op jit(solution)/shard_map/ppermute | solution.py:342
  52.3 12.5 %collective-permute-start.19 = (f32[5,4,8,128]{3,2,1,0:T(8,128)}, f32[5,4,8,128]{3,2,1,0:T(8,128)S(1)}, u32[]{:S(2)}, u32[]{:S(2)}) collective-permute-start(f32[5,4,8,128]{3,2,1,0:T(8,128)} %get-tuple-element.72), channel_id=1, source_target_pairs={{0,6},{1,7},{2,4},{3,5},{4,2},{5,3},{6,0},{7,1},{8,14},{9,15},{10,... | collective-permute-start | bytes 245768 | tf_op jit(solution)/shard_map/ppermute | solution.py:342
  53.1 13.8 %collective-permute-start.20 = (f32[5,4,8,128]{3,2,1,0:T(8,128)}, f32[5,4,8,128]{3,2,1,0:T(8,128)S(1)}, u32[]{:S(2)}, u32[]{:S(2)}) collective-permute-start(f32[5,4,8,128]{3,2,1,0:T(8,128)} %get-tuple-element.73), channel_id=1, source_target_pairs={{0,7},{1,6},{2,5},{3,4},{4,3},{5,2},{6,1},{7,0},{8,15},{9,14},{10,... | collective-permute-start | bytes 245768 | tf_op jit(solution)/shard_map/ppermute | solution.py:342
  58.4 9.6 %collective-permute-start.21 = (f32[2,64,128]{2,1,0:T(8,128)S(1)}, f32[2,64,128]{2,1,0:T(8,128)S(1)}, u32[]{:S(2)}, u32[]{:S(2)}) collective-permute-start(f32[2,64,128]{2,1,0:T(8,128)S(1)} %get-tuple-element.76), channel_id=1, source_target_pairs={{1,0},{2,1},{3,2},{4,3},{5,4},{6,5},{7,6},{8,7},{9,8},{10,9},{11,1... | collective-permute-start | bytes 196616 | tf_op jit(solution)/shard_map/ppermute | solution.py:392
  60.4 12.8 %collective-permute-start.10 = (f32[2,4,8,128]{3,2,1,0:T(8,128)S(1)}, f32[2,4,8,128]{3,2,1,0:T(8,128)S(1)}, u32[]{:S(2)}, u32[]{:S(2)}) collective-permute-start(f32[2,4,8,128]{3,2,1,0:T(8,128)S(1)} %get-tuple-element.62), channel_id=1, source_target_pairs={{0,4},{1,5},{2,6},{3,7},{4,0},{5,1},{6,2},{7,3},{8,12},{9,13},{10,... | collective-permute-start | bytes 98312 | tf_op jit(solution)/shard_map/ppermute | solution.py:342
  69.9 14.4 %collective-permute-start.22 = (f32[6,4,8,128]{3,2,1,0:T(8,128)S(1)}, f32[6,4,8,128]{3,2,1,0:T(8,128)S(1)}, u32[]{:S(2)}, u32[]{:S(2)}) collective-permute-start(f32[6,4,8,128]{3,2,1,0:T(8,128)S(1)} %get-tuple-element.79), channel_id=1, source_target_pairs={{0,1},{1,0},{2,3},{3,2},{4,5},{5,4},{6,7},{7,6},{8,9},{9,8},{10,11... | collective-permute-start | bytes 294920 | tf_op jit(solution)/shard_map/ppermute | solution.py:342
  69.9 15.2 %collective-permute-start.23 = (f32[6,4,8,128]{3,2,1,0:T(8,128)S(1)}, f32[6,4,8,128]{3,2,1,0:T(8,128)S(1)}, u32[]{:S(2)}, u32[]{:S(2)}) collective-permute-start(f32[6,4,8,128]{3,2,1,0:T(8,128)S(1)} %get-tuple-element.80), channel_id=1, source_target_pairs={{0,2},{1,3},{2,0},{3,1},{4,6},{5,7},{6,4},{7,5},{8,10},{9,11},{10,... | collective-permute-start | bytes 294920 | tf_op jit(solution)/shard_map/ppermute | solution.py:342
  69.9 5.6 %collective-permute-start.11 = (f32[2,4,8,128]{3,2,1,0:T(8,128)S(1)}, f32[2,4,8,128]{3,2,1,0:T(8,128)S(1)}, u32[]{:S(2)}, u32[]{:S(2)}) collective-permute-start(f32[2,4,8,128]{3,2,1,0:T(8,128)S(1)} %get-tuple-element.63), channel_id=1, source_target_pairs={{0,5},{1,4},{2,7},{3,6},{4,1},{5,0},{6,3},{7,2},{8,13},{9,12},{10,... | collective-permute-start | bytes 98312 | tf_op jit(solution)/shard_map/ppermute | solution.py:342
  73.3 5.6 %collective-permute-start.13 = (f32[2,4,8,128]{3,2,1,0:T(8,128)S(1)}, f32[2,4,8,128]{3,2,1,0:T(8,128)S(1)}, u32[]{:S(2)}, u32[]{:S(2)}) collective-permute-start(f32[2,4,8,128]{3,2,1,0:T(8,128)S(1)} %get-tuple-element.65), channel_id=1, source_target_pairs={{0,7},{1,6},{2,5},{3,4},{4,3},{5,2},{6,1},{7,0},{8,15},{9,14},{10,... | collective-permute-start | bytes 98312 | tf_op jit(solution)/shard_map/ppermute | solution.py:342
  79.9 7.2 %collective-permute-start.24 = (f32[6,4,8,128]{3,2,1,0:T(8,128)S(1)}, f32[6,4,8,128]{3,2,1,0:T(8,128)S(1)}, u32[]{:S(2)}, u32[]{:S(2)}) collective-permute-start(f32[6,4,8,128]{3,2,1,0:T(8,128)S(1)} %get-tuple-element.81), channel_id=1, source_target_pairs={{0,3},{1,2},{2,1},{3,0},{4,7},{5,6},{6,5},{7,4},{8,11},{9,10},{10,... | collective-permute-start | bytes 294920 | tf_op jit(solution)/shard_map/ppermute | solution.py:342
  80.6 12.9 %collective-permute-start.25 = (f32[6,4,8,128]{3,2,1,0:T(8,128)S(1)}, f32[6,4,8,128]{3,2,1,0:T(8,128)S(1)}, u32[]{:S(2)}, u32[]{:S(2)}) collective-permute-start(f32[6,4,8,128]{3,2,1,0:T(8,128)S(1)} %get-tuple-element.82), channel_id=1, source_target_pairs={{0,4},{1,5},{2,6},{3,7},{4,0},{5,1},{6,2},{7,3},{8,12},{9,13},{10,... | collective-permute-start | bytes 294920 | tf_op jit(solution)/shard_map/ppermute | solution.py:342
  82.8 12.8 %collective-permute-start.26 = (f32[6,4,8,128]{3,2,1,0:T(8,128)S(1)}, f32[6,4,8,128]{3,2,1,0:T(8,128)S(1)}, u32[]{:S(2)}, u32[]{:S(2)}) collective-permute-start(f32[6,4,8,128]{3,2,1,0:T(8,128)S(1)} %get-tuple-element.83), channel_id=1, source_target_pairs={{0,5},{1,4},{2,7},{3,6},{4,1},{5,0},{6,3},{7,2},{8,13},{9,12},{10,... | collective-permute-start | bytes 294920 | tf_op jit(solution)/shard_map/ppermute | solution.py:342
  84.4 14.1 %collective-permute-start.27 = (f32[6,4,8,128]{3,2,1,0:T(8,128)S(1)}, f32[6,4,8,128]{3,2,1,0:T(8,128)S(1)}, u32[]{:S(2)}, u32[]{:S(2)}) collective-permute-start(f32[6,4,8,128]{3,2,1,0:T(8,128)S(1)} %get-tuple-element.84), channel_id=1, source_target_pairs={{0,6},{1,7},{2,4},{3,5},{4,2},{5,3},{6,0},{7,1},{8,14},{9,15},{10,... | collective-permute-start | bytes 294920 | tf_op jit(solution)/shard_map/ppermute | solution.py:342
  85.1 16.6 %collective-permute-start.28 = (f32[6,4,8,128]{3,2,1,0:T(8,128)S(1)}, f32[6,4,8,128]{3,2,1,0:T(8,128)S(1)}, u32[]{:S(2)}, u32[]{:S(2)}) collective-permute-start(f32[6,4,8,128]{3,2,1,0:T(8,128)S(1)} %get-tuple-element.85), channel_id=1, source_target_pairs={{0,7},{1,6},{2,5},{3,4},{4,3},{5,2},{6,1},{7,0},{8,15},{9,14},{10,... | collective-permute-start | bytes 294920 | tf_op jit(solution)/shard_map/ppermute | solution.py:342
  (27 other events, 362.9 us)

commit v2 on v1

--- a/solution.py
+++ b/solution.py
@@ -39,13 +39,8 @@
 
 
 def pack_fields_kernel(cfg, me_ref, ids_ref, face_ref, *refs):
-    outs, tile_ref, sem, id_sem = refs[: cfg.n], refs[cfg.n], refs[cfg.n + 1], refs[cfg.n + 2]
+    outs, sem = refs[: cfg.n], refs[cfg.n]
     me = me_ref[0]
-    rows = lax.broadcasted_iota(jnp.int32, (SUB, LANES), 0)
-    ids = jnp.zeros((SUB, LANES), jnp.int32)
-    for slot in range(SUB):
-        ids = jnp.where(rows == slot, ids_ref[slot], ids)
-    tile_ref[...] = ids.astype(F32)[None]
     copies = []
     for k in range(cfg.n):
         dest = jnp.bitwise_xor(me, k)
@@ -57,11 +52,14 @@
                     sem.at[k * 3 + c],
                 )
             )
-        copies.append(
-            pltpu.make_async_copy(tile_ref, outs[k].at[pl.ds(3 * cfg.tiles, 1)], id_sem.at[k])
-        )
     for copy in copies:
         copy.start()
+    rows = lax.broadcasted_iota(jnp.int32, (SUB, LANES), 0)
+    ids = jnp.zeros((SUB, LANES), jnp.int32)
+    for slot in range(SUB):
+        ids = jnp.where(rows == slot, ids_ref[slot], ids)
+    for k in range(cfg.n):
+        outs[k][3 * cfg.tiles] = ids.astype(F32)
     for copy in copies:
         copy.wait()
 
@@ -346,12 +344,8 @@
         functools.partial(pack_fields_kernel, cfg),
         out_shape=[shape(3 * tiles + 1, SUB, LANES)] * n,
         in_specs=[smem, smem, anywhere],
-        out_specs=[anywhere] * n,
-        scratch_shapes=[
-            pltpu.VMEM((1, SUB, LANES), F32),
-            pltpu.SemaphoreType.DMA((3 * n,)),
-            pltpu.SemaphoreType.DMA((n,)),
-        ],
+        out_specs=[vmem] * n,
+        scratch_shapes=[pltpu.SemaphoreType.DMA((3 * n,))],
         name="pack_fields",
     )(me, block_ids, tiled(face_field))
     fields = exchange(sent)
@@ -359,7 +353,7 @@
         functools.partial(pack_conserved_kernel, cfg),
         out_shape=[shape(5, tiles, SUB, LANES)] * n,
         in_specs=[smem, anywhere],
-        out_specs=[anywhere] * n,
+        out_specs=[vmem] * n,
         scratch_shapes=[pltpu.SemaphoreType.DMA((n,))],
         name="pack_conserved",
     )(me, tiled(conserved))
@@ -411,7 +405,7 @@
     conserved_out, field_out = pl.pallas_call(
         functools.partial(unpack_kernel, cfg),
         out_shape=[shape(5, n * tiles, SUB, LANES), shape(3, n * tiles, SUB, LANES)],
-        in_specs=[smem] + [anywhere] * (2 * n),
+        in_specs=[smem] + [vmem] * (2 * n),
         out_specs=[anywhere] * 2,
         scratch_shapes=[pltpu.SemaphoreType.DMA((n, 3))],
         name="unpack",

time: 136 us -> 75.2 us (0.55)
  Pallas kernels: 73.7 us -> 12.7 us
    pallas_call x1, Pallas kernels: 33.1 us -> 2.45 us  [shards(): pl.pallas_call(functools.partial(unpack_kernel, cfg), out_shape=[shape(5,...]
    pallas_call x1, Pallas kernels: 21 us -> 2.07 us  [shards(): pl.pallas_call(functools.partial(pack_conserved_kernel, cfg), out_shape=[...]
    pallas_call x1, Pallas kernels: 14 us -> 2.58 us  [shards(): pl.pallas_call(functools.partial(pack_fields_kernel, cfg), out_shape=[sha...]
  transfers between devices with their start and end apart: 29 -> 29, of which waited for: 10 -> 9; matrix products, arithmetic and copies ran while one was open for 0% -> 0% of each run, Pallas kernels for 20% -> 10%
where the time goes in v2:
time: 75.2 us; the launch traced here: 74 us
  starting transfers between devices  36.1 us (48%)
  waiting for transfers between devices  23 us (31%)
  Pallas kernels  12.7 us (17%)
  local copies, waits for them, and re-layouts  1.24 us (2%)
  between operations  0.86 us (1%)
    ppermute x28, starting transfers between devices, exchange(): lax.ppermute(pieces[k], 'phi', [(s, s ^ k) for s in range(n)])  33.9 us
    ppermute x28, waiting for transfers between devices, exchange(): lax.ppermute(pieces[k], 'phi', [(s, s ^ k) for s in range(n)])  21.8 us
    pallas_call x1, Pallas kernels, shards(): pl.pallas_call(functools.partial(pack_fields_kernel, cfg), out_shape=[sha...  2.58 us
    pallas_call x1, Pallas kernels, shards(): pl.pallas_call(functools.partial(unpack_kernel, cfg), out_shape=[shape(5,...  2.45 us
    pallas_call x1, Pallas kernels, shards(): pl.pallas_call(functools.partial(operators_kernel, cfg), out_shape=[squar...  2.24 us
    ppermute x1, starting transfers between devices, shards(): lax.ppermute(halo, ('tile', 'phi'), [(s, s - cfg.split) for s in range(cf...  2.22 us
    pallas_call x1, Pallas kernels, shards(): pl.pallas_call(functools.partial(fields_kernel, cfg), out_shape=[shape(2,...  2.09 us
    pallas_call x1, Pallas kernels, shards(): pl.pallas_call(functools.partial(pack_conserved_kernel, cfg), out_shape=[...  2.07 us
  transfers between devices with their start and end apart: 29, of which 9 were waited for; matrix products, arithmetic and copies ran while one was open for 0% of the time, Pallas kernels for 10%

profile of v2, /device:TPU:13, one launch (start us, length us, event | category | flops | bytes accessed | tf_op | source)
XLA Modules:
  0.0 74.0 jit_solution(11962681354132892901)
XLA Ops:
  0.6 2.6 %pack_fields.1 = (f32[13,8,128]{2,1,0:T(8,128)}, f32[13,8,128]{2,1,0:T(8,128)}, f32[13,8,128]{2,1,0:T(8,128)}, f32[13,8,128]{2,1,0:T(8,128)}, f32[13,8,128]{2,1,...) custom-call(s32[1]{0:T(128)} %bitcast.me_ref, s32[8]{0:T(128)} %ids_ref.1, ...), custom_call_target="tpu_custom_call" | custom-call | tf_op jit(solution)/shard_map/pack_fields/pallas_call | solution.py:343
  4.2 1.5 %collective-permute-start.2 = (f32[13,8,128]{2,1,0:T(8,128)}, f32[13,8,128]{2,1,0:T(8,128)S(1)}, u32[]{:S(2)}, u32[]{:S(2)}) collective-permute-start(f32[13,8,128]{2,1,0:T(8,128)} %get-tuple-element.48), channel_id=1, source_target_pairs={{0,3},{1,2},{2,1},{3,0},{4,7},{5,6},{6,5},{7,4},{8,11},{9,10},{10,... | collective-permute-start | bytes 159752 | tf_op jit(solution)/shard_map/ppermute | solution.py:340
  5.7 2.3 %collective-permute-start.3 = (f32[13,8,128]{2,1,0:T(8,128)}, f32[13,8,128]{2,1,0:T(8,128)S(1)}, u32[]{:S(2)}, u32[]{:S(2)}) collective-permute-start(f32[13,8,128]{2,1,0:T(8,128)} %get-tuple-element.49), channel_id=1, source_target_pairs={{0,4},{1,5},{2,6},{3,7},{4,0},{5,1},{6,2},{7,3},{8,12},{9,13},{10,... | collective-permute-start | bytes 159752 | tf_op jit(solution)/shard_map/ppermute | solution.py:340
  8.4 2.1 %pack_conserved.1 = (f32[5,4,8,128]{3,2,1,0:T(8,128)}, f32[5,4,8,128]{3,2,1,0:T(8,128)}, f32[5,4,8,128]{3,2,1,0:T(8,128)}, f32[5,4,8,128]{3,2,1,0:T(8,128)}, f32...) custom-call(s32[1]{0:T(128)} %bitcast.me_ref, ...), custom_call_target="tpu_custom_call" | custom-call | tf_op jit(solution)/shard_map/pack_conserved/pallas_call | solution.py:352
  10.8 1.9 %collective-permute-start.16 = (f32[5,4,8,128]{3,2,1,0:T(8,128)}, f32[5,4,8,128]{3,2,1,0:T(8,128)S(1)}, u32[]{:S(2)}, u32[]{:S(2)}) collective-permute-start(f32[5,4,8,128]{3,2,1,0:T(8,128)} %get-tuple-element.69), channel_id=1, source_target_pairs={{0,3},{1,2},{2,1},{3,0},{4,7},{5,6},{6,5},{7,4},{8,11},{9,10},{10,... | collective-permute-start | bytes 245768 | tf_op jit(solution)/shard_map/ppermute | solution.py:340
  14.2 2.0 %collective-permute-done.5.refs_6_ = f32[13,8,128]{2,1,0:T(8,128)S(1)} collective-permute-done((f32[13,8,128]{2,1,0:T(8,128)S(1)}, f32[13,8,128]{2,1,0:T(8,128)S(1)}, u32[]{:S(2)}, u32[]{:S(2)}) %collective-permute-start.5) | collective-permute-done | bytes 53280 | tf_op jit(solution)/shard_map/ppermute | solution.py:340
  16.2 3.8 %collective-permute-start.17 = (f32[5,4,8,128]{3,2,1,0:T(8,128)}, f32[5,4,8,128]{3,2,1,0:T(8,128)S(1)}, u32[]{:S(2)}, u32[]{:S(2)}) collective-permute-start(f32[5,4,8,128]{3,2,1,0:T(8,128)} %get-tuple-element.70), channel_id=1, source_target_pairs={{0,4},{1,5},{2,6},{3,7},{4,0},{5,1},{6,2},{7,3},{8,12},{9,13},{10,... | collective-permute-start | bytes 245768 | tf_op jit(solution)/shard_map/ppermute | solution.py:340
  20.0 2.3 %collective-permute-start.18 = (f32[5,4,8,128]{3,2,1,0:T(8,128)}, f32[5,4,8,128]{3,2,1,0:T(8,128)S(1)}, u32[]{:S(2)}, u32[]{:S(2)}) collective-permute-start(f32[5,4,8,128]{3,2,1,0:T(8,128)} %get-tuple-element.71), channel_id=1, source_target_pairs={{0,5},{1,4},{2,7},{3,6},{4,1},{5,0},{6,3},{7,2},{8,13},{9,12},{10,... | collective-permute-start | bytes 245768 | tf_op jit(solution)/shard_map/ppermute | solution.py:340
  22.4 1.6 %collective-permute-start.19 = (f32[5,4,8,128]{3,2,1,0:T(8,128)}, f32[5,4,8,128]{3,2,1,0:T(8,128)S(1)}, u32[]{:S(2)}, u32[]{:S(2)}) collective-permute-start(f32[5,4,8,128]{3,2,1,0:T(8,128)} %get-tuple-element.72), channel_id=1, source_target_pairs={{0,6},{1,7},{2,4},{3,5},{4,2},{5,3},{6,0},{7,1},{8,14},{9,15},{10,... | collective-permute-start | bytes 245768 | tf_op jit(solution)/shard_map/ppermute | solution.py:340
  24.1 2.2 %operators.1 = (bf16[2,3,256,256]{3,2,1,0:T(8,128)(2,1)S(1)}, bf16[2,3,256,256]{3,2,1,0:T(8,128)(2,1)S(1)}, bf16[2,3,256,256]{3,2,1,0:T(8,128)(2,1)S(1)}, bf16[2...) custom-call(s32[1]{0:T(128)} %bitcast.me_ref, s32[16]{0:T(128)S(1)} %copy-done.4, f32[16]{0:T(128)S(1)} %copy-done.5), custom_call_target="tpu_custom_call" | custom-call | tf_op jit(solution)/shard_map/operators/pallas_call | solution.py:363
  26.4 2.1 %fields.1 = (f32[2,4,8,128]{3,2,1,0:T(8,128)S(1)}, f32[2,4,8,128]{3,2,1,0:T(8,128)S(1)}, f32[2,4,8,128]{3,2,1,0:T(8,128)S(1)}, f32[2,4,8,128]{3,2,1,0:T(8,128)S(...) custom-call(s32[1]{0:T(128)} %bitcast.me_ref, ...), custom_call_target="tpu_custom_call" | custom-call | tf_op jit(solution)/shard_map/fields/pallas_call | solution.py:372
  28.5 2.2 %collective-permute-start.21 = (f32[2,64,128]{2,1,0:T(8,128)S(1)}, f32[2,64,128]{2,1,0:T(8,128)S(1)}, u32[]{:S(2)}, u32[]{:S(2)}) collective-permute-start(f32[2,64,128]{2,1,0:T(8,128)S(1)} %get-tuple-element.76), channel_id=1, source_target_pairs={{1,0},{2,1},{3,2},{4,3},{5,4},{6,5},{7,6},{8,7},{9,8},{10,9},{11,1... | collective-permute-start | bytes 196616 | tf_op jit(solution)/shard_map/ppermute | solution.py:386
  30.7 3.5 %collective-permute-start.10 = (f32[2,4,8,128]{3,2,1,0:T(8,128)S(1)}, f32[2,4,8,128]{3,2,1,0:T(8,128)S(1)}, u32[]{:S(2)}, u32[]{:S(2)}) collective-permute-start(f32[2,4,8,128]{3,2,1,0:T(8,128)S(1)} %get-tuple-element.62), channel_id=1, source_target_pairs={{0,4},{1,5},{2,6},{3,7},{4,0},{5,1},{6,2},{7,3},{8,12},{9,13},{10,... | collective-permute-start | bytes 98312 | tf_op jit(solution)/shard_map/ppermute | solution.py:340
  34.3 2.3 %collective-permute-done.20.refs_7_ = f32[5,4,8,128]{3,2,1,0:T(8,128)S(1)} collective-permute-done((f32[5,4,8,128]{3,2,1,0:T(8,128)}, f32[5,4,8,128]{3,2,1,0:T(8,128)S(1)}, u32[]{:S(2)}, u32[]{:S(2)}) %collective-permute-start.20) | collective-permute-done | bytes 81952 | tf_op jit(solution)/shard_map/ppermute | solution.py:340
  41.3 1.9 %collective-permute-start.12 = (f32[2,4,8,128]{3,2,1,0:T(8,128)S(1)}, f32[2,4,8,128]{3,2,1,0:T(8,128)S(1)}, u32[]{:S(2)}, u32[]{:S(2)}) collective-permute-start(f32[2,4,8,128]{3,2,1,0:T(8,128)S(1)} %get-tuple-element.64), channel_id=1, source_target_pairs={{0,6},{1,7},{2,4},{3,5},{4,2},{5,3},{6,0},{7,1},{8,14},{9,15},{10,... | collective-permute-start | bytes 98312 | tf_op jit(solution)/shard_map/ppermute | solution.py:340
  43.2 1.6 %collective-permute-done.11.refs_5_ = f32[2,4,8,128]{3,2,1,0:T(8,128)S(1)} collective-permute-done((f32[2,4,8,128]{3,2,1,0:T(8,128)S(1)}, f32[2,4,8,128]{3,2,1,0:T(8,128)S(1)}, u32[]{:S(2)}, u32[]{:S(2)}) %collective-permute-start.11) | collective-permute-done | bytes 32800 | tf_op jit(solution)/shard_map/ppermute | solution.py:340
  46.2 1.9 %collective-permute-start.8 = (f32[2,4,8,128]{3,2,1,0:T(8,128)S(1)}, f32[2,4,8,128]{3,2,1,0:T(8,128)S(1)}, u32[]{:S(2)}, u32[]{:S(2)}) collective-permute-start(f32[2,4,8,128]{3,2,1,0:T(8,128)S(1)} %get-tuple-element.60), channel_id=1, source_target_pairs={{0,2},{1,3},{2,0},{3,1},{4,6},{5,7},{6,4},{7,5},{8,10},{9,11},{10,... | collective-permute-start | bytes 98312 | tf_op jit(solution)/shard_map/ppermute | solution.py:340
  49.8 2.2 %collective-permute-start.25 = (f32[6,4,8,128]{3,2,1,0:T(8,128)S(1)}, f32[6,4,8,128]{3,2,1,0:T(8,128)S(1)}, u32[]{:S(2)}, u32[]{:S(2)}) collective-permute-start(f32[6,4,8,128]{3,2,1,0:T(8,128)S(1)} %get-tuple-element.82), channel_id=1, source_target_pairs={{0,4},{1,5},{2,6},{3,7},{4,0},{5,1},{6,2},{7,3},{8,12},{9,13},{10,... | collective-permute-start | bytes 294920 | tf_op jit(solution)/shard_map/ppermute | solution.py:340
  54.7 1.5 %collective-permute-start.28 = (f32[6,4,8,128]{3,2,1,0:T(8,128)S(1)}, f32[6,4,8,128]{3,2,1,0:T(8,128)S(1)}, u32[]{:S(2)}, u32[]{:S(2)}) collective-permute-start(f32[6,4,8,128]{3,2,1,0:T(8,128)S(1)} %get-tuple-element.85), channel_id=1, source_target_pairs={{0,7},{1,6},{2,5},{3,4},{4,3},{5,2},{6,1},{7,0},{8,15},{9,14},{10,... | collective-permute-start | bytes 294920 | tf_op jit(solution)/shard_map/ppermute | solution.py:340
  56.3 6.0 %collective-permute-done.25.refs_12_ = f32[6,4,8,128]{3,2,1,0:T(8,128)S(1)} collective-permute-done((f32[6,4,8,128]{3,2,1,0:T(8,128)S(1)}, f32[6,4,8,128]{3,2,1,0:T(8,128)S(1)}, u32[]{:S(2)}, u32[]{:S(2)}) %collective-permute-start.25) | collective-permute-done | bytes 98336 | tf_op jit(solution)/shard_map/ppermute | solution.py:340
  62.3 2.2 %collective-permute-done.26.refs_13_ = f32[6,4,8,128]{3,2,1,0:T(8,128)S(1)} collective-permute-done((f32[6,4,8,128]{3,2,1,0:T(8,128)S(1)}, f32[6,4,8,128]{3,2,1,0:T(8,128)S(1)}, u32[]{:S(2)}, u32[]{:S(2)}) %collective-permute-start.26) | collective-permute-done | bytes 98336 | tf_op jit(solution)/shard_map/ppermute | solution.py:340
  64.6 3.2 %collective-permute-done.27.refs_14_ = f32[6,4,8,128]{3,2,1,0:T(8,128)S(1)} collective-permute-done((f32[6,4,8,128]{3,2,1,0:T(8,128)S(1)}, f32[6,4,8,128]{3,2,1,0:T(8,128)S(1)}, u32[]{:S(2)}, u32[]{:S(2)}) %collective-permute-start.27) | collective-permute-done | bytes 98336 | tf_op jit(solution)/shard_map/ppermute | solution.py:340
  67.7 3.2 %collective-permute-done.28.refs_15_ = f32[6,4,8,128]{3,2,1,0:T(8,128)S(1)} collective-permute-done((f32[6,4,8,128]{3,2,1,0:T(8,128)S(1)}, f32[6,4,8,128]{3,2,1,0:T(8,128)S(1)}, u32[]{:S(2)}, u32[]{:S(2)}) %collective-permute-start.28) | collective-permute-done | bytes 98336 | tf_op jit(solution)/shard_map/ppermute | solution.py:340
  71.5 2.4 %unpack.1 = (f32[5,32,8,128]{3,2,1,0:T(8,128)}, f32[3,32,8,128]{3,2,1,0:T(8,128)}) custom-call(s32[1]{0:T(128)} %bitcast.me_ref, f32[2,4,8,128]{3,2,1,0:T(8,128)} %copy-done.3, f32[2,4,8,128]{3,2,1,0:T(8,128)} %copy-done.17, f32[2,4,8,128]{3,2,1,0:T(8,128)} %copy-done.18, f32[2,4,8,128]{3,2,1,0:T(8,128)} %copy-done.19, f32[2,4,8,128]{3,2,1,0:T(8,128)} %copy-done.13, ...), custom_call_target="tpu_custom_call" | custom-call | tf_op jit(solution)/shard_map/unpack/pallas_call | solution.py:405
  (84 shorter events, 14.5 us)
Async XLA Ops:
  3.2 7.2 %collective-permute-start = (f32[13,8,128]{2,1,0:T(8,128)}, f32[13,8,128]{2,1,0:T(8,128)S(1)}, u32[]{:S(2)}, u32[]{:S(2)}) collective-permute-start(f32[13,8,128]{2,1,0:T(8,128)} %get-tuple-element.46), channel_id=1, source_target_pairs={{0,1},{1,0},{2,3},{3,2},{4,5},{5,4},{6,7},{7,6},{8,9},{9,8},{10,11... | collective-permute-start | bytes 159752 | tf_op jit(solution)/shard_map/ppermute | solution.py:340
  4.0 6.7 %collective-permute-start.1 = (f32[13,8,128]{2,1,0:T(8,128)}, f32[13,8,128]{2,1,0:T(8,128)S(1)}, u32[]{:S(2)}, u32[]{:S(2)}) collective-permute-start(f32[13,8,128]{2,1,0:T(8,128)} %get-tuple-element.47), channel_id=1, source_target_pairs={{0,2},{1,3},{2,0},{3,1},{4,6},{5,7},{6,4},{7,5},{8,10},{9,11},{10,... | collective-permute-start | bytes 159752 | tf_op jit(solution)/shard_map/ppermute | solution.py:340
  4.2 6.7 %collective-permute-start.2 = (f32[13,8,128]{2,1,0:T(8,128)}, f32[13,8,128]{2,1,0:T(8,128)S(1)}, u32[]{:S(2)}, u32[]{:S(2)}) collective-permute-start(f32[13,8,128]{2,1,0:T(8,128)} %get-tuple-element.48), channel_id=1, source_target_pairs={{0,3},{1,2},{2,1},{3,0},{4,7},{5,6},{6,5},{7,4},{8,11},{9,10},{10,... | collective-permute-start | bytes 159752 | tf_op jit(solution)/shard_map/ppermute | solution.py:340
  5.7 7.0 %collective-permute-start.3 = (f32[13,8,128]{2,1,0:T(8,128)}, f32[13,8,128]{2,1,0:T(8,128)S(1)}, u32[]{:S(2)}, u32[]{:S(2)}) collective-permute-start(f32[13,8,128]{2,1,0:T(8,128)} %get-tuple-element.49), channel_id=1, source_target_pairs={{0,4},{1,5},{2,6},{3,7},{4,0},{5,1},{6,2},{7,3},{8,12},{9,13},{10,... | collective-permute-start | bytes 159752 | tf_op jit(solution)/shard_map/ppermute | solution.py:340
  8.0 6.0 %collective-permute-start.4 = (f32[13,8,128]{2,1,0:T(8,128)}, f32[13,8,128]{2,1,0:T(8,128)S(1)}, u32[]{:S(2)}, u32[]{:S(2)}) collective-permute-start(f32[13,8,128]{2,1,0:T(8,128)} %get-tuple-element.50), channel_id=1, source_target_pairs={{0,5},{1,4},{2,7},{3,6},{4,1},{5,0},{6,3},{7,2},{8,13},{9,12},{10,... | collective-permute-start | bytes 159752 | tf_op jit(solution)/shard_map/ppermute | solution.py:340
  10.5 11.9 %collective-permute-start.14 = (f32[5,4,8,128]{3,2,1,0:T(8,128)}, f32[5,4,8,128]{3,2,1,0:T(8,128)S(1)}, u32[]{:S(2)}, u32[]{:S(2)}) collective-permute-start(f32[5,4,8,128]{3,2,1,0:T(8,128)} %get-tuple-element.67), channel_id=1, source_target_pairs={{0,1},{1,0},{2,3},{3,2},{4,5},{5,4},{6,7},{7,6},{8,9},{9,8},{10,11... | collective-permute-start | bytes 245768 | tf_op jit(solution)/shard_map/ppermute | solution.py:340
  10.6 13.3 %collective-permute-start.15 = (f32[5,4,8,128]{3,2,1,0:T(8,128)}, f32[5,4,8,128]{3,2,1,0:T(8,128)S(1)}, u32[]{:S(2)}, u32[]{:S(2)}) collective-permute-start(f32[5,4,8,128]{3,2,1,0:T(8,128)} %get-tuple-element.68), channel_id=1, source_target_pairs={{0,2},{1,3},{2,0},{3,1},{4,6},{5,7},{6,4},{7,5},{8,10},{9,11},{10,... | collective-permute-start | bytes 245768 | tf_op jit(solution)/shard_map/ppermute | solution.py:340
  10.8 17.7 %collective-permute-start.16 = (f32[5,4,8,128]{3,2,1,0:T(8,128)}, f32[5,4,8,128]{3,2,1,0:T(8,128)S(1)}, u32[]{:S(2)}, u32[]{:S(2)}) collective-permute-start(f32[5,4,8,128]{3,2,1,0:T(8,128)} %get-tuple-element.69), channel_id=1, source_target_pairs={{0,3},{1,2},{2,1},{3,0},{4,7},{5,6},{6,5},{7,4},{8,11},{9,10},{10,... | collective-permute-start | bytes 245768 | tf_op jit(solution)/shard_map/ppermute | solution.py:340
  14.0 6.0 %collective-permute-start.6 = (f32[13,8,128]{2,1,0:T(8,128)S(1)}, f32[13,8,128]{2,1,0:T(8,128)S(1)}, u32[]{:S(2)}, u32[]{:S(2)}) collective-permute-start(f32[13,8,128]{2,1,0:T(8,128)S(1)} %copy-done.20), channel_id=1, source_target_pairs={{0,7},{1,6},{2,5},{3,4},{4,3},{5,2},{6,1},{7,0},{8,15},{9,14},{10,... | collective-permute-start | bytes 159752 | tf_op jit(solution)/shard_map/ppermute | solution.py:340
  16.2 14.5 %collective-permute-start.17 = (f32[5,4,8,128]{3,2,1,0:T(8,128)}, f32[5,4,8,128]{3,2,1,0:T(8,128)S(1)}, u32[]{:S(2)}, u32[]{:S(2)}) collective-permute-start(f32[5,4,8,128]{3,2,1,0:T(8,128)} %get-tuple-element.70), channel_id=1, source_target_pairs={{0,4},{1,5},{2,6},{3,7},{4,0},{5,1},{6,2},{7,3},{8,12},{9,13},{10,... | collective-permute-start | bytes 245768 | tf_op jit(solution)/shard_map/ppermute | solution.py:340
  20.0 14.2 %collective-permute-start.18 = (f32[5,4,8,128]{3,2,1,0:T(8,128)}, f32[5,4,8,128]{3,2,1,0:T(8,128)S(1)}, u32[]{:S(2)}, u32[]{:S(2)}) collective-permute-start(f32[5,4,8,128]{3,2,1,0:T(8,128)} %get-tuple-element.71), channel_id=1, source_target_pairs={{0,5},{1,4},{2,7},{3,6},{4,1},{5,0},{6,3},{7,2},{8,13},{9,12},{10,... | collective-permute-start | bytes 245768 | tf_op jit(solution)/shard_map/ppermute | solution.py:340
  22.4 11.9 %collective-permute-start.19 = (f32[5,4,8,128]{3,2,1,0:T(8,128)}, f32[5,4,8,128]{3,2,1,0:T(8,128)S(1)}, u32[]{:S(2)}, u32[]{:S(2)}) collective-permute-start(f32[5,4,8,128]{3,2,1,0:T(8,128)} %get-tuple-element.72), channel_id=1, source_target_pairs={{0,6},{1,7},{2,4},{3,5},{4,2},{5,3},{6,0},{7,1},{8,14},{9,15},{10,... | collective-permute-start | bytes 245768 | tf_op jit(solution)/shard_map/ppermute | solution.py:340
  23.9 12.7 %collective-permute-start.20 = (f32[5,4,8,128]{3,2,1,0:T(8,128)}, f32[5,4,8,128]{3,2,1,0:T(8,128)S(1)}, u32[]{:S(2)}, u32[]{:S(2)}) collective-permute-start(f32[5,4,8,128]{3,2,1,0:T(8,128)} %get-tuple-element.73), channel_id=1, source_target_pairs={{0,7},{1,6},{2,5},{3,4},{4,3},{5,2},{6,1},{7,0},{8,15},{9,14},{10,... | collective-permute-start | bytes 245768 | tf_op jit(solution)/shard_map/ppermute | solution.py:340
  28.5 9.4 %collective-permute-start.21 = (f32[2,64,128]{2,1,0:T(8,128)S(1)}, f32[2,64,128]{2,1,0:T(8,128)S(1)}, u32[]{:S(2)}, u32[]{:S(2)}) collective-permute-start(f32[2,64,128]{2,1,0:T(8,128)S(1)} %get-tuple-element.76), channel_id=1, source_target_pairs={{1,0},{2,1},{3,2},{4,3},{5,4},{6,5},{7,6},{8,7},{9,8},{10,9},{11,1... | collective-permute-start | bytes 196616 | tf_op jit(solution)/shard_map/ppermute | solution.py:386
  30.7 12.4 %collective-permute-start.10 = (f32[2,4,8,128]{3,2,1,0:T(8,128)S(1)}, f32[2,4,8,128]{3,2,1,0:T(8,128)S(1)}, u32[]{:S(2)}, u32[]{:S(2)}) collective-permute-start(f32[2,4,8,128]{3,2,1,0:T(8,128)S(1)} %get-tuple-element.62), channel_id=1, source_target_pairs={{0,4},{1,5},{2,6},{3,7},{4,0},{5,1},{6,2},{7,3},{8,12},{9,13},{10,... | collective-permute-start | bytes 98312 | tf_op jit(solution)/shard_map/ppermute | solution.py:340
  39.9 13.6 %collective-permute-start.22 = (f32[6,4,8,128]{3,2,1,0:T(8,128)S(1)}, f32[6,4,8,128]{3,2,1,0:T(8,128)S(1)}, u32[]{:S(2)}, u32[]{:S(2)}) collective-permute-start(f32[6,4,8,128]{3,2,1,0:T(8,128)S(1)} %get-tuple-element.79), channel_id=1, source_target_pairs={{0,1},{1,0},{2,3},{3,2},{4,5},{5,4},{6,7},{7,6},{8,9},{9,8},{10,11... | collective-permute-start | bytes 294920 | tf_op jit(solution)/shard_map/ppermute | solution.py:340
  39.9 14.9 %collective-permute-start.23 = (f32[6,4,8,128]{3,2,1,0:T(8,128)S(1)}, f32[6,4,8,128]{3,2,1,0:T(8,128)S(1)}, u32[]{:S(2)}, u32[]{:S(2)}) collective-permute-start(f32[6,4,8,128]{3,2,1,0:T(8,128)S(1)} %get-tuple-element.80), channel_id=1, source_target_pairs={{0,2},{1,3},{2,0},{3,1},{4,6},{5,7},{6,4},{7,5},{8,10},{9,11},{10,... | collective-permute-start | bytes 294920 | tf_op jit(solution)/shard_map/ppermute | solution.py:340
  39.9 4.9 %collective-permute-start.11 = (f32[2,4,8,128]{3,2,1,0:T(8,128)S(1)}, f32[2,4,8,128]{3,2,1,0:T(8,128)S(1)}, u32[]{:S(2)}, u32[]{:S(2)}) collective-permute-start(f32[2,4,8,128]{3,2,1,0:T(8,128)S(1)} %get-tuple-element.63), channel_id=1, source_target_pairs={{0,5},{1,4},{2,7},{3,6},{4,1},{5,0},{6,3},{7,2},{8,13},{9,12},{10,... | collective-permute-start | bytes 98312 | tf_op jit(solution)/shard_map/ppermute | solution.py:340
  43.2 4.9 %collective-permute-start.13 = (f32[2,4,8,128]{3,2,1,0:T(8,128)S(1)}, f32[2,4,8,128]{3,2,1,0:T(8,128)S(1)}, u32[]{:S(2)}, u32[]{:S(2)}) collective-permute-start(f32[2,4,8,128]{3,2,1,0:T(8,128)S(1)} %get-tuple-element.65), channel_id=1, source_target_pairs={{0,7},{1,6},{2,5},{3,4},{4,3},{5,2},{6,1},{7,0},{8,15},{9,14},{10,... | collective-permute-start | bytes 98312 | tf_op jit(solution)/shard_map/ppermute | solution.py:340
  49.2 7.1 %collective-permute-start.24 = (f32[6,4,8,128]{3,2,1,0:T(8,128)S(1)}, f32[6,4,8,128]{3,2,1,0:T(8,128)S(1)}, u32[]{:S(2)}, u32[]{:S(2)}) collective-permute-start(f32[6,4,8,128]{3,2,1,0:T(8,128)S(1)} %get-tuple-element.81), channel_id=1, source_target_pairs={{0,3},{1,2},{2,1},{3,0},{4,7},{5,6},{6,5},{7,4},{8,11},{9,10},{10,... | collective-permute-start | bytes 294920 | tf_op jit(solution)/shard_map/ppermute | solution.py:340
  49.8 12.5 %collective-permute-start.25 = (f32[6,4,8,128]{3,2,1,0:T(8,128)S(1)}, f32[6,4,8,128]{3,2,1,0:T(8,128)S(1)}, u32[]{:S(2)}, u32[]{:S(2)}) collective-permute-start(f32[6,4,8,128]{3,2,1,0:T(8,128)S(1)} %get-tuple-element.82), channel_id=1, source_target_pairs={{0,4},{1,5},{2,6},{3,7},{4,0},{5,1},{6,2},{7,3},{8,12},{9,13},{10,... | collective-permute-start | bytes 294920 | tf_op jit(solution)/shard_map/ppermute | solution.py:340
  52.0 12.5 %collective-permute-start.26 = (f32[6,4,8,128]{3,2,1,0:T(8,128)S(1)}, f32[6,4,8,128]{3,2,1,0:T(8,128)S(1)}, u32[]{:S(2)}, u32[]{:S(2)}) collective-permute-start(f32[6,4,8,128]{3,2,1,0:T(8,128)S(1)} %get-tuple-element.83), channel_id=1, source_target_pairs={{0,5},{1,4},{2,7},{3,6},{4,1},{5,0},{6,3},{7,2},{8,13},{9,12},{10,... | collective-permute-start | bytes 294920 | tf_op jit(solution)/shard_map/ppermute | solution.py:340
  53.5 14.2 %collective-permute-start.27 = (f32[6,4,8,128]{3,2,1,0:T(8,128)S(1)}, f32[6,4,8,128]{3,2,1,0:T(8,128)S(1)}, u32[]{:S(2)}, u32[]{:S(2)}) collective-permute-start(f32[6,4,8,128]{3,2,1,0:T(8,128)S(1)} %get-tuple-element.84), channel_id=1, source_target_pairs={{0,6},{1,7},{2,4},{3,5},{4,2},{5,3},{6,0},{7,1},{8,14},{9,15},{10,... | collective-permute-start | bytes 294920 | tf_op jit(solution)/shard_map/ppermute | solution.py:340
  54.7 16.2 %collective-permute-start.28 = (f32[6,4,8,128]{3,2,1,0:T(8,128)S(1)}, f32[6,4,8,128]{3,2,1,0:T(8,128)S(1)}, u32[]{:S(2)}, u32[]{:S(2)}) collective-permute-start(f32[6,4,8,128]{3,2,1,0:T(8,128)S(1)} %get-tuple-element.85), channel_id=1, source_target_pairs={{0,7},{1,6},{2,5},{3,4},{4,3},{5,2},{6,1},{7,0},{8,15},{9,14},{10,... | collective-permute-start | bytes 294920 | tf_op jit(solution)/shard_map/ppermute | solution.py:340
  (27 other events, 305.3 us)

commit v3 on v2

--- a/solution.py
+++ b/solution.py
@@ -38,71 +38,65 @@
     return whole, shift - whole * BS
 
 
-def pack_fields_kernel(cfg, me_ref, ids_ref, face_ref, *refs):
-    outs, sem = refs[: cfg.n], refs[cfg.n]
-    me = me_ref[0]
-    copies = []
-    for k in range(cfg.n):
-        dest = jnp.bitwise_xor(me, k)
-        for c in range(3):
-            copies.append(
-                pltpu.make_async_copy(
-                    face_ref.at[c, pl.ds(dest * cfg.tiles, cfg.tiles)],
-                    outs[k].at[pl.ds(c * cfg.tiles, cfg.tiles)],
-                    sem.at[k * 3 + c],
-                )
-            )
+def start_all(copies):
     for copy in copies:
         copy.start()
+    return copies
+
+
+def wait_all(copies):
+    for copy in copies:
+        copy.wait()
+
+
+def copy_in(cfg, source_ref, count, dest, out_ref, at, sem):
+    return [
+        pltpu.make_async_copy(
+            source_ref.at[c, pl.ds(dest * cfg.tiles, cfg.tiles)],
+            out_ref.at[pl.ds(at + c * cfg.tiles, cfg.tiles)],
+            sem.at[c],
+        )
+        for c in range(count)
+    ]
+
+
+def id_tile(ids_ref):
     rows = lax.broadcasted_iota(jnp.int32, (SUB, LANES), 0)
     ids = jnp.zeros((SUB, LANES), jnp.int32)
     for slot in range(SUB):
         ids = jnp.where(rows == slot, ids_ref[slot], ids)
-    for k in range(cfg.n):
-        outs[k][3 * cfg.tiles] = ids.astype(F32)
-    for copy in copies:
-        copy.wait()
-
-
-def pack_conserved_kernel(cfg, me_ref, conserved_ref, *refs):
+    return ids.astype(F32)
+
+
+def pack_kernel(cfg, me_ref, source_ref, *refs):
     outs, sem = refs[: cfg.n], refs[cfg.n]
-    me = me_ref[0]
     copies = []
-    for k in range(cfg.n):
-        dest = jnp.bitwise_xor(me, k)
-        copies.append(
-            pltpu.make_async_copy(
-                conserved_ref.at[:, pl.ds(dest * cfg.tiles, cfg.tiles)], outs[k], sem.at[k]
+    for out, k in zip(outs, cfg.order):
+        dest = jnp.bitwise_xor(me_ref[0], k)
+        copies += copy_in(cfg, source_ref, source_ref.shape[0], dest, out, 0, sem.at[k])
+    wait_all(start_all(copies))
+
+
+def pack_fields_kernel(cfg, me_ref, ids_ref, *refs):
+    ids = id_tile(ids_ref)
+    for out in refs[1 : cfg.n + 1]:
+        out[3 * cfg.tiles] = ids
+    pack_kernel(cfg, me_ref, *refs)
+
+
+def unpack_kernel(cfg, me_ref, *refs):
+    pieces = refs[: cfg.n]
+    conserved_ref, field_ref, sem = refs[cfg.n :]
+    copies = []
+    for piece, k in zip(pieces, cfg.order):
+        at = pl.ds(jnp.bitwise_xor(me_ref[0], k) * cfg.tiles, cfg.tiles)
+        for j, (first, count, out) in enumerate(((0, 5, conserved_ref), (5, 3, field_ref))):
+            copies.append(
+                pltpu.make_async_copy(
+                    piece.at[pl.ds(first, count)], out.at[:, at], sem.at[k, j]
+                )
             )
-        )
-    for copy in copies:
-        copy.start()
-    for copy in copies:
-        copy.wait()
-
-
-def unpack_kernel(cfg, me_ref, *refs):
-    first, second = refs[: cfg.n], refs[cfg.n : 2 * cfg.n]
-    conserved_ref, field_ref, sem = refs[2 * cfg.n :]
-    me = me_ref[0]
-    copies = []
-    for k in range(cfg.n):
-        at = pl.ds(jnp.bitwise_xor(me, k) * cfg.tiles, cfg.tiles)
-        copies.append(
-            pltpu.make_async_copy(second[k].at[pl.ds(0, 5)], conserved_ref.at[:, at], sem.at[k, 0])
-        )
-        copies.append(
-            pltpu.make_async_copy(first[k], field_ref.at[pl.ds(0, 2), at], sem.at[k, 1])
-        )
-        copies.append(
-            pltpu.make_async_copy(
-                second[k].at[pl.ds(5, 1)], field_ref.at[pl.ds(2, 1), at], sem.at[k, 2]
-            )
-        )
-    for copy in copies:
-        copy.start()
-    for copy in copies:
-        copy.wait()
+    wait_all(start_all(copies))
 
 
 def operators_kernel(cfg, me_ref, shift_ref, frac_ref, mh_ref, ml_ref, gh_ref, gl_ref, tj_ref):
@@ -222,7 +216,7 @@
         for c in range(2):
             for k in range(n):
                 for t in range(per):
-                    outs[k][c, al * per + t] = remap[
+                    outs[cfg.order.index(k)][c, al * per + t] = remap[
                         c * slots + k * SUB : c * slots + (k + 1) * SUB,
                         t * LANES : (t + 1) * LANES,
                     ]
@@ -253,11 +247,14 @@
 
 
 def conserved_kernel(cfg, me_ref, *refs):
-    n, slots, wide = cfg.n, cfg.slots, cfg.lanes
+    n, slots, tiles, wide = cfg.n, cfg.slots, cfg.tiles, cfg.lanes
     pieces = refs[:n]
     mh_ref, ml_ref, rows_ref, bp_ref, halo_ref, polar_ref = refs[n : n + 6]
-    outs = refs[n + 6 :]
+    remapped = refs[n + 6 : 2 * n + 6]
+    outs = refs[2 * n + 6 :]
     me = me_ref[0]
+    for k in range(n):
+        outs[k][5:7] = remapped[k][...]
     per = wide // LANES
     for al in range(cfg.radii):
         taken = rows_ref[al]
@@ -265,7 +262,7 @@
         for c in range(5):
             x = jnp.concatenate(
                 [
-                    jnp.concatenate([p[c, al * per + t] for p in pieces], axis=0)
+                    jnp.concatenate([p[c * tiles + al * per + t] for p in pieces], axis=0)
                     for t in range(per)
                 ],
                 axis=1,
@@ -280,7 +277,7 @@
         for c in range(5):
             for k in range(n):
                 for t in range(per):
-                    outs[k][c, al * per + t] = out[
+                    outs[cfg.order.index(k)][c, al * per + t] = out[
                         c * slots + k * SUB : c * slots + (k + 1) * SUB,
                         t * LANES : (t + 1) * LANES,
                     ]
@@ -299,12 +296,13 @@
                     lane = lax.broadcasted_iota(jnp.int32, after.shape, 1)
                     after = jnp.where(lane < BS, after, 0.0)
                     bp = bp + pltpu.roll(after, LANES - BS, 1)
-            outs[k][5, t] = bp
+            outs[cfg.order.index(k)][7, t] = bp
 
 
 class Sizes:
     def __init__(self, n):
         self.n = n
+        self.order = list(range(n // 2, n)) + list(range(n // 2 - 1, -1, -1))
         self.rows = BS * BS // n
         self.tiles = self.rows * BS // LANES
         self.lanes = min(self.rows, BS) * BS
@@ -325,8 +323,11 @@
     per = cfg.lanes // LANES
     smem = pl.BlockSpec(memory_space=pltpu.SMEM)
     vmem = pl.BlockSpec(memory_space=pltpu.VMEM)
-    anywhere = pl.BlockSpec(memory_space=pl.ANY)
-    params = pltpu.CompilerParams(vmem_limit_bytes=48 * 2**20)
+    hbm = pl.BlockSpec(memory_space=pltpu.MemorySpace.HBM)
+
+    def grant(mib):
+        return pltpu.CompilerParams(vmem_limit_bytes=min(mib, 48) * 2**20)
+
     me = lax.axis_index("phi").astype(jnp.int32).reshape(1)
 
     def tiled(x):
@@ -336,28 +337,26 @@
         return x.transpose(2, 0, 1, 3).reshape(SUB, x.shape[0], n * tiles * LANES)
 
     def exchange(pieces):
-        return [pieces[0]] + [
-            lax.ppermute(pieces[k], "phi", [(s, s ^ k) for s in range(n)]) for k in range(1, n)
+        return [
+            lax.ppermute(piece, "phi", [(s, s ^ k) for s in range(n)]) if k else piece
+            for piece, k in zip(pieces, cfg.order)
         ]
 
-    sent = pl.pallas_call(
-        functools.partial(pack_fields_kernel, cfg),
-        out_shape=[shape(3 * tiles + 1, SUB, LANES)] * n,
-        in_specs=[smem, smem, anywhere],
-        out_specs=[vmem] * n,
-        scratch_shapes=[pltpu.SemaphoreType.DMA((3 * n,))],
-        name="pack_fields",
-    )(me, block_ids, tiled(face_field))
-    fields = exchange(sent)
-    sent = pl.pallas_call(
-        functools.partial(pack_conserved_kernel, cfg),
-        out_shape=[shape(5, tiles, SUB, LANES)] * n,
-        in_specs=[smem, anywhere],
-        out_specs=[vmem] * n,
-        scratch_shapes=[pltpu.SemaphoreType.DMA((n,))],
-        name="pack_conserved",
-    )(me, tiled(conserved))
-    fluid = exchange(sent)
+    def pack(kernel, count, name, *operands):
+        return pl.pallas_call(
+            functools.partial(kernel, cfg),
+            out_shape=[shape(count, SUB, LANES)] * n,
+            in_specs=[smem] * (len(operands) - 1) + [hbm],
+            out_specs=[vmem] * n,
+            scratch_shapes=[pltpu.SemaphoreType.DMA((n, 5))],
+            compiler_params=grant(2),
+            name=name,
+        )(*operands)
+
+    fields = exchange(
+        pack(pack_fields_kernel, 3 * tiles + 1, "pack_fields", me, block_ids, tiled(face_field))
+    )
+    fluid = exchange(pack(pack_kernel, 5 * tiles, "pack_conserved", me, tiled(conserved)))
 
     square = shape(cfg.radii, 3, cfg.lanes, cfg.lanes, dtype=BF16)
     mh, ml, gh, gl, tj = pl.pallas_call(
@@ -365,7 +364,7 @@
         out_shape=[square] * 4 + [shape(2, cfg.lanes, cfg.lanes, dtype=BF16)],
         in_specs=[smem] * 3,
         out_specs=[vmem] * 5,
-        compiler_params=params,
+        compiler_params=grant(8),
         name="operators",
     )(me, int_shift, frac_shift)
 
@@ -380,7 +379,7 @@
         ],
         in_specs=[smem] * 2 + [vmem] * (n + 5),
         out_specs=[vmem] * (n + 4),
-        compiler_params=params,
+        compiler_params=grant(2 * n),
         name="fields",
     )(me, int_shift, *fields, mh, ml, gh, gl, tj)
     halo = lax.ppermute(
@@ -392,24 +391,23 @@
             "phi",
             [(s, s - 1 if s % cfg.split else s + cfg.split - 1) for s in range(n)],
         )
-    first = exchange(first)
-    second = pl.pallas_call(
+    done = pl.pallas_call(
         functools.partial(conserved_kernel, cfg),
-        out_shape=[shape(6, tiles, SUB, LANES)] * n,
-        in_specs=[smem] + [vmem] * (n + 6),
+        out_shape=[shape(8, tiles, SUB, LANES)] * n,
+        in_specs=[smem] + [vmem] * (2 * n + 6),
         out_specs=[vmem] * n,
-        compiler_params=params,
+        compiler_params=grant(2 * n),
         name="conserved",
-    )(me, *fluid, mh, ml, taken, bp, halo, polar)
-    second = exchange(second)
+    )(me, *fluid, mh, ml, taken, bp, halo, polar, *first)
     conserved_out, field_out = pl.pallas_call(
         functools.partial(unpack_kernel, cfg),
         out_shape=[shape(5, n * tiles, SUB, LANES), shape(3, n * tiles, SUB, LANES)],
-        in_specs=[smem] + [vmem] * (2 * n),
-        out_specs=[anywhere] * 2,
-        scratch_shapes=[pltpu.SemaphoreType.DMA((n, 3))],
+        in_specs=[smem] + [vmem] * n,
+        out_specs=[hbm] * 2,
+        scratch_shapes=[pltpu.SemaphoreType.DMA((n, 2))],
+        compiler_params=grant(2),
         name="unpack",
-    )(me, *first, *second)
+    )(me, *exchange(done))
     return untiled(conserved_out), untiled(field_out)
 
 

time: 75.2 us -> 71.7 us (0.953)
  starting transfers between devices: 36.1 us -> 30.4 us
  waiting for transfers between devices: 23 us -> 27.5 us
  Pallas kernels: 12.7 us -> 9.45 us
  local copies, waits for them, and re-layouts: 1.24 us -> 2.91 us
    ppermute x28 -> x21, starting transfers between devices: 33.9 us -> 28.4 us  [exchange(): lax.ppermute(piece, 'phi', [(s, s ^ k) for s in range(n)])]
    ppermute x1, waiting for transfers between devices: 1.27 us -> 3.61 us  [shards(): lax.ppermute(halo, ('tile', 'phi'), [(s, s - cfg.split) for s in range(cf...]
    ppermute x28 -> x21, waiting for transfers between devices: 21.8 us -> 23.9 us  [exchange(): lax.ppermute(piece, 'phi', [(s, s ^ k) for s in range(n)])]
    pallas_call x2, Pallas kernels: 4.65 us -> 2.71 us  [pack(): pl.pallas_call(functools.partial(kernel, cfg), out_shape=[shape(count, SU...]
    unnamed x44 -> x10, local copies, waits for them, and re-layouts: 1.24 us -> 2.91 us
    pallas_call x1, Pallas kernels: 2.45 us -> 1.09 us  [shards(): pl.pallas_call(functools.partial(unpack_kernel, cfg), out_shape=[shape(5,...]
  transfers between devices with their start and end apart: 29 -> 22, of which waited for: 9 -> 7; matrix products, arithmetic and copies ran while one was open for 0% -> 0% of each run, Pallas kernels for 10% -> 8%
where the time goes in v3:
time: 71.7 us; the launch traced here: 70.9 us
  starting transfers between devices  30.4 us (42%)
  waiting for transfers between devices  27.5 us (38%)
  Pallas kernels  9.45 us (13%)
  local copies, waits for them, and re-layouts  2.91 us (4%)
  between operations  0.77 us (1%)
    ppermute x21, starting transfers between devices, exchange(): lax.ppermute(piece, 'phi', [(s, s ^ k) for s in range(n)])  28.4 us
    ppermute x21, waiting for transfers between devices, exchange(): lax.ppermute(piece, 'phi', [(s, s ^ k) for s in range(n)])  23.9 us
    ppermute x1, waiting for transfers between devices, shards(): lax.ppermute(halo, ('tile', 'phi'), [(s, s - cfg.split) for s in range(cf...  3.61 us
    unnamed x10, local copies, waits for them, and re-layouts  2.91 us
    pallas_call x2, Pallas kernels, pack(): pl.pallas_call(functools.partial(kernel, cfg), out_shape=[shape(count, SU...  2.71 us
    pallas_call x1, Pallas kernels, shards(): pl.pallas_call(functools.partial(operators_kernel, cfg), out_shape=[squar...  2.24 us
    pallas_call x1, Pallas kernels, shards(): pl.pallas_call(functools.partial(fields_kernel, cfg), out_shape=[shape(2,...  2.09 us
    ppermute x1, starting transfers between devices, shards(): lax.ppermute(halo, ('tile', 'phi'), [(s, s - cfg.split) for s in range(cf...  1.92 us
  transfers between devices with their start and end apart: 22, of which 7 were waited for; matrix products, arithmetic and copies ran while one was open for 0% of the time, Pallas kernels for 8%

profile of v3, /device:TPU:13, one launch (start us, length us, event | category | flops | bytes accessed | tf_op | source)
XLA Modules:
  0.0 70.9 jit_solution(1016591155026594430)
XLA Ops:
  2.3 1.5 %pack_fields.1 = (f32[13,8,128]{2,1,0:T(8,128)S(1)}, f32[13,8,128]{2,1,0:T(8,128)S(1)}, f32[13,8,128]{2,1,0:T(8,128)S(1)}, f32[13,8,128]{2,1,0:T(8,128)S(1)}, f3...) custom-call(s32[1]{0:T(128)} %bitcast.me_ref, ...), custom_call_target="tpu_custom_call" | custom-call | tf_op jit(solution)/shard_map/pack_fields/pallas_call | solution.py:346
  3.8 1.9 %collective-permute-start.10 = (f32[13,8,128]{2,1,0:T(8,128)S(1)}, f32[13,8,128]{2,1,0:T(8,128)S(1)}, u32[]{:S(2)}, u32[]{:S(2)}) collective-permute-start(f32[13,8,128]{2,1,0:T(8,128)S(1)} %get-tuple-element.58), channel_id=1, source_target_pairs={{0,7},{1,6},{2,5},{3,4},{4,3},{5,2},{6,1},{7,0},{8,15},{9,14},{10,... | collective-permute-start | bytes 159752 | tf_op jit(solution)/shard_map/ppermute | solution.py:341
  5.7 1.9 %collective-permute-start.11 = (f32[13,8,128]{2,1,0:T(8,128)S(1)}, f32[13,8,128]{2,1,0:T(8,128)S(1)}, u32[]{:S(2)}, u32[]{:S(2)}) collective-permute-start(f32[13,8,128]{2,1,0:T(8,128)S(1)} %get-tuple-element.59), channel_id=1, source_target_pairs={{0,3},{1,2},{2,1},{3,0},{4,7},{5,6},{6,5},{7,4},{8,11},{9,10},{10,... | collective-permute-start | bytes 159752 | tf_op jit(solution)/shard_map/ppermute | solution.py:341
  9.9 1.3 %pack_conserved.1 = (f32[20,8,128]{2,1,0:T(8,128)S(1)}, f32[20,8,128]{2,1,0:T(8,128)S(1)}, f32[20,8,128]{2,1,0:T(8,128)S(1)}, f32[20,8,128]{2,1,0:T(8,128)S(1)},...) custom-call(s32[1]{0:T(128)} %bitcast.me_ref, ...), custom_call_target="tpu_custom_call" | custom-call | tf_op jit(solution)/shard_map/pack_conserved/pallas_call | solution.py:346
  11.1 1.9 %collective-permute-start = (f32[20,8,128]{2,1,0:T(8,128)S(1)}, f32[20,8,128]{2,1,0:T(8,128)S(1)}, u32[]{:S(2)}, u32[]{:S(2)}) collective-permute-start(f32[20,8,128]{2,1,0:T(8,128)S(1)} %get-tuple-element.45), channel_id=1, source_target_pairs={{0,4},{1,5},{2,6},{3,7},{4,0},{5,1},{6,2},{7,3},{8,12},{9,13},{10,... | collective-permute-start | bytes 245768 | tf_op jit(solution)/shard_map/ppermute | solution.py:341
  14.0 2.4 %collective-permute-start.2 = (f32[20,8,128]{2,1,0:T(8,128)S(1)}, f32[20,8,128]{2,1,0:T(8,128)S(1)}, u32[]{:S(2)}, u32[]{:S(2)}) collective-permute-start(f32[20,8,128]{2,1,0:T(8,128)S(1)} %get-tuple-element.47), channel_id=1, source_target_pairs={{0,6},{1,7},{2,4},{3,5},{4,2},{5,3},{6,0},{7,1},{8,14},{9,15},{10,... | collective-permute-start | bytes 245768 | tf_op jit(solution)/shard_map/ppermute | solution.py:341
  16.4 1.2 %collective-permute-start.8 = (f32[13,8,128]{2,1,0:T(8,128)S(1)}, f32[13,8,128]{2,1,0:T(8,128)S(1)}, u32[]{:S(2)}, u32[]{:S(2)}) collective-permute-start(f32[13,8,128]{2,1,0:T(8,128)S(1)} %get-tuple-element.56), channel_id=1, source_target_pairs={{0,5},{1,4},{2,7},{3,6},{4,1},{5,0},{6,3},{7,2},{8,13},{9,12},{10,... | collective-permute-start | bytes 159752 | tf_op jit(solution)/shard_map/ppermute | solution.py:341
  18.4 8.4 %collective-permute-done.8.refs_1_ = f32[13,8,128]{2,1,0:T(8,128)S(1)} collective-permute-done((f32[13,8,128]{2,1,0:T(8,128)S(1)}, f32[13,8,128]{2,1,0:T(8,128)S(1)}, u32[]{:S(2)}, u32[]{:S(2)}) %collective-permute-start.8) | collective-permute-done | bytes 53280 | tf_op jit(solution)/shard_map/ppermute | solution.py:341
  26.7 1.6 %collective-permute-start.3 = (f32[20,8,128]{2,1,0:T(8,128)S(1)}, f32[20,8,128]{2,1,0:T(8,128)S(1)}, u32[]{:S(2)}, u32[]{:S(2)}) collective-permute-start(f32[20,8,128]{2,1,0:T(8,128)S(1)} %get-tuple-element.48), channel_id=1, source_target_pairs={{0,7},{1,6},{2,5},{3,4},{4,3},{5,2},{6,1},{7,0},{8,15},{9,14},{10,... | collective-permute-start | bytes 245768 | tf_op jit(solution)/shard_map/ppermute | solution.py:341
  28.3 1.5 %collective-permute-done.9.refs_2_ = f32[13,8,128]{2,1,0:T(8,128)S(1)} collective-permute-done((f32[13,8,128]{2,1,0:T(8,128)S(1)}, f32[13,8,128]{2,1,0:T(8,128)S(1)}, u32[]{:S(2)}, u32[]{:S(2)}) %collective-permute-start.9) | collective-permute-done | bytes 53280 | tf_op jit(solution)/shard_map/ppermute | solution.py:341
  29.9 2.5 %collective-permute-start.4 = (f32[20,8,128]{2,1,0:T(8,128)S(1)}, f32[20,8,128]{2,1,0:T(8,128)S(1)}, u32[]{:S(2)}, u32[]{:S(2)}) collective-permute-start(f32[20,8,128]{2,1,0:T(8,128)S(1)} %get-tuple-element.49), channel_id=1, source_target_pairs={{0,3},{1,2},{2,1},{3,0},{4,7},{5,6},{6,5},{7,4},{8,11},{9,10},{10,... | collective-permute-start | bytes 245768 | tf_op jit(solution)/shard_map/ppermute | solution.py:341
  33.1 2.2 %operators.1 = (bf16[2,3,256,256]{3,2,1,0:T(8,128)(2,1)S(1)}, bf16[2,3,256,256]{3,2,1,0:T(8,128)(2,1)S(1)}, bf16[2,3,256,256]{3,2,1,0:T(8,128)(2,1)S(1)}, bf16[2...) custom-call(s32[1]{0:T(128)} %bitcast.me_ref, s32[16]{0:T(128)S(1)} %copy-done.3, f32[16]{0:T(128)S(1)} %copy-done.4), custom_call_target="tpu_custom_call" | custom-call | tf_op jit(solution)/shard_map/operators/pallas_call | solution.py:362
  35.3 2.1 %fields.1 = (f32[2,4,8,128]{3,2,1,0:T(8,128)S(1)}, f32[2,4,8,128]{3,2,1,0:T(8,128)S(1)}, f32[2,4,8,128]{3,2,1,0:T(8,128)S(1)}, f32[2,4,8,128]{3,2,1,0:T(8,128)S(...) custom-call(s32[1]{0:T(128)} %bitcast.me_ref, ...), custom_call_target="tpu_custom_call" | custom-call | tf_op jit(solution)/shard_map/fields/pallas_call | solution.py:371
  37.4 1.9 %collective-permute-start.14 = (f32[2,64,128]{2,1,0:T(8,128)S(1)}, f32[2,64,128]{2,1,0:T(8,128)S(1)}, u32[]{:S(2)}, u32[]{:S(2)}) collective-permute-start(f32[2,64,128]{2,1,0:T(8,128)S(1)} %get-tuple-element.68), channel_id=1, source_target_pairs={{1,0},{2,1},{3,2},{4,3},{5,4},{6,5},{7,6},{8,7},{9,8},{10,9},{11,1... | collective-permute-start | bytes 196616 | tf_op jit(solution)/shard_map/ppermute | solution.py:385
  39.4 3.6 %collective-permute-done.14.refs_12_ = f32[2,64,128]{2,1,0:T(8,128)S(1)} collective-permute-done((f32[2,64,128]{2,1,0:T(8,128)S(1)}, f32[2,64,128]{2,1,0:T(8,128)S(1)}, u32[]{:S(2)}, u32[]{:S(2)}) %collective-permute-start.14) | collective-permute-done | bytes 65568 | tf_op jit(solution)/shard_map/ppermute | solution.py:385
  43.0 1.3 %conserved.1 = (f32[8,4,8,128]{3,2,1,0:T(8,128)S(1)}, f32[8,4,8,128]{3,2,1,0:T(8,128)S(1)}, f32[8,4,8,128]{3,2,1,0:T(8,128)S(1)}, f32[8,4,8,128]{3,2,1,0:T(8,128...) custom-call(s32[1]{0:T(128)} %bitcast.me_ref, ...), custom_call_target="tpu_custom_call" | custom-call | tf_op jit(solution)/shard_map/conserved/pallas_call | solution.py:394
  44.3 4.2 %collective-permute-start.15 = (f32[8,4,8,128]{3,2,1,0:T(8,128)S(1)}, f32[8,4,8,128]{3,2,1,0:T(8,128)S(1)}, u32[]{:S(2)}, u32[]{:S(2)}) collective-permute-start(f32[8,4,8,128]{3,2,1,0:T(8,128)S(1)} %get-tuple-element.78), channel_id=1, source_target_pairs={{0,4},{1,5},{2,6},{3,7},{4,0},{5,1},{6,2},{7,3},{8,12},{9,13},{10,... | collective-permute-start | bytes 393224 | tf_op jit(solution)/shard_map/ppermute | solution.py:341
  48.5 2.1 %collective-permute-start.18 = (f32[8,4,8,128]{3,2,1,0:T(8,128)S(1)}, f32[8,4,8,128]{3,2,1,0:T(8,128)S(1)}, u32[]{:S(2)}, u32[]{:S(2)}) collective-permute-start(f32[8,4,8,128]{3,2,1,0:T(8,128)S(1)} %get-tuple-element.81), channel_id=1, source_target_pairs={{0,7},{1,6},{2,5},{3,4},{4,3},{5,2},{6,1},{7,0},{8,15},{9,14},{10,... | collective-permute-start | bytes 393224 | tf_op jit(solution)/shard_map/ppermute | solution.py:341
  50.6 2.0 %collective-permute-start.19 = (f32[8,4,8,128]{3,2,1,0:T(8,128)S(1)}, f32[8,4,8,128]{3,2,1,0:T(8,128)S(1)}, u32[]{:S(2)}, u32[]{:S(2)}) collective-permute-start(f32[8,4,8,128]{3,2,1,0:T(8,128)S(1)} %get-tuple-element.82), channel_id=1, source_target_pairs={{0,3},{1,2},{2,1},{3,0},{4,7},{5,6},{6,5},{7,4},{8,11},{9,10},{10,... | collective-permute-start | bytes 393224 | tf_op jit(solution)/shard_map/ppermute | solution.py:341
  52.6 7.6 %collective-permute-done.15.refs_0_ = f32[8,4,8,128]{3,2,1,0:T(8,128)S(1)} collective-permute-done((f32[8,4,8,128]{3,2,1,0:T(8,128)S(1)}, f32[8,4,8,128]{3,2,1,0:T(8,128)S(1)}, u32[]{:S(2)}, u32[]{:S(2)}) %collective-permute-start.15) | collective-permute-done | bytes 131104 | tf_op jit(solution)/shard_map/ppermute | solution.py:341
  60.2 2.3 %collective-permute-start.20 = (f32[8,4,8,128]{3,2,1,0:T(8,128)S(1)}, f32[8,4,8,128]{3,2,1,0:T(8,128)S(1)}, u32[]{:S(2)}, u32[]{:S(2)}) collective-permute-start(f32[8,4,8,128]{3,2,1,0:T(8,128)S(1)} %get-tuple-element.83), channel_id=1, source_target_pairs={{0,2},{1,3},{2,0},{3,1},{4,6},{5,7},{6,4},{7,5},{8,10},{9,11},{10,... | collective-permute-start | bytes 393224 | tf_op jit(solution)/shard_map/ppermute | solution.py:341
  64.0 2.9 %collective-permute-done.17.refs_2_ = f32[8,4,8,128]{3,2,1,0:T(8,128)S(1)} collective-permute-done((f32[8,4,8,128]{3,2,1,0:T(8,128)S(1)}, f32[8,4,8,128]{3,2,1,0:T(8,128)S(1)}, u32[]{:S(2)}, u32[]{:S(2)}) %collective-permute-start.17) | collective-permute-done | bytes 131104 | tf_op jit(solution)/shard_map/ppermute | solution.py:341
  66.9 2.9 %collective-permute-done.18.refs_3_ = f32[8,4,8,128]{3,2,1,0:T(8,128)S(1)} collective-permute-done((f32[8,4,8,128]{3,2,1,0:T(8,128)S(1)}, f32[8,4,8,128]{3,2,1,0:T(8,128)S(1)}, u32[]{:S(2)}, u32[]{:S(2)}) %collective-permute-start.18) | collective-permute-done | bytes 131104 | tf_op jit(solution)/shard_map/ppermute | solution.py:341
  69.9 1.1 %unpack.1 = (f32[5,32,8,128]{3,2,1,0:T(8,128)}, f32[3,32,8,128]{3,2,1,0:T(8,128)}) custom-call(s32[1]{0:T(128)} %bitcast.me_ref, f32[8,4,8,128]{3,2,1,0:T(8,128)S(1)} %collective-permute-done.15.refs_0_, f32[8,4,8,128]{3,2,1,0:T(8,128)S(1)} %collective-permute-done.16.refs_1_, f32[8,4,8,128]{3,2,1,0:T(8,128)S(1)} %collective-permute-done.17.refs_2_, ...), custom_call_target="tpu_custom_call" | custom-call | tf_op jit(solution)/shard_map/unpack/pallas_call | solution.py:402
  (36 shorter events, 7.8 us)
Async XLA Ops:
  1.3 1.0 %copy-start.1 = (f32[8,3,4096]{2,0,1:T(8,128)S(1)}, f32[8,3,4096]{2,0,1:T(8,128)}, u32[]{:S(2)}) copy-start(f32[8,3,4096]{2,0,1:T(8,128)} %param.6) | copy-start | bytes 1179652
  3.8 7.4 %collective-permute-start.10 = (f32[13,8,128]{2,1,0:T(8,128)S(1)}, f32[13,8,128]{2,1,0:T(8,128)S(1)}, u32[]{:S(2)}, u32[]{:S(2)}) collective-permute-start(f32[13,8,128]{2,1,0:T(8,128)S(1)} %get-tuple-element.58), channel_id=1, source_target_pairs={{0,7},{1,6},{2,5},{3,4},{4,3},{5,2},{6,1},{7,0},{8,15},{9,14},{10,... | collective-permute-start | bytes 159752 | tf_op jit(solution)/shard_map/ppermute | solution.py:341
  5.7 7.4 %collective-permute-start.11 = (f32[13,8,128]{2,1,0:T(8,128)S(1)}, f32[13,8,128]{2,1,0:T(8,128)S(1)}, u32[]{:S(2)}, u32[]{:S(2)}) collective-permute-start(f32[13,8,128]{2,1,0:T(8,128)S(1)} %get-tuple-element.59), channel_id=1, source_target_pairs={{0,3},{1,2},{2,1},{3,0},{4,7},{5,6},{6,5},{7,4},{8,11},{9,10},{10,... | collective-permute-start | bytes 159752 | tf_op jit(solution)/shard_map/ppermute | solution.py:341
  7.6 6.4 %collective-permute-start.12 = (f32[13,8,128]{2,1,0:T(8,128)S(1)}, f32[13,8,128]{2,1,0:T(8,128)S(1)}, u32[]{:S(2)}, u32[]{:S(2)}) collective-permute-start(f32[13,8,128]{2,1,0:T(8,128)S(1)} %get-tuple-element.60), channel_id=1, source_target_pairs={{0,2},{1,3},{2,0},{3,1},{4,6},{5,7},{6,4},{7,5},{8,10},{9,11},{10,... | collective-permute-start | bytes 159752 | tf_op jit(solution)/shard_map/ppermute | solution.py:341
  7.9 8.5 %collective-permute-start.13 = (f32[13,8,128]{2,1,0:T(8,128)S(1)}, f32[13,8,128]{2,1,0:T(8,128)S(1)}, u32[]{:S(2)}, u32[]{:S(2)}) collective-permute-start(f32[13,8,128]{2,1,0:T(8,128)S(1)} %get-tuple-element.61), channel_id=1, source_target_pairs={{0,1},{1,0},{2,3},{3,2},{4,5},{5,4},{6,7},{7,6},{8,9},{9,8},{10,11... | collective-permute-start | bytes 159752 | tf_op jit(solution)/shard_map/ppermute | solution.py:341
  8.3 9.4 %collective-permute-start.7 = (f32[13,8,128]{2,1,0:T(8,128)S(1)}, f32[13,8,128]{2,1,0:T(8,128)S(1)}, u32[]{:S(2)}, u32[]{:S(2)}) collective-permute-start(f32[13,8,128]{2,1,0:T(8,128)S(1)} %get-tuple-element.55), channel_id=1, source_target_pairs={{0,4},{1,5},{2,6},{3,7},{4,0},{5,1},{6,2},{7,3},{8,12},{9,13},{10,... | collective-permute-start | bytes 159752 | tf_op jit(solution)/shard_map/ppermute | solution.py:341
  8.8 1.1 %copy-start = (f32[8,5,4096]{2,0,1:T(8,128)S(1)}, f32[8,5,4096]{2,0,1:T(8,128)}, u32[]{:S(2)}) copy-start(f32[8,5,4096]{2,0,1:T(8,128)} %param.5) | copy-start | bytes 1966084
  11.1 21.3 %collective-permute-start = (f32[20,8,128]{2,1,0:T(8,128)S(1)}, f32[20,8,128]{2,1,0:T(8,128)S(1)}, u32[]{:S(2)}, u32[]{:S(2)}) collective-permute-start(f32[20,8,128]{2,1,0:T(8,128)S(1)} %get-tuple-element.45), channel_id=1, source_target_pairs={{0,4},{1,5},{2,6},{3,7},{4,0},{5,1},{6,2},{7,3},{8,12},{9,13},{10,... | collective-permute-start | bytes 245768 | tf_op jit(solution)/shard_map/ppermute | solution.py:341
  13.1 19.3 %collective-permute-start.1 = (f32[20,8,128]{2,1,0:T(8,128)S(1)}, f32[20,8,128]{2,1,0:T(8,128)S(1)}, u32[]{:S(2)}, u32[]{:S(2)}) collective-permute-start(f32[20,8,128]{2,1,0:T(8,128)S(1)} %get-tuple-element.46), channel_id=1, source_target_pairs={{0,5},{1,4},{2,7},{3,6},{4,1},{5,0},{6,3},{7,2},{8,13},{9,12},{10,... | collective-permute-start | bytes 245768 | tf_op jit(solution)/shard_map/ppermute | solution.py:341
  14.0 23.4 %collective-permute-start.2 = (f32[20,8,128]{2,1,0:T(8,128)S(1)}, f32[20,8,128]{2,1,0:T(8,128)S(1)}, u32[]{:S(2)}, u32[]{:S(2)}) collective-permute-start(f32[20,8,128]{2,1,0:T(8,128)S(1)} %get-tuple-element.47), channel_id=1, source_target_pairs={{0,6},{1,7},{2,4},{3,5},{4,2},{5,3},{6,0},{7,1},{8,14},{9,15},{10,... | collective-permute-start | bytes 245768 | tf_op jit(solution)/shard_map/ppermute | solution.py:341
  16.4 10.3 %collective-permute-start.8 = (f32[13,8,128]{2,1,0:T(8,128)S(1)}, f32[13,8,128]{2,1,0:T(8,128)S(1)}, u32[]{:S(2)}, u32[]{:S(2)}) collective-permute-start(f32[13,8,128]{2,1,0:T(8,128)S(1)} %get-tuple-element.56), channel_id=1, source_target_pairs={{0,5},{1,4},{2,7},{3,6},{4,1},{5,0},{6,3},{7,2},{8,13},{9,12},{10,... | collective-permute-start | bytes 159752 | tf_op jit(solution)/shard_map/ppermute | solution.py:341
  17.7 12.2 %collective-permute-start.9 = (f32[13,8,128]{2,1,0:T(8,128)S(1)}, f32[13,8,128]{2,1,0:T(8,128)S(1)}, u32[]{:S(2)}, u32[]{:S(2)}) collective-permute-start(f32[13,8,128]{2,1,0:T(8,128)S(1)} %get-tuple-element.57), channel_id=1, source_target_pairs={{0,6},{1,7},{2,4},{3,5},{4,2},{5,3},{6,0},{7,1},{8,14},{9,15},{10,... | collective-permute-start | bytes 159752 | tf_op jit(solution)/shard_map/ppermute | solution.py:341
  26.7 12.6 %collective-permute-start.3 = (f32[20,8,128]{2,1,0:T(8,128)S(1)}, f32[20,8,128]{2,1,0:T(8,128)S(1)}, u32[]{:S(2)}, u32[]{:S(2)}) collective-permute-start(f32[20,8,128]{2,1,0:T(8,128)S(1)} %get-tuple-element.48), channel_id=1, source_target_pairs={{0,7},{1,6},{2,5},{3,4},{4,3},{5,2},{6,1},{7,0},{8,15},{9,14},{10,... | collective-permute-start | bytes 245768 | tf_op jit(solution)/shard_map/ppermute | solution.py:341
  29.9 9.5 %collective-permute-start.4 = (f32[20,8,128]{2,1,0:T(8,128)S(1)}, f32[20,8,128]{2,1,0:T(8,128)S(1)}, u32[]{:S(2)}, u32[]{:S(2)}) collective-permute-start(f32[20,8,128]{2,1,0:T(8,128)S(1)} %get-tuple-element.49), channel_id=1, source_target_pairs={{0,3},{1,2},{2,1},{3,0},{4,7},{5,6},{6,5},{7,4},{8,11},{9,10},{10,... | collective-permute-start | bytes 245768 | tf_op jit(solution)/shard_map/ppermute | solution.py:341
  32.4 7.0 %collective-permute-start.5 = (f32[20,8,128]{2,1,0:T(8,128)S(1)}, f32[20,8,128]{2,1,0:T(8,128)S(1)}, u32[]{:S(2)}, u32[]{:S(2)}) collective-permute-start(f32[20,8,128]{2,1,0:T(8,128)S(1)} %get-tuple-element.50), channel_id=1, source_target_pairs={{0,2},{1,3},{2,0},{3,1},{4,6},{5,7},{6,4},{7,5},{8,10},{9,11},{10,... | collective-permute-start | bytes 245768 | tf_op jit(solution)/shard_map/ppermute | solution.py:341
  32.4 7.0 %collective-permute-start.6 = (f32[20,8,128]{2,1,0:T(8,128)S(1)}, f32[20,8,128]{2,1,0:T(8,128)S(1)}, u32[]{:S(2)}, u32[]{:S(2)}) collective-permute-start(f32[20,8,128]{2,1,0:T(8,128)S(1)} %get-tuple-element.51), channel_id=1, source_target_pairs={{0,1},{1,0},{2,3},{3,2},{4,5},{5,4},{6,7},{7,6},{8,9},{9,8},{10,11... | collective-permute-start | bytes 245768 | tf_op jit(solution)/shard_map/ppermute | solution.py:341
  37.4 5.6 %collective-permute-start.14 = (f32[2,64,128]{2,1,0:T(8,128)S(1)}, f32[2,64,128]{2,1,0:T(8,128)S(1)}, u32[]{:S(2)}, u32[]{:S(2)}) collective-permute-start(f32[2,64,128]{2,1,0:T(8,128)S(1)} %get-tuple-element.68), channel_id=1, source_target_pairs={{1,0},{2,1},{3,2},{4,3},{5,4},{6,5},{7,6},{8,7},{9,8},{10,9},{11,1... | collective-permute-start | bytes 196616 | tf_op jit(solution)/shard_map/ppermute | solution.py:385
  44.3 15.9 %collective-permute-start.15 = (f32[8,4,8,128]{3,2,1,0:T(8,128)S(1)}, f32[8,4,8,128]{3,2,1,0:T(8,128)S(1)}, u32[]{:S(2)}, u32[]{:S(2)}) collective-permute-start(f32[8,4,8,128]{3,2,1,0:T(8,128)S(1)} %get-tuple-element.78), channel_id=1, source_target_pairs={{0,4},{1,5},{2,6},{3,7},{4,0},{5,1},{6,2},{7,3},{8,12},{9,13},{10,... | collective-permute-start | bytes 393224 | tf_op jit(solution)/shard_map/ppermute | solution.py:341
  48.5 14.5 %collective-permute-start.16 = (f32[8,4,8,128]{3,2,1,0:T(8,128)S(1)}, f32[8,4,8,128]{3,2,1,0:T(8,128)S(1)}, u32[]{:S(2)}, u32[]{:S(2)}) collective-permute-start(f32[8,4,8,128]{3,2,1,0:T(8,128)S(1)} %get-tuple-element.79), channel_id=1, source_target_pairs={{0,5},{1,4},{2,7},{3,6},{4,1},{5,0},{6,3},{7,2},{8,13},{9,12},{10,... | collective-permute-start | bytes 393224 | tf_op jit(solution)/shard_map/ppermute | solution.py:341
  48.5 18.4 %collective-permute-start.17 = (f32[8,4,8,128]{3,2,1,0:T(8,128)S(1)}, f32[8,4,8,128]{3,2,1,0:T(8,128)S(1)}, u32[]{:S(2)}, u32[]{:S(2)}) collective-permute-start(f32[8,4,8,128]{3,2,1,0:T(8,128)S(1)} %get-tuple-element.80), channel_id=1, source_target_pairs={{0,6},{1,7},{2,4},{3,5},{4,2},{5,3},{6,0},{7,1},{8,14},{9,15},{10,... | collective-permute-start | bytes 393224 | tf_op jit(solution)/shard_map/ppermute | solution.py:341
  48.5 21.4 %collective-permute-start.18 = (f32[8,4,8,128]{3,2,1,0:T(8,128)S(1)}, f32[8,4,8,128]{3,2,1,0:T(8,128)S(1)}, u32[]{:S(2)}, u32[]{:S(2)}) collective-permute-start(f32[8,4,8,128]{3,2,1,0:T(8,128)S(1)} %get-tuple-element.81), channel_id=1, source_target_pairs={{0,7},{1,6},{2,5},{3,4},{4,3},{5,2},{6,1},{7,0},{8,15},{9,14},{10,... | collective-permute-start | bytes 393224 | tf_op jit(solution)/shard_map/ppermute | solution.py:341
  50.6 19.3 %collective-permute-start.19 = (f32[8,4,8,128]{3,2,1,0:T(8,128)S(1)}, f32[8,4,8,128]{3,2,1,0:T(8,128)S(1)}, u32[]{:S(2)}, u32[]{:S(2)}) collective-permute-start(f32[8,4,8,128]{3,2,1,0:T(8,128)S(1)} %get-tuple-element.82), channel_id=1, source_target_pairs={{0,3},{1,2},{2,1},{3,0},{4,7},{5,6},{6,5},{7,4},{8,11},{9,10},{10,... | collective-permute-start | bytes 393224 | tf_op jit(solution)/shard_map/ppermute | solution.py:341
  60.2 9.7 %collective-permute-start.20 = (f32[8,4,8,128]{3,2,1,0:T(8,128)S(1)}, f32[8,4,8,128]{3,2,1,0:T(8,128)S(1)}, u32[]{:S(2)}, u32[]{:S(2)}) collective-permute-start(f32[8,4,8,128]{3,2,1,0:T(8,128)S(1)} %get-tuple-element.83), channel_id=1, source_target_pairs={{0,2},{1,3},{2,0},{3,1},{4,6},{5,7},{6,4},{7,5},{8,10},{9,11},{10,... | collective-permute-start | bytes 393224 | tf_op jit(solution)/shard_map/ppermute | solution.py:341
  63.0 6.8 %collective-permute-start.21 = (f32[8,4,8,128]{3,2,1,0:T(8,128)S(1)}, f32[8,4,8,128]{3,2,1,0:T(8,128)S(1)}, u32[]{:S(2)}, u32[]{:S(2)}) collective-permute-start(f32[8,4,8,128]{3,2,1,0:T(8,128)S(1)} %get-tuple-element.84), channel_id=1, source_target_pairs={{0,1},{1,0},{2,3},{3,2},{4,5},{5,4},{6,7},{7,6},{8,9},{9,8},{10,11... | collective-permute-start | bytes 393224 | tf_op jit(solution)/shard_map/ppermute | solution.py:341
  (3 other events, 2.0 us)

commit v4 on v3

v4 whole, which is shorter than its diff:
```python
import functools

import jax
import jax.numpy as jnp
from jax import lax
from jax.experimental import pallas as pl
from jax.experimental.pallas import tpu as pltpu
from jax.sharding import PartitionSpec as P

BS = 16
TB = 2
PB = 4
LANES = 128
SUB = 8
NODES = (-3, -2, -1, 0, 1, 2, 3)
F32 = jnp.float32
BF16 = jnp.bfloat16


def halves(x):
    hi = x.astype(BF16)
    return hi, (x - hi.astype(F32)).astype(BF16)


def thirds(x):
    hi = x.astype(BF16)
    rest = x - hi.astype(F32)
    mid = rest.astype(BF16)
    return hi, mid, (rest - mid.astype(F32)).astype(BF16)


def dot(a, b):
    return jnp.dot(a, b, preferred_element_type=F32)


def nearest_blocks(shift):
    whole = (shift + BS // 2) // BS
    return whole, shift - whole * BS


def start_all(copies):
    for copy in copies:
        copy.start()
    return copies


def wait_all(copies):
    for copy in copies:
        copy.wait()


def copy_in(cfg, source_ref, count, dest, out_ref, at, sem):
    return [
        pltpu.make_async_copy(
            source_ref.at[c, pl.ds(dest * cfg.tiles, cfg.tiles)],
            out_ref.at[pl.ds(at + c * cfg.tiles, cfg.tiles)],
            sem.at[c],
        )
        for c in range(count)
    ]


def id_tile(ids_ref):
    rows = lax.broadcasted_iota(jnp.int32, (SUB, LANES), 0)
    ids = jnp.zeros((SUB, LANES), jnp.int32)
    for slot in range(SUB):
        ids = jnp.where(rows == slot, ids_ref[slot], ids)
    return ids.astype(F32)


def pack_kernel(cfg, me_ref, ids_ref, face_ref, conserved_ref, *refs):
    outs, sem = refs[: cfg.n], refs[cfg.n]
    copies = []
    for out, k in zip(outs, cfg.order):
        dest = jnp.bitwise_xor(me_ref[0], k)
        copies += copy_in(cfg, face_ref, 3, dest, out, 0, sem.at[k, 0])
        copies += copy_in(cfg, conserved_ref, 5, dest, out, 3 * cfg.tiles, sem.at[k, 1])
    start_all(copies)
    ids = id_tile(ids_ref)
    for out in outs:
        out[8 * cfg.tiles] = ids
    wait_all(copies)


def unpack_kernel(cfg, me_ref, *refs):
    pieces, last_ref = refs[: cfg.n], refs[cfg.n]
    conserved_ref, field_ref, sem, last_sem = refs[cfg.n + 1 :]
    tiles, rest = cfg.tiles, cfg.tiles - cfg.per
    copies = []

    def put(source, out, sem):
        copies.append(pltpu.make_async_copy(source, out, sem))

    for piece, k in zip(pieces, cfg.order):
        source = jnp.bitwise_xor(me_ref[0], k)
        at = pl.ds(source * tiles, tiles)
        whole = piece.at[pl.ds(0, 7 * tiles)].reshape(7, tiles, SUB, LANES)
        put(whole.at[pl.ds(0, 5)], conserved_ref.at[:, at], sem.at[k, 0])
        put(whole.at[pl.ds(5, 2)], field_ref.at[pl.ds(0, 2), at], sem.at[k, 1])
        if rest:
            put(
                piece.at[pl.ds(7 * tiles, rest)],
                field_ref.at[2, pl.ds(source * tiles, rest)],
                sem.at[k, 2],
            )
    for source in range(cfg.n):
        put(
            last_ref.at[source],
            field_ref.at[2, pl.ds(source * tiles + rest, cfg.per)],
            last_sem.at[source],
        )
    wait_all(start_all(copies))


def operators_kernel(cfg, me_ref, shift_ref, frac_ref, mh_ref, ml_ref, gh_ref, gl_ref, tj_ref):
    size = cfg.lanes
    first = (me_ref[0] * cfg.rows) // BS
    row = lax.broadcasted_iota(jnp.int32, (size, size), 0)
    col = lax.broadcasted_iota(jnp.int32, (size, size), 1)
    same = (row // BS) == (col // BS)
    e_in, e_out = row % BS, col % BS
    zero = jnp.zeros((size, size), F32)
    tj_ref[0] = jnp.where(same & (e_in < e_out), 1.0, zero).astype(BF16)
    tj_ref[1] = jnp.where(same, 1.0, zero).astype(BF16)
    for al in range(cfg.radii):
        _, rest = nearest_blocks(shift_ref[first + al])
        position = -jnp.full((1, size), frac_ref[first + al], F32)
        lagrange = []
        for a in NODES:
            product = jnp.ones_like(position)
            for b in NODES:
                if b != a:
                    product = product * ((position - float(b)) * (1.0 / float(a - b)))
            lagrange.append(product)
        weights = []
        for m in range(-3, 3):
            total = jnp.zeros_like(position)
            if m >= 0:
                for a in range(m + 1, 4):
                    total = total - lagrange[a + 3]
            else:
                for a in range(-3, m + 1):
                    total = total + lagrange[a + 3]
            weights.append(total)
        for d in range(3):
            at = e_in + BS * (d - 1)
            tap = jnp.where(same, at - e_out + rest, 100)
            remap, flux = zero, zero
            for a in NODES:
                hit = tap == a
                remap = jnp.where(hit, lagrange[a + 3], remap)
                if a < 3:
                    flux = jnp.where(hit, weights[a + 3], flux)
            flux = flux - jnp.where(same & (at < e_out - rest), 1.0, zero)
            mh_ref[al, d], ml_ref[al, d] = halves(remap)
            gh_ref[al, d], gl_ref[al, d] = halves(flux)


def gather_matrix(cfg, me, ids, whole):
    shape = (cfg.slots, 3 * cfg.slots)
    target = lax.broadcasted_iota(jnp.int32, shape, 0)
    owner = jnp.bitwise_xor(target >> 3, me)
    q_out, b_out = owner * PB + (target & 3), (target >> 2) & 1
    v = jnp.broadcast_to(ids, shape)
    q_in, b_in = (v >> 3) * PB + (v & 3), (v >> 2) & 1
    same = b_in == b_out
    cells = cfg.n * PB
    rows = []
    for d in (-1, 0, 1):
        hit = same & (((q_out - whole + d - q_in + 2 * cells) & (cells - 1)) == 0)
        rows.append(jnp.where(hit, 1.0, 0.0))
    rows.append(jnp.where(same & (q_in == q_out), 1.0, 0.0))
    back = (q_out - 1 - q_in + cells) & (cells - 1)
    count = jnp.where(back <= whole, 1.0, 0.0) + jnp.where(back + cells <= whole, 1.0, 0.0)
    rows.append(jnp.where(same, count, 0.0))
    return rows


def three_dots(high, low, mh, ml):
    rows = high.shape[0]
    both = dot(jnp.concatenate([high, low], axis=0), mh)
    return both[:rows] + both[rows:] + dot(high, ml)


def rows_kernel(cfg, me_ref, shift_ref, *refs):
    n, slots, tiles, wide, per = cfg.n, cfg.slots, cfg.tiles, cfg.lanes, cfg.per
    pieces = refs[:n]
    mh_ref, ml_ref, gh_ref, gl_ref, tj_ref = refs[n : n + 5]
    outs = refs[n + 5 : 2 * n + 5]
    last_ref, halo_ref, polar_ref = refs[2 * n + 5 :]
    me = me_ref[0]
    first = (me * cfg.rows) // BS
    ids = jnp.concatenate([p[8 * tiles] for p in pieces] * 3, axis=0)
    ids = jnp.transpose(ids)[0:1].astype(jnp.int32)

    def source(c, al):
        x = jnp.concatenate(
            [
                jnp.concatenate([p[c * tiles + al * per + t] for p in pieces], axis=0)
                for t in range(per)
            ],
            axis=1,
        )
        return jnp.concatenate(thirds(x), axis=0)

    def by_owner(out_ref, value):
        for k in range(n):
            for t in range(per):
                out_ref[jnp.bitwise_xor(me, k), t] = value[
                    k * SUB : (k + 1) * SUB, t * LANES : (t + 1) * LANES
                ]

    def block(y, j):
        return y[j * slots : (j + 1) * slots]

    lane = lax.broadcasted_iota(jnp.int32, (slots, wide), 1)
    lower = (lax.broadcasted_iota(jnp.int32, (slots, wide), 0) >> 2) & 1 == 0
    total = []
    for al in range(cfg.radii):
        whole, _ = nearest_blocks(shift_ref[first + al])
        taken = jnp.concatenate(gather_matrix(cfg, me, ids, whole), axis=0).astype(BF16)
        ys = [dot(taken, source(c, al)) for c in range(2)]
        part = [halves(jnp.concatenate([block(y, j) for y in ys], axis=0)) for j in range(5)]
        flux = jnp.zeros((2 * slots, wide), F32)
        for d in range(3):
            flux = flux + three_dots(*part[d], gh_ref[al, d], gl_ref[al, d])
        for j in range(2):
            both = dot(jnp.concatenate(part[3 + j], axis=0), tj_ref[j])
            flux = flux + (both[: 2 * slots] + both[2 * slots :])
        radial, polar = flux[:slots], flux[slots:]
        if cfg.split == 1:
            up = jnp.where(lower, jnp.concatenate([polar[4:], polar[:4]], axis=0), 0.0)
            after = pltpu.roll(jnp.where(lane < BS, up, polar), wide - BS, 1)
        else:
            after = jnp.where(lane < wide - BS, pltpu.roll(polar, wide - BS, 1), 0.0)
        azimuthal = dot(taken[3 * slots : 4 * slots], source(2, al))
        total.append((azimuthal + (after - polar) - radial, radial))
        if al == 0:
            by_owner(halo_ref, radial)
            if cfg.split > 1:
                by_owner(polar_ref, polar)
            else:
                polar_ref[...] = jnp.zeros_like(polar_ref)
        ys = [dot(taken[: 3 * slots], source(3 + c, al)) for c in range(5)] + ys
        remap = jnp.zeros((7 * slots, wide), F32)
        for d in range(3):
            high, low = halves(jnp.concatenate([block(y, d) for y in ys], axis=0))
            remap = remap + three_dots(high, low, mh_ref[al, d], ml_ref[al, d])
        for out, k in zip(outs, cfg.order):
            for c in range(7):
                for t in range(per):
                    out[c * tiles + al * per + t] = remap[
                        c * slots + k * SUB : c * slots + (k + 1) * SUB,
                        t * LANES : (t + 1) * LANES,
                    ]
    for al in range(cfg.radii - 1):
        bp = total[al][0] + total[al + 1][1]
        for out, k in zip(outs, cfg.order):
            for t in range(per):
                out[7 * tiles + al * per + t] = bp[
                    k * SUB : (k + 1) * SUB, t * LANES : (t + 1) * LANES
                ]
    by_owner(last_ref, total[-1][0])


class Sizes:
    def __init__(self, n):
        self.n = n
        self.order = list(range(n // 2, n)) + list(range(n // 2 - 1, -1, -1))
        self.rows = BS * BS // n
        self.tiles = self.rows * BS // LANES
        self.lanes = min(self.rows, BS) * BS
        self.radii = max(1, self.rows // BS)
        self.per = self.lanes // LANES
        self.split = max(1, BS // self.rows)
        self.slots = n * SUB


def shape(*dims, dtype=F32):
    return jax.ShapeDtypeStruct(dims, dtype)


def shards(conserved, face_field, block_ids, int_shift, frac_shift):
    n = lax.axis_size("phi")
    cfg = Sizes(n)
    count = lax.axis_size("tile") * n
    tiles, per = cfg.tiles, cfg.per
    smem = pl.BlockSpec(memory_space=pltpu.SMEM)
    vmem = pl.BlockSpec(memory_space=pltpu.VMEM)
    hbm = pl.BlockSpec(memory_space=pltpu.MemorySpace.HBM)

    def grant(mib):
        return pltpu.CompilerParams(vmem_limit_bytes=min(mib, 48) * 2**20)

    me = lax.axis_index("phi").astype(jnp.int32).reshape(1)

    def tiled(x):
        return x.reshape(SUB, x.shape[1], n * tiles, LANES).transpose(1, 2, 0, 3)

    def untiled(x):
        return x.transpose(2, 0, 1, 3).reshape(SUB, x.shape[0], n * tiles * LANES)

    def exchange(pieces):
        return [
            lax.ppermute(piece, "phi", [(s, s ^ k) for s in range(n)]) if k else piece
            for piece, k in zip(pieces, cfg.order)
        ]

    packed = pl.pallas_call(
        functools.partial(pack_kernel, cfg),
        out_shape=[shape(8 * tiles + 1, SUB, LANES)] * n,
        in_specs=[smem, smem, hbm, hbm],
        out_specs=[vmem] * n,
        scratch_shapes=[pltpu.SemaphoreType.DMA((n, 2, 5))],
        compiler_params=grant(2),
        name="pack",
    )(me, block_ids, tiled(face_field), tiled(conserved))
    blocks = exchange(packed)

    square = shape(cfg.radii, 3, cfg.lanes, cfg.lanes, dtype=BF16)
    mh, ml, gh, gl, tj = pl.pallas_call(
        functools.partial(operators_kernel, cfg),
        out_shape=[square] * 4 + [shape(2, cfg.lanes, cfg.lanes, dtype=BF16)],
        in_specs=[smem] * 3,
        out_specs=[vmem] * 5,
        compiler_params=grant(8),
        name="operators",
    )(me, int_shift, frac_shift)

    by_owner = shape(n, per, SUB, LANES)
    *done, last, halo, polar = pl.pallas_call(
        functools.partial(rows_kernel, cfg),
        out_shape=[shape(8 * tiles - per, SUB, LANES)] * n
        + [by_owner, by_owner, by_owner if cfg.split > 1 else shape(1, 1, SUB, LANES)],
        in_specs=[smem] * 2 + [vmem] * (n + 5),
        out_specs=[vmem] * (n + 3),
        compiler_params=grant(2 * n),
        name="rows",
    )(me, int_shift, *blocks, mh, ml, gh, gl, tj)
    done = exchange(done)
    last = last + lax.ppermute(
        halo, ("tile", "phi"), [(s, s - cfg.split) for s in range(cfg.split, count)]
    )
    if cfg.split > 1:
        polar = lax.ppermute(
            polar,
            "phi",
            [(s, s - 1 if s % cfg.split else s + cfg.split - 1) for s in range(n)],
        )[:, 0, :, :BS]
        up = jnp.concatenate([polar[:, 4:], jnp.zeros_like(polar[:, :4])], axis=1)
        polar = jnp.where(me[0] % cfg.split == cfg.split - 1, up, polar)
        last = last.at[:, per - 1, :, LANES - BS :].add(polar)
    last = lax.all_to_all(last, "phi", split_axis=0, concat_axis=0, tiled=True)
    conserved_out, field_out = pl.pallas_call(
        functools.partial(unpack_kernel, cfg),
        out_shape=[shape(5, n * tiles, SUB, LANES), shape(3, n * tiles, SUB, LANES)],
        in_specs=[smem] + [vmem] * (n + 1),
        out_specs=[hbm] * 2,
        scratch_shapes=[pltpu.SemaphoreType.DMA((n, 3)), pltpu.SemaphoreType.DMA((n,))],
        compiler_params=grant(2),
        name="unpack",
    )(me, *done, last)
    return untiled(conserved_out), untiled(field_out)


def solution(mesh):
    return jax.shard_map(
        shards,
        mesh=mesh,
        in_specs=(
            P(("tile", "phi"), None, None),
            P(("tile", "phi"), None, None),
            P(("tile", "phi")),
            P("tile"),
            P("tile"),
        ),
        out_specs=(P(("tile", "phi"), None, None), P(("tile", "phi"), None, None)),
        check_vma=False,
    )
```

time: 71.7 us -> 69.9 us (0.975)
  the two profiles are of different devices: /device:TPU:13 before, /device:TPU:0 now
where the time goes in v4:
time: 69.9 us; the launch traced here: 69.6 us
  starting transfers between devices  35 us (50%)
  waiting for transfers between devices  21.3 us (30%)
  Pallas kernels  9.16 us (13%)
  local copies, waits for them, and re-layouts  2.74 us (4%)
  between operations  0.75 us (1%)
    ppermute x14, starting transfers between devices, exchange(): lax.ppermute(piece, 'phi', [(s, s ^ k) for s in range(n)])  30.3 us
    ppermute x14, waiting for transfers between devices, exchange(): lax.ppermute(piece, 'phi', [(s, s ^ k) for s in range(n)])  16.5 us
    all_to_all x1, waiting for transfers between devices, shards(): last = lax.all_to_all(last, 'phi', split_axis=0, concat_axis=0, tiled=True)  4.8 us
    all_to_all x1, starting transfers between devices, shards(): last = lax.all_to_all(last, 'phi', split_axis=0, concat_axis=0, tiled=True)  3.35 us
    pallas_call x1, Pallas kernels, shards(): pl.pallas_call(functools.partial(rows_kernel, cfg), out_shape=[shape(8 *...  2.94 us
    pallas_call x1, Pallas kernels, shards(): pl.pallas_call(functools.partial(pack_kernel, cfg), out_shape=[shape(8 *...  2.75 us
    unnamed x10, local copies, waits for them, and re-layouts  2.74 us
    pallas_call x1, Pallas kernels, shards(): pl.pallas_call(functools.partial(operators_kernel, cfg), out_shape=[squar...  2.24 us
  transfers between devices with their start and end apart: 16, of which 5 were waited for; matrix products, arithmetic and copies ran while one was open for 1% of the time, Pallas kernels for 3%

profile of v4, /device:TPU:0, one launch (start us, length us, event | category | flops | bytes accessed | tf_op | source)
XLA Modules:
  0.0 69.6 jit_solution(16577979306838893833)
XLA Ops:
  0.6 0.6 copy-done.2
  1.3 1.1 %copy-done = f32[8,5,4096]{2,0,1:T(8,128)S(1)} copy-done((f32[8,5,4096]{2,0,1:T(8,128)S(1)}, f32[8,5,4096]{2,0,1:T(8,128)}, u32[]{:S(2)}) %copy-start) | copy-done | bytes 655384
  2.4 1.0 %copy-done.1 = f32[8,3,4096]{2,0,1:T(8,128)S(1)} copy-done((f32[8,3,4096]{2,0,1:T(8,128)S(1)}, f32[8,3,4096]{2,0,1:T(8,128)}, u32[]{:S(2)}) %copy-start.1) | copy-done | bytes 393240
  3.4 2.7 %pack.1 = (f32[33,8,128]{2,1,0:T(8,128)S(1)}, f32[33,8,128]{2,1,0:T(8,128)S(1)}, f32[33,8,128]{2,1,0:T(8,128)S(1)}, f32[33,8,128]{2,1,0:T(8,128)S(1)}, f32[33,8,...) custom-call(s32[1]{0:T(128)} %bitcast.me_ref, ...), custom_call_target="tpu_custom_call" | custom-call | tf_op jit(solution)/shard_map/pack/pallas_call | solution.py:309
  6.1 4.1 %collective-permute-start = (f32[33,8,128]{2,1,0:T(8,128)S(1)}, f32[33,8,128]{2,1,0:T(8,128)S(1)}, u32[]{:S(2)}, u32[]{:S(2)}) collective-permute-start(f32[33,8,128]{2,1,0:T(8,128)S(1)} %get-tuple-element.27), channel_id=1, source_target_pairs={{0,4},{1,5},{2,6},{3,7},{4,0},{5,1},{6,2},{7,3},{8,12},{9,13},{10,... | collective-permute-start | bytes 405512 | tf_op jit(solution)/shard_map/ppermute | solution.py:305
  10.2 0.0 collective-permute-start.1
  10.2 3.1 %collective-permute-start.2 = (f32[33,8,128]{2,1,0:T(8,128)S(1)}, f32[33,8,128]{2,1,0:T(8,128)S(1)}, u32[]{:S(2)}, u32[]{:S(2)}) collective-permute-start(f32[33,8,128]{2,1,0:T(8,128)S(1)} %get-tuple-element.29), channel_id=1, source_target_pairs={{0,6},{1,7},{2,4},{3,5},{4,2},{5,3},{6,0},{7,1},{8,14},{9,15},{10,... | collective-permute-start | bytes 405512 | tf_op jit(solution)/shard_map/ppermute | solution.py:305
  13.3 0.6 collective-permute-start.3
  13.9 12.4 %collective-permute-done.refs_0_ = f32[33,8,128]{2,1,0:T(8,128)S(1)} collective-permute-done((f32[33,8,128]{2,1,0:T(8,128)S(1)}, f32[33,8,128]{2,1,0:T(8,128)S(1)}, u32[]{:S(2)}, u32[]{:S(2)}) %collective-permute-start) | collective-permute-done | bytes 135200 | tf_op jit(solution)/shard_map/ppermute | solution.py:305
  26.3 1.2 %collective-permute-done.1.refs_1_ = f32[33,8,128]{2,1,0:T(8,128)S(1)} collective-permute-done((f32[33,8,128]{2,1,0:T(8,128)S(1)}, f32[33,8,128]{2,1,0:T(8,128)S(1)}, u32[]{:S(2)}, u32[]{:S(2)}) %collective-permute-start.1) | collective-permute-done | bytes 135200 | tf_op jit(solution)/shard_map/ppermute | solution.py:305
  27.6 1.4 %collective-permute-start.6 = (f32[33,8,128]{2,1,0:T(8,128)S(1)}, f32[33,8,128]{2,1,0:T(8,128)S(1)}, u32[]{:S(2)}, u32[]{:S(2)}) collective-permute-start(f32[33,8,128]{2,1,0:T(8,128)S(1)} %get-tuple-element.33), channel_id=1, source_target_pairs={{0,1},{1,0},{2,3},{3,2},{4,5},{5,4},{6,7},{7,6},{8,9},{9,8},{10,11... | collective-permute-start | bytes 405512 | tf_op jit(solution)/shard_map/ppermute | solution.py:305
  29.0 2.2 %operators.1 = (bf16[2,3,256,256]{3,2,1,0:T(8,128)(2,1)S(1)}, bf16[2,3,256,256]{3,2,1,0:T(8,128)(2,1)S(1)}, bf16[2,3,256,256]{3,2,1,0:T(8,128)(2,1)S(1)}, bf16[2...) custom-call(s32[1]{0:T(128)} %bitcast.me_ref, s32[16]{0:T(128)S(1)} %copy-done.3, f32[16]{0:T(128)S(1)} %copy-done.4), custom_call_target="tpu_custom_call" | custom-call | tf_op jit(solution)/shard_map/operators/pallas_call | solution.py:321
  31.3 1.9 %collective-permute-done.5.refs_5_ = f32[33,8,128]{2,1,0:T(8,128)S(1)} collective-permute-done((f32[33,8,128]{2,1,0:T(8,128)S(1)}, f32[33,8,128]{2,1,0:T(8,128)S(1)}, u32[]{:S(2)}, u32[]{:S(2)}) %collective-permute-start.5) | collective-permute-done | bytes 135200 | tf_op jit(solution)/shard_map/ppermute | solution.py:305
  33.1 2.9 %rows.1 = (f32[30,8,128]{2,1,0:T(8,128)S(1)}, f32[30,8,128]{2,1,0:T(8,128)S(1)}, f32[30,8,128]{2,1,0:T(8,128)S(1)}, f32[30,8,128]{2,1,0:T(8,128)S(1)}, f32[30,8,...) custom-call(s32[1]{0:T(128)} %bitcast.me_ref, ...), custom_call_target="tpu_custom_call" | custom-call | tf_op jit(solution)/shard_map/rows/pallas_call | solution.py:331
  36.1 3.6 %collective-permute-start.7 = (f32[30,8,128]{2,1,0:T(8,128)S(1)}, f32[30,8,128]{2,1,0:T(8,128)S(1)}, u32[]{:S(2)}, u32[]{:S(2)}) collective-permute-start(f32[30,8,128]{2,1,0:T(8,128)S(1)} %get-tuple-element.40), channel_id=1, source_target_pairs={{0,4},{1,5},{2,6},{3,7},{4,0},{5,1},{6,2},{7,3},{8,12},{9,13},{10,... | collective-permute-start | bytes 368648 | tf_op jit(solution)/shard_map/ppermute | solution.py:305
  39.7 1.3 %collective-permute-start.14 = (f32[8,2,8,128]{3,2,1,0:T(8,128)S(1)}, f32[8,2,8,128]{3,2,1,0:T(8,128)S(1)}, u32[]{:S(2)}, u32[]{:S(2)}) collective-permute-start(f32[8,2,8,128]{3,2,1,0:T(8,128)S(1)} %get-tuple-element.49), channel_id=1, source_target_pairs={{1,0},{2,1},{3,2},{4,3},{5,4},{6,5},{7,6},{8,7},{9,8},{10,9},{11,1... | collective-permute-start | bytes 196616 | tf_op jit(solution)/shard_map/ppermute | solution.py:341
  41.0 4.8 %collective-permute-start.9 = (f32[30,8,128]{2,1,0:T(8,128)S(1)}, f32[30,8,128]{2,1,0:T(8,128)S(1)}, u32[]{:S(2)}, u32[]{:S(2)}) collective-permute-start(f32[30,8,128]{2,1,0:T(8,128)S(1)} %get-tuple-element.42), channel_id=1, source_target_pairs={{0,6},{1,7},{2,4},{3,5},{4,2},{5,3},{6,0},{7,1},{8,14},{9,15},{10,... | collective-permute-start | bytes 368648 | tf_op jit(solution)/shard_map/ppermute | solution.py:305
  45.8 12.5 %collective-permute-start.11 = (f32[30,8,128]{2,1,0:T(8,128)S(1)}, f32[30,8,128]{2,1,0:T(8,128)S(1)}, u32[]{:S(2)}, u32[]{:S(2)}) collective-permute-start(f32[30,8,128]{2,1,0:T(8,128)S(1)} %get-tuple-element.44), channel_id=1, source_target_pairs={{0,3},{1,2},{2,1},{3,0},{4,7},{5,6},{6,5},{7,4},{8,11},{9,10},{10,... | collective-permute-start | bytes 368648 | tf_op jit(solution)/shard_map/ppermute | solution.py:305
  58.4 0.1 collective-permute-start.13
  58.5 0.6 add.3
  59.1 3.4 %all-to-all-start = ((f32[8,2,8,128]{3,2,1,0:T(8,128)}), f32[8,2,8,128]{3,2,1,0:T(8,128)S(1)}, u32[]{:S(2)}, u32[]{:S(2)}) async-start(f32[8,2,8,128]{3,2,1,0:T(8,128)} %add.3), calls=%async_computation | async-start | bytes 131072 | tf_op jit(solution)/shard_map/all_to_all | solution.py:353
  62.5 1.0 %collective-permute-done.12.refs_5_ = f32[30,8,128]{2,1,0:T(8,128)S(1)} collective-permute-done((f32[30,8,128]{2,1,0:T(8,128)S(1)}, f32[30,8,128]{2,1,0:T(8,128)S(1)}, u32[]{:S(2)}, u32[]{:S(2)}) %collective-permute-start.12) | collective-permute-done | bytes 122912 | tf_op jit(solution)/shard_map/ppermute | solution.py:305
  63.5 4.8 %all-to-all-done.refs_8_ = f32[8,2,8,128]{3,2,1,0:T(8,128)S(1)} async-done(((f32[8,2,8,128]{3,2,1,0:T(8,128)}), f32[8,2,8,128]{3,2,1,0:T(8,128)S(1)}, u32[]{:S(2)}, u32[]{:S(2)}) %all-to-all-start) | async-done | bytes 65568 | tf_op jit(solution)/shard_map/all_to_all | solution.py:353
  68.3 1.2 %unpack.1 = (f32[5,32,8,128]{3,2,1,0:T(8,128)}, f32[3,32,8,128]{3,2,1,0:T(8,128)}) custom-call(s32[1]{0:T(128)} %bitcast.me_ref, f32[30,8,128]{2,1,0:T(8,128)S(1)} %collective-permute-done.7.refs_0_, f32[30,8,128]{2,1,0:T(8,128)S(1)} %collective-permute-done.8.refs_1_, f32[30,8,128]{2,1,0:T(8,128)S(1)} %collective-permute-done.9.refs_2_, ...), custom_call_target="tpu_custom_call" | custom-call | tf_op jit(solution)/shard_map/unpack/pallas_call | solution.py:354
  (23 shorter events, 0.1 us)
Async XLA Ops:
  0.6 0.7 copy-start.2
  1.3 1.1 %copy-start = (f32[8,5,4096]{2,0,1:T(8,128)S(1)}, f32[8,5,4096]{2,0,1:T(8,128)}, u32[]{:S(2)}) copy-start(f32[8,5,4096]{2,0,1:T(8,128)} %param.5) | copy-start | bytes 1966084
  2.4 1.0 %copy-start.1 = (f32[8,3,4096]{2,0,1:T(8,128)S(1)}, f32[8,3,4096]{2,0,1:T(8,128)}, u32[]{:S(2)}) copy-start(f32[8,3,4096]{2,0,1:T(8,128)} %param.6) | copy-start | bytes 1179652
  6.1 20.2 %collective-permute-start = (f32[33,8,128]{2,1,0:T(8,128)S(1)}, f32[33,8,128]{2,1,0:T(8,128)S(1)}, u32[]{:S(2)}, u32[]{:S(2)}) collective-permute-start(f32[33,8,128]{2,1,0:T(8,128)S(1)} %get-tuple-element.27), channel_id=1, source_target_pairs={{0,4},{1,5},{2,6},{3,7},{4,0},{5,1},{6,2},{7,3},{8,12},{9,13},{10,... | collective-permute-start | bytes 405512 | tf_op jit(solution)/shard_map/ppermute | solution.py:305
  10.2 17.3 %collective-permute-start.1 = (f32[33,8,128]{2,1,0:T(8,128)S(1)}, f32[33,8,128]{2,1,0:T(8,128)S(1)}, u32[]{:S(2)}, u32[]{:S(2)}) collective-permute-start(f32[33,8,128]{2,1,0:T(8,128)S(1)} %get-tuple-element.28), channel_id=1, source_target_pairs={{0,5},{1,4},{2,7},{3,6},{4,1},{5,0},{6,3},{7,2},{8,13},{9,12},{10,... | collective-permute-start | bytes 405512 | tf_op jit(solution)/shard_map/ppermute | solution.py:305
  10.2 21.0 %collective-permute-start.2 = (f32[33,8,128]{2,1,0:T(8,128)S(1)}, f32[33,8,128]{2,1,0:T(8,128)S(1)}, u32[]{:S(2)}, u32[]{:S(2)}) collective-permute-start(f32[33,8,128]{2,1,0:T(8,128)S(1)} %get-tuple-element.29), channel_id=1, source_target_pairs={{0,6},{1,7},{2,4},{3,5},{4,2},{5,3},{6,0},{7,1},{8,14},{9,15},{10,... | collective-permute-start | bytes 405512 | tf_op jit(solution)/shard_map/ppermute | solution.py:305
  13.3 17.9 %collective-permute-start.3 = (f32[33,8,128]{2,1,0:T(8,128)S(1)}, f32[33,8,128]{2,1,0:T(8,128)S(1)}, u32[]{:S(2)}, u32[]{:S(2)}) collective-permute-start(f32[33,8,128]{2,1,0:T(8,128)S(1)} %get-tuple-element.30), channel_id=1, source_target_pairs={{0,7},{1,6},{2,5},{3,4},{4,3},{5,2},{6,1},{7,0},{8,15},{9,14},{10,... | collective-permute-start | bytes 405512 | tf_op jit(solution)/shard_map/ppermute | solution.py:305
  13.9 17.3 %collective-permute-start.4 = (f32[33,8,128]{2,1,0:T(8,128)S(1)}, f32[33,8,128]{2,1,0:T(8,128)S(1)}, u32[]{:S(2)}, u32[]{:S(2)}) collective-permute-start(f32[33,8,128]{2,1,0:T(8,128)S(1)} %get-tuple-element.31), channel_id=1, source_target_pairs={{0,3},{1,2},{2,1},{3,0},{4,7},{5,6},{6,5},{7,4},{8,11},{9,10},{10,... | collective-permute-start | bytes 405512 | tf_op jit(solution)/shard_map/ppermute | solution.py:305
  26.3 2.7 %copy-start.3 = (s32[16]{0:T(128)S(1)}, s32[16]{0:T(128)}, u32[]{:S(2)}) copy-start(s32[16]{0:T(128)} %shift_ref.3) | copy-start | bytes 196
  26.3 2.7 %copy-start.4 = (f32[16]{0:T(128)S(1)}, f32[16]{0:T(128)}, u32[]{:S(2)}) copy-start(f32[16]{0:T(128)} %frac_ref.1) | copy-start | bytes 196
  26.3 6.8 %collective-permute-start.5 = (f32[33,8,128]{2,1,0:T(8,128)S(1)}, f32[33,8,128]{2,1,0:T(8,128)S(1)}, u32[]{:S(2)}, u32[]{:S(2)}) collective-permute-start(f32[33,8,128]{2,1,0:T(8,128)S(1)} %get-tuple-element.32), channel_id=1, source_target_pairs={{0,2},{1,3},{2,0},{3,1},{4,6},{5,7},{6,4},{7,5},{8,10},{9,11},{10,... | collective-permute-start | bytes 405512 | tf_op jit(solution)/shard_map/ppermute | solution.py:305
  27.6 5.6 %collective-permute-start.6 = (f32[33,8,128]{2,1,0:T(8,128)S(1)}, f32[33,8,128]{2,1,0:T(8,128)S(1)}, u32[]{:S(2)}, u32[]{:S(2)}) collective-permute-start(f32[33,8,128]{2,1,0:T(8,128)S(1)} %get-tuple-element.33), channel_id=1, source_target_pairs={{0,1},{1,0},{2,3},{3,2},{4,5},{5,4},{6,7},{7,6},{8,9},{9,8},{10,11... | collective-permute-start | bytes 405512 | tf_op jit(solution)/shard_map/ppermute | solution.py:305
  36.1 22.3 %collective-permute-start.7 = (f32[30,8,128]{2,1,0:T(8,128)S(1)}, f32[30,8,128]{2,1,0:T(8,128)S(1)}, u32[]{:S(2)}, u32[]{:S(2)}) collective-permute-start(f32[30,8,128]{2,1,0:T(8,128)S(1)} %get-tuple-element.40), channel_id=1, source_target_pairs={{0,4},{1,5},{2,6},{3,7},{4,0},{5,1},{6,2},{7,3},{8,12},{9,13},{10,... | collective-permute-start | bytes 368648 | tf_op jit(solution)/shard_map/ppermute | solution.py:305
  39.7 18.6 %collective-permute-start.8 = (f32[30,8,128]{2,1,0:T(8,128)S(1)}, f32[30,8,128]{2,1,0:T(8,128)S(1)}, u32[]{:S(2)}, u32[]{:S(2)}) collective-permute-start(f32[30,8,128]{2,1,0:T(8,128)S(1)} %get-tuple-element.41), channel_id=1, source_target_pairs={{0,5},{1,4},{2,7},{3,6},{4,1},{5,0},{6,3},{7,2},{8,13},{9,12},{10,... | collective-permute-start | bytes 368648 | tf_op jit(solution)/shard_map/ppermute | solution.py:305
  39.7 6.1 %collective-permute-start.14 = (f32[8,2,8,128]{3,2,1,0:T(8,128)S(1)}, f32[8,2,8,128]{3,2,1,0:T(8,128)S(1)}, u32[]{:S(2)}, u32[]{:S(2)}) collective-permute-start(f32[8,2,8,128]{3,2,1,0:T(8,128)S(1)} %get-tuple-element.49), channel_id=1, source_target_pairs={{1,0},{2,1},{3,2},{4,3},{5,4},{6,5},{7,6},{8,7},{9,8},{10,9},{11,1... | collective-permute-start | bytes 196616 | tf_op jit(solution)/shard_map/ppermute | solution.py:341
  41.0 21.5 %collective-permute-start.9 = (f32[30,8,128]{2,1,0:T(8,128)S(1)}, f32[30,8,128]{2,1,0:T(8,128)S(1)}, u32[]{:S(2)}, u32[]{:S(2)}) collective-permute-start(f32[30,8,128]{2,1,0:T(8,128)S(1)} %get-tuple-element.42), channel_id=1, source_target_pairs={{0,6},{1,7},{2,4},{3,5},{4,2},{5,3},{6,0},{7,1},{8,14},{9,15},{10,... | collective-permute-start | bytes 368648 | tf_op jit(solution)/shard_map/ppermute | solution.py:305
  45.8 16.7 %collective-permute-start.10 = (f32[30,8,128]{2,1,0:T(8,128)S(1)}, f32[30,8,128]{2,1,0:T(8,128)S(1)}, u32[]{:S(2)}, u32[]{:S(2)}) collective-permute-start(f32[30,8,128]{2,1,0:T(8,128)S(1)} %get-tuple-element.43), channel_id=1, source_target_pairs={{0,7},{1,6},{2,5},{3,4},{4,3},{5,2},{6,1},{7,0},{8,15},{9,14},{10,... | collective-permute-start | bytes 368648 | tf_op jit(solution)/shard_map/ppermute | solution.py:305
  45.8 16.7 %collective-permute-start.11 = (f32[30,8,128]{2,1,0:T(8,128)S(1)}, f32[30,8,128]{2,1,0:T(8,128)S(1)}, u32[]{:S(2)}, u32[]{:S(2)}) collective-permute-start(f32[30,8,128]{2,1,0:T(8,128)S(1)} %get-tuple-element.44), channel_id=1, source_target_pairs={{0,3},{1,2},{2,1},{3,0},{4,7},{5,6},{6,5},{7,4},{8,11},{9,10},{10,... | collective-permute-start | bytes 368648 | tf_op jit(solution)/shard_map/ppermute | solution.py:305
  58.3 5.2 %collective-permute-start.12 = (f32[30,8,128]{2,1,0:T(8,128)S(1)}, f32[30,8,128]{2,1,0:T(8,128)S(1)}, u32[]{:S(2)}, u32[]{:S(2)}) collective-permute-start(f32[30,8,128]{2,1,0:T(8,128)S(1)} %get-tuple-element.45), channel_id=1, source_target_pairs={{0,2},{1,3},{2,0},{3,1},{4,6},{5,7},{6,4},{7,5},{8,10},{9,11},{10,... | collective-permute-start | bytes 368648 | tf_op jit(solution)/shard_map/ppermute | solution.py:305
  58.4 5.2 %collective-permute-start.13 = (f32[30,8,128]{2,1,0:T(8,128)S(1)}, f32[30,8,128]{2,1,0:T(8,128)S(1)}, u32[]{:S(2)}, u32[]{:S(2)}) collective-permute-start(f32[30,8,128]{2,1,0:T(8,128)S(1)} %get-tuple-element.46), channel_id=1, source_target_pairs={{0,1},{1,0},{2,3},{3,2},{4,5},{5,4},{6,7},{7,6},{8,9},{9,8},{10,11... | collective-permute-start | bytes 368648 | tf_op jit(solution)/shard_map/ppermute | solution.py:305
  59.1 9.2 %all-to-all-start = ((f32[8,2,8,128]{3,2,1,0:T(8,128)}), f32[8,2,8,128]{3,2,1,0:T(8,128)S(1)}, u32[]{:S(2)}, u32[]{:S(2)}) async-start(f32[8,2,8,128]{3,2,1,0:T(8,128)} %add.3), calls=%async_computation | async-start | bytes 131072 | tf_op jit(solution)/shard_map/all_to_all | solution.py:353

commit v5 on v4

v5 whole, which is shorter than its diff:
```python
import functools

import jax
import jax.numpy as jnp
from jax import lax
from jax.experimental import pallas as pl
from jax.experimental.pallas import tpu as pltpu
from jax.sharding import PartitionSpec as P

BS = 16
TB = 2
PB = 4
LANES = 128
SUB = 8
NODES = (-3, -2, -1, 0, 1, 2, 3)
F32 = jnp.float32
BF16 = jnp.bfloat16


def halves(x):
    hi = x.astype(BF16)
    return hi, (x - hi.astype(F32)).astype(BF16)


def thirds(x):
    hi = x.astype(BF16)
    rest = x - hi.astype(F32)
    mid = rest.astype(BF16)
    return hi, mid, (rest - mid.astype(F32)).astype(BF16)


def dot(a, b):
    return jnp.dot(a, b, preferred_element_type=F32)


def nearest_blocks(shift):
    whole = (shift + BS // 2) // BS
    return whole, shift - whole * BS


def start_all(copies):
    for copy in copies:
        copy.start()
    return copies


def wait_all(copies):
    for copy in copies:
        copy.wait()


def pack_kernel(cfg, me_ref, ids_ref, face_ref, conserved_ref, *refs):
    outs, (all_ref, id_ref, sem) = refs[: cfg.n], refs[cfg.n :]
    copies = [pltpu.make_async_copy(ids_ref, id_ref, sem.at[8])]
    for c in range(8):
        source = face_ref.at[c] if c < 3 else conserved_ref.at[c - 3]
        copies.append(pltpu.make_async_copy(source, all_ref.at[c], sem.at[c]))
    start_all(copies)
    dests = [jnp.bitwise_xor(me_ref[0], k) * cfg.tiles for k in cfg.order]
    copies[0].wait()
    rows = lax.broadcasted_iota(jnp.int32, (SUB, LANES), 0)
    ids = jnp.zeros((SUB, LANES), jnp.int32)
    for slot in range(SUB):
        ids = jnp.where(rows == slot, id_ref[slot], ids)
    for out in outs:
        out[8 * cfg.tiles] = ids.astype(F32)
    for c in range(8):
        copies[1 + c].wait()
        for out, dest in zip(outs, dests):
            out[c * cfg.tiles : (c + 1) * cfg.tiles] = all_ref[c, pl.ds(dest, cfg.tiles)]


def unpack_kernel(cfg, me_ref, *refs):
    pieces, (conserved_ref, field_ref, sem) = refs[: cfg.n], refs[cfg.n :]
    copies = []
    for piece, k in zip(pieces, cfg.order):
        at = pl.ds(jnp.bitwise_xor(me_ref[0], k) * cfg.tiles, cfg.tiles)
        for j, (first, count, out) in enumerate(((0, 5, conserved_ref), (5, 3, field_ref))):
            copies.append(
                pltpu.make_async_copy(
                    piece.at[pl.ds(first, count)], out.at[:, at], sem.at[k, j]
                )
            )
    wait_all(start_all(copies))


def operators_kernel(cfg, me_ref, shift_ref, frac_ref, mh_ref, ml_ref, gh_ref, gl_ref, tj_ref):
    size = cfg.lanes
    first = (me_ref[0] * cfg.rows) // BS
    row = lax.broadcasted_iota(jnp.int32, (size, size), 0)
    col = lax.broadcasted_iota(jnp.int32, (size, size), 1)
    same = (row // BS) == (col // BS)
    e_in, e_out = row % BS, col % BS
    zero = jnp.zeros((size, size), F32)
    tj_ref[0] = jnp.where(same & (e_in < e_out), 1.0, zero).astype(BF16)
    tj_ref[1] = jnp.where(same, 1.0, zero).astype(BF16)
    for al in range(cfg.radii):
        _, rest = nearest_blocks(shift_ref[first + al])
        position = -jnp.full((1, size), frac_ref[first + al], F32)
        lagrange = []
        for a in NODES:
            product = jnp.ones_like(position)
            for b in NODES:
                if b != a:
                    product = product * ((position - float(b)) * (1.0 / float(a - b)))
            lagrange.append(product)
        weights = []
        for m in range(-3, 3):
            total = jnp.zeros_like(position)
            if m >= 0:
                for a in range(m + 1, 4):
                    total = total - lagrange[a + 3]
            else:
                for a in range(-3, m + 1):
                    total = total + lagrange[a + 3]
            weights.append(total)
        for d in range(3):
            at = e_in + BS * (d - 1)
            tap = jnp.where(same, at - e_out + rest, 100)
            remap, flux = zero, zero
            for a in NODES:
                hit = tap == a
                remap = jnp.where(hit, lagrange[a + 3], remap)
                if a < 3:
                    flux = jnp.where(hit, weights[a + 3], flux)
            flux = flux - jnp.where(same & (at < e_out - rest), 1.0, zero)
            mh_ref[al, d], ml_ref[al, d] = halves(remap)
            gh_ref[al, d], gl_ref[al, d] = halves(flux)


def gather_matrix(cfg, me, ids, whole):
    shape = (cfg.slots, 3 * cfg.slots)
    target = lax.broadcasted_iota(jnp.int32, shape, 0)
    owner = jnp.bitwise_xor(target >> 3, me)
    q_out, b_out = owner * PB + (target & 3), (target >> 2) & 1
    v = jnp.broadcast_to(ids, shape)
    q_in, b_in = (v >> 3) * PB + (v & 3), (v >> 2) & 1
    same = b_in == b_out
    cells = cfg.n * PB
    rows = []
    for d in (-1, 0, 1):
        hit = same & (((q_out - whole + d - q_in + 2 * cells) & (cells - 1)) == 0)
        rows.append(jnp.where(hit, 1.0, 0.0))
    rows.append(jnp.where(same & (q_in == q_out), 1.0, 0.0))
    back = (q_out - 1 - q_in + cells) & (cells - 1)
    count = jnp.where(back <= whole, 1.0, 0.0) + jnp.where(back + cells <= whole, 1.0, 0.0)
    rows.append(jnp.where(same, count, 0.0))
    return rows


def three_dots(high, low, mh, ml):
    rows = high.shape[0]
    both = dot(jnp.concatenate([high, low], axis=0), mh)
    return both[:rows] + both[rows:] + dot(high, ml)


def source(cfg, pieces, c, al):
    x = jnp.concatenate(
        [
            jnp.concatenate([p[c * cfg.tiles + al * cfg.per + t] for p in pieces], axis=0)
            for t in range(cfg.per)
        ],
        axis=1,
    )
    return jnp.concatenate(thirds(x), axis=0)


def numbers(cfg, pieces):
    ids = jnp.concatenate([p[8 * cfg.tiles] for p in pieces] * 3, axis=0)
    return jnp.transpose(ids)[0:1].astype(jnp.int32)


def whole_fluxes(cfg, ys, al, gh_ref, gl_ref, tj_ref):
    slots = cfg.slots
    part = [
        halves(jnp.concatenate([y[j * slots : (j + 1) * slots] for y in ys], axis=0))
        for j in range(5)
    ]
    flux = 0.0
    for d in range(3):
        flux = flux + three_dots(*part[d], gh_ref[al, d], gl_ref[al, d])
    for j in range(2):
        both = dot(jnp.concatenate(part[3 + j], axis=0), tj_ref[j])
        rows = both.shape[0] // 2
        flux = flux + (both[:rows] + both[rows:])
    return flux


def by_owner(cfg, me, out_ref, value):
    for k in range(cfg.n):
        for t in range(cfg.per):
            out_ref[jnp.bitwise_xor(me, k), t] = value[
                k * SUB : (k + 1) * SUB, t * LANES : (t + 1) * LANES
            ]


def edge_kernel(cfg, me_ref, shift_ref, *refs):
    pieces, (gh_ref, gl_ref, tj_ref, halo_ref) = refs[: cfg.n], refs[cfg.n :]
    me = me_ref[0]
    whole, _ = nearest_blocks(shift_ref[(me * cfg.rows) // BS])
    taken = gather_matrix(cfg, me, numbers(cfg, pieces), whole)
    y = dot(jnp.concatenate(taken, axis=0).astype(BF16), source(cfg, pieces, 0, 0))
    by_owner(cfg, me, halo_ref, whole_fluxes(cfg, [y], 0, gh_ref, gl_ref, tj_ref))


def rows_kernel(cfg, me_ref, shift_ref, *refs):
    n, slots, tiles, wide, per = cfg.n, cfg.slots, cfg.tiles, cfg.lanes, cfg.per
    pieces = refs[:n]
    mh_ref, ml_ref, gh_ref, gl_ref, tj_ref, out_ref, polar_ref = refs[n:]
    me = me_ref[0]
    first = (me * cfg.rows) // BS
    ids = numbers(cfg, pieces)

    def put(c, al, value):
        for k in range(n):
            for t in range(per):
                out_ref[k, c, al * per + t] = value[
                    k * SUB : (k + 1) * SUB, t * LANES : (t + 1) * LANES
                ]

    lane = lax.broadcasted_iota(jnp.int32, (slots, wide), 1)
    lower = (lax.broadcasted_iota(jnp.int32, (slots, wide), 0) >> 2) & 1 == 0
    total = []
    for al in range(cfg.radii):
        whole, _ = nearest_blocks(shift_ref[first + al])
        taken = jnp.concatenate(gather_matrix(cfg, me, ids, whole), axis=0).astype(BF16)
        ys = [dot(taken, source(cfg, pieces, c, al)) for c in range(2)]
        flux = whole_fluxes(cfg, ys, al, gh_ref, gl_ref, tj_ref)
        radial, polar = flux[:slots], flux[slots:]
        if cfg.split == 1:
            up = jnp.where(lower, jnp.concatenate([polar[4:], polar[:4]], axis=0), 0.0)
            after = pltpu.roll(jnp.where(lane < BS, up, polar), wide - BS, 1)
            polar_ref[...] = jnp.zeros_like(polar_ref)
        else:
            after = jnp.where(lane < wide - BS, pltpu.roll(polar, wide - BS, 1), 0.0)
            by_owner(cfg, me, polar_ref, polar)
        azimuthal = dot(taken[3 * slots : 4 * slots], source(cfg, pieces, 2, al))
        total.append((azimuthal + (after - polar) - radial, radial))
        ys = [dot(taken[: 3 * slots], source(cfg, pieces, 3 + c, al)) for c in range(5)] + ys
        remap = 0.0
        for d in range(3):
            high, low = halves(
                jnp.concatenate([y[d * slots : (d + 1) * slots] for y in ys], axis=0)
            )
            remap = remap + three_dots(high, low, mh_ref[al, d], ml_ref[al, d])
        for c in range(7):
            put(c, al, remap[c * slots : (c + 1) * slots])
    for al in range(cfg.radii):
        bp = total[al][0]
        put(7, al, bp + total[al + 1][1] if al + 1 < cfg.radii else bp)


def finish_kernel(cfg, me_ref, rows_ref, halo_ref, polar_ref, *outs):
    me, rest = me_ref[0], cfg.tiles - cfg.per
    for out, k in zip(outs, cfg.order):
        owner = jnp.bitwise_xor(me, k)
        out[...] = rows_ref[k]
        out[7, rest:] = rows_ref[k, 7, rest:] + halo_ref[owner]
        if cfg.split > 1:
            after = polar_ref[owner, 0]
            row = lax.broadcasted_iota(jnp.int32, after.shape, 0)
            lane = lax.broadcasted_iota(jnp.int32, after.shape, 1)
            up = jnp.where(row < 4, jnp.concatenate([after[4:], after[:4]], axis=0), 0.0)
            after = jnp.where(lax.rem(me, cfg.split) == cfg.split - 1, up, after)
            after = pltpu.roll(jnp.where(lane < BS, after, 0.0), LANES - BS, 1)
            out[7, cfg.tiles - 1] = out[7, cfg.tiles - 1] + after


class Sizes:
    def __init__(self, n):
        self.n = n
        self.order = list(range(n // 2, n)) + list(range(n // 2 - 1, -1, -1))
        self.rows = BS * BS // n
        self.tiles = self.rows * BS // LANES
        self.lanes = min(self.rows, BS) * BS
        self.radii = max(1, self.rows // BS)
        self.per = self.lanes // LANES
        self.split = max(1, BS // self.rows)
        self.slots = n * SUB


def shape(*dims, dtype=F32):
    return jax.ShapeDtypeStruct(dims, dtype)


def shards(conserved, face_field, block_ids, int_shift, frac_shift):
    n = lax.axis_size("phi")
    cfg = Sizes(n)
    count = lax.axis_size("tile") * n
    tiles, per = cfg.tiles, cfg.per
    smem = pl.BlockSpec(memory_space=pltpu.SMEM)
    vmem = pl.BlockSpec(memory_space=pltpu.VMEM)
    hbm = pl.BlockSpec(memory_space=pltpu.MemorySpace.HBM)

    def grant(mib):
        return pltpu.CompilerParams(vmem_limit_bytes=min(mib, 48) * 2**20)

    me = lax.axis_index("phi").astype(jnp.int32).reshape(1)

    def tiled(x):
        return x.reshape(SUB, x.shape[1], n * tiles, LANES).transpose(1, 2, 0, 3)

    def untiled(x):
        return x.transpose(2, 0, 1, 3).reshape(SUB, x.shape[0], n * tiles * LANES)

    def exchange(pieces):
        return [
            lax.ppermute(piece, "phi", [(s, s ^ k) for s in range(n)]) if k else piece
            for piece, k in zip(pieces, cfg.order)
        ]

    def in_hbm(x):
        return pltpu.with_memory_space_constraint(x, pltpu.MemorySpace.HBM)

    packed = pl.pallas_call(
        functools.partial(pack_kernel, cfg),
        out_shape=[shape(8 * tiles + 1, SUB, LANES)] * n,
        in_specs=[smem, hbm, hbm, hbm],
        out_specs=[vmem] * n,
        scratch_shapes=[
            pltpu.VMEM((8, n * tiles, SUB, LANES), F32),
            pltpu.SMEM((SUB,), jnp.int32),
            pltpu.SemaphoreType.DMA((9,)),
        ],
        compiler_params=grant(3),
        name="pack",
    )(me, in_hbm(block_ids), in_hbm(tiled(face_field)), in_hbm(tiled(conserved)))
    blocks = exchange(packed)

    square = shape(cfg.radii, 3, cfg.lanes, cfg.lanes, dtype=BF16)
    mh, ml, gh, gl, tj = pl.pallas_call(
        functools.partial(operators_kernel, cfg),
        out_shape=[square] * 4 + [shape(2, cfg.lanes, cfg.lanes, dtype=BF16)],
        in_specs=[smem] * 3,
        out_specs=[vmem] * 5,
        compiler_params=grant(8),
        name="operators",
    )(me, int_shift, frac_shift)

    owners = shape(n, per, SUB, LANES)
    halo = pl.pallas_call(
        functools.partial(edge_kernel, cfg),
        out_shape=owners,
        in_specs=[smem] * 2 + [vmem] * (n + 3),
        out_specs=vmem,
        compiler_params=grant(2 * n),
        name="edge",
    )(me, int_shift, *blocks, gh, gl, tj)
    halo = lax.ppermute(
        halo, ("tile", "phi"), [(s, s - cfg.split) for s in range(cfg.split, count)]
    )
    rows, polar = pl.pallas_call(
        functools.partial(rows_kernel, cfg),
        out_shape=[
            shape(n, 8, tiles, SUB, LANES),
            owners if cfg.split > 1 else shape(1, 1, SUB, LANES),
        ],
        in_specs=[smem] * 2 + [vmem] * (n + 5),
        out_specs=[vmem] * 2,
        compiler_params=grant(2 * n),
        name="rows",
    )(me, int_shift, *blocks, mh, ml, gh, gl, tj)
    if cfg.split > 1:
        polar = lax.ppermute(
            polar,
            "phi",
            [(s, s - 1 if s % cfg.split else s + cfg.split - 1) for s in range(n)],
        )
    done = pl.pallas_call(
        functools.partial(finish_kernel, cfg),
        out_shape=[shape(8, tiles, SUB, LANES)] * n,
        in_specs=[smem] + [vmem] * 3,
        out_specs=[vmem] * n,
        compiler_params=grant(2),
        name="finish",
    )(me, rows, halo, polar)
    conserved_out, field_out = pl.pallas_call(
        functools.partial(unpack_kernel, cfg),
        out_shape=[shape(5, n * tiles, SUB, LANES), shape(3, n * tiles, SUB, LANES)],
        in_specs=[smem] + [vmem] * n,
        out_specs=[hbm] * 2,
        scratch_shapes=[pltpu.SemaphoreType.DMA((n, 2))],
        compiler_params=grant(2),
        name="unpack",
    )(me, *exchange(done))
    return untiled(conserved_out), untiled(field_out)


def solution(mesh):
    return jax.shard_map(
        shards,
        mesh=mesh,
        in_specs=(
            P(("tile", "phi"), None, None),
            P(("tile", "phi"), None, None),
            P(("tile", "phi")),
            P("tile"),
            P("tile"),
        ),
        out_specs=(P(("tile", "phi"), None, None), P(("tile", "phi"), None, None)),
        check_vma=False,
    )
```

time: 69.9 us -> 63.2 us (0.904)
  the two profiles are of different devices: /device:TPU:0 before, /device:TPU:13 now
where the time goes in v5:
time: 63.2 us; the launch traced here: 62 us
  waiting for transfers between devices  32.1 us (51%)
  starting transfers between devices  20.4 us (32%)
  Pallas kernels  8.79 us (14%)
  between operations  0.7 us (1%)
    ppermute x14, waiting for transfers between devices, exchange(): lax.ppermute(piece, 'phi', [(s, s ^ k) for s in range(n)])  31.2 us
    ppermute x14, starting transfers between devices, exchange(): lax.ppermute(piece, 'phi', [(s, s ^ k) for s in range(n)])  18 us
    pallas_call x1, Pallas kernels, shards(): pl.pallas_call(functools.partial(rows_kernel, cfg), out_shape=[shape(n, 8...  2.96 us
    ppermute x1, starting transfers between devices, shards(): lax.ppermute(halo, ('tile', 'phi'), [(s, s - cfg.split) for s in range(cf...  2.4 us
    pallas_call x1, Pallas kernels, shards(): pl.pallas_call(functools.partial(operators_kernel, cfg), out_shape=[squar...  2.24 us
    pallas_call x1, Pallas kernels, shards(): pl.pallas_call(functools.partial(pack_kernel, cfg), out_shape=[shape(8 *...  1.37 us
  transfers between devices with their start and end apart: 15, of which 9 were waited for; matrix products, arithmetic and copies ran while one was open for 0% of the time, Pallas kernels for 8%

profile of v5, /device:TPU:13, one launch (start us, length us, event | category | flops | bytes accessed | tf_op | source)
XLA Modules:
  0.0 62.0 jit_solution(13486614431968110872)
XLA Ops:
  0.6 1.4 %pack.1 = (f32[33,8,128]{2,1,0:T(8,128)S(1)}, f32[33,8,128]{2,1,0:T(8,128)S(1)}, f32[33,8,128]{2,1,0:T(8,128)S(1)}, f32[33,8,128]{2,1,0:T(8,128)S(1)}, f32[33,8,...) custom-call(s32[1]{0:T(128)} %bitcast.me_ref, s32[8]{0:T(128)} %ids_ref.1, ...), custom_call_target="tpu_custom_call" | custom-call | tf_op jit(solution)/shard_map/pack/pallas_call | solution.py:315
  2.0 2.4 %collective-permute-start = (f32[33,8,128]{2,1,0:T(8,128)S(1)}, f32[33,8,128]{2,1,0:T(8,128)S(1)}, u32[]{:S(2)}, u32[]{:S(2)}) collective-permute-start(f32[33,8,128]{2,1,0:T(8,128)S(1)} %get-tuple-element.27), channel_id=1, source_target_pairs={{0,4},{1,5},{2,6},{3,7},{4,0},{5,1},{6,2},{7,3},{8,12},{9,13},{10,... | collective-permute-start | bytes 405512 | tf_op jit(solution)/shard_map/ppermute | solution.py:308
  4.4 0.9 %collective-permute-start.1 = (f32[33,8,128]{2,1,0:T(8,128)S(1)}, f32[33,8,128]{2,1,0:T(8,128)S(1)}, u32[]{:S(2)}, u32[]{:S(2)}) collective-permute-start(f32[33,8,128]{2,1,0:T(8,128)S(1)} %get-tuple-element.28), channel_id=1, source_target_pairs={{0,5},{1,4},{2,7},{3,6},{4,1},{5,0},{6,3},{7,2},{8,13},{9,12},{10,... | collective-permute-start | bytes 405512 | tf_op jit(solution)/shard_map/ppermute | solution.py:308
  5.3 1.3 %collective-permute-start.2 = (f32[33,8,128]{2,1,0:T(8,128)S(1)}, f32[33,8,128]{2,1,0:T(8,128)S(1)}, u32[]{:S(2)}, u32[]{:S(2)}) collective-permute-start(f32[33,8,128]{2,1,0:T(8,128)S(1)} %get-tuple-element.29), channel_id=1, source_target_pairs={{0,6},{1,7},{2,4},{3,5},{4,2},{5,3},{6,0},{7,1},{8,14},{9,15},{10,... | collective-permute-start | bytes 405512 | tf_op jit(solution)/shard_map/ppermute | solution.py:308
  6.6 0.4 collective-permute-start.3
  7.0 2.1 %collective-permute-start.4 = (f32[33,8,128]{2,1,0:T(8,128)S(1)}, f32[33,8,128]{2,1,0:T(8,128)S(1)}, u32[]{:S(2)}, u32[]{:S(2)}) collective-permute-start(f32[33,8,128]{2,1,0:T(8,128)S(1)} %get-tuple-element.31), channel_id=1, source_target_pairs={{0,3},{1,2},{2,1},{3,0},{4,7},{5,6},{6,5},{7,4},{8,11},{9,10},{10,... | collective-permute-start | bytes 405512 | tf_op jit(solution)/shard_map/ppermute | solution.py:308
  9.1 10.1 %collective-permute-done.refs_0_ = f32[33,8,128]{2,1,0:T(8,128)S(1)} collective-permute-done((f32[33,8,128]{2,1,0:T(8,128)S(1)}, f32[33,8,128]{2,1,0:T(8,128)S(1)}, u32[]{:S(2)}, u32[]{:S(2)}) %collective-permute-start) | collective-permute-done | bytes 135200 | tf_op jit(solution)/shard_map/ppermute | solution.py:308
  19.3 2.8 %collective-permute-done.1.refs_1_ = f32[33,8,128]{2,1,0:T(8,128)S(1)} collective-permute-done((f32[33,8,128]{2,1,0:T(8,128)S(1)}, f32[33,8,128]{2,1,0:T(8,128)S(1)}, u32[]{:S(2)}, u32[]{:S(2)}) %collective-permute-start.1) | collective-permute-done | bytes 135200 | tf_op jit(solution)/shard_map/ppermute | solution.py:308
  22.1 0.6 collective-permute-start.6
  22.7 2.2 %operators.1 = (bf16[2,3,256,256]{3,2,1,0:T(8,128)(2,1)S(1)}, bf16[2,3,256,256]{3,2,1,0:T(8,128)(2,1)S(1)}, bf16[2,3,256,256]{3,2,1,0:T(8,128)(2,1)S(1)}, bf16[2...) custom-call(s32[1]{0:T(128)} %bitcast.me_ref, s32[16]{0:T(128)S(1)} %copy-done, f32[16]{0:T(128)S(1)} %copy-done.1), custom_call_target="tpu_custom_call" | custom-call | tf_op jit(solution)/shard_map/operators/pallas_call | solution.py:331
  25.0 2.9 %collective-permute-done.3.refs_3_ = f32[33,8,128]{2,1,0:T(8,128)S(1)} collective-permute-done((f32[33,8,128]{2,1,0:T(8,128)S(1)}, f32[33,8,128]{2,1,0:T(8,128)S(1)}, u32[]{:S(2)}, u32[]{:S(2)}) %collective-permute-start.3) | collective-permute-done | bytes 135200 | tf_op jit(solution)/shard_map/ppermute | solution.py:308
  27.9 1.1 %edge.1 = f32[8,2,8,128]{3,2,1,0:T(8,128)S(1)} custom-call(s32[1]{0:T(128)} %bitcast.me_ref, s32[16]{0:T(128)S(1)} %copy-done, f32[33,8,128]{2,1,0:T(8,128)S(1)} %collective-permute-done.refs_0_, f32[33,8,128]{2,1,0:T(8,128)S(1)} %collective-permute-done.1.refs_1_, f32[33,8,128]{2,1,0:T(8,128)S(1)} %collective-permute-done.2.refs_2_, ...), custom_call_target="tpu_custom_call" | custom-call | tf_op jit(solution)/shard_map/edge/pallas_call | solution.py:341
  29.0 2.4 %collective-permute-start.7 = (f32[8,2,8,128]{3,2,1,0:T(8,128)S(1)}, f32[8,2,8,128]{3,2,1,0:T(8,128)S(1)}, u32[]{:S(2)}, u32[]{:S(2)}) collective-permute-start(f32[8,2,8,128]{3,2,1,0:T(8,128)S(1)} %edge.1), channel_id=1, source_target_pairs={{1,0},{2,1},{3,2},{4,3},{5,4},{6,5},{7,6},{8,7},{9,8},{10,9},{11,1... | collective-permute-start | bytes 196616 | tf_op jit(solution)/shard_map/ppermute | solution.py:349
  31.4 3.0 %rows.1 = (f32[8,8,4,8,128]{4,3,2,1,0:T(8,128)S(1)}, f32[1,1,8,128]{3,2,1,0:T(8,128)S(1)}) custom-call(s32[1]{0:T(128)} %bitcast.me_ref, s32[16]{0:T(128)S(1)} %copy-done, f32[33,8,128]{2,1,0:T(8,128)S(1)} %collective-permute-done.refs_0_, f32[33,8,128]{2,1,0:T(8,128)S(1)} %collective-permute-done.1.refs_1_, ...), custom_call_target="tpu_custom_call" | custom-call | tf_op jit(solution)/shard_map/rows/pallas_call | solution.py:352
  34.3 1.0 %collective-permute-done.7.halo_ref = f32[8,2,8,128]{3,2,1,0:T(8,128)S(1)} collective-permute-done((f32[8,2,8,128]{3,2,1,0:T(8,128)S(1)}, f32[8,2,8,128]{3,2,1,0:T(8,128)S(1)}, u32[]{:S(2)}, u32[]{:S(2)}) %collective-permute-start.7) | collective-permute-done | bytes 65568 | tf_op jit(solution)/shard_map/ppermute | solution.py:349
  35.4 4.6 %collective-permute-start.8 = (f32[8,4,8,128]{3,2,1,0:T(8,128)S(1)}, f32[8,4,8,128]{3,2,1,0:T(8,128)S(1)}, u32[]{:S(2)}, u32[]{:S(2)}) collective-permute-start(f32[8,4,8,128]{3,2,1,0:T(8,128)S(1)} %get-tuple-element.42), channel_id=1, source_target_pairs={{0,4},{1,5},{2,6},{3,7},{4,0},{5,1},{6,2},{7,3},{8,12},{9,13},{10,... | collective-permute-start | bytes 393224 | tf_op jit(solution)/shard_map/ppermute | solution.py:308
  40.2 1.9 %collective-permute-start.11 = (f32[8,4,8,128]{3,2,1,0:T(8,128)S(1)}, f32[8,4,8,128]{3,2,1,0:T(8,128)S(1)}, u32[]{:S(2)}, u32[]{:S(2)}) collective-permute-start(f32[8,4,8,128]{3,2,1,0:T(8,128)S(1)} %get-tuple-element.45), channel_id=1, source_target_pairs={{0,7},{1,6},{2,5},{3,4},{4,3},{5,2},{6,1},{7,0},{8,15},{9,14},{10,... | collective-permute-start | bytes 393224 | tf_op jit(solution)/shard_map/ppermute | solution.py:308
  42.1 3.0 %collective-permute-start.12 = (f32[8,4,8,128]{3,2,1,0:T(8,128)S(1)}, f32[8,4,8,128]{3,2,1,0:T(8,128)S(1)}, u32[]{:S(2)}, u32[]{:S(2)}) collective-permute-start(f32[8,4,8,128]{3,2,1,0:T(8,128)S(1)} %get-tuple-element.46), channel_id=1, source_target_pairs={{0,3},{1,2},{2,1},{3,0},{4,7},{5,6},{6,5},{7,4},{8,11},{9,10},{10,... | collective-permute-start | bytes 393224 | tf_op jit(solution)/shard_map/ppermute | solution.py:308
  45.1 7.4 %collective-permute-done.8.refs_0_ = f32[8,4,8,128]{3,2,1,0:T(8,128)S(1)} collective-permute-done((f32[8,4,8,128]{3,2,1,0:T(8,128)S(1)}, f32[8,4,8,128]{3,2,1,0:T(8,128)S(1)}, u32[]{:S(2)}, u32[]{:S(2)}) %collective-permute-start.8) | collective-permute-done | bytes 131104 | tf_op jit(solution)/shard_map/ppermute | solution.py:308
  52.5 2.8 %collective-permute-done.9.refs_1_ = f32[8,4,8,128]{3,2,1,0:T(8,128)S(1)} collective-permute-done((f32[8,4,8,128]{3,2,1,0:T(8,128)S(1)}, f32[8,4,8,128]{3,2,1,0:T(8,128)S(1)}, u32[]{:S(2)}, u32[]{:S(2)}) %collective-permute-start.9) | collective-permute-done | bytes 131104 | tf_op jit(solution)/shard_map/ppermute | solution.py:308
  55.3 0.5 collective-permute-start.14
  55.8 2.3 %collective-permute-done.10.refs_2_ = f32[8,4,8,128]{3,2,1,0:T(8,128)S(1)} collective-permute-done((f32[8,4,8,128]{3,2,1,0:T(8,128)S(1)}, f32[8,4,8,128]{3,2,1,0:T(8,128)S(1)}, u32[]{:S(2)}, u32[]{:S(2)}) %collective-permute-start.10) | collective-permute-done | bytes 131104 | tf_op jit(solution)/shard_map/ppermute | solution.py:308
  58.1 2.8 %collective-permute-done.11.refs_3_ = f32[8,4,8,128]{3,2,1,0:T(8,128)S(1)} collective-permute-done((f32[8,4,8,128]{3,2,1,0:T(8,128)S(1)}, f32[8,4,8,128]{3,2,1,0:T(8,128)S(1)}, u32[]{:S(2)}, u32[]{:S(2)}) %collective-permute-start.11) | collective-permute-done | bytes 131104 | tf_op jit(solution)/shard_map/ppermute | solution.py:308
  60.9 1.1 %unpack.1 = (f32[5,32,8,128]{3,2,1,0:T(8,128)}, f32[3,32,8,128]{3,2,1,0:T(8,128)}) custom-call(s32[1]{0:T(128)} %bitcast.me_ref, f32[8,4,8,128]{3,2,1,0:T(8,128)S(1)} %collective-permute-done.8.refs_0_, f32[8,4,8,128]{3,2,1,0:T(8,128)S(1)} %collective-permute-done.9.refs_1_, f32[8,4,8,128]{3,2,1,0:T(8,128)S(1)} %collective-permute-done.10.refs_2_, ...), custom_call_target="tpu_custom_call" | custom-call | tf_op jit(solution)/shard_map/unpack/pallas_call | solution.py:377
  (16 shorter events, 0.4 us)
Async XLA Ops:
  2.0 17.2 %collective-permute-start = (f32[33,8,128]{2,1,0:T(8,128)S(1)}, f32[33,8,128]{2,1,0:T(8,128)S(1)}, u32[]{:S(2)}, u32[]{:S(2)}) collective-permute-start(f32[33,8,128]{2,1,0:T(8,128)S(1)} %get-tuple-element.27), channel_id=1, source_target_pairs={{0,4},{1,5},{2,6},{3,7},{4,0},{5,1},{6,2},{7,3},{8,12},{9,13},{10,... | collective-permute-start | bytes 405512 | tf_op jit(solution)/shard_map/ppermute | solution.py:308
  4.4 17.7 %collective-permute-start.1 = (f32[33,8,128]{2,1,0:T(8,128)S(1)}, f32[33,8,128]{2,1,0:T(8,128)S(1)}, u32[]{:S(2)}, u32[]{:S(2)}) collective-permute-start(f32[33,8,128]{2,1,0:T(8,128)S(1)} %get-tuple-element.28), channel_id=1, source_target_pairs={{0,5},{1,4},{2,7},{3,6},{4,1},{5,0},{6,3},{7,2},{8,13},{9,12},{10,... | collective-permute-start | bytes 405512 | tf_op jit(solution)/shard_map/ppermute | solution.py:308
  5.3 19.7 %collective-permute-start.2 = (f32[33,8,128]{2,1,0:T(8,128)S(1)}, f32[33,8,128]{2,1,0:T(8,128)S(1)}, u32[]{:S(2)}, u32[]{:S(2)}) collective-permute-start(f32[33,8,128]{2,1,0:T(8,128)S(1)} %get-tuple-element.29), channel_id=1, source_target_pairs={{0,6},{1,7},{2,4},{3,5},{4,2},{5,3},{6,0},{7,1},{8,14},{9,15},{10,... | collective-permute-start | bytes 405512 | tf_op jit(solution)/shard_map/ppermute | solution.py:308
  6.6 21.3 %collective-permute-start.3 = (f32[33,8,128]{2,1,0:T(8,128)S(1)}, f32[33,8,128]{2,1,0:T(8,128)S(1)}, u32[]{:S(2)}, u32[]{:S(2)}) collective-permute-start(f32[33,8,128]{2,1,0:T(8,128)S(1)} %get-tuple-element.30), channel_id=1, source_target_pairs={{0,7},{1,6},{2,5},{3,4},{4,3},{5,2},{6,1},{7,0},{8,15},{9,14},{10,... | collective-permute-start | bytes 405512 | tf_op jit(solution)/shard_map/ppermute | solution.py:308
  7.0 20.9 %collective-permute-start.4 = (f32[33,8,128]{2,1,0:T(8,128)S(1)}, f32[33,8,128]{2,1,0:T(8,128)S(1)}, u32[]{:S(2)}, u32[]{:S(2)}) collective-permute-start(f32[33,8,128]{2,1,0:T(8,128)S(1)} %get-tuple-element.31), channel_id=1, source_target_pairs={{0,3},{1,2},{2,1},{3,0},{4,7},{5,6},{6,5},{7,4},{8,11},{9,10},{10,... | collective-permute-start | bytes 405512 | tf_op jit(solution)/shard_map/ppermute | solution.py:308
  19.2 3.5 %copy-start = (s32[16]{0:T(128)S(1)}, s32[16]{0:T(128)}, u32[]{:S(2)}) copy-start(s32[16]{0:T(128)} %shift_ref.5) | copy-start | bytes 196
  19.2 3.5 %copy-start.1 = (f32[16]{0:T(128)S(1)}, f32[16]{0:T(128)}, u32[]{:S(2)}) copy-start(f32[16]{0:T(128)} %frac_ref.1) | copy-start | bytes 196
  19.2 8.7 %collective-permute-start.5 = (f32[33,8,128]{2,1,0:T(8,128)S(1)}, f32[33,8,128]{2,1,0:T(8,128)S(1)}, u32[]{:S(2)}, u32[]{:S(2)}) collective-permute-start(f32[33,8,128]{2,1,0:T(8,128)S(1)} %get-tuple-element.32), channel_id=1, source_target_pairs={{0,2},{1,3},{2,0},{3,1},{4,6},{5,7},{6,4},{7,5},{8,10},{9,11},{10,... | collective-permute-start | bytes 405512 | tf_op jit(solution)/shard_map/ppermute | solution.py:308
  22.1 5.8 %collective-permute-start.6 = (f32[33,8,128]{2,1,0:T(8,128)S(1)}, f32[33,8,128]{2,1,0:T(8,128)S(1)}, u32[]{:S(2)}, u32[]{:S(2)}) collective-permute-start(f32[33,8,128]{2,1,0:T(8,128)S(1)} %get-tuple-element.33), channel_id=1, source_target_pairs={{0,1},{1,0},{2,3},{3,2},{4,5},{5,4},{6,7},{7,6},{8,9},{9,8},{10,11... | collective-permute-start | bytes 405512 | tf_op jit(solution)/shard_map/ppermute | solution.py:308
  29.0 6.3 %collective-permute-start.7 = (f32[8,2,8,128]{3,2,1,0:T(8,128)S(1)}, f32[8,2,8,128]{3,2,1,0:T(8,128)S(1)}, u32[]{:S(2)}, u32[]{:S(2)}) collective-permute-start(f32[8,2,8,128]{3,2,1,0:T(8,128)S(1)} %edge.1), channel_id=1, source_target_pairs={{1,0},{2,1},{3,2},{4,3},{5,4},{6,5},{7,6},{8,7},{9,8},{10,9},{11,1... | collective-permute-start | bytes 196616 | tf_op jit(solution)/shard_map/ppermute | solution.py:349
  35.4 17.1 %collective-permute-start.8 = (f32[8,4,8,128]{3,2,1,0:T(8,128)S(1)}, f32[8,4,8,128]{3,2,1,0:T(8,128)S(1)}, u32[]{:S(2)}, u32[]{:S(2)}) collective-permute-start(f32[8,4,8,128]{3,2,1,0:T(8,128)S(1)} %get-tuple-element.42), channel_id=1, source_target_pairs={{0,4},{1,5},{2,6},{3,7},{4,0},{5,1},{6,2},{7,3},{8,12},{9,13},{10,... | collective-permute-start | bytes 393224 | tf_op jit(solution)/shard_map/ppermute | solution.py:308
  40.0 15.3 %collective-permute-start.9 = (f32[8,4,8,128]{3,2,1,0:T(8,128)S(1)}, f32[8,4,8,128]{3,2,1,0:T(8,128)S(1)}, u32[]{:S(2)}, u32[]{:S(2)}) collective-permute-start(f32[8,4,8,128]{3,2,1,0:T(8,128)S(1)} %get-tuple-element.43), channel_id=1, source_target_pairs={{0,5},{1,4},{2,7},{3,6},{4,1},{5,0},{6,3},{7,2},{8,13},{9,12},{10,... | collective-permute-start | bytes 393224 | tf_op jit(solution)/shard_map/ppermute | solution.py:308
  40.0 18.1 %collective-permute-start.10 = (f32[8,4,8,128]{3,2,1,0:T(8,128)S(1)}, f32[8,4,8,128]{3,2,1,0:T(8,128)S(1)}, u32[]{:S(2)}, u32[]{:S(2)}) collective-permute-start(f32[8,4,8,128]{3,2,1,0:T(8,128)S(1)} %get-tuple-element.44), channel_id=1, source_target_pairs={{0,6},{1,7},{2,4},{3,5},{4,2},{5,3},{6,0},{7,1},{8,14},{9,15},{10,... | collective-permute-start | bytes 393224 | tf_op jit(solution)/shard_map/ppermute | solution.py:308
  40.2 20.7 %collective-permute-start.11 = (f32[8,4,8,128]{3,2,1,0:T(8,128)S(1)}, f32[8,4,8,128]{3,2,1,0:T(8,128)S(1)}, u32[]{:S(2)}, u32[]{:S(2)}) collective-permute-start(f32[8,4,8,128]{3,2,1,0:T(8,128)S(1)} %get-tuple-element.45), channel_id=1, source_target_pairs={{0,7},{1,6},{2,5},{3,4},{4,3},{5,2},{6,1},{7,0},{8,15},{9,14},{10,... | collective-permute-start | bytes 393224 | tf_op jit(solution)/shard_map/ppermute | solution.py:308
  42.1 18.8 %collective-permute-start.12 = (f32[8,4,8,128]{3,2,1,0:T(8,128)S(1)}, f32[8,4,8,128]{3,2,1,0:T(8,128)S(1)}, u32[]{:S(2)}, u32[]{:S(2)}) collective-permute-start(f32[8,4,8,128]{3,2,1,0:T(8,128)S(1)} %get-tuple-element.46), channel_id=1, source_target_pairs={{0,3},{1,2},{2,1},{3,0},{4,7},{5,6},{6,5},{7,4},{8,11},{9,10},{10,... | collective-permute-start | bytes 393224 | tf_op jit(solution)/shard_map/ppermute | solution.py:308
  52.5 8.4 %collective-permute-start.13 = (f32[8,4,8,128]{3,2,1,0:T(8,128)S(1)}, f32[8,4,8,128]{3,2,1,0:T(8,128)S(1)}, u32[]{:S(2)}, u32[]{:S(2)}) collective-permute-start(f32[8,4,8,128]{3,2,1,0:T(8,128)S(1)} %get-tuple-element.47), channel_id=1, source_target_pairs={{0,2},{1,3},{2,0},{3,1},{4,6},{5,7},{6,4},{7,5},{8,10},{9,11},{10,... | collective-permute-start | bytes 393224 | tf_op jit(solution)/shard_map/ppermute | solution.py:308
  55.3 5.6 %collective-permute-start.14 = (f32[8,4,8,128]{3,2,1,0:T(8,128)S(1)}, f32[8,4,8,128]{3,2,1,0:T(8,128)S(1)}, u32[]{:S(2)}, u32[]{:S(2)}) collective-permute-start(f32[8,4,8,128]{3,2,1,0:T(8,128)S(1)} %get-tuple-element.48), channel_id=1, source_target_pairs={{0,1},{1,0},{2,3},{3,2},{4,5},{5,4},{6,7},{7,6},{8,9},{9,8},{10,11... | collective-permute-start | bytes 393224 | tf_op jit(solution)/shard_map/ppermute | solution.py:308

commit v6 on v5

--- a/solution.py
+++ b/solution.py
@@ -50,24 +50,29 @@
 
 
 def pack_kernel(cfg, me_ref, ids_ref, face_ref, conserved_ref, *refs):
-    outs, (all_ref, id_ref, sem) = refs[: cfg.n], refs[cfg.n :]
+    n, tiles = cfg.n, cfg.tiles
+    half = n // 2
+    outs, (all_ref, id_ref, sem) = refs[: n + half], refs[n + half :]
     copies = [pltpu.make_async_copy(ids_ref, id_ref, sem.at[8])]
     for c in range(8):
-        source = face_ref.at[c] if c < 3 else conserved_ref.at[c - 3]
-        copies.append(pltpu.make_async_copy(source, all_ref.at[c], sem.at[c]))
+        from_ref = face_ref.at[c] if c < 3 else conserved_ref.at[c - 3]
+        copies.append(pltpu.make_async_copy(from_ref, all_ref.at[c], sem.at[c]))
     start_all(copies)
-    dests = [jnp.bitwise_xor(me_ref[0], k) * cfg.tiles for k in cfg.order]
+    dests = [jnp.bitwise_xor(me_ref[0], k) * tiles for k in cfg.order]
     copies[0].wait()
     rows = lax.broadcasted_iota(jnp.int32, (SUB, LANES), 0)
     ids = jnp.zeros((SUB, LANES), jnp.int32)
     for slot in range(SUB):
         ids = jnp.where(rows == slot, id_ref[slot], ids)
-    for out in outs:
-        out[8 * cfg.tiles] = ids.astype(F32)
+    for out in outs[:n]:
+        out[4 * tiles] = ids.astype(F32)
     for c in range(8):
         copies[1 + c].wait()
-        for out, dest in zip(outs, dests):
-            out[c * cfg.tiles : (c + 1) * cfg.tiles] = all_ref[c, pl.ds(dest, cfg.tiles)]
+        for j, dest in enumerate(dests):
+            out, at = outs[j], c * tiles + (c >= 4)
+            if c >= 4 and j < half:
+                out, at = outs[n + j], (c - 4) * tiles
+            out[at : at + tiles] = all_ref[c, pl.ds(dest, tiles)]
 
 
 def unpack_kernel(cfg, me_ref, *refs):
@@ -154,10 +159,10 @@
     return both[:rows] + both[rows:] + dot(high, ml)
 
 
-def source(cfg, pieces, c, al):
+def source(cfg, tiles_of, al):
     x = jnp.concatenate(
         [
-            jnp.concatenate([p[c * cfg.tiles + al * cfg.per + t] for p in pieces], axis=0)
+            jnp.concatenate([p[at + al * cfg.per + t] for p, at in tiles_of], axis=0)
             for t in range(cfg.per)
         ],
         axis=1,
@@ -165,8 +170,17 @@
     return jnp.concatenate(thirds(x), axis=0)
 
 
+def first_half(cfg, pieces, c):
+    return [(p, c * cfg.tiles) for p in pieces]
+
+
+def second_half(cfg, pieces, c):
+    near = [0] * (cfg.n // 2) + [4 * cfg.tiles + 1] * (cfg.n // 2)
+    return [(p, at + c * cfg.tiles) for p, at in zip(pieces, near)]
+
+
 def numbers(cfg, pieces):
-    ids = jnp.concatenate([p[8 * cfg.tiles] for p in pieces] * 3, axis=0)
+    ids = jnp.concatenate([p[4 * cfg.tiles] for p in pieces] * 3, axis=0)
     return jnp.transpose(ids)[0:1].astype(jnp.int32)
 
 
@@ -199,14 +213,23 @@
     me = me_ref[0]
     whole, _ = nearest_blocks(shift_ref[(me * cfg.rows) // BS])
     taken = gather_matrix(cfg, me, numbers(cfg, pieces), whole)
-    y = dot(jnp.concatenate(taken, axis=0).astype(BF16), source(cfg, pieces, 0, 0))
+    y = dot(jnp.concatenate(taken, axis=0).astype(BF16), source(cfg, first_half(cfg, pieces, 0), 0))
     by_owner(cfg, me, halo_ref, whole_fluxes(cfg, [y], 0, gh_ref, gl_ref, tj_ref))
 
 
-def rows_kernel(cfg, me_ref, shift_ref, *refs):
-    n, slots, tiles, wide, per = cfg.n, cfg.slots, cfg.tiles, cfg.lanes, cfg.per
+def remapped(cfg, ys, al, mh_ref, ml_ref):
+    total = 0.0
+    for d in range(3):
+        at = slice(d * cfg.slots, (d + 1) * cfg.slots)
+        high, low = halves(jnp.concatenate([y[at] for y in ys], axis=0))
+        total = total + three_dots(high, low, mh_ref[al, d], ml_ref[al, d])
+    return total
+
+
+def fields_kernel(cfg, me_ref, shift_ref, *refs):
+    n, slots, wide, per = cfg.n, cfg.slots, cfg.lanes, cfg.per
     pieces = refs[:n]
-    mh_ref, ml_ref, gh_ref, gl_ref, tj_ref, out_ref, polar_ref = refs[n:]
+    mh_ref, ml_ref, gh_ref, gl_ref, tj_ref, out_ref, taken_ref, polar_ref = refs[n:]
     me = me_ref[0]
     first = (me * cfg.rows) // BS
     ids = numbers(cfg, pieces)
@@ -224,7 +247,8 @@
     for al in range(cfg.radii):
         whole, _ = nearest_blocks(shift_ref[first + al])
         taken = jnp.concatenate(gather_matrix(cfg, me, ids, whole), axis=0).astype(BF16)
-        ys = [dot(taken, source(cfg, pieces, c, al)) for c in range(2)]
+        taken_ref[al] = taken[: 3 * slots]
+        ys = [dot(taken, source(cfg, first_half(cfg, pieces, c), al)) for c in range(2)]
         flux = whole_fluxes(cfg, ys, al, gh_ref, gl_ref, tj_ref)
         radial, polar = flux[:slots], flux[slots:]
         if cfg.split == 1:
@@ -234,28 +258,41 @@
         else:
             after = jnp.where(lane < wide - BS, pltpu.roll(polar, wide - BS, 1), 0.0)
             by_owner(cfg, me, polar_ref, polar)
-        azimuthal = dot(taken[3 * slots : 4 * slots], source(cfg, pieces, 2, al))
+        azimuthal = dot(
+            taken[3 * slots : 4 * slots], source(cfg, first_half(cfg, pieces, 2), al)
+        )
         total.append((azimuthal + (after - polar) - radial, radial))
-        ys = [dot(taken[: 3 * slots], source(cfg, pieces, 3 + c, al)) for c in range(5)] + ys
-        remap = 0.0
-        for d in range(3):
-            high, low = halves(
-                jnp.concatenate([y[d * slots : (d + 1) * slots] for y in ys], axis=0)
-            )
-            remap = remap + three_dots(high, low, mh_ref[al, d], ml_ref[al, d])
-        for c in range(7):
-            put(c, al, remap[c * slots : (c + 1) * slots])
+        ys.append(dot(taken[: 3 * slots], source(cfg, first_half(cfg, pieces, 3), al)))
+        remap = remapped(cfg, ys, al, mh_ref, ml_ref)
+        for c, at in enumerate((1, 2, 0)):
+            put(at, al, remap[c * slots : (c + 1) * slots])
     for al in range(cfg.radii):
         bp = total[al][0]
-        put(7, al, bp + total[al + 1][1] if al + 1 < cfg.radii else bp)
-
-
-def finish_kernel(cfg, me_ref, rows_ref, halo_ref, polar_ref, *outs):
+        put(3, al, bp + total[al + 1][1] if al + 1 < cfg.radii else bp)
+
+
+def finish_kernel(cfg, me_ref, *refs):
+    n, slots, per = cfg.n, cfg.slots, cfg.per
+    pieces = refs[:n]
+    mh_ref, ml_ref, taken_ref, rows_ref, halo_ref, polar_ref = refs[n : n + 6]
+    outs = refs[n + 6 :]
     me, rest = me_ref[0], cfg.tiles - cfg.per
+    for al in range(cfg.radii):
+        taken = taken_ref[al]
+        ys = [dot(taken, source(cfg, second_half(cfg, pieces, c), al)) for c in range(4)]
+        remap = remapped(cfg, ys, al, mh_ref, ml_ref)
+        for out, k in zip(outs, cfg.order):
+            for c in range(4):
+                for t in range(per):
+                    out[1 + c, al * per + t] = remap[
+                        c * slots + k * SUB : c * slots + (k + 1) * SUB,
+                        t * LANES : (t + 1) * LANES,
+                    ]
     for out, k in zip(outs, cfg.order):
         owner = jnp.bitwise_xor(me, k)
-        out[...] = rows_ref[k]
-        out[7, rest:] = rows_ref[k, 7, rest:] + halo_ref[owner]
+        out[0] = rows_ref[k, 0]
+        out[5:8] = rows_ref[k, 1:4]
+        out[7, rest:] = rows_ref[k, 3, rest:] + halo_ref[owner]
         if cfg.split > 1:
             after = polar_ref[owner, 0]
             row = lax.broadcasted_iota(jnp.int32, after.shape, 0)
@@ -303,10 +340,12 @@
     def untiled(x):
         return x.transpose(2, 0, 1, 3).reshape(SUB, x.shape[0], n * tiles * LANES)
 
-    def exchange(pieces):
+    half = n // 2
+
+    def exchange(pieces, order):
         return [
             lax.ppermute(piece, "phi", [(s, s ^ k) for s in range(n)]) if k else piece
-            for piece, k in zip(pieces, cfg.order)
+            for piece, k in zip(pieces, order)
         ]
 
     def in_hbm(x):
@@ -314,9 +353,11 @@
 
     packed = pl.pallas_call(
         functools.partial(pack_kernel, cfg),
-        out_shape=[shape(8 * tiles + 1, SUB, LANES)] * n,
-        in_specs=[smem, hbm, hbm, hbm],
-        out_specs=[vmem] * n,
+        out_shape=[shape(4 * tiles + 1, SUB, LANES)] * half
+        + [shape(8 * tiles + 1, SUB, LANES)] * half
+        + [shape(4 * tiles, SUB, LANES)] * half,
+        in_specs=[smem] + [hbm] * 3,
+        out_specs=[vmem] * (n + half),
         scratch_shapes=[
             pltpu.VMEM((8, n * tiles, SUB, LANES), F32),
             pltpu.SMEM((SUB,), jnp.int32),
@@ -325,7 +366,8 @@
         compiler_params=grant(3),
         name="pack",
     )(me, in_hbm(block_ids), in_hbm(tiled(face_field)), in_hbm(tiled(conserved)))
-    blocks = exchange(packed)
+    first = exchange(packed[:n], cfg.order)
+    far_second = exchange(packed[n:], cfg.order)
 
     square = shape(cfg.radii, 3, cfg.lanes, cfg.lanes, dtype=BF16)
     mh, ml, gh, gl, tj = pl.pallas_call(
@@ -345,21 +387,22 @@
         out_specs=vmem,
         compiler_params=grant(2 * n),
         name="edge",
-    )(me, int_shift, *blocks, gh, gl, tj)
+    )(me, int_shift, *first, gh, gl, tj)
     halo = lax.ppermute(
         halo, ("tile", "phi"), [(s, s - cfg.split) for s in range(cfg.split, count)]
     )
-    rows, polar = pl.pallas_call(
-        functools.partial(rows_kernel, cfg),
+    rows, taken, polar = pl.pallas_call(
+        functools.partial(fields_kernel, cfg),
         out_shape=[
-            shape(n, 8, tiles, SUB, LANES),
+            shape(n, 4, tiles, SUB, LANES),
+            shape(cfg.radii, 3 * cfg.slots, 3 * cfg.slots, dtype=BF16),
             owners if cfg.split > 1 else shape(1, 1, SUB, LANES),
         ],
         in_specs=[smem] * 2 + [vmem] * (n + 5),
-        out_specs=[vmem] * 2,
+        out_specs=[vmem] * 3,
         compiler_params=grant(2 * n),
-        name="rows",
-    )(me, int_shift, *blocks, mh, ml, gh, gl, tj)
+        name="fields",
+    )(me, int_shift, *first, mh, ml, gh, gl, tj)
     if cfg.split > 1:
         polar = lax.ppermute(
             polar,
@@ -369,11 +412,11 @@
     done = pl.pallas_call(
         functools.partial(finish_kernel, cfg),
         out_shape=[shape(8, tiles, SUB, LANES)] * n,
-        in_specs=[smem] + [vmem] * 3,
+        in_specs=[smem] + [vmem] * (n + 6),
         out_specs=[vmem] * n,
-        compiler_params=grant(2),
+        compiler_params=grant(2 * n),
         name="finish",
-    )(me, rows, halo, polar)
+    )(me, *far_second, *first[half:], mh, ml, taken, rows, halo, polar)
     conserved_out, field_out = pl.pallas_call(
         functools.partial(unpack_kernel, cfg),
         out_shape=[shape(5, n * tiles, SUB, LANES), shape(3, n * tiles, SUB, LANES)],
@@ -382,7 +425,7 @@
         scratch_shapes=[pltpu.SemaphoreType.DMA((n, 2))],
         compiler_params=grant(2),
         name="unpack",
-    )(me, *exchange(done))
+    )(me, *exchange(done, cfg.order))
     return untiled(conserved_out), untiled(field_out)
 
 

time: 63.2 us -> 59.3 us (0.938)
  waiting for transfers between devices: 32.1 us -> 24 us
  starting transfers between devices: 20.4 us -> 24.9 us
    ppermute x14 -> x18, waiting for transfers between devices: 31.2 us -> 23.5 us  [exchange(): lax.ppermute(piece, 'phi', [(s, s ^ k) for s in range(n)])]
    ppermute x14 -> x18, starting transfers between devices: 18 us -> 22.8 us  [exchange(): lax.ppermute(piece, 'phi', [(s, s ^ k) for s in range(n)])]
    pallas_call x1, Pallas kernels: 0.07 us -> 1.06 us  [shards(): pl.pallas_call(functools.partial(finish_kernel, cfg), out_shape=[shape(8,...]
    pallas_call x2, Pallas kernels: 4.33 us -> 3.52 us  [the longest x1 2.15 us: shards(): pl.pallas_call(functools.partial(fields_kernel, cfg), out_shape=[shape(n,...]
  transfers between devices with their start and end apart: 15 -> 19, of which waited for: 9 -> 9; matrix products, arithmetic and copies ran while one was open for 0% -> 0% of each run, Pallas kernels for 8% -> 9%
where the time goes in v6:
time: 59.3 us; the launch traced here: 58.6 us
  starting transfers between devices  24.9 us (42%)
  waiting for transfers between devices  24 us (40%)
  Pallas kernels  8.97 us (15%)
  between operations  0.72 us (1%)
    ppermute x18, waiting for transfers between devices, exchange(): lax.ppermute(piece, 'phi', [(s, s ^ k) for s in range(n)])  23.5 us
    ppermute x18, starting transfers between devices, exchange(): lax.ppermute(piece, 'phi', [(s, s ^ k) for s in range(n)])  22.8 us
    pallas_call x1, Pallas kernels, shards(): pl.pallas_call(functools.partial(operators_kernel, cfg), out_shape=[squar...  2.24 us
    pallas_call x1, Pallas kernels, shards(): pl.pallas_call(functools.partial(fields_kernel, cfg), out_shape=[shape(n,...  2.15 us
    ppermute x1, starting transfers between devices, shards(): lax.ppermute(halo, ('tile', 'phi'), [(s, s - cfg.split) for s in range(cf...  2.08 us
    pallas_call x1, Pallas kernels, shards(): pl.pallas_call(functools.partial(pack_kernel, cfg), out_shape=[shape(4 *...  1.37 us
  transfers between devices with their start and end apart: 19, of which 9 were waited for; matrix products, arithmetic and copies ran while one was open for 0% of the time, Pallas kernels for 9%

profile of v6, /device:TPU:13, one launch (start us, length us, event | category | flops | bytes accessed | tf_op | source)
XLA Modules:
  0.0 58.6 jit_solution(16182370378436932790)
XLA Ops:
  0.6 1.4 %pack.1 = (f32[17,8,128]{2,1,0:T(8,128)S(1)}, f32[17,8,128]{2,1,0:T(8,128)S(1)}, f32[17,8,128]{2,1,0:T(8,128)S(1)}, f32[17,8,128]{2,1,0:T(8,128)S(1)}, f32[33,8,...) custom-call(s32[1]{0:T(128)} %bitcast.me_ref, ...), custom_call_target="tpu_custom_call" | custom-call | tf_op jit(solution)/shard_map/pack/pallas_call | solution.py:354
  2.0 2.4 %collective-permute-start.7 = (f32[17,8,128]{2,1,0:T(8,128)S(1)}, f32[17,8,128]{2,1,0:T(8,128)S(1)}, u32[]{:S(2)}, u32[]{:S(2)}) collective-permute-start(f32[17,8,128]{2,1,0:T(8,128)S(1)} %get-tuple-element.42), channel_id=1, source_target_pairs={{0,4},{1,5},{2,6},{3,7},{4,0},{5,1},{6,2},{7,3},{8,12},{9,13},{10,... | collective-permute-start | bytes 208904 | tf_op jit(solution)/shard_map/ppermute | solution.py:347
  5.4 1.3 %collective-permute-start.5 = (f32[33,8,128]{2,1,0:T(8,128)S(1)}, f32[33,8,128]{2,1,0:T(8,128)S(1)}, u32[]{:S(2)}, u32[]{:S(2)}) collective-permute-start(f32[33,8,128]{2,1,0:T(8,128)S(1)} %get-tuple-element.37), channel_id=1, source_target_pairs={{0,2},{1,3},{2,0},{3,1},{4,6},{5,7},{6,4},{7,5},{8,10},{9,11},{10,... | collective-permute-start | bytes 405512 | tf_op jit(solution)/shard_map/ppermute | solution.py:347
  7.4 1.4 %collective-permute-done.7.refs_0_ = f32[17,8,128]{2,1,0:T(8,128)S(1)} collective-permute-done((f32[17,8,128]{2,1,0:T(8,128)S(1)}, f32[17,8,128]{2,1,0:T(8,128)S(1)}, u32[]{:S(2)}, u32[]{:S(2)}) %collective-permute-start.7) | collective-permute-done | bytes 69664 | tf_op jit(solution)/shard_map/ppermute | solution.py:347
  8.8 1.8 %collective-permute-done.8.refs_1_ = f32[17,8,128]{2,1,0:T(8,128)S(1)} collective-permute-done((f32[17,8,128]{2,1,0:T(8,128)S(1)}, f32[17,8,128]{2,1,0:T(8,128)S(1)}, u32[]{:S(2)}, u32[]{:S(2)}) %collective-permute-start.8) | collective-permute-done | bytes 69664 | tf_op jit(solution)/shard_map/ppermute | solution.py:347
  11.3 2.2 %operators.1 = (bf16[2,3,256,256]{3,2,1,0:T(8,128)(2,1)S(1)}, bf16[2,3,256,256]{3,2,1,0:T(8,128)(2,1)S(1)}, bf16[2,3,256,256]{3,2,1,0:T(8,128)(2,1)S(1)}, bf16[2...) custom-call(s32[1]{0:T(128)} %bitcast.me_ref, s32[16]{0:T(128)S(1)} %copy-done, f32[16]{0:T(128)S(1)} %copy-done.1), custom_call_target="tpu_custom_call" | custom-call | tf_op jit(solution)/shard_map/operators/pallas_call | solution.py:373
  13.6 5.2 %collective-permute-start = (f32[16,8,128]{2,1,0:T(8,128)S(1)}, f32[16,8,128]{2,1,0:T(8,128)S(1)}, u32[]{:S(2)}, u32[]{:S(2)}) collective-permute-start(f32[16,8,128]{2,1,0:T(8,128)S(1)} %get-tuple-element.32), channel_id=1, source_target_pairs={{0,4},{1,5},{2,6},{3,7},{4,0},{5,1},{6,2},{7,3},{8,12},{9,13},{10,... | collective-permute-start | bytes 196616 | tf_op jit(solution)/shard_map/ppermute | solution.py:347
  18.8 1.6 %collective-permute-start.1 = (f32[16,8,128]{2,1,0:T(8,128)S(1)}, f32[16,8,128]{2,1,0:T(8,128)S(1)}, u32[]{:S(2)}, u32[]{:S(2)}) collective-permute-start(f32[16,8,128]{2,1,0:T(8,128)S(1)} %get-tuple-element.33), channel_id=1, source_target_pairs={{0,5},{1,4},{2,7},{3,6},{4,1},{5,0},{6,3},{7,2},{8,13},{9,12},{10,... | collective-permute-start | bytes 196616 | tf_op jit(solution)/shard_map/ppermute | solution.py:347
  20.4 1.2 %collective-permute-start.2 = (f32[16,8,128]{2,1,0:T(8,128)S(1)}, f32[16,8,128]{2,1,0:T(8,128)S(1)}, u32[]{:S(2)}, u32[]{:S(2)}) collective-permute-start(f32[16,8,128]{2,1,0:T(8,128)S(1)} %get-tuple-element.34), channel_id=1, source_target_pairs={{0,6},{1,7},{2,4},{3,5},{4,2},{5,3},{6,0},{7,1},{8,14},{9,15},{10,... | collective-permute-start | bytes 196616 | tf_op jit(solution)/shard_map/ppermute | solution.py:347
  22.1 1.0 %edge.1 = f32[8,2,8,128]{3,2,1,0:T(8,128)S(1)} custom-call(s32[1]{0:T(128)} %bitcast.me_ref, s32[16]{0:T(128)S(1)} %copy-done, f32[17,8,128]{2,1,0:T(8,128)S(1)} %collective-permute-done.7.refs_0_, f32[17,8,128]{2,1,0:T(8,128)S(1)} %collective-permute-done.8.refs_1_, f32[17,8,128]{2,1,0:T(8,128)S(1)} %collective-permute-done.9.refs_2_, ...), custom_call_target="tpu_custom_call" | custom-call | tf_op jit(solution)/shard_map/edge/pallas_call | solution.py:383
  23.1 2.1 %collective-permute-start.11 = (f32[8,2,8,128]{3,2,1,0:T(8,128)S(1)}, f32[8,2,8,128]{3,2,1,0:T(8,128)S(1)}, u32[]{:S(2)}, u32[]{:S(2)}) collective-permute-start(f32[8,2,8,128]{3,2,1,0:T(8,128)S(1)} %edge.1), channel_id=1, source_target_pairs={{1,0},{2,1},{3,2},{4,3},{5,4},{6,5},{7,6},{8,7},{9,8},{10,9},{11,1... | collective-permute-start | bytes 196616 | tf_op jit(solution)/shard_map/ppermute | solution.py:391
  25.2 2.2 %fields.1 = (f32[8,4,4,8,128]{4,3,2,1,0:T(8,128)S(1)}, bf16[2,192,192]{2,1,0:T(8,128)(2,1)S(1)}, f32[1,1,8,128]{3,2,1,0:T(8,128)S(1)}) custom-call(s32[1]{0:T(128)} %bitcast.me_ref, s32[16]{0:T(128)S(1)} %copy-done, f32[17,8,128]{2,1,0:T(8,128)S(1)} %collective-permute-done.7.refs_0_, f32[17,8,128]{2,1,0:T(8,128)S(1)} %collective-permute-done.8.refs_1_, ...), custom_call_target="tpu_custom_call" | custom-call | tf_op jit(solution)/shard_map/fields/pallas_call | solution.py:394
  27.4 2.4 %collective-permute-done.2.refs_2_ = f32[16,8,128]{2,1,0:T(8,128)S(1)} collective-permute-done((f32[16,8,128]{2,1,0:T(8,128)S(1)}, f32[16,8,128]{2,1,0:T(8,128)S(1)}, u32[]{:S(2)}, u32[]{:S(2)}) %collective-permute-start.2) | collective-permute-done | bytes 65568 | tf_op jit(solution)/shard_map/ppermute | solution.py:347
  29.8 1.4 %collective-permute-done.3.refs_3_ = f32[16,8,128]{2,1,0:T(8,128)S(1)} collective-permute-done((f32[16,8,128]{2,1,0:T(8,128)S(1)}, f32[16,8,128]{2,1,0:T(8,128)S(1)}, u32[]{:S(2)}, u32[]{:S(2)}) %collective-permute-start.3) | collective-permute-done | bytes 65568 | tf_op jit(solution)/shard_map/ppermute | solution.py:347
  31.7 1.1 %finish.1 = (f32[8,4,8,128]{3,2,1,0:T(8,128)S(1)}, f32[8,4,8,128]{3,2,1,0:T(8,128)S(1)}, f32[8,4,8,128]{3,2,1,0:T(8,128)S(1)}, f32[8,4,8,128]{3,2,1,0:T(8,128)S(...) custom-call(s32[1]{0:T(128)} %bitcast.me_ref, ...), custom_call_target="tpu_custom_call" | custom-call | tf_op jit(solution)/shard_map/finish/pallas_call | solution.py:412
  32.7 2.7 %collective-permute-start.12 = (f32[8,4,8,128]{3,2,1,0:T(8,128)S(1)}, f32[8,4,8,128]{3,2,1,0:T(8,128)S(1)}, u32[]{:S(2)}, u32[]{:S(2)}) collective-permute-start(f32[8,4,8,128]{3,2,1,0:T(8,128)S(1)} %get-tuple-element.52), channel_id=1, source_target_pairs={{0,4},{1,5},{2,6},{3,7},{4,0},{5,1},{6,2},{7,3},{8,12},{9,13},{10,... | collective-permute-start | bytes 393224 | tf_op jit(solution)/shard_map/ppermute | solution.py:347
  35.6 1.9 %collective-permute-start.15 = (f32[8,4,8,128]{3,2,1,0:T(8,128)S(1)}, f32[8,4,8,128]{3,2,1,0:T(8,128)S(1)}, u32[]{:S(2)}, u32[]{:S(2)}) collective-permute-start(f32[8,4,8,128]{3,2,1,0:T(8,128)S(1)} %get-tuple-element.55), channel_id=1, source_target_pairs={{0,7},{1,6},{2,5},{3,4},{4,3},{5,2},{6,1},{7,0},{8,15},{9,14},{10,... | collective-permute-start | bytes 393224 | tf_op jit(solution)/shard_map/ppermute | solution.py:347
  37.5 2.3 %collective-permute-start.16 = (f32[8,4,8,128]{3,2,1,0:T(8,128)S(1)}, f32[8,4,8,128]{3,2,1,0:T(8,128)S(1)}, u32[]{:S(2)}, u32[]{:S(2)}) collective-permute-start(f32[8,4,8,128]{3,2,1,0:T(8,128)S(1)} %get-tuple-element.56), channel_id=1, source_target_pairs={{0,3},{1,2},{2,1},{3,0},{4,7},{5,6},{6,5},{7,4},{8,11},{9,10},{10,... | collective-permute-start | bytes 393224 | tf_op jit(solution)/shard_map/ppermute | solution.py:347
  39.8 8.7 %collective-permute-done.12.refs_0_ = f32[8,4,8,128]{3,2,1,0:T(8,128)S(1)} collective-permute-done((f32[8,4,8,128]{3,2,1,0:T(8,128)S(1)}, f32[8,4,8,128]{3,2,1,0:T(8,128)S(1)}, u32[]{:S(2)}, u32[]{:S(2)}) %collective-permute-start.12) | collective-permute-done | bytes 131104 | tf_op jit(solution)/shard_map/ppermute | solution.py:347
  48.5 2.8 %collective-permute-done.13.refs_1_ = f32[8,4,8,128]{3,2,1,0:T(8,128)S(1)} collective-permute-done((f32[8,4,8,128]{3,2,1,0:T(8,128)S(1)}, f32[8,4,8,128]{3,2,1,0:T(8,128)S(1)}, u32[]{:S(2)}, u32[]{:S(2)}) %collective-permute-start.13) | collective-permute-done | bytes 131104 | tf_op jit(solution)/shard_map/ppermute | solution.py:347
  51.3 1.2 %collective-permute-start.18 = (f32[8,4,8,128]{3,2,1,0:T(8,128)S(1)}, f32[8,4,8,128]{3,2,1,0:T(8,128)S(1)}, u32[]{:S(2)}, u32[]{:S(2)}) collective-permute-start(f32[8,4,8,128]{3,2,1,0:T(8,128)S(1)} %get-tuple-element.58), channel_id=1, source_target_pairs={{0,1},{1,0},{2,3},{3,2},{4,5},{5,4},{6,7},{7,6},{8,9},{9,8},{10,11... | collective-permute-start | bytes 393224 | tf_op jit(solution)/shard_map/ppermute | solution.py:347
  52.5 1.6 %collective-permute-done.14.refs_2_ = f32[8,4,8,128]{3,2,1,0:T(8,128)S(1)} collective-permute-done((f32[8,4,8,128]{3,2,1,0:T(8,128)S(1)}, f32[8,4,8,128]{3,2,1,0:T(8,128)S(1)}, u32[]{:S(2)}, u32[]{:S(2)}) %collective-permute-start.14) | collective-permute-done | bytes 131104 | tf_op jit(solution)/shard_map/ppermute | solution.py:347
  54.1 3.4 %collective-permute-done.15.refs_3_ = f32[8,4,8,128]{3,2,1,0:T(8,128)S(1)} collective-permute-done((f32[8,4,8,128]{3,2,1,0:T(8,128)S(1)}, f32[8,4,8,128]{3,2,1,0:T(8,128)S(1)}, u32[]{:S(2)}, u32[]{:S(2)}) %collective-permute-start.15) | collective-permute-done | bytes 131104 | tf_op jit(solution)/shard_map/ppermute | solution.py:347
  57.5 1.1 %unpack.1 = (f32[5,32,8,128]{3,2,1,0:T(8,128)}, f32[3,32,8,128]{3,2,1,0:T(8,128)}) custom-call(s32[1]{0:T(128)} %bitcast.me_ref, f32[8,4,8,128]{3,2,1,0:T(8,128)S(1)} %collective-permute-done.12.refs_0_, f32[8,4,8,128]{3,2,1,0:T(8,128)S(1)} %collective-permute-done.13.refs_1_, f32[8,4,8,128]{3,2,1,0:T(8,128)S(1)} %collective-permute-done.14.refs_2_, ...), custom_call_target="tpu_custom_call" | custom-call | tf_op jit(solution)/shard_map/unpack/pallas_call | solution.py:420
  (24 shorter events, 3.6 us)
Async XLA Ops:
  2.0 6.8 %collective-permute-start.7 = (f32[17,8,128]{2,1,0:T(8,128)S(1)}, f32[17,8,128]{2,1,0:T(8,128)S(1)}, u32[]{:S(2)}, u32[]{:S(2)}) collective-permute-start(f32[17,8,128]{2,1,0:T(8,128)S(1)} %get-tuple-element.42), channel_id=1, source_target_pairs={{0,4},{1,5},{2,6},{3,7},{4,0},{5,1},{6,2},{7,3},{8,12},{9,13},{10,... | collective-permute-start | bytes 208904 | tf_op jit(solution)/shard_map/ppermute | solution.py:347
  4.4 6.3 %collective-permute-start.8 = (f32[17,8,128]{2,1,0:T(8,128)S(1)}, f32[17,8,128]{2,1,0:T(8,128)S(1)}, u32[]{:S(2)}, u32[]{:S(2)}) collective-permute-start(f32[17,8,128]{2,1,0:T(8,128)S(1)} %get-tuple-element.43), channel_id=1, source_target_pairs={{0,5},{1,4},{2,7},{3,6},{4,1},{5,0},{6,3},{7,2},{8,13},{9,12},{10,... | collective-permute-start | bytes 208904 | tf_op jit(solution)/shard_map/ppermute | solution.py:347
  5.3 15.1 %collective-permute-start.4 = (f32[33,8,128]{2,1,0:T(8,128)S(1)}, f32[33,8,128]{2,1,0:T(8,128)S(1)}, u32[]{:S(2)}, u32[]{:S(2)}) collective-permute-start(f32[33,8,128]{2,1,0:T(8,128)S(1)} %get-tuple-element.36), channel_id=1, source_target_pairs={{0,3},{1,2},{2,1},{3,0},{4,7},{5,6},{6,5},{7,4},{8,11},{9,10},{10,... | collective-permute-start | bytes 405512 | tf_op jit(solution)/shard_map/ppermute | solution.py:347
  5.4 16.1 %collective-permute-start.5 = (f32[33,8,128]{2,1,0:T(8,128)S(1)}, f32[33,8,128]{2,1,0:T(8,128)S(1)}, u32[]{:S(2)}, u32[]{:S(2)}) collective-permute-start(f32[33,8,128]{2,1,0:T(8,128)S(1)} %get-tuple-element.37), channel_id=1, source_target_pairs={{0,2},{1,3},{2,0},{3,1},{4,6},{5,7},{6,4},{7,5},{8,10},{9,11},{10,... | collective-permute-start | bytes 405512 | tf_op jit(solution)/shard_map/ppermute | solution.py:347
  6.7 15.4 %collective-permute-start.6 = (f32[33,8,128]{2,1,0:T(8,128)S(1)}, f32[33,8,128]{2,1,0:T(8,128)S(1)}, u32[]{:S(2)}, u32[]{:S(2)}) collective-permute-start(f32[33,8,128]{2,1,0:T(8,128)S(1)} %get-tuple-element.38), channel_id=1, source_target_pairs={{0,1},{1,0},{2,3},{3,2},{4,5},{5,4},{6,7},{7,6},{8,9},{9,8},{10,11... | collective-permute-start | bytes 405512 | tf_op jit(solution)/shard_map/ppermute | solution.py:347
  8.8 2.5 %copy-start = (s32[16]{0:T(128)S(1)}, s32[16]{0:T(128)}, u32[]{:S(2)}) copy-start(s32[16]{0:T(128)} %shift_ref.5) | copy-start | bytes 196
  8.8 2.5 %copy-start.1 = (f32[16]{0:T(128)S(1)}, f32[16]{0:T(128)}, u32[]{:S(2)}) copy-start(f32[16]{0:T(128)} %frac_ref.1) | copy-start | bytes 196
  8.8 4.8 %collective-permute-start.9 = (f32[17,8,128]{2,1,0:T(8,128)S(1)}, f32[17,8,128]{2,1,0:T(8,128)S(1)}, u32[]{:S(2)}, u32[]{:S(2)}) collective-permute-start(f32[17,8,128]{2,1,0:T(8,128)S(1)} %get-tuple-element.44), channel_id=1, source_target_pairs={{0,6},{1,7},{2,4},{3,5},{4,2},{5,3},{6,0},{7,1},{8,14},{9,15},{10,... | collective-permute-start | bytes 208904 | tf_op jit(solution)/shard_map/ppermute | solution.py:347
  10.6 8.1 %collective-permute-start.10 = (f32[17,8,128]{2,1,0:T(8,128)S(1)}, f32[17,8,128]{2,1,0:T(8,128)S(1)}, u32[]{:S(2)}, u32[]{:S(2)}) collective-permute-start(f32[17,8,128]{2,1,0:T(8,128)S(1)} %get-tuple-element.45), channel_id=1, source_target_pairs={{0,7},{1,6},{2,5},{3,4},{4,3},{5,2},{6,1},{7,0},{8,15},{9,14},{10,... | collective-permute-start | bytes 208904 | tf_op jit(solution)/shard_map/ppermute | solution.py:347
  13.6 13.8 %collective-permute-start = (f32[16,8,128]{2,1,0:T(8,128)S(1)}, f32[16,8,128]{2,1,0:T(8,128)S(1)}, u32[]{:S(2)}, u32[]{:S(2)}) collective-permute-start(f32[16,8,128]{2,1,0:T(8,128)S(1)} %get-tuple-element.32), channel_id=1, source_target_pairs={{0,4},{1,5},{2,6},{3,7},{4,0},{5,1},{6,2},{7,3},{8,12},{9,13},{10,... | collective-permute-start | bytes 196616 | tf_op jit(solution)/shard_map/ppermute | solution.py:347
  18.8 8.6 %collective-permute-start.1 = (f32[16,8,128]{2,1,0:T(8,128)S(1)}, f32[16,8,128]{2,1,0:T(8,128)S(1)}, u32[]{:S(2)}, u32[]{:S(2)}) collective-permute-start(f32[16,8,128]{2,1,0:T(8,128)S(1)} %get-tuple-element.33), channel_id=1, source_target_pairs={{0,5},{1,4},{2,7},{3,6},{4,1},{5,0},{6,3},{7,2},{8,13},{9,12},{10,... | collective-permute-start | bytes 196616 | tf_op jit(solution)/shard_map/ppermute | solution.py:347
  20.4 9.5 %collective-permute-start.2 = (f32[16,8,128]{2,1,0:T(8,128)S(1)}, f32[16,8,128]{2,1,0:T(8,128)S(1)}, u32[]{:S(2)}, u32[]{:S(2)}) collective-permute-start(f32[16,8,128]{2,1,0:T(8,128)S(1)} %get-tuple-element.34), channel_id=1, source_target_pairs={{0,6},{1,7},{2,4},{3,5},{4,2},{5,3},{6,0},{7,1},{8,14},{9,15},{10,... | collective-permute-start | bytes 196616 | tf_op jit(solution)/shard_map/ppermute | solution.py:347
  21.5 9.7 %collective-permute-start.3 = (f32[16,8,128]{2,1,0:T(8,128)S(1)}, f32[16,8,128]{2,1,0:T(8,128)S(1)}, u32[]{:S(2)}, u32[]{:S(2)}) collective-permute-start(f32[16,8,128]{2,1,0:T(8,128)S(1)} %get-tuple-element.35), channel_id=1, source_target_pairs={{0,7},{1,6},{2,5},{3,4},{4,3},{5,2},{6,1},{7,0},{8,15},{9,14},{10,... | collective-permute-start | bytes 196616 | tf_op jit(solution)/shard_map/ppermute | solution.py:347
  23.1 8.6 %collective-permute-start.11 = (f32[8,2,8,128]{3,2,1,0:T(8,128)S(1)}, f32[8,2,8,128]{3,2,1,0:T(8,128)S(1)}, u32[]{:S(2)}, u32[]{:S(2)}) collective-permute-start(f32[8,2,8,128]{3,2,1,0:T(8,128)S(1)} %edge.1), channel_id=1, source_target_pairs={{1,0},{2,1},{3,2},{4,3},{5,4},{6,5},{7,6},{8,7},{9,8},{10,9},{11,1... | collective-permute-start | bytes 196616 | tf_op jit(solution)/shard_map/ppermute | solution.py:391
  32.7 15.7 %collective-permute-start.12 = (f32[8,4,8,128]{3,2,1,0:T(8,128)S(1)}, f32[8,4,8,128]{3,2,1,0:T(8,128)S(1)}, u32[]{:S(2)}, u32[]{:S(2)}) collective-permute-start(f32[8,4,8,128]{3,2,1,0:T(8,128)S(1)} %get-tuple-element.52), channel_id=1, source_target_pairs={{0,4},{1,5},{2,6},{3,7},{4,0},{5,1},{6,2},{7,3},{8,12},{9,13},{10,... | collective-permute-start | bytes 393224 | tf_op jit(solution)/shard_map/ppermute | solution.py:347
  35.4 15.8 %collective-permute-start.13 = (f32[8,4,8,128]{3,2,1,0:T(8,128)S(1)}, f32[8,4,8,128]{3,2,1,0:T(8,128)S(1)}, u32[]{:S(2)}, u32[]{:S(2)}) collective-permute-start(f32[8,4,8,128]{3,2,1,0:T(8,128)S(1)} %get-tuple-element.53), channel_id=1, source_target_pairs={{0,5},{1,4},{2,7},{3,6},{4,1},{5,0},{6,3},{7,2},{8,13},{9,12},{10,... | collective-permute-start | bytes 393224 | tf_op jit(solution)/shard_map/ppermute | solution.py:347
  35.4 18.7 %collective-permute-start.14 = (f32[8,4,8,128]{3,2,1,0:T(8,128)S(1)}, f32[8,4,8,128]{3,2,1,0:T(8,128)S(1)}, u32[]{:S(2)}, u32[]{:S(2)}) collective-permute-start(f32[8,4,8,128]{3,2,1,0:T(8,128)S(1)} %get-tuple-element.54), channel_id=1, source_target_pairs={{0,6},{1,7},{2,4},{3,5},{4,2},{5,3},{6,0},{7,1},{8,14},{9,15},{10,... | collective-permute-start | bytes 393224 | tf_op jit(solution)/shard_map/ppermute | solution.py:347
  35.6 21.8 %collective-permute-start.15 = (f32[8,4,8,128]{3,2,1,0:T(8,128)S(1)}, f32[8,4,8,128]{3,2,1,0:T(8,128)S(1)}, u32[]{:S(2)}, u32[]{:S(2)}) collective-permute-start(f32[8,4,8,128]{3,2,1,0:T(8,128)S(1)} %get-tuple-element.55), channel_id=1, source_target_pairs={{0,7},{1,6},{2,5},{3,4},{4,3},{5,2},{6,1},{7,0},{8,15},{9,14},{10,... | collective-permute-start | bytes 393224 | tf_op jit(solution)/shard_map/ppermute | solution.py:347
  37.5 19.9 %collective-permute-start.16 = (f32[8,4,8,128]{3,2,1,0:T(8,128)S(1)}, f32[8,4,8,128]{3,2,1,0:T(8,128)S(1)}, u32[]{:S(2)}, u32[]{:S(2)}) collective-permute-start(f32[8,4,8,128]{3,2,1,0:T(8,128)S(1)} %get-tuple-element.56), channel_id=1, source_target_pairs={{0,3},{1,2},{2,1},{3,0},{4,7},{5,6},{6,5},{7,4},{8,11},{9,10},{10,... | collective-permute-start | bytes 393224 | tf_op jit(solution)/shard_map/ppermute | solution.py:347
  48.5 9.0 %collective-permute-start.17 = (f32[8,4,8,128]{3,2,1,0:T(8,128)S(1)}, f32[8,4,8,128]{3,2,1,0:T(8,128)S(1)}, u32[]{:S(2)}, u32[]{:S(2)}) collective-permute-start(f32[8,4,8,128]{3,2,1,0:T(8,128)S(1)} %get-tuple-element.57), channel_id=1, source_target_pairs={{0,2},{1,3},{2,0},{3,1},{4,6},{5,7},{6,4},{7,5},{8,10},{9,11},{10,... | collective-permute-start | bytes 393224 | tf_op jit(solution)/shard_map/ppermute | solution.py:347
  51.3 6.2 %collective-permute-start.18 = (f32[8,4,8,128]{3,2,1,0:T(8,128)S(1)}, f32[8,4,8,128]{3,2,1,0:T(8,128)S(1)}, u32[]{:S(2)}, u32[]{:S(2)}) collective-permute-start(f32[8,4,8,128]{3,2,1,0:T(8,128)S(1)} %get-tuple-element.58), channel_id=1, source_target_pairs={{0,1},{1,0},{2,3},{3,2},{4,5},{5,4},{6,7},{7,6},{8,9},{9,8},{10,11... | collective-permute-start | bytes 393224 | tf_op jit(solution)/shard_map/ppermute | solution.py:347

commit v7 on v6

--- a/solution.py
+++ b/solution.py
@@ -76,16 +76,34 @@
 
 
 def unpack_kernel(cfg, me_ref, *refs):
-    pieces, (conserved_ref, field_ref, sem) = refs[: cfg.n], refs[cfg.n :]
+    n, tiles, rest = cfg.n, cfg.tiles, cfg.tiles - cfg.per
+    half = n // 2
+    pieces, (conserved_ref, field_ref, sem) = refs[: n + half], refs[n + half :]
     copies = []
-    for piece, k in zip(pieces, cfg.order):
-        at = pl.ds(jnp.bitwise_xor(me_ref[0], k) * cfg.tiles, cfg.tiles)
-        for j, (first, count, out) in enumerate(((0, 5, conserved_ref), (5, 3, field_ref))):
-            copies.append(
-                pltpu.make_async_copy(
-                    piece.at[pl.ds(first, count)], out.at[:, at], sem.at[k, j]
-                )
-            )
+    for j, k in enumerate(cfg.order):
+        at = jnp.bitwise_xor(me_ref[0], k) * tiles
+        here = pl.ds(at, tiles)
+        first, second = pieces[j], pieces[n + j] if j < half else pieces[j]
+        skip = 0 if j < half else 3 * tiles + rest
+        parts = [
+            (first.at[pl.ds(0, tiles)], conserved_ref.at[0, here]),
+            (
+                first.at[pl.ds(tiles, 2 * tiles)].reshape(2, tiles, SUB, LANES),
+                field_ref.at[pl.ds(0, 2), here],
+            ),
+            (
+                second.at[pl.ds(skip, 4 * tiles)].reshape(4, tiles, SUB, LANES),
+                conserved_ref.at[pl.ds(1, 4), here],
+            ),
+            (
+                second.at[pl.ds(skip + 4 * tiles, cfg.per)],
+                field_ref.at[2, pl.ds(at + rest, cfg.per)],
+            ),
+        ]
+        if rest:
+            parts.append((first.at[pl.ds(3 * tiles, rest)], field_ref.at[2, pl.ds(at, rest)]))
+        for i, (piece, out) in enumerate(parts):
+            copies.append(pltpu.make_async_copy(piece, out, sem.at[j, i]))
     wait_all(start_all(copies))
 
 
@@ -95,10 +113,15 @@
     row = lax.broadcasted_iota(jnp.int32, (size, size), 0)
     col = lax.broadcasted_iota(jnp.int32, (size, size), 1)
     same = (row // BS) == (col // BS)
-    e_in, e_out = row % BS, col % BS
-    zero = jnp.zeros((size, size), F32)
-    tj_ref[0] = jnp.where(same & (e_in < e_out), 1.0, zero).astype(BF16)
-    tj_ref[1] = jnp.where(same, 1.0, zero).astype(BF16)
+    e_in = lax.broadcasted_iota(jnp.int32, (BS, size), 0)
+    e_out = lax.broadcasted_iota(jnp.int32, (BS, size), 1) % BS
+    zero = jnp.zeros((BS, size), F32)
+
+    def spread(pattern):
+        return jnp.where(same, jnp.concatenate([pattern] * (size // BS), axis=0), 0.0)
+
+    tj_ref[0] = spread(jnp.where(e_in < e_out, 1.0, zero)).astype(BF16)
+    tj_ref[1] = spread(zero + 1.0).astype(BF16)
     for al in range(cfg.radii):
         _, rest = nearest_blocks(shift_ref[first + al])
         position = -jnp.full((1, size), frac_ref[first + al], F32)
@@ -121,16 +144,18 @@
             weights.append(total)
         for d in range(3):
             at = e_in + BS * (d - 1)
-            tap = jnp.where(same, at - e_out + rest, 100)
+            tap = at - e_out + rest
             remap, flux = zero, zero
             for a in NODES:
                 hit = tap == a
                 remap = jnp.where(hit, lagrange[a + 3], remap)
                 if a < 3:
                     flux = jnp.where(hit, weights[a + 3], flux)
-            flux = flux - jnp.where(same & (at < e_out - rest), 1.0, zero)
-            mh_ref[al, d], ml_ref[al, d] = halves(remap)
-            gh_ref[al, d], gl_ref[al, d] = halves(flux)
+            flux = flux - jnp.where(at < e_out - rest, 1.0, zero)
+            for value, high_ref, low_ref in ((remap, mh_ref, ml_ref), (flux, gh_ref, gl_ref)):
+                high = value.astype(BF16).astype(F32)
+                high_ref[al, d] = spread(high).astype(BF16)
+                low_ref[al, d] = spread(value - high).astype(BF16)
 
 
 def gather_matrix(cfg, me, ids, whole):
@@ -227,19 +252,26 @@
 
 
 def fields_kernel(cfg, me_ref, shift_ref, *refs):
-    n, slots, wide, per = cfg.n, cfg.slots, cfg.lanes, cfg.per
+    n, slots, tiles, wide, per = cfg.n, cfg.slots, cfg.tiles, cfg.lanes, cfg.per
+    half = n // 2
     pieces = refs[:n]
-    mh_ref, ml_ref, gh_ref, gl_ref, tj_ref, out_ref, taken_ref, polar_ref = refs[n:]
+    mh_ref, ml_ref, gh_ref, gl_ref, tj_ref = refs[n : n + 5]
+    outs = refs[n + 5 : n + 5 + half]
+    near_ref, last_ref, taken_ref, polar_ref = refs[n + 5 + half :]
     me = me_ref[0]
     first = (me * cfg.rows) // BS
     ids = numbers(cfg, pieces)
 
     def put(c, al, value):
-        for k in range(n):
+        for j, k in enumerate(cfg.order):
             for t in range(per):
-                out_ref[k, c, al * per + t] = value[
-                    k * SUB : (k + 1) * SUB, t * LANES : (t + 1) * LANES
-                ]
+                tile = value[k * SUB : (k + 1) * SUB, t * LANES : (t + 1) * LANES]
+                if c == 3 and al == cfg.radii - 1:
+                    last_ref[j, t] = tile
+                elif j < half:
+                    outs[j][c * tiles + al * per + t] = tile
+                else:
+                    near_ref[j - half, c * tiles + al * per + t] = tile
 
     lane = lax.broadcasted_iota(jnp.int32, (slots, wide), 1)
     lower = (lax.broadcasted_iota(jnp.int32, (slots, wide), 0) >> 2) & 1 == 0
@@ -272,35 +304,37 @@
 
 
 def finish_kernel(cfg, me_ref, *refs):
-    n, slots, per = cfg.n, cfg.slots, cfg.per
+    n, slots, tiles, per = cfg.n, cfg.slots, cfg.tiles, cfg.per
+    half, first = n // 2, 4 * cfg.tiles - cfg.per
     pieces = refs[:n]
-    mh_ref, ml_ref, taken_ref, rows_ref, halo_ref, polar_ref = refs[n : n + 6]
-    outs = refs[n + 6 :]
-    me, rest = me_ref[0], cfg.tiles - cfg.per
+    mh_ref, ml_ref, taken_ref, near_ref, last_ref, halo_ref, polar_ref = refs[n : n + 7]
+    outs = refs[n + 7 :]
+    me = me_ref[0]
+    skip = [0] * half + [first] * half
     for al in range(cfg.radii):
         taken = taken_ref[al]
         ys = [dot(taken, source(cfg, second_half(cfg, pieces, c), al)) for c in range(4)]
         remap = remapped(cfg, ys, al, mh_ref, ml_ref)
-        for out, k in zip(outs, cfg.order):
+        for out, k, at in zip(outs, cfg.order, skip):
             for c in range(4):
                 for t in range(per):
-                    out[1 + c, al * per + t] = remap[
+                    out[at + c * tiles + al * per + t] = remap[
                         c * slots + k * SUB : c * slots + (k + 1) * SUB,
                         t * LANES : (t + 1) * LANES,
                     ]
-    for out, k in zip(outs, cfg.order):
+    for j, (out, k, at) in enumerate(zip(outs, cfg.order, skip)):
         owner = jnp.bitwise_xor(me, k)
-        out[0] = rows_ref[k, 0]
-        out[5:8] = rows_ref[k, 1:4]
-        out[7, rest:] = rows_ref[k, 3, rest:] + halo_ref[owner]
+        if j >= half:
+            out[:first] = near_ref[j - half]
+        bp = last_ref[j] + halo_ref[owner]
         if cfg.split > 1:
             after = polar_ref[owner, 0]
             row = lax.broadcasted_iota(jnp.int32, after.shape, 0)
             lane = lax.broadcasted_iota(jnp.int32, after.shape, 1)
             up = jnp.where(row < 4, jnp.concatenate([after[4:], after[:4]], axis=0), 0.0)
             after = jnp.where(lax.rem(me, cfg.split) == cfg.split - 1, up, after)
-            after = pltpu.roll(jnp.where(lane < BS, after, 0.0), LANES - BS, 1)
-            out[7, cfg.tiles - 1] = out[7, cfg.tiles - 1] + after
+            bp = bp + pltpu.roll(jnp.where(lane < BS, after, 0.0), LANES - BS, 1)[None]
+        out[at + 4 * tiles : at + 4 * tiles + per] = bp
 
 
 class Sizes:
@@ -391,15 +425,18 @@
     halo = lax.ppermute(
         halo, ("tile", "phi"), [(s, s - cfg.split) for s in range(cfg.split, count)]
     )
-    rows, taken, polar = pl.pallas_call(
+    early = 4 * tiles - per
+    *far_early, near_early, last, taken, polar = pl.pallas_call(
         functools.partial(fields_kernel, cfg),
-        out_shape=[
-            shape(n, 4, tiles, SUB, LANES),
+        out_shape=[shape(early, SUB, LANES)] * half
+        + [
+            shape(half, early, SUB, LANES),
+            owners,
             shape(cfg.radii, 3 * cfg.slots, 3 * cfg.slots, dtype=BF16),
             owners if cfg.split > 1 else shape(1, 1, SUB, LANES),
         ],
         in_specs=[smem] * 2 + [vmem] * (n + 5),
-        out_specs=[vmem] * 3,
+        out_specs=[vmem] * (half + 4),
         compiler_params=grant(2 * n),
         name="fields",
     )(me, int_shift, *first, mh, ml, gh, gl, tj)
@@ -409,23 +446,26 @@
             "phi",
             [(s, s - 1 if s % cfg.split else s + cfg.split - 1) for s in range(n)],
         )
-    done = pl.pallas_call(
+    late = pl.pallas_call(
         functools.partial(finish_kernel, cfg),
-        out_shape=[shape(8, tiles, SUB, LANES)] * n,
-        in_specs=[smem] + [vmem] * (n + 6),
+        out_shape=[shape(4 * tiles + per, SUB, LANES)] * half
+        + [shape(8 * tiles, SUB, LANES)] * half,
+        in_specs=[smem] + [vmem] * (n + 7),
         out_specs=[vmem] * n,
         compiler_params=grant(2 * n),
         name="finish",
-    )(me, *far_second, *first[half:], mh, ml, taken, rows, halo, polar)
+    )(me, *far_second, *first[half:], mh, ml, taken, near_early, last, halo, polar)
+    far_early = exchange(far_early, cfg.order)
+    late = exchange(late, cfg.order)
     conserved_out, field_out = pl.pallas_call(
         functools.partial(unpack_kernel, cfg),
         out_shape=[shape(5, n * tiles, SUB, LANES), shape(3, n * tiles, SUB, LANES)],
-        in_specs=[smem] + [vmem] * n,
+        in_specs=[smem] + [vmem] * (n + half),
         out_specs=[hbm] * 2,
-        scratch_shapes=[pltpu.SemaphoreType.DMA((n, 2))],
+        scratch_shapes=[pltpu.SemaphoreType.DMA((n, 5))],
         compiler_params=grant(2),
         name="unpack",
-    )(me, *exchange(done, cfg.order))
+    )(me, *far_early, *late[half:], *late[:half])
     return untiled(conserved_out), untiled(field_out)
 
 

time: 59.3 us -> 59.7 us (level)
  the two profiles are of different devices: /device:TPU:13 before, /device:TPU:4 now
where the time goes in v7:
time: 59.7 us; the launch traced here: 59.6 us
  starting transfers between devices  30.7 us (51%)
  waiting for transfers between devices  20 us (34%)
  Pallas kernels  8.08 us (14%)
  between operations  0.76 us (1%)
    ppermute x22, starting transfers between devices, exchange(): lax.ppermute(piece, 'phi', [(s, s ^ k) for s in range(n)])  27.3 us
    ppermute x22, waiting for transfers between devices, exchange(): lax.ppermute(piece, 'phi', [(s, s ^ k) for s in range(n)])  20 us
    ppermute x1, starting transfers between devices, shards(): lax.ppermute(halo, ('tile', 'phi'), [(s, s - cfg.split) for s in range(cf...  3.44 us
    pallas_call x1, Pallas kernels, shards(): pl.pallas_call(functools.partial(fields_kernel, cfg), out_shape=[shape(ea...  2.16 us
    pallas_call x1, Pallas kernels, shards(): pl.pallas_call(functools.partial(pack_kernel, cfg), out_shape=[shape(4 *...  1.37 us
    pallas_call x1, Pallas kernels, shards(): pl.pallas_call(functools.partial(unpack_kernel, cfg), out_shape=[shape(5,...  1.32 us
  transfers between devices with their start and end apart: 23, of which 7 were waited for; matrix products, arithmetic and copies ran while one was open for 0% of the time, Pallas kernels for 9%

profile of v7, /device:TPU:4, one launch (start us, length us, event | category | flops | bytes accessed | tf_op | source)
XLA Modules:
  0.0 59.6 jit_solution(17132912994377822565)
XLA Ops:
  0.6 1.4 %pack.1 = (f32[17,8,128]{2,1,0:T(8,128)S(1)}, f32[17,8,128]{2,1,0:T(8,128)S(1)}, f32[17,8,128]{2,1,0:T(8,128)S(1)}, f32[17,8,128]{2,1,0:T(8,128)S(1)}, f32[33,8,...) custom-call(s32[1]{0:T(128)} %bitcast.me_ref, ...), custom_call_target="tpu_custom_call" | custom-call | tf_op jit(solution)/shard_map/pack/pallas_call | solution.py:388
  2.0 2.7 %collective-permute-start = (f32[17,8,128]{2,1,0:T(8,128)S(1)}, f32[17,8,128]{2,1,0:T(8,128)S(1)}, u32[]{:S(2)}, u32[]{:S(2)}) collective-permute-start(f32[17,8,128]{2,1,0:T(8,128)S(1)} %get-tuple-element.37), channel_id=1, source_target_pairs={{0,4},{1,5},{2,6},{3,7},{4,0},{5,1},{6,2},{7,3},{8,12},{9,13},{10,... | collective-permute-start | bytes 208904 | tf_op jit(solution)/shard_map/ppermute | solution.py:381
  4.7 1.6 %collective-permute-start.4 = (f32[33,8,128]{2,1,0:T(8,128)S(1)}, f32[33,8,128]{2,1,0:T(8,128)S(1)}, u32[]{:S(2)}, u32[]{:S(2)}) collective-permute-start(f32[33,8,128]{2,1,0:T(8,128)S(1)} %get-tuple-element.41), channel_id=1, source_target_pairs={{0,3},{1,2},{2,1},{3,0},{4,7},{5,6},{6,5},{7,4},{8,11},{9,10},{10,... | collective-permute-start | bytes 405512 | tf_op jit(solution)/shard_map/ppermute | solution.py:381
  6.8 2.0 %collective-permute-done.refs_0_ = f32[17,8,128]{2,1,0:T(8,128)S(1)} collective-permute-done((f32[17,8,128]{2,1,0:T(8,128)S(1)}, f32[17,8,128]{2,1,0:T(8,128)S(1)}, u32[]{:S(2)}, u32[]{:S(2)}) %collective-permute-start) | collective-permute-done | bytes 69664 | tf_op jit(solution)/shard_map/ppermute | solution.py:381
  8.8 4.8 %collective-permute-start.2 = (f32[17,8,128]{2,1,0:T(8,128)S(1)}, f32[17,8,128]{2,1,0:T(8,128)S(1)}, u32[]{:S(2)}, u32[]{:S(2)}) collective-permute-start(f32[17,8,128]{2,1,0:T(8,128)S(1)} %get-tuple-element.39), channel_id=1, source_target_pairs={{0,6},{1,7},{2,4},{3,5},{4,2},{5,3},{6,0},{7,1},{8,14},{9,15},{10,... | collective-permute-start | bytes 208904 | tf_op jit(solution)/shard_map/ppermute | solution.py:381
  14.5 3.4 %collective-permute-done.2.refs_2_ = f32[17,8,128]{2,1,0:T(8,128)S(1)} collective-permute-done((f32[17,8,128]{2,1,0:T(8,128)S(1)}, f32[17,8,128]{2,1,0:T(8,128)S(1)}, u32[]{:S(2)}, u32[]{:S(2)}) %collective-permute-start.2) | collective-permute-done | bytes 69664 | tf_op jit(solution)/shard_map/ppermute | solution.py:381
  17.9 1.8 %collective-permute-done.3.refs_3_ = f32[17,8,128]{2,1,0:T(8,128)S(1)} collective-permute-done((f32[17,8,128]{2,1,0:T(8,128)S(1)}, f32[17,8,128]{2,1,0:T(8,128)S(1)}, u32[]{:S(2)}, u32[]{:S(2)}) %collective-permute-start.3) | collective-permute-done | bytes 69664 | tf_op jit(solution)/shard_map/ppermute | solution.py:381
  20.2 0.9 %collective-permute-start.13 = (f32[16,8,128]{2,1,0:T(8,128)S(1)}, f32[16,8,128]{2,1,0:T(8,128)S(1)}, u32[]{:S(2)}, u32[]{:S(2)}) collective-permute-start(f32[16,8,128]{2,1,0:T(8,128)S(1)} %get-tuple-element.56), channel_id=1, source_target_pairs={{0,6},{1,7},{2,4},{3,5},{4,2},{5,3},{6,0},{7,1},{8,14},{9,15},{10,... | collective-permute-start | bytes 196616 | tf_op jit(solution)/shard_map/ppermute | solution.py:381
  21.2 2.9 %collective-permute-start.14 = (f32[16,8,128]{2,1,0:T(8,128)S(1)}, f32[16,8,128]{2,1,0:T(8,128)S(1)}, u32[]{:S(2)}, u32[]{:S(2)}) collective-permute-start(f32[16,8,128]{2,1,0:T(8,128)S(1)} %get-tuple-element.57), channel_id=1, source_target_pairs={{0,7},{1,6},{2,5},{3,4},{4,3},{5,2},{6,1},{7,0},{8,15},{9,14},{10,... | collective-permute-start | bytes 196616 | tf_op jit(solution)/shard_map/ppermute | solution.py:381
  24.1 1.1 %operators.1 = (bf16[2,3,256,256]{3,2,1,0:T(8,128)(2,1)S(1)}, bf16[2,3,256,256]{3,2,1,0:T(8,128)(2,1)S(1)}, bf16[2,3,256,256]{3,2,1,0:T(8,128)(2,1)S(1)}, bf16[2...) custom-call(s32[1]{0:T(128)} %bitcast.me_ref, s32[16]{0:T(128)S(1)} %copy-done, f32[16]{0:T(128)S(1)} %copy-done.1), custom_call_target="tpu_custom_call" | custom-call | tf_op jit(solution)/shard_map/operators/pallas_call | solution.py:407
  25.2 1.1 %edge.1 = f32[8,2,8,128]{3,2,1,0:T(8,128)S(1)} custom-call(s32[1]{0:T(128)} %bitcast.me_ref, s32[16]{0:T(128)S(1)} %copy-done, f32[17,8,128]{2,1,0:T(8,128)S(1)} %collective-permute-done.refs_0_, f32[17,8,128]{2,1,0:T(8,128)S(1)} %collective-permute-done.1.refs_1_, f32[17,8,128]{2,1,0:T(8,128)S(1)} %collective-permute-done.2.refs_2_, ...), custom_call_target="tpu_custom_call" | custom-call | tf_op jit(solution)/shard_map/edge/pallas_call | solution.py:417
  26.3 3.4 %collective-permute-start.15 = (f32[8,2,8,128]{3,2,1,0:T(8,128)S(1)}, f32[8,2,8,128]{3,2,1,0:T(8,128)S(1)}, u32[]{:S(2)}, u32[]{:S(2)}) collective-permute-start(f32[8,2,8,128]{3,2,1,0:T(8,128)S(1)} %edge.1), channel_id=1, source_target_pairs={{1,0},{2,1},{3,2},{4,3},{5,4},{6,5},{7,6},{8,7},{9,8},{10,9},{11,1... | collective-permute-start | bytes 196616 | tf_op jit(solution)/shard_map/ppermute | solution.py:425
  29.7 2.2 %fields.1 = (f32[14,8,128]{2,1,0:T(8,128)S(1)}, f32[14,8,128]{2,1,0:T(8,128)S(1)}, f32[14,8,128]{2,1,0:T(8,128)S(1)}, f32[14,8,128]{2,1,0:T(8,128)S(1)}, f32[4,1...) custom-call(s32[1]{0:T(128)} %bitcast.me_ref, ...), custom_call_target="tpu_custom_call" | custom-call | tf_op jit(solution)/shard_map/fields/pallas_call | solution.py:429
  32.0 1.2 %collective-permute-start.8 = (f32[14,8,128]{2,1,0:T(8,128)S(1)}, f32[14,8,128]{2,1,0:T(8,128)S(1)}, u32[]{:S(2)}, u32[]{:S(2)}) collective-permute-start(f32[14,8,128]{2,1,0:T(8,128)S(1)} %get-tuple-element.51), channel_id=1, source_target_pairs={{0,5},{1,4},{2,7},{3,6},{4,1},{5,0},{6,3},{7,2},{8,13},{9,12},{10,... | collective-permute-start | bytes 172040 | tf_op jit(solution)/shard_map/ppermute | solution.py:381
  33.2 2.1 %collective-permute-start.9 = (f32[14,8,128]{2,1,0:T(8,128)S(1)}, f32[14,8,128]{2,1,0:T(8,128)S(1)}, u32[]{:S(2)}, u32[]{:S(2)}) collective-permute-start(f32[14,8,128]{2,1,0:T(8,128)S(1)} %get-tuple-element.52), channel_id=1, source_target_pairs={{0,6},{1,7},{2,4},{3,5},{4,2},{5,3},{6,0},{7,1},{8,14},{9,15},{10,... | collective-permute-start | bytes 172040 | tf_op jit(solution)/shard_map/ppermute | solution.py:381
  35.3 2.9 %collective-permute-start.10 = (f32[14,8,128]{2,1,0:T(8,128)S(1)}, f32[14,8,128]{2,1,0:T(8,128)S(1)}, u32[]{:S(2)}, u32[]{:S(2)}) collective-permute-start(f32[14,8,128]{2,1,0:T(8,128)S(1)} %get-tuple-element.53), channel_id=1, source_target_pairs={{0,7},{1,6},{2,5},{3,4},{4,3},{5,2},{6,1},{7,0},{8,15},{9,14},{10,... | collective-permute-start | bytes 172040 | tf_op jit(solution)/shard_map/ppermute | solution.py:381
  38.2 1.1 %finish.1 = (f32[18,8,128]{2,1,0:T(8,128)S(1)}, f32[18,8,128]{2,1,0:T(8,128)S(1)}, f32[18,8,128]{2,1,0:T(8,128)S(1)}, f32[18,8,128]{2,1,0:T(8,128)S(1)}, f32[32,...) custom-call(s32[1]{0:T(128)} %bitcast.me_ref, ...), custom_call_target="tpu_custom_call" | custom-call | tf_op jit(solution)/shard_map/finish/pallas_call | solution.py:449
  39.3 4.0 %collective-permute-done.7.refs_0_ = f32[14,8,128]{2,1,0:T(8,128)S(1)} collective-permute-done((f32[14,8,128]{2,1,0:T(8,128)S(1)}, f32[14,8,128]{2,1,0:T(8,128)S(1)}, u32[]{:S(2)}, u32[]{:S(2)}) %collective-permute-start.7) | collective-permute-done | bytes 57376 | tf_op jit(solution)/shard_map/ppermute | solution.py:381
  43.3 4.6 %collective-permute-start.17 = (f32[32,8,128]{2,1,0:T(8,128)S(1)}, f32[32,8,128]{2,1,0:T(8,128)S(1)}, u32[]{:S(2)}, u32[]{:S(2)}) collective-permute-start(f32[32,8,128]{2,1,0:T(8,128)S(1)} %get-tuple-element.63), channel_id=1, source_target_pairs={{0,2},{1,3},{2,0},{3,1},{4,6},{5,7},{6,4},{7,5},{8,10},{9,11},{10,... | collective-permute-start | bytes 393224 | tf_op jit(solution)/shard_map/ppermute | solution.py:381
  47.9 2.3 %collective-permute-done.19.refs_8_ = f32[18,8,128]{2,1,0:T(8,128)S(1)} collective-permute-done((f32[18,8,128]{2,1,0:T(8,128)S(1)}, f32[18,8,128]{2,1,0:T(8,128)S(1)}, u32[]{:S(2)}, u32[]{:S(2)}) %collective-permute-start.19) | collective-permute-done | bytes 73760 | tf_op jit(solution)/shard_map/ppermute | solution.py:381
  50.5 1.2 %collective-permute-start.22 = (f32[18,8,128]{2,1,0:T(8,128)S(1)}, f32[18,8,128]{2,1,0:T(8,128)S(1)}, u32[]{:S(2)}, u32[]{:S(2)}) collective-permute-start(f32[18,8,128]{2,1,0:T(8,128)S(1)} %get-tuple-element.69), channel_id=1, source_target_pairs={{0,7},{1,6},{2,5},{3,4},{4,3},{5,2},{6,1},{7,0},{8,15},{9,14},{10,... | collective-permute-start | bytes 221192 | tf_op jit(solution)/shard_map/ppermute | solution.py:381
  51.7 5.3 %collective-permute-done.21.refs_10_ = f32[18,8,128]{2,1,0:T(8,128)S(1)} collective-permute-done((f32[18,8,128]{2,1,0:T(8,128)S(1)}, f32[18,8,128]{2,1,0:T(8,128)S(1)}, u32[]{:S(2)}, u32[]{:S(2)}) %collective-permute-start.21) | collective-permute-done | bytes 73760 | tf_op jit(solution)/shard_map/ppermute | solution.py:381
  57.0 1.3 %collective-permute-done.17.refs_5_ = f32[32,8,128]{2,1,0:T(8,128)S(1)} collective-permute-done((f32[32,8,128]{2,1,0:T(8,128)S(1)}, f32[32,8,128]{2,1,0:T(8,128)S(1)}, u32[]{:S(2)}, u32[]{:S(2)}) %collective-permute-start.17) | collective-permute-done | bytes 131104 | tf_op jit(solution)/shard_map/ppermute | solution.py:381
  58.3 1.3 %unpack.1 = (f32[5,32,8,128]{3,2,1,0:T(8,128)}, f32[3,32,8,128]{3,2,1,0:T(8,128)}) custom-call(s32[1]{0:T(128)} %bitcast.me_ref, f32[14,8,128]{2,1,0:T(8,128)S(1)} %collective-permute-done.7.refs_0_, f32[14,8,128]{2,1,0:T(8,128)S(1)} %collective-permute-done.8.refs_1_, f32[14,8,128]{2,1,0:T(8,128)S(1)} %collective-permute-done.9.refs_2_, ...), custom_call_target="tpu_custom_call" | custom-call | tf_op jit(solution)/shard_map/unpack/pallas_call | solution.py:460
  (32 shorter events, 2.4 us)
Async XLA Ops:
  2.0 6.8 %collective-permute-start = (f32[17,8,128]{2,1,0:T(8,128)S(1)}, f32[17,8,128]{2,1,0:T(8,128)S(1)}, u32[]{:S(2)}, u32[]{:S(2)}) collective-permute-start(f32[17,8,128]{2,1,0:T(8,128)S(1)} %get-tuple-element.37), channel_id=1, source_target_pairs={{0,4},{1,5},{2,6},{3,7},{4,0},{5,1},{6,2},{7,3},{8,12},{9,13},{10,... | collective-permute-start | bytes 208904 | tf_op jit(solution)/shard_map/ppermute | solution.py:381
  4.7 9.0 %collective-permute-start.1 = (f32[17,8,128]{2,1,0:T(8,128)S(1)}, f32[17,8,128]{2,1,0:T(8,128)S(1)}, u32[]{:S(2)}, u32[]{:S(2)}) collective-permute-start(f32[17,8,128]{2,1,0:T(8,128)S(1)} %get-tuple-element.38), channel_id=1, source_target_pairs={{0,5},{1,4},{2,7},{3,6},{4,1},{5,0},{6,3},{7,2},{8,13},{9,12},{10,... | collective-permute-start | bytes 208904 | tf_op jit(solution)/shard_map/ppermute | solution.py:381
  4.7 15.6 %collective-permute-start.4 = (f32[33,8,128]{2,1,0:T(8,128)S(1)}, f32[33,8,128]{2,1,0:T(8,128)S(1)}, u32[]{:S(2)}, u32[]{:S(2)}) collective-permute-start(f32[33,8,128]{2,1,0:T(8,128)S(1)} %get-tuple-element.41), channel_id=1, source_target_pairs={{0,3},{1,2},{2,1},{3,0},{4,7},{5,6},{6,5},{7,4},{8,11},{9,10},{10,... | collective-permute-start | bytes 405512 | tf_op jit(solution)/shard_map/ppermute | solution.py:381
  6.3 14.9 %collective-permute-start.5 = (f32[33,8,128]{2,1,0:T(8,128)S(1)}, f32[33,8,128]{2,1,0:T(8,128)S(1)}, u32[]{:S(2)}, u32[]{:S(2)}) collective-permute-start(f32[33,8,128]{2,1,0:T(8,128)S(1)} %get-tuple-element.42), channel_id=1, source_target_pairs={{0,2},{1,3},{2,0},{3,1},{4,6},{5,7},{6,4},{7,5},{8,10},{9,11},{10,... | collective-permute-start | bytes 405512 | tf_op jit(solution)/shard_map/ppermute | solution.py:381
  6.8 18.5 %collective-permute-start.6 = (f32[33,8,128]{2,1,0:T(8,128)S(1)}, f32[33,8,128]{2,1,0:T(8,128)S(1)}, u32[]{:S(2)}, u32[]{:S(2)}) collective-permute-start(f32[33,8,128]{2,1,0:T(8,128)S(1)} %get-tuple-element.43), channel_id=1, source_target_pairs={{0,1},{1,0},{2,3},{3,2},{4,5},{5,4},{6,7},{7,6},{8,9},{9,8},{10,11... | collective-permute-start | bytes 405512 | tf_op jit(solution)/shard_map/ppermute | solution.py:381
  8.8 9.1 %collective-permute-start.2 = (f32[17,8,128]{2,1,0:T(8,128)S(1)}, f32[17,8,128]{2,1,0:T(8,128)S(1)}, u32[]{:S(2)}, u32[]{:S(2)}) collective-permute-start(f32[17,8,128]{2,1,0:T(8,128)S(1)} %get-tuple-element.39), channel_id=1, source_target_pairs={{0,6},{1,7},{2,4},{3,5},{4,2},{5,3},{6,0},{7,1},{8,14},{9,15},{10,... | collective-permute-start | bytes 208904 | tf_op jit(solution)/shard_map/ppermute | solution.py:381
  13.6 6.0 %collective-permute-start.3 = (f32[17,8,128]{2,1,0:T(8,128)S(1)}, f32[17,8,128]{2,1,0:T(8,128)S(1)}, u32[]{:S(2)}, u32[]{:S(2)}) collective-permute-start(f32[17,8,128]{2,1,0:T(8,128)S(1)} %get-tuple-element.40), channel_id=1, source_target_pairs={{0,7},{1,6},{2,5},{3,4},{4,3},{5,2},{6,1},{7,0},{8,15},{9,14},{10,... | collective-permute-start | bytes 208904 | tf_op jit(solution)/shard_map/ppermute | solution.py:381
  17.9 14.0 %collective-permute-start.11 = (f32[16,8,128]{2,1,0:T(8,128)S(1)}, f32[16,8,128]{2,1,0:T(8,128)S(1)}, u32[]{:S(2)}, u32[]{:S(2)}) collective-permute-start(f32[16,8,128]{2,1,0:T(8,128)S(1)} %get-tuple-element.54), channel_id=1, source_target_pairs={{0,4},{1,5},{2,6},{3,7},{4,0},{5,1},{6,2},{7,3},{8,12},{9,13},{10,... | collective-permute-start | bytes 196616 | tf_op jit(solution)/shard_map/ppermute | solution.py:381
  19.6 12.4 %collective-permute-start.12 = (f32[16,8,128]{2,1,0:T(8,128)S(1)}, f32[16,8,128]{2,1,0:T(8,128)S(1)}, u32[]{:S(2)}, u32[]{:S(2)}) collective-permute-start(f32[16,8,128]{2,1,0:T(8,128)S(1)} %get-tuple-element.55), channel_id=1, source_target_pairs={{0,5},{1,4},{2,7},{3,6},{4,1},{5,0},{6,3},{7,2},{8,13},{9,12},{10,... | collective-permute-start | bytes 196616 | tf_op jit(solution)/shard_map/ppermute | solution.py:381
  20.2 3.8 %copy-start.1 = (f32[16]{0:T(128)S(1)}, f32[16]{0:T(128)}, u32[]{:S(2)}) copy-start(f32[16]{0:T(128)} %frac_ref.1) | copy-start | bytes 196
  20.2 13.0 %collective-permute-start.13 = (f32[16,8,128]{2,1,0:T(8,128)S(1)}, f32[16,8,128]{2,1,0:T(8,128)S(1)}, u32[]{:S(2)}, u32[]{:S(2)}) collective-permute-start(f32[16,8,128]{2,1,0:T(8,128)S(1)} %get-tuple-element.56), channel_id=1, source_target_pairs={{0,6},{1,7},{2,4},{3,5},{4,2},{5,3},{6,0},{7,1},{8,14},{9,15},{10,... | collective-permute-start | bytes 196616 | tf_op jit(solution)/shard_map/ppermute | solution.py:381
  21.2 14.1 %collective-permute-start.14 = (f32[16,8,128]{2,1,0:T(8,128)S(1)}, f32[16,8,128]{2,1,0:T(8,128)S(1)}, u32[]{:S(2)}, u32[]{:S(2)}) collective-permute-start(f32[16,8,128]{2,1,0:T(8,128)S(1)} %get-tuple-element.57), channel_id=1, source_target_pairs={{0,7},{1,6},{2,5},{3,4},{4,3},{5,2},{6,1},{7,0},{8,15},{9,14},{10,... | collective-permute-start | bytes 196616 | tf_op jit(solution)/shard_map/ppermute | solution.py:381
  26.3 11.9 %collective-permute-start.15 = (f32[8,2,8,128]{3,2,1,0:T(8,128)S(1)}, f32[8,2,8,128]{3,2,1,0:T(8,128)S(1)}, u32[]{:S(2)}, u32[]{:S(2)}) collective-permute-start(f32[8,2,8,128]{3,2,1,0:T(8,128)S(1)} %edge.1), channel_id=1, source_target_pairs={{1,0},{2,1},{3,2},{4,3},{5,4},{6,5},{7,6},{8,7},{9,8},{10,9},{11,1... | collective-permute-start | bytes 196616 | tf_op jit(solution)/shard_map/ppermute | solution.py:425
  31.9 11.4 %collective-permute-start.7 = (f32[14,8,128]{2,1,0:T(8,128)S(1)}, f32[14,8,128]{2,1,0:T(8,128)S(1)}, u32[]{:S(2)}, u32[]{:S(2)}) collective-permute-start(f32[14,8,128]{2,1,0:T(8,128)S(1)} %get-tuple-element.50), channel_id=1, source_target_pairs={{0,4},{1,5},{2,6},{3,7},{4,0},{5,1},{6,2},{7,3},{8,12},{9,13},{10,... | collective-permute-start | bytes 172040 | tf_op jit(solution)/shard_map/ppermute | solution.py:381
  32.0 11.3 %collective-permute-start.8 = (f32[14,8,128]{2,1,0:T(8,128)S(1)}, f32[14,8,128]{2,1,0:T(8,128)S(1)}, u32[]{:S(2)}, u32[]{:S(2)}) collective-permute-start(f32[14,8,128]{2,1,0:T(8,128)S(1)} %get-tuple-element.51), channel_id=1, source_target_pairs={{0,5},{1,4},{2,7},{3,6},{4,1},{5,0},{6,3},{7,2},{8,13},{9,12},{10,... | collective-permute-start | bytes 172040 | tf_op jit(solution)/shard_map/ppermute | solution.py:381
  33.2 10.1 %collective-permute-start.9 = (f32[14,8,128]{2,1,0:T(8,128)S(1)}, f32[14,8,128]{2,1,0:T(8,128)S(1)}, u32[]{:S(2)}, u32[]{:S(2)}) collective-permute-start(f32[14,8,128]{2,1,0:T(8,128)S(1)} %get-tuple-element.52), channel_id=1, source_target_pairs={{0,6},{1,7},{2,4},{3,5},{4,2},{5,3},{6,0},{7,1},{8,14},{9,15},{10,... | collective-permute-start | bytes 172040 | tf_op jit(solution)/shard_map/ppermute | solution.py:381
  35.3 12.6 %collective-permute-start.10 = (f32[14,8,128]{2,1,0:T(8,128)S(1)}, f32[14,8,128]{2,1,0:T(8,128)S(1)}, u32[]{:S(2)}, u32[]{:S(2)}) collective-permute-start(f32[14,8,128]{2,1,0:T(8,128)S(1)} %get-tuple-element.53), channel_id=1, source_target_pairs={{0,7},{1,6},{2,5},{3,4},{4,3},{5,2},{6,1},{7,0},{8,15},{9,14},{10,... | collective-permute-start | bytes 172040 | tf_op jit(solution)/shard_map/ppermute | solution.py:381
  39.2 10.9 %collective-permute-start.19 = (f32[18,8,128]{2,1,0:T(8,128)S(1)}, f32[18,8,128]{2,1,0:T(8,128)S(1)}, u32[]{:S(2)}, u32[]{:S(2)}) collective-permute-start(f32[18,8,128]{2,1,0:T(8,128)S(1)} %get-tuple-element.66), channel_id=1, source_target_pairs={{0,4},{1,5},{2,6},{3,7},{4,0},{5,1},{6,2},{7,3},{8,12},{9,13},{10,... | collective-permute-start | bytes 221192 | tf_op jit(solution)/shard_map/ppermute | solution.py:381
  43.3 7.1 %collective-permute-start.20 = (f32[18,8,128]{2,1,0:T(8,128)S(1)}, f32[18,8,128]{2,1,0:T(8,128)S(1)}, u32[]{:S(2)}, u32[]{:S(2)}) collective-permute-start(f32[18,8,128]{2,1,0:T(8,128)S(1)} %get-tuple-element.67), channel_id=1, source_target_pairs={{0,5},{1,4},{2,7},{3,6},{4,1},{5,0},{6,3},{7,2},{8,13},{9,12},{10,... | collective-permute-start | bytes 221192 | tf_op jit(solution)/shard_map/ppermute | solution.py:381
  43.3 13.7 %collective-permute-start.16 = (f32[32,8,128]{2,1,0:T(8,128)S(1)}, f32[32,8,128]{2,1,0:T(8,128)S(1)}, u32[]{:S(2)}, u32[]{:S(2)}) collective-permute-start(f32[32,8,128]{2,1,0:T(8,128)S(1)} %get-tuple-element.62), channel_id=1, source_target_pairs={{0,3},{1,2},{2,1},{3,0},{4,7},{5,6},{6,5},{7,4},{8,11},{9,10},{10,... | collective-permute-start | bytes 393224 | tf_op jit(solution)/shard_map/ppermute | solution.py:381
  43.3 14.9 %collective-permute-start.17 = (f32[32,8,128]{2,1,0:T(8,128)S(1)}, f32[32,8,128]{2,1,0:T(8,128)S(1)}, u32[]{:S(2)}, u32[]{:S(2)}) collective-permute-start(f32[32,8,128]{2,1,0:T(8,128)S(1)} %get-tuple-element.63), channel_id=1, source_target_pairs={{0,2},{1,3},{2,0},{3,1},{4,6},{5,7},{6,4},{7,5},{8,10},{9,11},{10,... | collective-permute-start | bytes 393224 | tf_op jit(solution)/shard_map/ppermute | solution.py:381
  47.9 10.3 %collective-permute-start.18 = (f32[32,8,128]{2,1,0:T(8,128)S(1)}, f32[32,8,128]{2,1,0:T(8,128)S(1)}, u32[]{:S(2)}, u32[]{:S(2)}) collective-permute-start(f32[32,8,128]{2,1,0:T(8,128)S(1)} %get-tuple-element.64), channel_id=1, source_target_pairs={{0,1},{1,0},{2,3},{3,2},{4,5},{5,4},{6,7},{7,6},{8,9},{9,8},{10,11... | collective-permute-start | bytes 393224 | tf_op jit(solution)/shard_map/ppermute | solution.py:381
  50.2 6.8 %collective-permute-start.21 = (f32[18,8,128]{2,1,0:T(8,128)S(1)}, f32[18,8,128]{2,1,0:T(8,128)S(1)}, u32[]{:S(2)}, u32[]{:S(2)}) collective-permute-start(f32[18,8,128]{2,1,0:T(8,128)S(1)} %get-tuple-element.68), channel_id=1, source_target_pairs={{0,6},{1,7},{2,4},{3,5},{4,2},{5,3},{6,0},{7,1},{8,14},{9,15},{10,... | collective-permute-start | bytes 221192 | tf_op jit(solution)/shard_map/ppermute | solution.py:381
  50.5 6.5 %collective-permute-start.22 = (f32[18,8,128]{2,1,0:T(8,128)S(1)}, f32[18,8,128]{2,1,0:T(8,128)S(1)}, u32[]{:S(2)}, u32[]{:S(2)}) collective-permute-start(f32[18,8,128]{2,1,0:T(8,128)S(1)} %get-tuple-element.69), channel_id=1, source_target_pairs={{0,7},{1,6},{2,5},{3,4},{4,3},{5,2},{6,1},{7,0},{8,15},{9,14},{10,... | collective-permute-start | bytes 221192 | tf_op jit(solution)/shard_map/ppermute | solution.py:381
  (1 other events, 3.8 us)

commit v8 on v6

--- a/solution.py
+++ b/solution.py
@@ -38,6 +38,11 @@
     return whole, shift - whole * BS
 
 
+def place(cfg, me_ref):
+    phi, tile = lax.rem(me_ref[0], cfg.n), lax.div(me_ref[0], cfg.n)
+    return phi, jnp.bitwise_xor(phi, lax.rem(tile, 2) * (cfg.n - 1))
+
+
 def start_all(copies):
     for copy in copies:
         copy.start()
@@ -50,6 +55,7 @@
 
 
 def pack_kernel(cfg, me_ref, ids_ref, face_ref, conserved_ref, *refs):
+    me, group = place(cfg, me_ref)
     n, tiles = cfg.n, cfg.tiles
     half = n // 2
     outs, (all_ref, id_ref, sem) = refs[: n + half], refs[n + half :]
@@ -58,7 +64,7 @@
         from_ref = face_ref.at[c] if c < 3 else conserved_ref.at[c - 3]
         copies.append(pltpu.make_async_copy(from_ref, all_ref.at[c], sem.at[c]))
     start_all(copies)
-    dests = [jnp.bitwise_xor(me_ref[0], k) * tiles for k in cfg.order]
+    dests = [jnp.bitwise_xor(group, k) * tiles for k in cfg.order]
     copies[0].wait()
     rows = lax.broadcasted_iota(jnp.int32, (SUB, LANES), 0)
     ids = jnp.zeros((SUB, LANES), jnp.int32)
@@ -76,10 +82,11 @@
 
 
 def unpack_kernel(cfg, me_ref, *refs):
+    me, group = place(cfg, me_ref)
     pieces, (conserved_ref, field_ref, sem) = refs[: cfg.n], refs[cfg.n :]
     copies = []
     for piece, k in zip(pieces, cfg.order):
-        at = pl.ds(jnp.bitwise_xor(me_ref[0], k) * cfg.tiles, cfg.tiles)
+        at = pl.ds(jnp.bitwise_xor(group, k) * cfg.tiles, cfg.tiles)
         for j, (first, count, out) in enumerate(((0, 5, conserved_ref), (5, 3, field_ref))):
             copies.append(
                 pltpu.make_async_copy(
@@ -90,15 +97,21 @@
 
 
 def operators_kernel(cfg, me_ref, shift_ref, frac_ref, mh_ref, ml_ref, gh_ref, gl_ref, tj_ref):
+    me, group = place(cfg, me_ref)
     size = cfg.lanes
-    first = (me_ref[0] * cfg.rows) // BS
+    first = (group * cfg.rows) // BS
     row = lax.broadcasted_iota(jnp.int32, (size, size), 0)
     col = lax.broadcasted_iota(jnp.int32, (size, size), 1)
     same = (row // BS) == (col // BS)
-    e_in, e_out = row % BS, col % BS
-    zero = jnp.zeros((size, size), F32)
-    tj_ref[0] = jnp.where(same & (e_in < e_out), 1.0, zero).astype(BF16)
-    tj_ref[1] = jnp.where(same, 1.0, zero).astype(BF16)
+    e_in = lax.broadcasted_iota(jnp.int32, (BS, size), 0)
+    e_out = lax.broadcasted_iota(jnp.int32, (BS, size), 1) % BS
+    zero = jnp.zeros((BS, size), F32)
+
+    def spread(pattern):
+        return jnp.where(same, jnp.concatenate([pattern] * (size // BS), axis=0), 0.0)
+
+    tj_ref[0] = spread(jnp.where(e_in < e_out, 1.0, zero)).astype(BF16)
+    tj_ref[1] = spread(zero + 1.0).astype(BF16)
     for al in range(cfg.radii):
         _, rest = nearest_blocks(shift_ref[first + al])
         position = -jnp.full((1, size), frac_ref[first + al], F32)
@@ -121,16 +134,18 @@
             weights.append(total)
         for d in range(3):
             at = e_in + BS * (d - 1)
-            tap = jnp.where(same, at - e_out + rest, 100)
+            tap = at - e_out + rest
             remap, flux = zero, zero
             for a in NODES:
                 hit = tap == a
                 remap = jnp.where(hit, lagrange[a + 3], remap)
                 if a < 3:
                     flux = jnp.where(hit, weights[a + 3], flux)
-            flux = flux - jnp.where(same & (at < e_out - rest), 1.0, zero)
-            mh_ref[al, d], ml_ref[al, d] = halves(remap)
-            gh_ref[al, d], gl_ref[al, d] = halves(flux)
+            flux = flux - jnp.where(at < e_out - rest, 1.0, zero)
+            for value, high_ref, low_ref in ((remap, mh_ref, ml_ref), (flux, gh_ref, gl_ref)):
+                high = value.astype(BF16).astype(F32)
+                high_ref[al, d] = spread(high).astype(BF16)
+                low_ref[al, d] = spread(value - high).astype(BF16)
 
 
 def gather_matrix(cfg, me, ids, whole):
@@ -209,9 +224,9 @@
 
 
 def edge_kernel(cfg, me_ref, shift_ref, *refs):
+    me, group = place(cfg, me_ref)
     pieces, (gh_ref, gl_ref, tj_ref, halo_ref) = refs[: cfg.n], refs[cfg.n :]
-    me = me_ref[0]
-    whole, _ = nearest_blocks(shift_ref[(me * cfg.rows) // BS])
+    whole, _ = nearest_blocks(shift_ref[(group * cfg.rows) // BS])
     taken = gather_matrix(cfg, me, numbers(cfg, pieces), whole)
     y = dot(jnp.concatenate(taken, axis=0).astype(BF16), source(cfg, first_half(cfg, pieces, 0), 0))
     by_owner(cfg, me, halo_ref, whole_fluxes(cfg, [y], 0, gh_ref, gl_ref, tj_ref))
@@ -227,11 +242,11 @@
 
 
 def fields_kernel(cfg, me_ref, shift_ref, *refs):
+    me, group = place(cfg, me_ref)
     n, slots, wide, per = cfg.n, cfg.slots, cfg.lanes, cfg.per
     pieces = refs[:n]
     mh_ref, ml_ref, gh_ref, gl_ref, tj_ref, out_ref, taken_ref, polar_ref = refs[n:]
-    me = me_ref[0]
-    first = (me * cfg.rows) // BS
+    first = (group * cfg.rows) // BS
     ids = numbers(cfg, pieces)
 
     def put(c, al, value):
@@ -272,11 +287,12 @@
 
 
 def finish_kernel(cfg, me_ref, *refs):
+    me, group = place(cfg, me_ref)
     n, slots, per = cfg.n, cfg.slots, cfg.per
     pieces = refs[:n]
     mh_ref, ml_ref, taken_ref, rows_ref, halo_ref, polar_ref = refs[n : n + 6]
     outs = refs[n + 6 :]
-    me, rest = me_ref[0], cfg.tiles - cfg.per
+    rest = cfg.tiles - cfg.per
     for al in range(cfg.radii):
         taken = taken_ref[al]
         ys = [dot(taken, source(cfg, second_half(cfg, pieces, c), al)) for c in range(4)]
@@ -298,7 +314,7 @@
             row = lax.broadcasted_iota(jnp.int32, after.shape, 0)
             lane = lax.broadcasted_iota(jnp.int32, after.shape, 1)
             up = jnp.where(row < 4, jnp.concatenate([after[4:], after[:4]], axis=0), 0.0)
-            after = jnp.where(lax.rem(me, cfg.split) == cfg.split - 1, up, after)
+            after = jnp.where(lax.rem(group, cfg.split) == cfg.split - 1, up, after)
             after = pltpu.roll(jnp.where(lane < BS, after, 0.0), LANES - BS, 1)
             out[7, cfg.tiles - 1] = out[7, cfg.tiles - 1] + after
 
@@ -332,7 +348,11 @@
     def grant(mib):
         return pltpu.CompilerParams(vmem_limit_bytes=min(mib, 48) * 2**20)
 
-    me = lax.axis_index("phi").astype(jnp.int32).reshape(1)
+    me = lax.axis_index(("tile", "phi")).astype(jnp.int32).reshape(1)
+
+    def holder(group):
+        tile, place = divmod(group, n)
+        return tile * n + (place ^ (tile % 2 * (n - 1)))
 
     def tiled(x):
         return x.reshape(SUB, x.shape[1], n * tiles, LANES).transpose(1, 2, 0, 3)
@@ -389,7 +409,9 @@
         name="edge",
     )(me, int_shift, *first, gh, gl, tj)
     halo = lax.ppermute(
-        halo, ("tile", "phi"), [(s, s - cfg.split) for s in range(cfg.split, count)]
+        halo,
+        ("tile", "phi"),
+        [(holder(s), holder(s - cfg.split)) for s in range(cfg.split, count)],
     )
     rows, taken, polar = pl.pallas_call(
         functools.partial(fields_kernel, cfg),
@@ -406,8 +428,11 @@
     if cfg.split > 1:
         polar = lax.ppermute(
             polar,
-            "phi",
-            [(s, s - 1 if s % cfg.split else s + cfg.split - 1) for s in range(n)],
+            ("tile", "phi"),
+            [
+                (holder(s), holder(s - 1 if s % cfg.split else s + cfg.split - 1))
+                for s in range(count)
+            ],
         )
     done = pl.pallas_call(
         functools.partial(finish_kernel, cfg),

time: 59.3 us -> 58.3 us (0.983)
  starting transfers between devices: 24.9 us -> 26.9 us
  waiting for transfers between devices: 24 us -> 22.6 us
  Pallas kernels: 8.97 us -> 7.87 us
    ppermute x18, starting transfers between devices: 22.8 us -> 24.8 us  [exchange(): lax.ppermute(piece, 'phi', [(s, s ^ k) for s in range(n)])]
    ppermute x18, waiting for transfers between devices: 23.5 us -> 22 us  [exchange(): lax.ppermute(piece, 'phi', [(s, s ^ k) for s in range(n)])]
    pallas_call x1, Pallas kernels: 2.24 us -> 1.13 us  [shards(): pl.pallas_call(functools.partial(operators_kernel, cfg), out_shape=[squar...]
  transfers between devices with their start and end apart: 19 -> 19, of which waited for: 9 -> 9; matrix products, arithmetic and copies ran while one was open for 0% -> 0% of each run, Pallas kernels for 9% -> 7%
where the time goes in v8:
time: 58.3 us; the launch traced here: 58.1 us
  starting transfers between devices  26.9 us (46%)
  waiting for transfers between devices  22.6 us (39%)
  Pallas kernels  7.87 us (13%)
  between operations  0.74 us (1%)
    ppermute x18, starting transfers between devices, exchange(): lax.ppermute(piece, 'phi', [(s, s ^ k) for s in range(n)])  24.8 us
    ppermute x18, waiting for transfers between devices, exchange(): lax.ppermute(piece, 'phi', [(s, s ^ k) for s in range(n)])  22 us
    pallas_call x1, Pallas kernels, shards(): pl.pallas_call(functools.partial(fields_kernel, cfg), out_shape=[shape(n,...  2.15 us
    ppermute x1, starting transfers between devices, shards(): lax.ppermute(halo, ('tile', 'phi'), [(holder(s), holder(s - cfg.split)) f...  2.08 us
    pallas_call x1, Pallas kernels, shards(): pl.pallas_call(functools.partial(pack_kernel, cfg), out_shape=[shape(4 *...  1.38 us
  transfers between devices with their start and end apart: 19, of which 9 were waited for; matrix products, arithmetic and copies ran while one was open for 0% of the time, Pallas kernels for 7%

profile of v8, /device:TPU:13, one launch (start us, length us, event | category | flops | bytes accessed | tf_op | source)
XLA Modules:
  0.0 58.1 jit_solution(16825917714771329845)
XLA Ops:
  0.6 1.4 %pack.1 = (f32[17,8,128]{2,1,0:T(8,128)S(1)}, f32[17,8,128]{2,1,0:T(8,128)S(1)}, f32[17,8,128]{2,1,0:T(8,128)S(1)}, f32[17,8,128]{2,1,0:T(8,128)S(1)}, f32[33,8,...) custom-call(s32[1]{0:T(128)} %bitcast.me_ref, ...), custom_call_target="tpu_custom_call" | custom-call | tf_op jit(solution)/shard_map/pack/pallas_call | solution.py:374
  2.0 2.4 %collective-permute-start.7 = (f32[17,8,128]{2,1,0:T(8,128)S(1)}, f32[17,8,128]{2,1,0:T(8,128)S(1)}, u32[]{:S(2)}, u32[]{:S(2)}) collective-permute-start(f32[17,8,128]{2,1,0:T(8,128)S(1)} %get-tuple-element.42), channel_id=1, source_target_pairs={{0,4},{1,5},{2,6},{3,7},{4,0},{5,1},{6,2},{7,3},{8,12},{9,13},{10,... | collective-permute-start | bytes 208904 | tf_op jit(solution)/shard_map/ppermute | solution.py:367
  5.4 1.3 %collective-permute-start.5 = (f32[33,8,128]{2,1,0:T(8,128)S(1)}, f32[33,8,128]{2,1,0:T(8,128)S(1)}, u32[]{:S(2)}, u32[]{:S(2)}) collective-permute-start(f32[33,8,128]{2,1,0:T(8,128)S(1)} %get-tuple-element.37), channel_id=1, source_target_pairs={{0,2},{1,3},{2,0},{3,1},{4,6},{5,7},{6,4},{7,5},{8,10},{9,11},{10,... | collective-permute-start | bytes 405512 | tf_op jit(solution)/shard_map/ppermute | solution.py:367
  7.4 1.4 %collective-permute-done.7.refs_0_ = f32[17,8,128]{2,1,0:T(8,128)S(1)} collective-permute-done((f32[17,8,128]{2,1,0:T(8,128)S(1)}, f32[17,8,128]{2,1,0:T(8,128)S(1)}, u32[]{:S(2)}, u32[]{:S(2)}) %collective-permute-start.7) | collective-permute-done | bytes 69664 | tf_op jit(solution)/shard_map/ppermute | solution.py:367
  8.8 1.8 %collective-permute-done.8.refs_1_ = f32[17,8,128]{2,1,0:T(8,128)S(1)} collective-permute-done((f32[17,8,128]{2,1,0:T(8,128)S(1)}, f32[17,8,128]{2,1,0:T(8,128)S(1)}, u32[]{:S(2)}, u32[]{:S(2)}) %collective-permute-start.8) | collective-permute-done | bytes 69664 | tf_op jit(solution)/shard_map/ppermute | solution.py:367
  11.3 1.1 %operators.1 = (bf16[2,3,256,256]{3,2,1,0:T(8,128)(2,1)S(1)}, bf16[2,3,256,256]{3,2,1,0:T(8,128)(2,1)S(1)}, bf16[2,3,256,256]{3,2,1,0:T(8,128)(2,1)S(1)}, bf16[2...) custom-call(s32[1]{0:T(128)} %bitcast.me_ref, s32[16]{0:T(128)S(1)} %copy-done, f32[16]{0:T(128)S(1)} %copy-done.1), custom_call_target="tpu_custom_call" | custom-call | tf_op jit(solution)/shard_map/operators/pallas_call | solution.py:393
  12.5 5.2 %collective-permute-start = (f32[16,8,128]{2,1,0:T(8,128)S(1)}, f32[16,8,128]{2,1,0:T(8,128)S(1)}, u32[]{:S(2)}, u32[]{:S(2)}) collective-permute-start(f32[16,8,128]{2,1,0:T(8,128)S(1)} %get-tuple-element.32), channel_id=1, source_target_pairs={{0,4},{1,5},{2,6},{3,7},{4,0},{5,1},{6,2},{7,3},{8,12},{9,13},{10,... | collective-permute-start | bytes 196616 | tf_op jit(solution)/shard_map/ppermute | solution.py:367
  17.7 2.7 %collective-permute-start.1 = (f32[16,8,128]{2,1,0:T(8,128)S(1)}, f32[16,8,128]{2,1,0:T(8,128)S(1)}, u32[]{:S(2)}, u32[]{:S(2)}) collective-permute-start(f32[16,8,128]{2,1,0:T(8,128)S(1)} %get-tuple-element.33), channel_id=1, source_target_pairs={{0,5},{1,4},{2,7},{3,6},{4,1},{5,0},{6,3},{7,2},{8,13},{9,12},{10,... | collective-permute-start | bytes 196616 | tf_op jit(solution)/shard_map/ppermute | solution.py:367
  20.4 1.2 %collective-permute-start.2 = (f32[16,8,128]{2,1,0:T(8,128)S(1)}, f32[16,8,128]{2,1,0:T(8,128)S(1)}, u32[]{:S(2)}, u32[]{:S(2)}) collective-permute-start(f32[16,8,128]{2,1,0:T(8,128)S(1)} %get-tuple-element.34), channel_id=1, source_target_pairs={{0,6},{1,7},{2,4},{3,5},{4,2},{5,3},{6,0},{7,1},{8,14},{9,15},{10,... | collective-permute-start | bytes 196616 | tf_op jit(solution)/shard_map/ppermute | solution.py:367
  22.1 1.1 %edge.1 = f32[8,2,8,128]{3,2,1,0:T(8,128)S(1)} custom-call(s32[1]{0:T(128)} %bitcast.me_ref, s32[16]{0:T(128)S(1)} %copy-done, f32[17,8,128]{2,1,0:T(8,128)S(1)} %collective-permute-done.7.refs_0_, f32[17,8,128]{2,1,0:T(8,128)S(1)} %collective-permute-done.8.refs_1_, f32[17,8,128]{2,1,0:T(8,128)S(1)} %collective-permute-done.9.refs_2_, ...), custom_call_target="tpu_custom_call" | custom-call | tf_op jit(solution)/shard_map/edge/pallas_call | solution.py:403
  23.1 2.1 %collective-permute-start.11 = (f32[8,2,8,128]{3,2,1,0:T(8,128)S(1)}, f32[8,2,8,128]{3,2,1,0:T(8,128)S(1)}, u32[]{:S(2)}, u32[]{:S(2)}) collective-permute-start(f32[8,2,8,128]{3,2,1,0:T(8,128)S(1)} %edge.1), channel_id=1, source_target_pairs={{1,0},{2,1},{3,2},{4,3},{5,4},{6,5},{7,6},{15,7},{14,15},{13,14},{... | collective-permute-start | bytes 196616 | tf_op jit(solution)/shard_map/ppermute | solution.py:411
  25.2 2.2 %fields.1 = (f32[8,4,4,8,128]{4,3,2,1,0:T(8,128)S(1)}, bf16[2,192,192]{2,1,0:T(8,128)(2,1)S(1)}, f32[1,1,8,128]{3,2,1,0:T(8,128)S(1)}) custom-call(s32[1]{0:T(128)} %bitcast.me_ref, s32[16]{0:T(128)S(1)} %copy-done, f32[17,8,128]{2,1,0:T(8,128)S(1)} %collective-permute-done.7.refs_0_, f32[17,8,128]{2,1,0:T(8,128)S(1)} %collective-permute-done.8.refs_1_, ...), custom_call_target="tpu_custom_call" | custom-call | tf_op jit(solution)/shard_map/fields/pallas_call | solution.py:416
  27.4 2.3 %collective-permute-done.2.refs_2_ = f32[16,8,128]{2,1,0:T(8,128)S(1)} collective-permute-done((f32[16,8,128]{2,1,0:T(8,128)S(1)}, f32[16,8,128]{2,1,0:T(8,128)S(1)}, u32[]{:S(2)}, u32[]{:S(2)}) %collective-permute-start.2) | collective-permute-done | bytes 65568 | tf_op jit(solution)/shard_map/ppermute | solution.py:367
  29.7 1.4 %collective-permute-done.3.refs_3_ = f32[16,8,128]{2,1,0:T(8,128)S(1)} collective-permute-done((f32[16,8,128]{2,1,0:T(8,128)S(1)}, f32[16,8,128]{2,1,0:T(8,128)S(1)}, u32[]{:S(2)}, u32[]{:S(2)}) %collective-permute-start.3) | collective-permute-done | bytes 65568 | tf_op jit(solution)/shard_map/ppermute | solution.py:367
  31.7 1.1 %finish.1 = (f32[8,4,8,128]{3,2,1,0:T(8,128)S(1)}, f32[8,4,8,128]{3,2,1,0:T(8,128)S(1)}, f32[8,4,8,128]{3,2,1,0:T(8,128)S(1)}, f32[8,4,8,128]{3,2,1,0:T(8,128)S(...) custom-call(s32[1]{0:T(128)} %bitcast.me_ref, ...), custom_call_target="tpu_custom_call" | custom-call | tf_op jit(solution)/shard_map/finish/pallas_call | solution.py:437
  32.8 2.4 %collective-permute-start.13 = (f32[8,4,8,128]{3,2,1,0:T(8,128)S(1)}, f32[8,4,8,128]{3,2,1,0:T(8,128)S(1)}, u32[]{:S(2)}, u32[]{:S(2)}) collective-permute-start(f32[8,4,8,128]{3,2,1,0:T(8,128)S(1)} %get-tuple-element.53), channel_id=1, source_target_pairs={{0,5},{1,4},{2,7},{3,6},{4,1},{5,0},{6,3},{7,2},{8,13},{9,12},{10,... | collective-permute-start | bytes 393224 | tf_op jit(solution)/shard_map/ppermute | solution.py:367
  35.5 1.7 %collective-permute-start.15 = (f32[8,4,8,128]{3,2,1,0:T(8,128)S(1)}, f32[8,4,8,128]{3,2,1,0:T(8,128)S(1)}, u32[]{:S(2)}, u32[]{:S(2)}) collective-permute-start(f32[8,4,8,128]{3,2,1,0:T(8,128)S(1)} %get-tuple-element.55), channel_id=1, source_target_pairs={{0,7},{1,6},{2,5},{3,4},{4,3},{5,2},{6,1},{7,0},{8,15},{9,14},{10,... | collective-permute-start | bytes 393224 | tf_op jit(solution)/shard_map/ppermute | solution.py:367
  37.2 1.5 %collective-permute-start.16 = (f32[8,4,8,128]{3,2,1,0:T(8,128)S(1)}, f32[8,4,8,128]{3,2,1,0:T(8,128)S(1)}, u32[]{:S(2)}, u32[]{:S(2)}) collective-permute-start(f32[8,4,8,128]{3,2,1,0:T(8,128)S(1)} %get-tuple-element.56), channel_id=1, source_target_pairs={{0,3},{1,2},{2,1},{3,0},{4,7},{5,6},{6,5},{7,4},{8,11},{9,10},{10,... | collective-permute-start | bytes 393224 | tf_op jit(solution)/shard_map/ppermute | solution.py:367
  38.8 8.7 %collective-permute-done.12.refs_0_ = f32[8,4,8,128]{3,2,1,0:T(8,128)S(1)} collective-permute-done((f32[8,4,8,128]{3,2,1,0:T(8,128)S(1)}, f32[8,4,8,128]{3,2,1,0:T(8,128)S(1)}, u32[]{:S(2)}, u32[]{:S(2)}) %collective-permute-start.12) | collective-permute-done | bytes 131104 | tf_op jit(solution)/shard_map/ppermute | solution.py:367
  47.4 1.8 %collective-permute-start.17 = (f32[8,4,8,128]{3,2,1,0:T(8,128)S(1)}, f32[8,4,8,128]{3,2,1,0:T(8,128)S(1)}, u32[]{:S(2)}, u32[]{:S(2)}) collective-permute-start(f32[8,4,8,128]{3,2,1,0:T(8,128)S(1)} %get-tuple-element.57), channel_id=1, source_target_pairs={{0,2},{1,3},{2,0},{3,1},{4,6},{5,7},{6,4},{7,5},{8,10},{9,11},{10,... | collective-permute-start | bytes 393224 | tf_op jit(solution)/shard_map/ppermute | solution.py:367
  50.2 1.3 %collective-permute-start.18 = (f32[8,4,8,128]{3,2,1,0:T(8,128)S(1)}, f32[8,4,8,128]{3,2,1,0:T(8,128)S(1)}, u32[]{:S(2)}, u32[]{:S(2)}) collective-permute-start(f32[8,4,8,128]{3,2,1,0:T(8,128)S(1)} %get-tuple-element.58), channel_id=1, source_target_pairs={{0,1},{1,0},{2,3},{3,2},{4,5},{5,4},{6,7},{7,6},{8,9},{9,8},{10,11... | collective-permute-start | bytes 393224 | tf_op jit(solution)/shard_map/ppermute | solution.py:367
  51.5 2.1 %collective-permute-done.14.refs_2_ = f32[8,4,8,128]{3,2,1,0:T(8,128)S(1)} collective-permute-done((f32[8,4,8,128]{3,2,1,0:T(8,128)S(1)}, f32[8,4,8,128]{3,2,1,0:T(8,128)S(1)}, u32[]{:S(2)}, u32[]{:S(2)}) %collective-permute-start.14) | collective-permute-done | bytes 131104 | tf_op jit(solution)/shard_map/ppermute | solution.py:367
  53.7 3.3 %collective-permute-done.15.refs_3_ = f32[8,4,8,128]{3,2,1,0:T(8,128)S(1)} collective-permute-done((f32[8,4,8,128]{3,2,1,0:T(8,128)S(1)}, f32[8,4,8,128]{3,2,1,0:T(8,128)S(1)}, u32[]{:S(2)}, u32[]{:S(2)}) %collective-permute-start.15) | collective-permute-done | bytes 131104 | tf_op jit(solution)/shard_map/ppermute | solution.py:367
  57.0 1.1 %unpack.1 = (f32[5,32,8,128]{3,2,1,0:T(8,128)}, f32[3,32,8,128]{3,2,1,0:T(8,128)}) custom-call(s32[1]{0:T(128)} %bitcast.me_ref, f32[8,4,8,128]{3,2,1,0:T(8,128)S(1)} %collective-permute-done.12.refs_0_, f32[8,4,8,128]{3,2,1,0:T(8,128)S(1)} %collective-permute-done.13.refs_1_, f32[8,4,8,128]{3,2,1,0:T(8,128)S(1)} %collective-permute-done.14.refs_2_, ...), custom_call_target="tpu_custom_call" | custom-call | tf_op jit(solution)/shard_map/unpack/pallas_call | solution.py:445
  (24 shorter events, 4.8 us)
Async XLA Ops:
  2.0 6.8 %collective-permute-start.7 = (f32[17,8,128]{2,1,0:T(8,128)S(1)}, f32[17,8,128]{2,1,0:T(8,128)S(1)}, u32[]{:S(2)}, u32[]{:S(2)}) collective-permute-start(f32[17,8,128]{2,1,0:T(8,128)S(1)} %get-tuple-element.42), channel_id=1, source_target_pairs={{0,4},{1,5},{2,6},{3,7},{4,0},{5,1},{6,2},{7,3},{8,12},{9,13},{10,... | collective-permute-start | bytes 208904 | tf_op jit(solution)/shard_map/ppermute | solution.py:367
  4.4 6.3 %collective-permute-start.8 = (f32[17,8,128]{2,1,0:T(8,128)S(1)}, f32[17,8,128]{2,1,0:T(8,128)S(1)}, u32[]{:S(2)}, u32[]{:S(2)}) collective-permute-start(f32[17,8,128]{2,1,0:T(8,128)S(1)} %get-tuple-element.43), channel_id=1, source_target_pairs={{0,5},{1,4},{2,7},{3,6},{4,1},{5,0},{6,3},{7,2},{8,13},{9,12},{10,... | collective-permute-start | bytes 208904 | tf_op jit(solution)/shard_map/ppermute | solution.py:367
  5.3 15.1 %collective-permute-start.4 = (f32[33,8,128]{2,1,0:T(8,128)S(1)}, f32[33,8,128]{2,1,0:T(8,128)S(1)}, u32[]{:S(2)}, u32[]{:S(2)}) collective-permute-start(f32[33,8,128]{2,1,0:T(8,128)S(1)} %get-tuple-element.36), channel_id=1, source_target_pairs={{0,3},{1,2},{2,1},{3,0},{4,7},{5,6},{6,5},{7,4},{8,11},{9,10},{10,... | collective-permute-start | bytes 405512 | tf_op jit(solution)/shard_map/ppermute | solution.py:367
  5.4 16.1 %collective-permute-start.5 = (f32[33,8,128]{2,1,0:T(8,128)S(1)}, f32[33,8,128]{2,1,0:T(8,128)S(1)}, u32[]{:S(2)}, u32[]{:S(2)}) collective-permute-start(f32[33,8,128]{2,1,0:T(8,128)S(1)} %get-tuple-element.37), channel_id=1, source_target_pairs={{0,2},{1,3},{2,0},{3,1},{4,6},{5,7},{6,4},{7,5},{8,10},{9,11},{10,... | collective-permute-start | bytes 405512 | tf_op jit(solution)/shard_map/ppermute | solution.py:367
  6.7 15.4 %collective-permute-start.6 = (f32[33,8,128]{2,1,0:T(8,128)S(1)}, f32[33,8,128]{2,1,0:T(8,128)S(1)}, u32[]{:S(2)}, u32[]{:S(2)}) collective-permute-start(f32[33,8,128]{2,1,0:T(8,128)S(1)} %get-tuple-element.38), channel_id=1, source_target_pairs={{0,1},{1,0},{2,3},{3,2},{4,5},{5,4},{6,7},{7,6},{8,9},{9,8},{10,11... | collective-permute-start | bytes 405512 | tf_op jit(solution)/shard_map/ppermute | solution.py:367
  8.8 2.5 %copy-start = (s32[16]{0:T(128)S(1)}, s32[16]{0:T(128)}, u32[]{:S(2)}) copy-start(s32[16]{0:T(128)} %shift_ref.5) | copy-start | bytes 196
  8.8 2.5 %copy-start.1 = (f32[16]{0:T(128)S(1)}, f32[16]{0:T(128)}, u32[]{:S(2)}) copy-start(f32[16]{0:T(128)} %frac_ref.1) | copy-start | bytes 196
  8.8 3.7 %collective-permute-start.9 = (f32[17,8,128]{2,1,0:T(8,128)S(1)}, f32[17,8,128]{2,1,0:T(8,128)S(1)}, u32[]{:S(2)}, u32[]{:S(2)}) collective-permute-start(f32[17,8,128]{2,1,0:T(8,128)S(1)} %get-tuple-element.44), channel_id=1, source_target_pairs={{0,6},{1,7},{2,4},{3,5},{4,2},{5,3},{6,0},{7,1},{8,14},{9,15},{10,... | collective-permute-start | bytes 208904 | tf_op jit(solution)/shard_map/ppermute | solution.py:367
  10.7 7.0 %collective-permute-start.10 = (f32[17,8,128]{2,1,0:T(8,128)S(1)}, f32[17,8,128]{2,1,0:T(8,128)S(1)}, u32[]{:S(2)}, u32[]{:S(2)}) collective-permute-start(f32[17,8,128]{2,1,0:T(8,128)S(1)} %get-tuple-element.45), channel_id=1, source_target_pairs={{0,7},{1,6},{2,5},{3,4},{4,3},{5,2},{6,1},{7,0},{8,15},{9,14},{10,... | collective-permute-start | bytes 208904 | tf_op jit(solution)/shard_map/ppermute | solution.py:367
  12.5 14.9 %collective-permute-start = (f32[16,8,128]{2,1,0:T(8,128)S(1)}, f32[16,8,128]{2,1,0:T(8,128)S(1)}, u32[]{:S(2)}, u32[]{:S(2)}) collective-permute-start(f32[16,8,128]{2,1,0:T(8,128)S(1)} %get-tuple-element.32), channel_id=1, source_target_pairs={{0,4},{1,5},{2,6},{3,7},{4,0},{5,1},{6,2},{7,3},{8,12},{9,13},{10,... | collective-permute-start | bytes 196616 | tf_op jit(solution)/shard_map/ppermute | solution.py:367
  17.7 9.7 %collective-permute-start.1 = (f32[16,8,128]{2,1,0:T(8,128)S(1)}, f32[16,8,128]{2,1,0:T(8,128)S(1)}, u32[]{:S(2)}, u32[]{:S(2)}) collective-permute-start(f32[16,8,128]{2,1,0:T(8,128)S(1)} %get-tuple-element.33), channel_id=1, source_target_pairs={{0,5},{1,4},{2,7},{3,6},{4,1},{5,0},{6,3},{7,2},{8,13},{9,12},{10,... | collective-permute-start | bytes 196616 | tf_op jit(solution)/shard_map/ppermute | solution.py:367
  20.4 9.4 %collective-permute-start.2 = (f32[16,8,128]{2,1,0:T(8,128)S(1)}, f32[16,8,128]{2,1,0:T(8,128)S(1)}, u32[]{:S(2)}, u32[]{:S(2)}) collective-permute-start(f32[16,8,128]{2,1,0:T(8,128)S(1)} %get-tuple-element.34), channel_id=1, source_target_pairs={{0,6},{1,7},{2,4},{3,5},{4,2},{5,3},{6,0},{7,1},{8,14},{9,15},{10,... | collective-permute-start | bytes 196616 | tf_op jit(solution)/shard_map/ppermute | solution.py:367
  21.5 9.6 %collective-permute-start.3 = (f32[16,8,128]{2,1,0:T(8,128)S(1)}, f32[16,8,128]{2,1,0:T(8,128)S(1)}, u32[]{:S(2)}, u32[]{:S(2)}) collective-permute-start(f32[16,8,128]{2,1,0:T(8,128)S(1)} %get-tuple-element.35), channel_id=1, source_target_pairs={{0,7},{1,6},{2,5},{3,4},{4,3},{5,2},{6,1},{7,0},{8,15},{9,14},{10,... | collective-permute-start | bytes 196616 | tf_op jit(solution)/shard_map/ppermute | solution.py:367
  23.1 8.6 %collective-permute-start.11 = (f32[8,2,8,128]{3,2,1,0:T(8,128)S(1)}, f32[8,2,8,128]{3,2,1,0:T(8,128)S(1)}, u32[]{:S(2)}, u32[]{:S(2)}) collective-permute-start(f32[8,2,8,128]{3,2,1,0:T(8,128)S(1)} %edge.1), channel_id=1, source_target_pairs={{1,0},{2,1},{3,2},{4,3},{5,4},{6,5},{7,6},{15,7},{14,15},{13,14},{... | collective-permute-start | bytes 196616 | tf_op jit(solution)/shard_map/ppermute | solution.py:411
  32.8 14.7 %collective-permute-start.12 = (f32[8,4,8,128]{3,2,1,0:T(8,128)S(1)}, f32[8,4,8,128]{3,2,1,0:T(8,128)S(1)}, u32[]{:S(2)}, u32[]{:S(2)}) collective-permute-start(f32[8,4,8,128]{3,2,1,0:T(8,128)S(1)} %get-tuple-element.52), channel_id=1, source_target_pairs={{0,4},{1,5},{2,6},{3,7},{4,0},{5,1},{6,2},{7,3},{8,12},{9,13},{10,... | collective-permute-start | bytes 393224 | tf_op jit(solution)/shard_map/ppermute | solution.py:367
  32.8 17.4 %collective-permute-start.13 = (f32[8,4,8,128]{3,2,1,0:T(8,128)S(1)}, f32[8,4,8,128]{3,2,1,0:T(8,128)S(1)}, u32[]{:S(2)}, u32[]{:S(2)}) collective-permute-start(f32[8,4,8,128]{3,2,1,0:T(8,128)S(1)} %get-tuple-element.53), channel_id=1, source_target_pairs={{0,5},{1,4},{2,7},{3,6},{4,1},{5,0},{6,3},{7,2},{8,13},{9,12},{10,... | collective-permute-start | bytes 393224 | tf_op jit(solution)/shard_map/ppermute | solution.py:367
  35.2 18.5 %collective-permute-start.14 = (f32[8,4,8,128]{3,2,1,0:T(8,128)S(1)}, f32[8,4,8,128]{3,2,1,0:T(8,128)S(1)}, u32[]{:S(2)}, u32[]{:S(2)}) collective-permute-start(f32[8,4,8,128]{3,2,1,0:T(8,128)S(1)} %get-tuple-element.54), channel_id=1, source_target_pairs={{0,6},{1,7},{2,4},{3,5},{4,2},{5,3},{6,0},{7,1},{8,14},{9,15},{10,... | collective-permute-start | bytes 393224 | tf_op jit(solution)/shard_map/ppermute | solution.py:367
  35.5 21.5 %collective-permute-start.15 = (f32[8,4,8,128]{3,2,1,0:T(8,128)S(1)}, f32[8,4,8,128]{3,2,1,0:T(8,128)S(1)}, u32[]{:S(2)}, u32[]{:S(2)}) collective-permute-start(f32[8,4,8,128]{3,2,1,0:T(8,128)S(1)} %get-tuple-element.55), channel_id=1, source_target_pairs={{0,7},{1,6},{2,5},{3,4},{4,3},{5,2},{6,1},{7,0},{8,15},{9,14},{10,... | collective-permute-start | bytes 393224 | tf_op jit(solution)/shard_map/ppermute | solution.py:367
  37.2 19.8 %collective-permute-start.16 = (f32[8,4,8,128]{3,2,1,0:T(8,128)S(1)}, f32[8,4,8,128]{3,2,1,0:T(8,128)S(1)}, u32[]{:S(2)}, u32[]{:S(2)}) collective-permute-start(f32[8,4,8,128]{3,2,1,0:T(8,128)S(1)} %get-tuple-element.56), channel_id=1, source_target_pairs={{0,3},{1,2},{2,1},{3,0},{4,7},{5,6},{6,5},{7,4},{8,11},{9,10},{10,... | collective-permute-start | bytes 393224 | tf_op jit(solution)/shard_map/ppermute | solution.py:367
  47.4 9.6 %collective-permute-start.17 = (f32[8,4,8,128]{3,2,1,0:T(8,128)S(1)}, f32[8,4,8,128]{3,2,1,0:T(8,128)S(1)}, u32[]{:S(2)}, u32[]{:S(2)}) collective-permute-start(f32[8,4,8,128]{3,2,1,0:T(8,128)S(1)} %get-tuple-element.57), channel_id=1, source_target_pairs={{0,2},{1,3},{2,0},{3,1},{4,6},{5,7},{6,4},{7,5},{8,10},{9,11},{10,... | collective-permute-start | bytes 393224 | tf_op jit(solution)/shard_map/ppermute | solution.py:367
  50.2 6.8 %collective-permute-start.18 = (f32[8,4,8,128]{3,2,1,0:T(8,128)S(1)}, f32[8,4,8,128]{3,2,1,0:T(8,128)S(1)}, u32[]{:S(2)}, u32[]{:S(2)}) collective-permute-start(f32[8,4,8,128]{3,2,1,0:T(8,128)S(1)} %get-tuple-element.58), channel_id=1, source_target_pairs={{0,1},{1,0},{2,3},{3,2},{4,5},{5,4},{6,7},{7,6},{8,9},{9,8},{10,11... | collective-permute-start | bytes 393224 | tf_op jit(solution)/shard_map/ppermute | solution.py:367

commit v9 on v8

--- a/solution.py
+++ b/solution.py
@@ -81,23 +81,24 @@
             out[at : at + tiles] = all_ref[c, pl.ds(dest, tiles)]
 
 
-def unpack_kernel(cfg, me_ref, *refs):
-    me, group = place(cfg, me_ref)
-    pieces, (conserved_ref, field_ref, sem) = refs[: cfg.n], refs[cfg.n :]
+def unpack_kernel(cfg, orders, me_ref, *refs):
+    me, group = place(cfg, me_ref)
+    pieces, (conserved_ref, field_ref, sem) = refs[: len(orders)], refs[-3:]
     copies = []
-    for piece, k in zip(pieces, cfg.order):
+    for i, (piece, k) in enumerate(zip(pieces, orders)):
         at = pl.ds(jnp.bitwise_xor(group, k) * cfg.tiles, cfg.tiles)
         for j, (first, count, out) in enumerate(((0, 5, conserved_ref), (5, 3, field_ref))):
             copies.append(
                 pltpu.make_async_copy(
-                    piece.at[pl.ds(first, count)], out.at[:, at], sem.at[k, j]
+                    piece.at[pl.ds(first, count)], out.at[:, at], sem.at[i, j]
                 )
             )
     wait_all(start_all(copies))
 
 
-def operators_kernel(cfg, me_ref, shift_ref, frac_ref, mh_ref, ml_ref, gh_ref, gl_ref, tj_ref):
-    me, group = place(cfg, me_ref)
+def operators_kernel(cfg, me_ref, shift_ref, frac_ref, *refs):
+    me, group = place(cfg, me_ref)
+    mh_ref, ml_ref, gh_ref, gl_ref, tj_ref, whole_ref = refs
     size = cfg.lanes
     first = (group * cfg.rows) // BS
     row = lax.broadcasted_iota(jnp.int32, (size, size), 0)
@@ -113,7 +114,8 @@
     tj_ref[0] = spread(jnp.where(e_in < e_out, 1.0, zero)).astype(BF16)
     tj_ref[1] = spread(zero + 1.0).astype(BF16)
     for al in range(cfg.radii):
-        _, rest = nearest_blocks(shift_ref[first + al])
+        whole, rest = nearest_blocks(shift_ref[first + al])
+        whole_ref[al] = jnp.full((SUB, 3 * cfg.slots), whole, jnp.int32)
         position = -jnp.full((1, size), frac_ref[first + al], F32)
         lagrange = []
         for a in NODES:
@@ -223,30 +225,28 @@
             ]
 
 
-def edge_kernel(cfg, me_ref, shift_ref, *refs):
-    me, group = place(cfg, me_ref)
-    pieces, (gh_ref, gl_ref, tj_ref, halo_ref) = refs[: cfg.n], refs[cfg.n :]
-    whole, _ = nearest_blocks(shift_ref[(group * cfg.rows) // BS])
-    taken = gather_matrix(cfg, me, numbers(cfg, pieces), whole)
+def edge_kernel(cfg, me_ref, *refs):
+    me, group = place(cfg, me_ref)
+    pieces, (gh_ref, gl_ref, tj_ref, whole_ref, halo_ref) = refs[: cfg.n], refs[cfg.n :]
+    taken = gather_matrix(cfg, me, numbers(cfg, pieces), whole_ref[0, 0:1])
     y = dot(jnp.concatenate(taken, axis=0).astype(BF16), source(cfg, first_half(cfg, pieces, 0), 0))
     by_owner(cfg, me, halo_ref, whole_fluxes(cfg, [y], 0, gh_ref, gl_ref, tj_ref))
 
 
-def remapped(cfg, ys, al, mh_ref, ml_ref):
+def remapped(count, ys, al, mh_ref, ml_ref):
     total = 0.0
     for d in range(3):
-        at = slice(d * cfg.slots, (d + 1) * cfg.slots)
+        at = slice(d * count, (d + 1) * count)
         high, low = halves(jnp.concatenate([y[at] for y in ys], axis=0))
         total = total + three_dots(high, low, mh_ref[al, d], ml_ref[al, d])
     return total
 
 
-def fields_kernel(cfg, me_ref, shift_ref, *refs):
+def fields_kernel(cfg, me_ref, *refs):
     me, group = place(cfg, me_ref)
     n, slots, wide, per = cfg.n, cfg.slots, cfg.lanes, cfg.per
     pieces = refs[:n]
-    mh_ref, ml_ref, gh_ref, gl_ref, tj_ref, out_ref, taken_ref, polar_ref = refs[n:]
-    first = (group * cfg.rows) // BS
+    mh_ref, ml_ref, gh_ref, gl_ref, tj_ref, whole_ref, out_ref, taken_ref, polar_ref = refs[n:]
     ids = numbers(cfg, pieces)
 
     def put(c, al, value):
@@ -260,8 +260,8 @@
     lower = (lax.broadcasted_iota(jnp.int32, (slots, wide), 0) >> 2) & 1 == 0
     total = []
     for al in range(cfg.radii):
-        whole, _ = nearest_blocks(shift_ref[first + al])
-        taken = jnp.concatenate(gather_matrix(cfg, me, ids, whole), axis=0).astype(BF16)
+        taken = gather_matrix(cfg, me, ids, whole_ref[al, 0:1])
+        taken = jnp.concatenate(taken, axis=0).astype(BF16)
         taken_ref[al] = taken[: 3 * slots]
         ys = [dot(taken, source(cfg, first_half(cfg, pieces, c), al)) for c in range(2)]
         flux = whole_fluxes(cfg, ys, al, gh_ref, gl_ref, tj_ref)
@@ -278,7 +278,7 @@
         )
         total.append((azimuthal + (after - polar) - radial, radial))
         ys.append(dot(taken[: 3 * slots], source(cfg, first_half(cfg, pieces, 3), al)))
-        remap = remapped(cfg, ys, al, mh_ref, ml_ref)
+        remap = remapped(slots, ys, al, mh_ref, ml_ref)
         for c, at in enumerate((1, 2, 0)):
             put(at, al, remap[c * slots : (c + 1) * slots])
     for al in range(cfg.radii):
@@ -286,25 +286,29 @@
         put(3, al, bp + total[al + 1][1] if al + 1 < cfg.radii else bp)
 
 
-def finish_kernel(cfg, me_ref, *refs):
+def finish_kernel(cfg, orders, me_ref, *refs):
     me, group = place(cfg, me_ref)
     n, slots, per = cfg.n, cfg.slots, cfg.per
     pieces = refs[:n]
     mh_ref, ml_ref, taken_ref, rows_ref, halo_ref, polar_ref = refs[n : n + 6]
-    outs = refs[n + 6 :]
-    rest = cfg.tiles - cfg.per
+    outs, mark_ref = refs[-len(orders) - 1 : -1], refs[-1]
+    mark_ref[...] = jnp.zeros_like(mark_ref)
+    rest = cfg.tiles - per
+    low, count = min(orders) * SUB, len(orders) * SUB
     for al in range(cfg.radii):
-        taken = taken_ref[al]
+        taken = jnp.concatenate(
+            [taken_ref[al, d * slots + low : d * slots + low + count] for d in range(3)], axis=0
+        )
         ys = [dot(taken, source(cfg, second_half(cfg, pieces, c), al)) for c in range(4)]
-        remap = remapped(cfg, ys, al, mh_ref, ml_ref)
-        for out, k in zip(outs, cfg.order):
+        remap = remapped(count, ys, al, mh_ref, ml_ref)
+        for out, k in zip(outs, orders):
             for c in range(4):
                 for t in range(per):
+                    at = c * count + k * SUB - low
                     out[1 + c, al * per + t] = remap[
-                        c * slots + k * SUB : c * slots + (k + 1) * SUB,
-                        t * LANES : (t + 1) * LANES,
+                        at : at + SUB, t * LANES : (t + 1) * LANES
                     ]
-    for out, k in zip(outs, cfg.order):
+    for out, k in zip(outs, orders):
         owner = jnp.bitwise_xor(me, k)
         out[0] = rows_ref[k, 0]
         out[5:8] = rows_ref[k, 1:4]
@@ -327,6 +331,7 @@
         self.tiles = self.rows * BS // LANES
         self.lanes = min(self.rows, BS) * BS
         self.radii = max(1, self.rows // BS)
+        self.last = self.order[n // 4 : n // 2]
         self.per = self.lanes // LANES
         self.split = max(1, BS // self.rows)
         self.slots = n * SUB
@@ -390,11 +395,15 @@
     far_second = exchange(packed[n:], cfg.order)
 
     square = shape(cfg.radii, 3, cfg.lanes, cfg.lanes, dtype=BF16)
-    mh, ml, gh, gl, tj = pl.pallas_call(
+    mh, ml, gh, gl, tj, whole = pl.pallas_call(
         functools.partial(operators_kernel, cfg),
-        out_shape=[square] * 4 + [shape(2, cfg.lanes, cfg.lanes, dtype=BF16)],
+        out_shape=[square] * 4
+        + [
+            shape(2, cfg.lanes, cfg.lanes, dtype=BF16),
+            shape(cfg.radii, SUB, 3 * cfg.slots, dtype=jnp.int32),
+        ],
         in_specs=[smem] * 3,
-        out_specs=[vmem] * 5,
+        out_specs=[vmem] * 6,
         compiler_params=grant(8),
         name="operators",
     )(me, int_shift, frac_shift)
@@ -403,11 +412,11 @@
     halo = pl.pallas_call(
         functools.partial(edge_kernel, cfg),
         out_shape=owners,
-        in_specs=[smem] * 2 + [vmem] * (n + 3),
+        in_specs=[smem] + [vmem] * (n + 4),
         out_specs=vmem,
         compiler_params=grant(2 * n),
         name="edge",
-    )(me, int_shift, *first, gh, gl, tj)
+    )(me, *first, gh, gl, tj, whole)
     halo = lax.ppermute(
         halo,
         ("tile", "phi"),
@@ -420,11 +429,11 @@
             shape(cfg.radii, 3 * cfg.slots, 3 * cfg.slots, dtype=BF16),
             owners if cfg.split > 1 else shape(1, 1, SUB, LANES),
         ],
-        in_specs=[smem] * 2 + [vmem] * (n + 5),
+        in_specs=[smem] + [vmem] * (n + 6),
         out_specs=[vmem] * 3,
         compiler_params=grant(2 * n),
         name="fields",
-    )(me, int_shift, *first, mh, ml, gh, gl, tj)
+    )(me, *first, mh, ml, gh, gl, tj, whole)
     if cfg.split > 1:
         polar = lax.ppermute(
             polar,
@@ -434,23 +443,32 @@
                 for s in range(count)
             ],
         )
-    done = pl.pallas_call(
-        functools.partial(finish_kernel, cfg),
-        out_shape=[shape(8, tiles, SUB, LANES)] * n,
-        in_specs=[smem] + [vmem] * (n + 6),
-        out_specs=[vmem] * n,
-        compiler_params=grant(2 * n),
-        name="finish",
-    )(me, *far_second, *first[half:], mh, ml, taken, rows, halo, polar)
-    conserved_out, field_out = pl.pallas_call(
-        functools.partial(unpack_kernel, cfg),
-        out_shape=[shape(5, n * tiles, SUB, LANES), shape(3, n * tiles, SUB, LANES)],
-        in_specs=[smem] + [vmem] * n,
-        out_specs=[hbm] * 2,
-        scratch_shapes=[pltpu.SemaphoreType.DMA((n, 2))],
-        compiler_params=grant(2),
-        name="unpack",
-    )(me, *exchange(done, cfg.order))
+    done, token = [], []
+    for name, orders in (("finish_far", cfg.order[:half]), ("finish_near", cfg.order[half:])):
+        *pieces, mark = pl.pallas_call(
+            functools.partial(finish_kernel, cfg, orders),
+            out_shape=[shape(8, tiles, SUB, LANES)] * half + [shape(SUB, LANES)],
+            in_specs=[smem] + [vmem] * (n + 6 + len(token)),
+            out_specs=[vmem] * (half + 1),
+            compiler_params=grant(2 * n),
+            name=name,
+        )(me, *far_second, *first[half:], mh, ml, taken, rows, halo, polar, *token)
+        done, token = done + pieces, [mark]
+    back = exchange(done, cfg.order)
+    outs = ()
+    for name, late in (("unpack_early", False), ("unpack_late", True)):
+        orders = [k for k in cfg.order if (k in cfg.last) == late]
+        outs = pl.pallas_call(
+            functools.partial(unpack_kernel, cfg, orders),
+            out_shape=[shape(5, n * tiles, SUB, LANES), shape(3, n * tiles, SUB, LANES)],
+            in_specs=[smem] + [vmem] * len(orders) + [hbm] * len(outs),
+            out_specs=[hbm] * 2,
+            input_output_aliases={1 + len(orders) + i: i for i in range(len(outs))},
+            scratch_shapes=[pltpu.SemaphoreType.DMA((n, 2))],
+            compiler_params=grant(2),
+            name=name,
+        )(me, *[back[cfg.order.index(k)] for k in orders], *outs)
+    conserved_out, field_out = outs
     return untiled(conserved_out), untiled(field_out)
 
 

time: 58.3 us -> 57.4 us (0.985)
  starting transfers between devices: 26.9 us -> 23.2 us
  waiting for transfers between devices: 22.6 us -> 24.6 us
    ppermute x18, starting transfers between devices: 24.8 us -> 21.1 us  [exchange(): lax.ppermute(piece, 'phi', [(s, s ^ k) for s in range(n)])]
    ppermute x18, waiting for transfers between devices: 22 us -> 24.1 us  [exchange(): lax.ppermute(piece, 'phi', [(s, s ^ k) for s in range(n)])]
    pallas_call x2 -> x4, Pallas kernels: 2.17 us -> 3.69 us  [the longest x2 1.84 us: shards(): pl.pallas_call(functools.partial(finish_kernel, cfg, orders), out_shape=[...]
  transfers between devices with their start and end apart: 19 -> 19, of which waited for: 9 -> 9; matrix products, arithmetic and copies ran while one was open for 0% -> 0% of each run, Pallas kernels for 7% -> 10%
where the time goes in v9:
time: 57.4 us; the launch traced here: 56.9 us
  waiting for transfers between devices  24.6 us (43%)
  starting transfers between devices  23.2 us (40%)
  Pallas kernels  8.33 us (15%)
  between operations  0.74 us (1%)
    ppermute x18, waiting for transfers between devices, exchange(): lax.ppermute(piece, 'phi', [(s, s ^ k) for s in range(n)])  24.1 us
    ppermute x18, starting transfers between devices, exchange(): lax.ppermute(piece, 'phi', [(s, s ^ k) for s in range(n)])  21.1 us
    ppermute x1, starting transfers between devices, shards(): lax.ppermute(halo, ('tile', 'phi'), [(holder(s), holder(s - cfg.split)) f...  2.08 us
    pallas_call x2, Pallas kernels, shards(): pl.pallas_call(functools.partial(finish_kernel, cfg, orders), out_shape=[...  1.84 us
    pallas_call x2, Pallas kernels, shards(): pl.pallas_call(functools.partial(unpack_kernel, cfg, orders), out_shape=[...  1.84 us
    pallas_call x1, Pallas kernels, shards(): pl.pallas_call(functools.partial(fields_kernel, cfg), out_shape=[shape(n,...  1.64 us
    pallas_call x1, Pallas kernels, shards(): pl.pallas_call(functools.partial(pack_kernel, cfg), out_shape=[shape(4 *...  1.38 us
  transfers between devices with their start and end apart: 19, of which 9 were waited for; matrix products, arithmetic and copies ran while one was open for 0% of the time, Pallas kernels for 10%

profile of v9, /device:TPU:13, one launch (start us, length us, event | category | flops | bytes accessed | tf_op | source)
XLA Modules:
  0.0 56.9 jit_solution(3216089883359746543)
XLA Ops:
  0.6 1.4 %pack.1 = (f32[17,8,128]{2,1,0:T(8,128)S(1)}, f32[17,8,128]{2,1,0:T(8,128)S(1)}, f32[17,8,128]{2,1,0:T(8,128)S(1)}, f32[17,8,128]{2,1,0:T(8,128)S(1)}, f32[33,8,...) custom-call(s32[1]{0:T(128)} %bitcast.me_ref, ...), custom_call_target="tpu_custom_call" | custom-call | tf_op jit(solution)/shard_map/pack/pallas_call | solution.py:379
  2.0 2.4 %collective-permute-start.7 = (f32[17,8,128]{2,1,0:T(8,128)S(1)}, f32[17,8,128]{2,1,0:T(8,128)S(1)}, u32[]{:S(2)}, u32[]{:S(2)}) collective-permute-start(f32[17,8,128]{2,1,0:T(8,128)S(1)} %get-tuple-element.46), channel_id=1, source_target_pairs={{0,4},{1,5},{2,6},{3,7},{4,0},{5,1},{6,2},{7,3},{8,12},{9,13},{10,... | collective-permute-start | bytes 208904 | tf_op jit(solution)/shard_map/ppermute | solution.py:372
  4.4 0.9 %collective-permute-start.8 = (f32[17,8,128]{2,1,0:T(8,128)S(1)}, f32[17,8,128]{2,1,0:T(8,128)S(1)}, u32[]{:S(2)}, u32[]{:S(2)}) collective-permute-start(f32[17,8,128]{2,1,0:T(8,128)S(1)} %get-tuple-element.47), channel_id=1, source_target_pairs={{0,5},{1,4},{2,7},{3,6},{4,1},{5,0},{6,3},{7,2},{8,13},{9,12},{10,... | collective-permute-start | bytes 208904 | tf_op jit(solution)/shard_map/ppermute | solution.py:372
  5.4 1.3 %collective-permute-start.5 = (f32[33,8,128]{2,1,0:T(8,128)S(1)}, f32[33,8,128]{2,1,0:T(8,128)S(1)}, u32[]{:S(2)}, u32[]{:S(2)}) collective-permute-start(f32[33,8,128]{2,1,0:T(8,128)S(1)} %get-tuple-element.41), channel_id=1, source_target_pairs={{0,2},{1,3},{2,0},{3,1},{4,6},{5,7},{6,4},{7,5},{8,10},{9,11},{10,... | collective-permute-start | bytes 405512 | tf_op jit(solution)/shard_map/ppermute | solution.py:372
  7.4 1.4 %collective-permute-done.7.refs_0_ = f32[17,8,128]{2,1,0:T(8,128)S(1)} collective-permute-done((f32[17,8,128]{2,1,0:T(8,128)S(1)}, f32[17,8,128]{2,1,0:T(8,128)S(1)}, u32[]{:S(2)}, u32[]{:S(2)}) %collective-permute-start.7) | collective-permute-done | bytes 69664 | tf_op jit(solution)/shard_map/ppermute | solution.py:372
  8.8 1.8 %collective-permute-done.8.refs_1_ = f32[17,8,128]{2,1,0:T(8,128)S(1)} collective-permute-done((f32[17,8,128]{2,1,0:T(8,128)S(1)}, f32[17,8,128]{2,1,0:T(8,128)S(1)}, u32[]{:S(2)}, u32[]{:S(2)}) %collective-permute-start.8) | collective-permute-done | bytes 69664 | tf_op jit(solution)/shard_map/ppermute | solution.py:372
  11.3 1.1 %operators.1 = (bf16[2,3,256,256]{3,2,1,0:T(8,128)(2,1)S(1)}, bf16[2,3,256,256]{3,2,1,0:T(8,128)(2,1)S(1)}, bf16[2,3,256,256]{3,2,1,0:T(8,128)(2,1)S(1)}, bf16[2...) custom-call(s32[1]{0:T(128)} %bitcast.me_ref, s32[16]{0:T(128)S(1)} %copy-done, ...), custom_call_target="tpu_custom_call" | custom-call | tf_op jit(solution)/shard_map/operators/pallas_call | solution.py:398
  12.5 5.2 %collective-permute-start = (f32[16,8,128]{2,1,0:T(8,128)S(1)}, f32[16,8,128]{2,1,0:T(8,128)S(1)}, u32[]{:S(2)}, u32[]{:S(2)}) collective-permute-start(f32[16,8,128]{2,1,0:T(8,128)S(1)} %get-tuple-element.36), channel_id=1, source_target_pairs={{0,4},{1,5},{2,6},{3,7},{4,0},{5,1},{6,2},{7,3},{8,12},{9,13},{10,... | collective-permute-start | bytes 196616 | tf_op jit(solution)/shard_map/ppermute | solution.py:372
  17.7 2.7 %collective-permute-start.1 = (f32[16,8,128]{2,1,0:T(8,128)S(1)}, f32[16,8,128]{2,1,0:T(8,128)S(1)}, u32[]{:S(2)}, u32[]{:S(2)}) collective-permute-start(f32[16,8,128]{2,1,0:T(8,128)S(1)} %get-tuple-element.37), channel_id=1, source_target_pairs={{0,5},{1,4},{2,7},{3,6},{4,1},{5,0},{6,3},{7,2},{8,13},{9,12},{10,... | collective-permute-start | bytes 196616 | tf_op jit(solution)/shard_map/ppermute | solution.py:372
  20.4 1.2 %collective-permute-start.2 = (f32[16,8,128]{2,1,0:T(8,128)S(1)}, f32[16,8,128]{2,1,0:T(8,128)S(1)}, u32[]{:S(2)}, u32[]{:S(2)}) collective-permute-start(f32[16,8,128]{2,1,0:T(8,128)S(1)} %get-tuple-element.38), channel_id=1, source_target_pairs={{0,6},{1,7},{2,4},{3,5},{4,2},{5,3},{6,0},{7,1},{8,14},{9,15},{10,... | collective-permute-start | bytes 196616 | tf_op jit(solution)/shard_map/ppermute | solution.py:372
  22.6 2.1 %collective-permute-start.11 = (f32[8,2,8,128]{3,2,1,0:T(8,128)S(1)}, f32[8,2,8,128]{3,2,1,0:T(8,128)S(1)}, u32[]{:S(2)}, u32[]{:S(2)}) collective-permute-start(f32[8,2,8,128]{3,2,1,0:T(8,128)S(1)} %edge.1), channel_id=1, source_target_pairs={{1,0},{2,1},{3,2},{4,3},{5,4},{6,5},{7,6},{15,7},{14,15},{13,14},{... | collective-permute-start | bytes 196616 | tf_op jit(solution)/shard_map/ppermute | solution.py:420
  24.7 1.6 %fields.1 = (f32[8,4,4,8,128]{4,3,2,1,0:T(8,128)S(1)}, bf16[2,192,192]{2,1,0:T(8,128)(2,1)S(1)}, f32[1,1,8,128]{3,2,1,0:T(8,128)S(1)}) custom-call(s32[1]{0:T(128)} %bitcast.me_ref, f32[17,8,128]{2,1,0:T(8,128)S(1)} %collective-permute-done.7.refs_0_, f32[17,8,128]{2,1,0:T(8,128)S(1)} %collective-permute-done.8.refs_1_, ...), custom_call_target="tpu_custom_call" | custom-call | tf_op jit(solution)/shard_map/fields/pallas_call | solution.py:425
  26.3 3.4 %collective-permute-done.2.refs_2_ = f32[16,8,128]{2,1,0:T(8,128)S(1)} collective-permute-done((f32[16,8,128]{2,1,0:T(8,128)S(1)}, f32[16,8,128]{2,1,0:T(8,128)S(1)}, u32[]{:S(2)}, u32[]{:S(2)}) %collective-permute-start.2) | collective-permute-done | bytes 65568 | tf_op jit(solution)/shard_map/ppermute | solution.py:372
  29.7 1.4 %collective-permute-done.3.refs_3_ = f32[16,8,128]{2,1,0:T(8,128)S(1)} collective-permute-done((f32[16,8,128]{2,1,0:T(8,128)S(1)}, f32[16,8,128]{2,1,0:T(8,128)S(1)}, u32[]{:S(2)}, u32[]{:S(2)}) %collective-permute-start.3) | collective-permute-done | bytes 65568 | tf_op jit(solution)/shard_map/ppermute | solution.py:372
  32.5 2.4 %collective-permute-start.15 = (f32[8,4,8,128]{3,2,1,0:T(8,128)S(1)}, f32[8,4,8,128]{3,2,1,0:T(8,128)S(1)}, u32[]{:S(2)}, u32[]{:S(2)}) collective-permute-start(f32[8,4,8,128]{3,2,1,0:T(8,128)S(1)} %get-tuple-element.60), channel_id=1, source_target_pairs={{0,5},{1,4},{2,7},{3,6},{4,1},{5,0},{6,3},{7,2},{8,13},{9,12},{10,... | collective-permute-start | bytes 393224 | tf_op jit(solution)/shard_map/ppermute | solution.py:372
  34.9 1.1 %finish_near.1 = (f32[8,4,8,128]{3,2,1,0:T(8,128)S(1)}, f32[8,4,8,128]{3,2,1,0:T(8,128)S(1)}, f32[8,4,8,128]{3,2,1,0:T(8,128)S(1)}, f32[8,4,8,128]{3,2,1,0:T(8,128)S(1)}, f32[8,128]{1,0:T(8,128)}) custom-call(s32[1]{0:T(128)} %bitcast.me_ref, f32[16,8,128]{2,1,0:T(8,128)S(1)} %collective-permute-done.refs_0_, ...), custom_call_target="tpu_custom_call" | custom-call | tf_op jit(solution)/shard_map/finish_near/pallas_call | solution.py:448
  36.0 1.7 %collective-permute-start.17 = (f32[8,4,8,128]{3,2,1,0:T(8,128)S(1)}, f32[8,4,8,128]{3,2,1,0:T(8,128)S(1)}, u32[]{:S(2)}, u32[]{:S(2)}) collective-permute-start(f32[8,4,8,128]{3,2,1,0:T(8,128)S(1)} %get-tuple-element.63), channel_id=1, source_target_pairs={{0,2},{1,3},{2,0},{3,1},{4,6},{5,7},{6,4},{7,5},{8,10},{9,11},{10,... | collective-permute-start | bytes 393224 | tf_op jit(solution)/shard_map/ppermute | solution.py:372
  38.2 3.3 %collective-permute-done.14.refs_0_ = f32[8,4,8,128]{3,2,1,0:T(8,128)S(1)} collective-permute-done((f32[8,4,8,128]{3,2,1,0:T(8,128)S(1)}, f32[8,4,8,128]{3,2,1,0:T(8,128)S(1)}, u32[]{:S(2)}, u32[]{:S(2)}) %collective-permute-start.14) | collective-permute-done | bytes 131104 | tf_op jit(solution)/shard_map/ppermute | solution.py:372
  41.4 2.8 %collective-permute-done.15.refs_1_ = f32[8,4,8,128]{3,2,1,0:T(8,128)S(1)} collective-permute-done((f32[8,4,8,128]{3,2,1,0:T(8,128)S(1)}, f32[8,4,8,128]{3,2,1,0:T(8,128)S(1)}, u32[]{:S(2)}, u32[]{:S(2)}) %collective-permute-start.15) | collective-permute-done | bytes 131104 | tf_op jit(solution)/shard_map/ppermute | solution.py:372
  44.2 0.8 %collective-permute-start.13 = (f32[8,4,8,128]{3,2,1,0:T(8,128)S(1)}, f32[8,4,8,128]{3,2,1,0:T(8,128)S(1)}, u32[]{:S(2)}, u32[]{:S(2)}) collective-permute-start(f32[8,4,8,128]{3,2,1,0:T(8,128)S(1)} %get-tuple-element.58), channel_id=1, source_target_pairs={{0,7},{1,6},{2,5},{3,4},{4,3},{5,2},{6,1},{7,0},{8,15},{9,14},{10,... | collective-permute-start | bytes 393224 | tf_op jit(solution)/shard_map/ppermute | solution.py:372
  45.1 1.0 %unpack_early.1 = (f32[5,32,8,128]{3,2,1,0:T(8,128)}, f32[3,32,8,128]{3,2,1,0:T(8,128)}) custom-call(s32[1]{0:T(128)} %bitcast.me_ref, f32[8,4,8,128]{3,2,1,0:T(8,128)S(1)} %collective-permute-done.14.refs_0_, f32[8,4,8,128]{3,2,1,0:T(8,128)S(1)} %collective-permute-done.15.refs_1_, f32[8,4,8,128]{3,2,1,0:T(8,128)S(1)} %collective-permute-done.16.refs_2_, ...), custom_call_target="tpu_custom_call" | custom-call | tf_op jit(solution)/shard_map/unpack_early/pallas_call | solution.py:461
  46.1 7.1 %collective-permute-done.12.refs_0_ = f32[8,4,8,128]{3,2,1,0:T(8,128)S(1)} collective-permute-done((f32[8,4,8,128]{3,2,1,0:T(8,128)S(1)}, f32[8,4,8,128]{3,2,1,0:T(8,128)S(1)}, u32[]{:S(2)}, u32[]{:S(2)}) %collective-permute-start.12) | collective-permute-done | bytes 131104 | tf_op jit(solution)/shard_map/ppermute | solution.py:372
  53.2 2.9 %collective-permute-done.13.refs_1_ = f32[8,4,8,128]{3,2,1,0:T(8,128)S(1)} collective-permute-done((f32[8,4,8,128]{3,2,1,0:T(8,128)S(1)}, f32[8,4,8,128]{3,2,1,0:T(8,128)S(1)}, u32[]{:S(2)}, u32[]{:S(2)}) %collective-permute-start.13) | collective-permute-done | bytes 131104 | tf_op jit(solution)/shard_map/ppermute | solution.py:372
  56.1 0.8 %unpack_late.1 = (f32[5,32,8,128]{3,2,1,0:T(8,128)}, f32[3,32,8,128]{3,2,1,0:T(8,128)}) custom-call(s32[1]{0:T(128)} %bitcast.me_ref, f32[8,4,8,128]{3,2,1,0:T(8,128)S(1)} %collective-permute-done.12.refs_0_, f32[8,4,8,128]{3,2,1,0:T(8,128)S(1)} %collective-permute-done.13.refs_1_, ...), custom_call_target="tpu_custom_call", output_to_operand_aliasing={{0}: (3, {}), {1}: (4, {})} | custom-call | tf_op jit(solution)/shard_map/unpack_late/pallas_call | solution.py:461
  (26 shorter events, 4.4 us)
Async XLA Ops:
  2.0 6.8 %collective-permute-start.7 = (f32[17,8,128]{2,1,0:T(8,128)S(1)}, f32[17,8,128]{2,1,0:T(8,128)S(1)}, u32[]{:S(2)}, u32[]{:S(2)}) collective-permute-start(f32[17,8,128]{2,1,0:T(8,128)S(1)} %get-tuple-element.46), channel_id=1, source_target_pairs={{0,4},{1,5},{2,6},{3,7},{4,0},{5,1},{6,2},{7,3},{8,12},{9,13},{10,... | collective-permute-start | bytes 208904 | tf_op jit(solution)/shard_map/ppermute | solution.py:372
  4.4 6.3 %collective-permute-start.8 = (f32[17,8,128]{2,1,0:T(8,128)S(1)}, f32[17,8,128]{2,1,0:T(8,128)S(1)}, u32[]{:S(2)}, u32[]{:S(2)}) collective-permute-start(f32[17,8,128]{2,1,0:T(8,128)S(1)} %get-tuple-element.47), channel_id=1, source_target_pairs={{0,5},{1,4},{2,7},{3,6},{4,1},{5,0},{6,3},{7,2},{8,13},{9,12},{10,... | collective-permute-start | bytes 208904 | tf_op jit(solution)/shard_map/ppermute | solution.py:372
  5.3 15.1 %collective-permute-start.4 = (f32[33,8,128]{2,1,0:T(8,128)S(1)}, f32[33,8,128]{2,1,0:T(8,128)S(1)}, u32[]{:S(2)}, u32[]{:S(2)}) collective-permute-start(f32[33,8,128]{2,1,0:T(8,128)S(1)} %get-tuple-element.40), channel_id=1, source_target_pairs={{0,3},{1,2},{2,1},{3,0},{4,7},{5,6},{6,5},{7,4},{8,11},{9,10},{10,... | collective-permute-start | bytes 405512 | tf_op jit(solution)/shard_map/ppermute | solution.py:372
  5.4 16.1 %collective-permute-start.5 = (f32[33,8,128]{2,1,0:T(8,128)S(1)}, f32[33,8,128]{2,1,0:T(8,128)S(1)}, u32[]{:S(2)}, u32[]{:S(2)}) collective-permute-start(f32[33,8,128]{2,1,0:T(8,128)S(1)} %get-tuple-element.41), channel_id=1, source_target_pairs={{0,2},{1,3},{2,0},{3,1},{4,6},{5,7},{6,4},{7,5},{8,10},{9,11},{10,... | collective-permute-start | bytes 405512 | tf_op jit(solution)/shard_map/ppermute | solution.py:372
  6.7 15.4 %collective-permute-start.6 = (f32[33,8,128]{2,1,0:T(8,128)S(1)}, f32[33,8,128]{2,1,0:T(8,128)S(1)}, u32[]{:S(2)}, u32[]{:S(2)}) collective-permute-start(f32[33,8,128]{2,1,0:T(8,128)S(1)} %get-tuple-element.42), channel_id=1, source_target_pairs={{0,1},{1,0},{2,3},{3,2},{4,5},{5,4},{6,7},{7,6},{8,9},{9,8},{10,11... | collective-permute-start | bytes 405512 | tf_op jit(solution)/shard_map/ppermute | solution.py:372
  8.8 2.5 %copy-start = (s32[16]{0:T(128)S(1)}, s32[16]{0:T(128)}, u32[]{:S(2)}) copy-start(s32[16]{0:T(128)} %shift_ref.1) | copy-start | bytes 196
  8.8 2.5 %copy-start.1 = (f32[16]{0:T(128)S(1)}, f32[16]{0:T(128)}, u32[]{:S(2)}) copy-start(f32[16]{0:T(128)} %frac_ref.1) | copy-start | bytes 196
  8.8 3.7 %collective-permute-start.9 = (f32[17,8,128]{2,1,0:T(8,128)S(1)}, f32[17,8,128]{2,1,0:T(8,128)S(1)}, u32[]{:S(2)}, u32[]{:S(2)}) collective-permute-start(f32[17,8,128]{2,1,0:T(8,128)S(1)} %get-tuple-element.48), channel_id=1, source_target_pairs={{0,6},{1,7},{2,4},{3,5},{4,2},{5,3},{6,0},{7,1},{8,14},{9,15},{10,... | collective-permute-start | bytes 208904 | tf_op jit(solution)/shard_map/ppermute | solution.py:372
  10.7 7.0 %collective-permute-start.10 = (f32[17,8,128]{2,1,0:T(8,128)S(1)}, f32[17,8,128]{2,1,0:T(8,128)S(1)}, u32[]{:S(2)}, u32[]{:S(2)}) collective-permute-start(f32[17,8,128]{2,1,0:T(8,128)S(1)} %get-tuple-element.49), channel_id=1, source_target_pairs={{0,7},{1,6},{2,5},{3,4},{4,3},{5,2},{6,1},{7,0},{8,15},{9,14},{10,... | collective-permute-start | bytes 208904 | tf_op jit(solution)/shard_map/ppermute | solution.py:372
  12.5 13.8 %collective-permute-start = (f32[16,8,128]{2,1,0:T(8,128)S(1)}, f32[16,8,128]{2,1,0:T(8,128)S(1)}, u32[]{:S(2)}, u32[]{:S(2)}) collective-permute-start(f32[16,8,128]{2,1,0:T(8,128)S(1)} %get-tuple-element.36), channel_id=1, source_target_pairs={{0,4},{1,5},{2,6},{3,7},{4,0},{5,1},{6,2},{7,3},{8,12},{9,13},{10,... | collective-permute-start | bytes 196616 | tf_op jit(solution)/shard_map/ppermute | solution.py:372
  17.7 8.7 %collective-permute-start.1 = (f32[16,8,128]{2,1,0:T(8,128)S(1)}, f32[16,8,128]{2,1,0:T(8,128)S(1)}, u32[]{:S(2)}, u32[]{:S(2)}) collective-permute-start(f32[16,8,128]{2,1,0:T(8,128)S(1)} %get-tuple-element.37), channel_id=1, source_target_pairs={{0,5},{1,4},{2,7},{3,6},{4,1},{5,0},{6,3},{7,2},{8,13},{9,12},{10,... | collective-permute-start | bytes 196616 | tf_op jit(solution)/shard_map/ppermute | solution.py:372
  20.4 9.4 %collective-permute-start.2 = (f32[16,8,128]{2,1,0:T(8,128)S(1)}, f32[16,8,128]{2,1,0:T(8,128)S(1)}, u32[]{:S(2)}, u32[]{:S(2)}) collective-permute-start(f32[16,8,128]{2,1,0:T(8,128)S(1)} %get-tuple-element.38), channel_id=1, source_target_pairs={{0,6},{1,7},{2,4},{3,5},{4,2},{5,3},{6,0},{7,1},{8,14},{9,15},{10,... | collective-permute-start | bytes 196616 | tf_op jit(solution)/shard_map/ppermute | solution.py:372
  21.5 9.6 %collective-permute-start.3 = (f32[16,8,128]{2,1,0:T(8,128)S(1)}, f32[16,8,128]{2,1,0:T(8,128)S(1)}, u32[]{:S(2)}, u32[]{:S(2)}) collective-permute-start(f32[16,8,128]{2,1,0:T(8,128)S(1)} %get-tuple-element.39), channel_id=1, source_target_pairs={{0,7},{1,6},{2,5},{3,4},{4,3},{5,2},{6,1},{7,0},{8,15},{9,14},{10,... | collective-permute-start | bytes 196616 | tf_op jit(solution)/shard_map/ppermute | solution.py:372
  22.6 9.1 %collective-permute-start.11 = (f32[8,2,8,128]{3,2,1,0:T(8,128)S(1)}, f32[8,2,8,128]{3,2,1,0:T(8,128)S(1)}, u32[]{:S(2)}, u32[]{:S(2)}) collective-permute-start(f32[8,2,8,128]{3,2,1,0:T(8,128)S(1)} %edge.1), channel_id=1, source_target_pairs={{1,0},{2,1},{3,2},{4,3},{5,4},{6,5},{7,6},{15,7},{14,15},{13,14},{... | collective-permute-start | bytes 196616 | tf_op jit(solution)/shard_map/ppermute | solution.py:420
  32.4 9.0 %collective-permute-start.14 = (f32[8,4,8,128]{3,2,1,0:T(8,128)S(1)}, f32[8,4,8,128]{3,2,1,0:T(8,128)S(1)}, u32[]{:S(2)}, u32[]{:S(2)}) collective-permute-start(f32[8,4,8,128]{3,2,1,0:T(8,128)S(1)} %get-tuple-element.59), channel_id=1, source_target_pairs={{0,4},{1,5},{2,6},{3,7},{4,0},{5,1},{6,2},{7,3},{8,12},{9,13},{10,... | collective-permute-start | bytes 393224 | tf_op jit(solution)/shard_map/ppermute | solution.py:372
  32.5 11.8 %collective-permute-start.15 = (f32[8,4,8,128]{3,2,1,0:T(8,128)S(1)}, f32[8,4,8,128]{3,2,1,0:T(8,128)S(1)}, u32[]{:S(2)}, u32[]{:S(2)}) collective-permute-start(f32[8,4,8,128]{3,2,1,0:T(8,128)S(1)} %get-tuple-element.60), channel_id=1, source_target_pairs={{0,5},{1,4},{2,7},{3,6},{4,1},{5,0},{6,3},{7,2},{8,13},{9,12},{10,... | collective-permute-start | bytes 393224 | tf_op jit(solution)/shard_map/ppermute | solution.py:372
  36.0 9.1 %collective-permute-start.16 = (f32[8,4,8,128]{3,2,1,0:T(8,128)S(1)}, f32[8,4,8,128]{3,2,1,0:T(8,128)S(1)}, u32[]{:S(2)}, u32[]{:S(2)}) collective-permute-start(f32[8,4,8,128]{3,2,1,0:T(8,128)S(1)} %get-tuple-element.62), channel_id=1, source_target_pairs={{0,3},{1,2},{2,1},{3,0},{4,7},{5,6},{6,5},{7,4},{8,11},{9,10},{10,... | collective-permute-start | bytes 393224 | tf_op jit(solution)/shard_map/ppermute | solution.py:372
  36.0 9.1 %collective-permute-start.17 = (f32[8,4,8,128]{3,2,1,0:T(8,128)S(1)}, f32[8,4,8,128]{3,2,1,0:T(8,128)S(1)}, u32[]{:S(2)}, u32[]{:S(2)}) collective-permute-start(f32[8,4,8,128]{3,2,1,0:T(8,128)S(1)} %get-tuple-element.63), channel_id=1, source_target_pairs={{0,2},{1,3},{2,0},{3,1},{4,6},{5,7},{6,4},{7,5},{8,10},{9,11},{10,... | collective-permute-start | bytes 393224 | tf_op jit(solution)/shard_map/ppermute | solution.py:372
  37.7 7.4 %collective-permute-start.18 = (f32[8,4,8,128]{3,2,1,0:T(8,128)S(1)}, f32[8,4,8,128]{3,2,1,0:T(8,128)S(1)}, u32[]{:S(2)}, u32[]{:S(2)}) collective-permute-start(f32[8,4,8,128]{3,2,1,0:T(8,128)S(1)} %get-tuple-element.64), channel_id=1, source_target_pairs={{0,1},{1,0},{2,3},{3,2},{4,5},{5,4},{6,7},{7,6},{8,9},{9,8},{10,11... | collective-permute-start | bytes 393224 | tf_op jit(solution)/shard_map/ppermute | solution.py:372
  41.4 11.7 %collective-permute-start.12 = (f32[8,4,8,128]{3,2,1,0:T(8,128)S(1)}, f32[8,4,8,128]{3,2,1,0:T(8,128)S(1)}, u32[]{:S(2)}, u32[]{:S(2)}) collective-permute-start(f32[8,4,8,128]{3,2,1,0:T(8,128)S(1)} %get-tuple-element.57), channel_id=1, source_target_pairs={{0,6},{1,7},{2,4},{3,5},{4,2},{5,3},{6,0},{7,1},{8,14},{9,15},{10,... | collective-permute-start | bytes 393224 | tf_op jit(solution)/shard_map/ppermute | solution.py:372
  44.2 11.8 %collective-permute-start.13 = (f32[8,4,8,128]{3,2,1,0:T(8,128)S(1)}, f32[8,4,8,128]{3,2,1,0:T(8,128)S(1)}, u32[]{:S(2)}, u32[]{:S(2)}) collective-permute-start(f32[8,4,8,128]{3,2,1,0:T(8,128)S(1)} %get-tuple-element.58), channel_id=1, source_target_pairs={{0,7},{1,6},{2,5},{3,4},{4,3},{5,2},{6,1},{7,0},{8,15},{9,14},{10,... | collective-permute-start | bytes 393224 | tf_op jit(solution)/shard_map/ppermute | solution.py:372

commit v10 on v9

--- a/solution.py
+++ b/solution.py
@@ -54,13 +54,14 @@
         copy.wait()
 
 
-def pack_kernel(cfg, me_ref, ids_ref, face_ref, conserved_ref, *refs):
+def pack_kernel(cfg, late, me_ref, ids_ref, face_ref, conserved_ref, *refs):
     me, group = place(cfg, me_ref)
     n, tiles = cfg.n, cfg.tiles
     half = n // 2
-    outs, (all_ref, id_ref, sem) = refs[: n + half], refs[n + half :]
+    all_ref, id_ref, sem = refs[-3:]
+    outs = refs[1:-3] if late else refs[:half]
     copies = [pltpu.make_async_copy(ids_ref, id_ref, sem.at[8])]
-    for c in range(8):
+    for c in range(8 if late else 4):
         from_ref = face_ref.at[c] if c < 3 else conserved_ref.at[c - 3]
         copies.append(pltpu.make_async_copy(from_ref, all_ref.at[c], sem.at[c]))
     start_all(copies)
@@ -70,15 +71,19 @@
     ids = jnp.zeros((SUB, LANES), jnp.int32)
     for slot in range(SUB):
         ids = jnp.where(rows == slot, id_ref[slot], ids)
-    for out in outs[:n]:
+    for out in outs[:half]:
         out[4 * tiles] = ids.astype(F32)
-    for c in range(8):
-        copies[1 + c].wait()
-        for j, dest in enumerate(dests):
-            out, at = outs[j], c * tiles + (c >= 4)
-            if c >= 4 and j < half:
-                out, at = outs[n + j], (c - 4) * tiles
-            out[at : at + tiles] = all_ref[c, pl.ds(dest, tiles)]
+    if not late:
+        refs[half][...] = jnp.zeros((SUB, LANES), F32)
+    for c, copy in enumerate(copies[1:]):
+        copy.wait()
+        for j in range(half):
+            at = c * tiles + (c >= 4)
+            dest = dests[half + j] if late else dests[j]
+            outs[j][at : at + tiles] = all_ref[c, pl.ds(dest, tiles)]
+            if late and c >= 4:
+                at = (c - 4) * tiles
+                outs[half + j][at : at + tiles] = all_ref[c, pl.ds(dests[j], tiles)]
 
 
 def unpack_kernel(cfg, orders, me_ref, *refs):
@@ -98,7 +103,7 @@
 
 def operators_kernel(cfg, me_ref, shift_ref, frac_ref, *refs):
     me, group = place(cfg, me_ref)
-    mh_ref, ml_ref, gh_ref, gl_ref, tj_ref, whole_ref = refs
+    mh_ref, ml_ref, gh_ref, gl_ref, tj_ref, whole_ref, side_ref = refs
     size = cfg.lanes
     first = (group * cfg.rows) // BS
     row = lax.broadcasted_iota(jnp.int32, (size, size), 0)
@@ -110,6 +115,11 @@
 
     def spread(pattern):
         return jnp.where(same, jnp.concatenate([pattern] * (size // BS), axis=0), 0.0)
+
+    def store(value, high_ref, low_ref, al, j):
+        high = value.astype(BF16).astype(F32)
+        high_ref[al, j] = spread(high).astype(BF16)
+        low_ref[al, j] = spread(value - high).astype(BF16)
 
     tj_ref[0] = spread(jnp.where(e_in < e_out, 1.0, zero)).astype(BF16)
     tj_ref[1] = spread(zero + 1.0).astype(BF16)
@@ -134,6 +144,9 @@
                 for a in range(-3, m + 1):
                     total = total + lagrange[a + 3]
             weights.append(total)
+        before = lax.broadcasted_iota(jnp.int32, (SUB, size), 1) % BS >= BS // 2 - rest
+        side_ref[al] = before.astype(jnp.int32)
+        beside = zero
         for d in range(3):
             at = e_in + BS * (d - 1)
             tap = at - e_out + rest
@@ -144,10 +157,12 @@
                 if a < 3:
                     flux = jnp.where(hit, weights[a + 3], flux)
             flux = flux - jnp.where(at < e_out - rest, 1.0, zero)
-            for value, high_ref, low_ref in ((remap, mh_ref, ml_ref), (flux, gh_ref, gl_ref)):
-                high = value.astype(BF16).astype(F32)
-                high_ref[al, d] = spread(high).astype(BF16)
-                low_ref[al, d] = spread(value - high).astype(BF16)
+            store(flux, gh_ref, gl_ref, al, d)
+            if d == 1:
+                store(remap, mh_ref, ml_ref, al, 0)
+            else:
+                beside = beside + remap
+        store(beside, mh_ref, ml_ref, al, 1)
 
 
 def gather_matrix(cfg, me, ids, whole):
@@ -233,20 +248,23 @@
     by_owner(cfg, me, halo_ref, whole_fluxes(cfg, [y], 0, gh_ref, gl_ref, tj_ref))
 
 
-def remapped(count, ys, al, mh_ref, ml_ref):
-    total = 0.0
-    for d in range(3):
-        at = slice(d * count, (d + 1) * count)
-        high, low = halves(jnp.concatenate([y[at] for y in ys], axis=0))
-        total = total + three_dots(high, low, mh_ref[al, d], ml_ref[al, d])
-    return total
+def remapped(count, ys, al, mh_ref, ml_ref, side_ref):
+    before = side_ref[al, 0:1] > 0
+
+    def rows(d):
+        return jnp.concatenate([y[d * count : (d + 1) * count] for y in ys], axis=0)
+
+    own = three_dots(*halves(rows(1)), mh_ref[al, 0], ml_ref[al, 0])
+    beside = halves(jnp.where(before, rows(0), rows(2)))
+    return own + three_dots(*beside, mh_ref[al, 1], ml_ref[al, 1])
 
 
 def fields_kernel(cfg, me_ref, *refs):
     me, group = place(cfg, me_ref)
     n, slots, wide, per = cfg.n, cfg.slots, cfg.lanes, cfg.per
     pieces = refs[:n]
-    mh_ref, ml_ref, gh_ref, gl_ref, tj_ref, whole_ref, out_ref, taken_ref, polar_ref = refs[n:]
+    mh_ref, ml_ref, gh_ref, gl_ref, tj_ref, whole_ref = refs[n : n + 6]
+    side_ref, out_ref, taken_ref, polar_ref = refs[n + 6 :]
     ids = numbers(cfg, pieces)
 
     def put(c, al, value):
@@ -278,7 +296,7 @@
         )
         total.append((azimuthal + (after - polar) - radial, radial))
         ys.append(dot(taken[: 3 * slots], source(cfg, first_half(cfg, pieces, 3), al)))
-        remap = remapped(slots, ys, al, mh_ref, ml_ref)
+        remap = remapped(slots, ys, al, mh_ref, ml_ref, side_ref)
         for c, at in enumerate((1, 2, 0)):
             put(at, al, remap[c * slots : (c + 1) * slots])
     for al in range(cfg.radii):
@@ -290,7 +308,7 @@
     me, group = place(cfg, me_ref)
     n, slots, per = cfg.n, cfg.slots, cfg.per
     pieces = refs[:n]
-    mh_ref, ml_ref, taken_ref, rows_ref, halo_ref, polar_ref = refs[n : n + 6]
+    mh_ref, ml_ref, side_ref, taken_ref, rows_ref, halo_ref, polar_ref = refs[n : n + 7]
     outs, mark_ref = refs[-len(orders) - 1 : -1], refs[-1]
     mark_ref[...] = jnp.zeros_like(mark_ref)
     rest = cfg.tiles - per
@@ -300,7 +318,7 @@
             [taken_ref[al, d * slots + low : d * slots + low + count] for d in range(3)], axis=0
         )
         ys = [dot(taken, source(cfg, second_half(cfg, pieces, c), al)) for c in range(4)]
-        remap = remapped(count, ys, al, mh_ref, ml_ref)
+        remap = remapped(count, ys, al, mh_ref, ml_ref, side_ref)
         for out, k in zip(outs, orders):
             for c in range(4):
                 for t in range(per):
@@ -376,34 +394,46 @@
     def in_hbm(x):
         return pltpu.with_memory_space_constraint(x, pltpu.MemorySpace.HBM)
 
-    packed = pl.pallas_call(
-        functools.partial(pack_kernel, cfg),
-        out_shape=[shape(4 * tiles + 1, SUB, LANES)] * half
-        + [shape(8 * tiles + 1, SUB, LANES)] * half
-        + [shape(4 * tiles, SUB, LANES)] * half,
-        in_specs=[smem] + [hbm] * 3,
-        out_specs=[vmem] * (n + half),
-        scratch_shapes=[
-            pltpu.VMEM((8, n * tiles, SUB, LANES), F32),
-            pltpu.SMEM((SUB,), jnp.int32),
-            pltpu.SemaphoreType.DMA((9,)),
-        ],
-        compiler_params=grant(3),
-        name="pack",
-    )(me, in_hbm(block_ids), in_hbm(tiled(face_field)), in_hbm(tiled(conserved)))
+    sources = (in_hbm(block_ids), in_hbm(tiled(face_field)), in_hbm(tiled(conserved)))
+    packed, token = [], []
+    for late, shapes in (
+        (False, [shape(4 * tiles + 1, SUB, LANES)] * half + [shape(SUB, LANES)]),
+        (
+            True,
+            [shape(8 * tiles + 1, SUB, LANES)] * half + [shape(4 * tiles, SUB, LANES)] * half,
+        ),
+    ):
+        pieces = pl.pallas_call(
+            functools.partial(pack_kernel, cfg, late),
+            out_shape=shapes,
+            in_specs=[smem] + [hbm] * 3 + [vmem] * len(token),
+            out_specs=[vmem] * len(shapes),
+            scratch_shapes=[
+                pltpu.VMEM((8, n * tiles, SUB, LANES), F32),
+                pltpu.SMEM((SUB,), jnp.int32),
+                pltpu.SemaphoreType.DMA((9,)),
+            ],
+            compiler_params=grant(3),
+            name="pack_late" if late else "pack_early",
+        )(me, *sources, *token)
+        packed, token = packed + list(pieces[: None if late else half]), list(pieces[half:])[:1]
     first = exchange(packed[:n], cfg.order)
     far_second = exchange(packed[n:], cfg.order)
 
-    square = shape(cfg.radii, 3, cfg.lanes, cfg.lanes, dtype=BF16)
-    mh, ml, gh, gl, tj, whole = pl.pallas_call(
+    def square(count):
+        return shape(cfg.radii, count, cfg.lanes, cfg.lanes, dtype=BF16)
+
+    mh, ml, gh, gl, tj, whole, side = pl.pallas_call(
         functools.partial(operators_kernel, cfg),
-        out_shape=[square] * 4
+        out_shape=[square(2)] * 2
+        + [square(3)] * 2
         + [
             shape(2, cfg.lanes, cfg.lanes, dtype=BF16),
             shape(cfg.radii, SUB, 3 * cfg.slots, dtype=jnp.int32),
+            shape(cfg.radii, SUB, cfg.lanes, dtype=jnp.int32),
         ],
         in_specs=[smem] * 3,
-        out_specs=[vmem] * 6,
+        out_specs=[vmem] * 7,
         compiler_params=grant(8),
         name="operators",
     )(me, int_shift, frac_shift)
@@ -429,11 +459,11 @@
             shape(cfg.radii, 3 * cfg.slots, 3 * cfg.slots, dtype=BF16),
             owners if cfg.split > 1 else shape(1, 1, SUB, LANES),
         ],
-        in_specs=[smem] + [vmem] * (n + 6),
+        in_specs=[smem] + [vmem] * (n + 7),
         out_specs=[vmem] * 3,
         compiler_params=grant(2 * n),
         name="fields",
-    )(me, *first, mh, ml, gh, gl, tj, whole)
+    )(me, *first, mh, ml, gh, gl, tj, whole, side)
     if cfg.split > 1:
         polar = lax.ppermute(
             polar,
@@ -448,11 +478,11 @@
         *pieces, mark = pl.pallas_call(
             functools.partial(finish_kernel, cfg, orders),
             out_shape=[shape(8, tiles, SUB, LANES)] * half + [shape(SUB, LANES)],
-            in_specs=[smem] + [vmem] * (n + 6 + len(token)),
+            in_specs=[smem] + [vmem] * (n + 7 + len(token)),
             out_specs=[vmem] * (half + 1),
             compiler_params=grant(2 * n),
             name=name,
-        )(me, *far_second, *first[half:], mh, ml, taken, rows, halo, polar, *token)
+        )(me, *far_second, *first[half:], mh, ml, side, taken, rows, halo, polar, *token)
         done, token = done + pieces, [mark]
     back = exchange(done, cfg.order)
     outs = ()

time: 57.4 us -> 57.2 us (level)
  waiting for transfers between devices: 24.6 us -> 22 us
  starting transfers between devices: 23.2 us -> 25 us
  Pallas kernels: 8.33 us -> 9.16 us
    ppermute x18, waiting for transfers between devices: 24.1 us -> 21.2 us  [exchange(): lax.ppermute(piece, 'phi', [(s, s ^ k) for s in range(n)])]
    ppermute x18, starting transfers between devices: 21.1 us -> 22.9 us  [exchange(): lax.ppermute(piece, 'phi', [(s, s ^ k) for s in range(n)])]
    pallas_call x1 -> x2, Pallas kernels: 1.38 us -> 2.55 us  [shards(): pl.pallas_call(functools.partial(pack_kernel, cfg, late), out_shape=shape...]
  transfers between devices with their start and end apart: 19 -> 19, of which waited for: 9 -> 9; matrix products, arithmetic and copies ran while one was open for 0% -> 0% of each run, Pallas kernels for 10% -> 11%
where the time goes in v10:
time: 57.2 us; the launch traced here: 56.8 us
  starting transfers between devices  25 us (44%)
  waiting for transfers between devices  22 us (38%)
  Pallas kernels  9.16 us (16%)
  between operations  0.75 us (1%)
    ppermute x18, starting transfers between devices, exchange(): lax.ppermute(piece, 'phi', [(s, s ^ k) for s in range(n)])  22.9 us
    ppermute x18, waiting for transfers between devices, exchange(): lax.ppermute(piece, 'phi', [(s, s ^ k) for s in range(n)])  21.2 us
    pallas_call x2, Pallas kernels, shards(): pl.pallas_call(functools.partial(pack_kernel, cfg, late), out_shape=shape...  2.55 us
    ppermute x1, starting transfers between devices, shards(): lax.ppermute(halo, ('tile', 'phi'), [(holder(s), holder(s - cfg.split)) f...  2.09 us
    pallas_call x2, Pallas kernels, shards(): pl.pallas_call(functools.partial(unpack_kernel, cfg, orders), out_shape=[...  1.85 us
    pallas_call x2, Pallas kernels, shards(): pl.pallas_call(functools.partial(finish_kernel, cfg, orders), out_shape=[...  1.66 us
    pallas_call x1, Pallas kernels, shards(): pl.pallas_call(functools.partial(fields_kernel, cfg), out_shape=[shape(n,...  1.54 us
  transfers between devices with their start and end apart: 19, of which 9 were waited for; matrix products, arithmetic and copies ran while one was open for 0% of the time, Pallas kernels for 11%

profile of v10, /device:TPU:13, one launch (start us, length us, event | category | flops | bytes accessed | tf_op | source)
XLA Modules:
  0.0 56.8 jit_solution(11400622108660231531)
XLA Ops:
  0.6 1.2 %pack_early.1 = (f32[17,8,128]{2,1,0:T(8,128)S(1)}, f32[17,8,128]{2,1,0:T(8,128)S(1)}, f32[17,8,128]{2,1,0:T(8,128)S(1)}, f32[17,8,128]{2,1,0:T(8,128)S(1)}, f32[8,128]{1,0:T(8,128)S(1)}) custom-call(s32[1]{0:T(128)} %bitcast.me_ref, s32[8]{0:T(128)} %ids_ref.3, f32[3,32,8,128]{3,2,1,0:T(8,128)} %bitcast.15, f32[5,32,8,128]{3,2,1,0:T(8,128)} %bitcast.13), custom_call_target="tpu_custom_call" | custom-call | tf_op jit(solution)/shard_map/pack_early/pallas_call | solution.py:406
  1.8 2.4 %collective-permute-start.7 = (f32[17,8,128]{2,1,0:T(8,128)S(1)}, f32[17,8,128]{2,1,0:T(8,128)S(1)}, u32[]{:S(2)}, u32[]{:S(2)}) collective-permute-start(f32[17,8,128]{2,1,0:T(8,128)S(1)} %get-tuple-element.50), channel_id=1, source_target_pairs={{0,4},{1,5},{2,6},{3,7},{4,0},{5,1},{6,2},{7,3},{8,12},{9,13},{10,... | collective-permute-start | bytes 208904 | tf_op jit(solution)/shard_map/ppermute | solution.py:390
  4.2 0.9 %collective-permute-start.8 = (f32[17,8,128]{2,1,0:T(8,128)S(1)}, f32[17,8,128]{2,1,0:T(8,128)S(1)}, u32[]{:S(2)}, u32[]{:S(2)}) collective-permute-start(f32[17,8,128]{2,1,0:T(8,128)S(1)} %get-tuple-element.51), channel_id=1, source_target_pairs={{0,5},{1,4},{2,7},{3,6},{4,1},{5,0},{6,3},{7,2},{8,13},{9,12},{10,... | collective-permute-start | bytes 208904 | tf_op jit(solution)/shard_map/ppermute | solution.py:390
  5.1 1.4 %pack_late.1 = (f32[33,8,128]{2,1,0:T(8,128)S(1)}, f32[33,8,128]{2,1,0:T(8,128)S(1)}, f32[33,8,128]{2,1,0:T(8,128)S(1)}, f32[33,8,128]{2,1,0:T(8,128)S(1)}, f32[...) custom-call(s32[1]{0:T(128)} %bitcast.me_ref, ...), custom_call_target="tpu_custom_call" | custom-call | tf_op jit(solution)/shard_map/pack_late/pallas_call | solution.py:406
  6.7 1.3 %collective-permute-start.5 = (f32[33,8,128]{2,1,0:T(8,128)S(1)}, f32[33,8,128]{2,1,0:T(8,128)S(1)}, u32[]{:S(2)}, u32[]{:S(2)}) collective-permute-start(f32[33,8,128]{2,1,0:T(8,128)S(1)} %get-tuple-element.44), channel_id=1, source_target_pairs={{0,2},{1,3},{2,0},{3,1},{4,6},{5,7},{6,4},{7,5},{8,10},{9,11},{10,... | collective-permute-start | bytes 405512 | tf_op jit(solution)/shard_map/ppermute | solution.py:390
  8.9 1.1 %collective-permute-start.9 = (f32[17,8,128]{2,1,0:T(8,128)S(1)}, f32[17,8,128]{2,1,0:T(8,128)S(1)}, u32[]{:S(2)}, u32[]{:S(2)}) collective-permute-start(f32[17,8,128]{2,1,0:T(8,128)S(1)} %get-tuple-element.52), channel_id=1, source_target_pairs={{0,6},{1,7},{2,4},{3,5},{4,2},{5,3},{6,0},{7,1},{8,14},{9,15},{10,... | collective-permute-start | bytes 208904 | tf_op jit(solution)/shard_map/ppermute | solution.py:390
  11.3 1.1 %operators.1 = (bf16[2,2,256,256]{3,2,1,0:T(8,128)(2,1)S(1)}, bf16[2,2,256,256]{3,2,1,0:T(8,128)(2,1)S(1)}, bf16[2,3,256,256]{3,2,1,0:T(8,128)(2,1)S(1)}, bf16[2...) custom-call(s32[1]{0:T(128)} %bitcast.me_ref, ...), custom_call_target="tpu_custom_call" | custom-call | tf_op jit(solution)/shard_map/operators/pallas_call | solution.py:426
  12.3 5.3 %collective-permute-start = (f32[16,8,128]{2,1,0:T(8,128)S(1)}, f32[16,8,128]{2,1,0:T(8,128)S(1)}, u32[]{:S(2)}, u32[]{:S(2)}) collective-permute-start(f32[16,8,128]{2,1,0:T(8,128)S(1)} %get-tuple-element.39), channel_id=1, source_target_pairs={{0,4},{1,5},{2,6},{3,7},{4,0},{5,1},{6,2},{7,3},{8,12},{9,13},{10,... | collective-permute-start | bytes 196616 | tf_op jit(solution)/shard_map/ppermute | solution.py:390
  17.6 2.6 %collective-permute-start.1 = (f32[16,8,128]{2,1,0:T(8,128)S(1)}, f32[16,8,128]{2,1,0:T(8,128)S(1)}, u32[]{:S(2)}, u32[]{:S(2)}) collective-permute-start(f32[16,8,128]{2,1,0:T(8,128)S(1)} %get-tuple-element.40), channel_id=1, source_target_pairs={{0,5},{1,4},{2,7},{3,6},{4,1},{5,0},{6,3},{7,2},{8,13},{9,12},{10,... | collective-permute-start | bytes 196616 | tf_op jit(solution)/shard_map/ppermute | solution.py:390
  20.2 1.3 %collective-permute-start.2 = (f32[16,8,128]{2,1,0:T(8,128)S(1)}, f32[16,8,128]{2,1,0:T(8,128)S(1)}, u32[]{:S(2)}, u32[]{:S(2)}) collective-permute-start(f32[16,8,128]{2,1,0:T(8,128)S(1)} %get-tuple-element.41), channel_id=1, source_target_pairs={{0,6},{1,7},{2,4},{3,5},{4,2},{5,3},{6,0},{7,1},{8,14},{9,15},{10,... | collective-permute-start | bytes 196616 | tf_op jit(solution)/shard_map/ppermute | solution.py:390
  22.4 2.1 %collective-permute-start.11 = (f32[8,2,8,128]{3,2,1,0:T(8,128)S(1)}, f32[8,2,8,128]{3,2,1,0:T(8,128)S(1)}, u32[]{:S(2)}, u32[]{:S(2)}) collective-permute-start(f32[8,2,8,128]{3,2,1,0:T(8,128)S(1)} %edge.1), channel_id=1, source_target_pairs={{1,0},{2,1},{3,2},{4,3},{5,4},{6,5},{7,6},{15,7},{14,15},{13,14},{... | collective-permute-start | bytes 196616 | tf_op jit(solution)/shard_map/ppermute | solution.py:450
  24.5 1.5 %fields.1 = (f32[8,4,4,8,128]{4,3,2,1,0:T(8,128)S(1)}, bf16[2,192,192]{2,1,0:T(8,128)(2,1)S(1)}, f32[1,1,8,128]{3,2,1,0:T(8,128)S(1)}) custom-call(s32[1]{0:T(128)} %bitcast.me_ref, f32[17,8,128]{2,1,0:T(8,128)S(1)} %collective-permute-done.7.refs_0_, f32[17,8,128]{2,1,0:T(8,128)S(1)} %collective-permute-done.8.refs_1_, ...), custom_call_target="tpu_custom_call" | custom-call | tf_op jit(solution)/shard_map/fields/pallas_call | solution.py:455
  26.1 3.0 %collective-permute-done.2.refs_2_ = f32[16,8,128]{2,1,0:T(8,128)S(1)} collective-permute-done((f32[16,8,128]{2,1,0:T(8,128)S(1)}, f32[16,8,128]{2,1,0:T(8,128)S(1)}, u32[]{:S(2)}, u32[]{:S(2)}) %collective-permute-start.2) | collective-permute-done | bytes 65568 | tf_op jit(solution)/shard_map/ppermute | solution.py:390
  29.1 1.6 %collective-permute-done.3.refs_3_ = f32[16,8,128]{2,1,0:T(8,128)S(1)} collective-permute-done((f32[16,8,128]{2,1,0:T(8,128)S(1)}, f32[16,8,128]{2,1,0:T(8,128)S(1)}, u32[]{:S(2)}, u32[]{:S(2)}) %collective-permute-start.3) | collective-permute-done | bytes 65568 | tf_op jit(solution)/shard_map/ppermute | solution.py:390
  32.0 2.1 %collective-permute-start.15 = (f32[8,4,8,128]{3,2,1,0:T(8,128)S(1)}, f32[8,4,8,128]{3,2,1,0:T(8,128)S(1)}, u32[]{:S(2)}, u32[]{:S(2)}) collective-permute-start(f32[8,4,8,128]{3,2,1,0:T(8,128)S(1)} %get-tuple-element.64), channel_id=1, source_target_pairs={{0,5},{1,4},{2,7},{3,6},{4,1},{5,0},{6,3},{7,2},{8,13},{9,12},{10,... | collective-permute-start | bytes 393224 | tf_op jit(solution)/shard_map/ppermute | solution.py:390
  34.1 1.0 %finish_near.1 = (f32[8,4,8,128]{3,2,1,0:T(8,128)S(1)}, f32[8,4,8,128]{3,2,1,0:T(8,128)S(1)}, f32[8,4,8,128]{3,2,1,0:T(8,128)S(1)}, f32[8,4,8,128]{3,2,1,0:T(8,128)S(1)}, f32[8,128]{1,0:T(8,128)}) custom-call(s32[1]{0:T(128)} %bitcast.me_ref, f32[16,8,128]{2,1,0:T(8,128)S(1)} %collective-permute-done.refs_0_, ...), custom_call_target="tpu_custom_call" | custom-call | tf_op jit(solution)/shard_map/finish_near/pallas_call | solution.py:478
  35.1 2.0 %collective-permute-start.17 = (f32[8,4,8,128]{3,2,1,0:T(8,128)S(1)}, f32[8,4,8,128]{3,2,1,0:T(8,128)S(1)}, u32[]{:S(2)}, u32[]{:S(2)}) collective-permute-start(f32[8,4,8,128]{3,2,1,0:T(8,128)S(1)} %get-tuple-element.67), channel_id=1, source_target_pairs={{0,2},{1,3},{2,0},{3,1},{4,6},{5,7},{6,4},{7,5},{8,10},{9,11},{10,... | collective-permute-start | bytes 393224 | tf_op jit(solution)/shard_map/ppermute | solution.py:390
  37.3 3.7 %collective-permute-done.14.refs_0_ = f32[8,4,8,128]{3,2,1,0:T(8,128)S(1)} collective-permute-done((f32[8,4,8,128]{3,2,1,0:T(8,128)S(1)}, f32[8,4,8,128]{3,2,1,0:T(8,128)S(1)}, u32[]{:S(2)}, u32[]{:S(2)}) %collective-permute-start.14) | collective-permute-done | bytes 131104 | tf_op jit(solution)/shard_map/ppermute | solution.py:390
  41.0 2.6 %collective-permute-done.15.refs_1_ = f32[8,4,8,128]{3,2,1,0:T(8,128)S(1)} collective-permute-done((f32[8,4,8,128]{3,2,1,0:T(8,128)S(1)}, f32[8,4,8,128]{3,2,1,0:T(8,128)S(1)}, u32[]{:S(2)}, u32[]{:S(2)}) %collective-permute-start.15) | collective-permute-done | bytes 131104 | tf_op jit(solution)/shard_map/ppermute | solution.py:390
  43.5 1.7 %collective-permute-start.13 = (f32[8,4,8,128]{3,2,1,0:T(8,128)S(1)}, f32[8,4,8,128]{3,2,1,0:T(8,128)S(1)}, u32[]{:S(2)}, u32[]{:S(2)}) collective-permute-start(f32[8,4,8,128]{3,2,1,0:T(8,128)S(1)} %get-tuple-element.62), channel_id=1, source_target_pairs={{0,7},{1,6},{2,5},{3,4},{4,3},{5,2},{6,1},{7,0},{8,15},{9,14},{10,... | collective-permute-start | bytes 393224 | tf_op jit(solution)/shard_map/ppermute | solution.py:390
  45.3 1.0 %unpack_early.1 = (f32[5,32,8,128]{3,2,1,0:T(8,128)}, f32[3,32,8,128]{3,2,1,0:T(8,128)}) custom-call(s32[1]{0:T(128)} %bitcast.me_ref, f32[8,4,8,128]{3,2,1,0:T(8,128)S(1)} %collective-permute-done.14.refs_0_, f32[8,4,8,128]{3,2,1,0:T(8,128)S(1)} %collective-permute-done.15.refs_1_, f32[8,4,8,128]{3,2,1,0:T(8,128)S(1)} %collective-permute-done.16.refs_2_, ...), custom_call_target="tpu_custom_call" | custom-call | tf_op jit(solution)/shard_map/unpack_early/pallas_call | solution.py:491
  46.3 6.6 %collective-permute-done.12.refs_0_ = f32[8,4,8,128]{3,2,1,0:T(8,128)S(1)} collective-permute-done((f32[8,4,8,128]{3,2,1,0:T(8,128)S(1)}, f32[8,4,8,128]{3,2,1,0:T(8,128)S(1)}, u32[]{:S(2)}, u32[]{:S(2)}) %collective-permute-start.12) | collective-permute-done | bytes 131104 | tf_op jit(solution)/shard_map/ppermute | solution.py:390
  52.9 3.2 %collective-permute-done.13.refs_1_ = f32[8,4,8,128]{3,2,1,0:T(8,128)S(1)} collective-permute-done((f32[8,4,8,128]{3,2,1,0:T(8,128)S(1)}, f32[8,4,8,128]{3,2,1,0:T(8,128)S(1)}, u32[]{:S(2)}, u32[]{:S(2)}) %collective-permute-start.13) | collective-permute-done | bytes 131104 | tf_op jit(solution)/shard_map/ppermute | solution.py:390
  56.0 0.8 %unpack_late.1 = (f32[5,32,8,128]{3,2,1,0:T(8,128)}, f32[3,32,8,128]{3,2,1,0:T(8,128)}) custom-call(s32[1]{0:T(128)} %bitcast.me_ref, f32[8,4,8,128]{3,2,1,0:T(8,128)S(1)} %collective-permute-done.12.refs_0_, f32[8,4,8,128]{3,2,1,0:T(8,128)S(1)} %collective-permute-done.13.refs_1_, ...), custom_call_target="tpu_custom_call", output_to_operand_aliasing={{0}: (3, {}), {1}: (4, {})} | custom-call | tf_op jit(solution)/shard_map/unpack_late/pallas_call | solution.py:491
  (27 shorter events, 4.8 us)
Async XLA Ops:
  1.8 7.1 %collective-permute-start.7 = (f32[17,8,128]{2,1,0:T(8,128)S(1)}, f32[17,8,128]{2,1,0:T(8,128)S(1)}, u32[]{:S(2)}, u32[]{:S(2)}) collective-permute-start(f32[17,8,128]{2,1,0:T(8,128)S(1)} %get-tuple-element.50), channel_id=1, source_target_pairs={{0,4},{1,5},{2,6},{3,7},{4,0},{5,1},{6,2},{7,3},{8,12},{9,13},{10,... | collective-permute-start | bytes 208904 | tf_op jit(solution)/shard_map/ppermute | solution.py:390
  4.2 6.3 %collective-permute-start.8 = (f32[17,8,128]{2,1,0:T(8,128)S(1)}, f32[17,8,128]{2,1,0:T(8,128)S(1)}, u32[]{:S(2)}, u32[]{:S(2)}) collective-permute-start(f32[17,8,128]{2,1,0:T(8,128)S(1)} %get-tuple-element.51), channel_id=1, source_target_pairs={{0,5},{1,4},{2,7},{3,6},{4,1},{5,0},{6,3},{7,2},{8,13},{9,12},{10,... | collective-permute-start | bytes 208904 | tf_op jit(solution)/shard_map/ppermute | solution.py:390
  6.5 13.7 %collective-permute-start.4 = (f32[33,8,128]{2,1,0:T(8,128)S(1)}, f32[33,8,128]{2,1,0:T(8,128)S(1)}, u32[]{:S(2)}, u32[]{:S(2)}) collective-permute-start(f32[33,8,128]{2,1,0:T(8,128)S(1)} %get-tuple-element.43), channel_id=1, source_target_pairs={{0,3},{1,2},{2,1},{3,0},{4,7},{5,6},{6,5},{7,4},{8,11},{9,10},{10,... | collective-permute-start | bytes 405512 | tf_op jit(solution)/shard_map/ppermute | solution.py:390
  6.7 14.9 %collective-permute-start.5 = (f32[33,8,128]{2,1,0:T(8,128)S(1)}, f32[33,8,128]{2,1,0:T(8,128)S(1)}, u32[]{:S(2)}, u32[]{:S(2)}) collective-permute-start(f32[33,8,128]{2,1,0:T(8,128)S(1)} %get-tuple-element.44), channel_id=1, source_target_pairs={{0,2},{1,3},{2,0},{3,1},{4,6},{5,7},{6,4},{7,5},{8,10},{9,11},{10,... | collective-permute-start | bytes 405512 | tf_op jit(solution)/shard_map/ppermute | solution.py:390
  8.0 14.0 %collective-permute-start.6 = (f32[33,8,128]{2,1,0:T(8,128)S(1)}, f32[33,8,128]{2,1,0:T(8,128)S(1)}, u32[]{:S(2)}, u32[]{:S(2)}) collective-permute-start(f32[33,8,128]{2,1,0:T(8,128)S(1)} %get-tuple-element.45), channel_id=1, source_target_pairs={{0,1},{1,0},{2,3},{3,2},{4,5},{5,4},{6,7},{7,6},{8,9},{9,8},{10,11... | collective-permute-start | bytes 405512 | tf_op jit(solution)/shard_map/ppermute | solution.py:390
  8.9 2.3 %copy-start = (s32[16]{0:T(128)S(1)}, s32[16]{0:T(128)}, u32[]{:S(2)}) copy-start(s32[16]{0:T(128)} %shift_ref.1) | copy-start | bytes 196
  8.9 2.3 %copy-start.1 = (f32[16]{0:T(128)S(1)}, f32[16]{0:T(128)}, u32[]{:S(2)}) copy-start(f32[16]{0:T(128)} %frac_ref.1) | copy-start | bytes 196
  8.9 3.4 %collective-permute-start.9 = (f32[17,8,128]{2,1,0:T(8,128)S(1)}, f32[17,8,128]{2,1,0:T(8,128)S(1)}, u32[]{:S(2)}, u32[]{:S(2)}) collective-permute-start(f32[17,8,128]{2,1,0:T(8,128)S(1)} %get-tuple-element.52), channel_id=1, source_target_pairs={{0,6},{1,7},{2,4},{3,5},{4,2},{5,3},{6,0},{7,1},{8,14},{9,15},{10,... | collective-permute-start | bytes 208904 | tf_op jit(solution)/shard_map/ppermute | solution.py:390
  10.5 7.2 %collective-permute-start.10 = (f32[17,8,128]{2,1,0:T(8,128)S(1)}, f32[17,8,128]{2,1,0:T(8,128)S(1)}, u32[]{:S(2)}, u32[]{:S(2)}) collective-permute-start(f32[17,8,128]{2,1,0:T(8,128)S(1)} %get-tuple-element.53), channel_id=1, source_target_pairs={{0,7},{1,6},{2,5},{3,4},{4,3},{5,2},{6,1},{7,0},{8,15},{9,14},{10,... | collective-permute-start | bytes 208904 | tf_op jit(solution)/shard_map/ppermute | solution.py:390
  12.3 13.7 %collective-permute-start = (f32[16,8,128]{2,1,0:T(8,128)S(1)}, f32[16,8,128]{2,1,0:T(8,128)S(1)}, u32[]{:S(2)}, u32[]{:S(2)}) collective-permute-start(f32[16,8,128]{2,1,0:T(8,128)S(1)} %get-tuple-element.39), channel_id=1, source_target_pairs={{0,4},{1,5},{2,6},{3,7},{4,0},{5,1},{6,2},{7,3},{8,12},{9,13},{10,... | collective-permute-start | bytes 196616 | tf_op jit(solution)/shard_map/ppermute | solution.py:390
  17.6 8.4 %collective-permute-start.1 = (f32[16,8,128]{2,1,0:T(8,128)S(1)}, f32[16,8,128]{2,1,0:T(8,128)S(1)}, u32[]{:S(2)}, u32[]{:S(2)}) collective-permute-start(f32[16,8,128]{2,1,0:T(8,128)S(1)} %get-tuple-element.40), channel_id=1, source_target_pairs={{0,5},{1,4},{2,7},{3,6},{4,1},{5,0},{6,3},{7,2},{8,13},{9,12},{10,... | collective-permute-start | bytes 196616 | tf_op jit(solution)/shard_map/ppermute | solution.py:390
  20.2 8.9 %collective-permute-start.2 = (f32[16,8,128]{2,1,0:T(8,128)S(1)}, f32[16,8,128]{2,1,0:T(8,128)S(1)}, u32[]{:S(2)}, u32[]{:S(2)}) collective-permute-start(f32[16,8,128]{2,1,0:T(8,128)S(1)} %get-tuple-element.41), channel_id=1, source_target_pairs={{0,6},{1,7},{2,4},{3,5},{4,2},{5,3},{6,0},{7,1},{8,14},{9,15},{10,... | collective-permute-start | bytes 196616 | tf_op jit(solution)/shard_map/ppermute | solution.py:390
  21.5 9.1 %collective-permute-start.3 = (f32[16,8,128]{2,1,0:T(8,128)S(1)}, f32[16,8,128]{2,1,0:T(8,128)S(1)}, u32[]{:S(2)}, u32[]{:S(2)}) collective-permute-start(f32[16,8,128]{2,1,0:T(8,128)S(1)} %get-tuple-element.42), channel_id=1, source_target_pairs={{0,7},{1,6},{2,5},{3,4},{4,3},{5,2},{6,1},{7,0},{8,15},{9,14},{10,... | collective-permute-start | bytes 196616 | tf_op jit(solution)/shard_map/ppermute | solution.py:390
  22.4 8.9 %collective-permute-start.11 = (f32[8,2,8,128]{3,2,1,0:T(8,128)S(1)}, f32[8,2,8,128]{3,2,1,0:T(8,128)S(1)}, u32[]{:S(2)}, u32[]{:S(2)}) collective-permute-start(f32[8,2,8,128]{3,2,1,0:T(8,128)S(1)} %edge.1), channel_id=1, source_target_pairs={{1,0},{2,1},{3,2},{4,3},{5,4},{6,5},{7,6},{15,7},{14,15},{13,14},{... | collective-permute-start | bytes 196616 | tf_op jit(solution)/shard_map/ppermute | solution.py:450
  32.0 9.0 %collective-permute-start.14 = (f32[8,4,8,128]{3,2,1,0:T(8,128)S(1)}, f32[8,4,8,128]{3,2,1,0:T(8,128)S(1)}, u32[]{:S(2)}, u32[]{:S(2)}) collective-permute-start(f32[8,4,8,128]{3,2,1,0:T(8,128)S(1)} %get-tuple-element.63), channel_id=1, source_target_pairs={{0,4},{1,5},{2,6},{3,7},{4,0},{5,1},{6,2},{7,3},{8,12},{9,13},{10,... | collective-permute-start | bytes 393224 | tf_op jit(solution)/shard_map/ppermute | solution.py:390
  32.0 11.5 %collective-permute-start.15 = (f32[8,4,8,128]{3,2,1,0:T(8,128)S(1)}, f32[8,4,8,128]{3,2,1,0:T(8,128)S(1)}, u32[]{:S(2)}, u32[]{:S(2)}) collective-permute-start(f32[8,4,8,128]{3,2,1,0:T(8,128)S(1)} %get-tuple-element.64), channel_id=1, source_target_pairs={{0,5},{1,4},{2,7},{3,6},{4,1},{5,0},{6,3},{7,2},{8,13},{9,12},{10,... | collective-permute-start | bytes 393224 | tf_op jit(solution)/shard_map/ppermute | solution.py:390
  35.1 10.1 %collective-permute-start.16 = (f32[8,4,8,128]{3,2,1,0:T(8,128)S(1)}, f32[8,4,8,128]{3,2,1,0:T(8,128)S(1)}, u32[]{:S(2)}, u32[]{:S(2)}) collective-permute-start(f32[8,4,8,128]{3,2,1,0:T(8,128)S(1)} %get-tuple-element.66), channel_id=1, source_target_pairs={{0,3},{1,2},{2,1},{3,0},{4,7},{5,6},{6,5},{7,4},{8,11},{9,10},{10,... | collective-permute-start | bytes 393224 | tf_op jit(solution)/shard_map/ppermute | solution.py:390
  35.1 10.1 %collective-permute-start.17 = (f32[8,4,8,128]{3,2,1,0:T(8,128)S(1)}, f32[8,4,8,128]{3,2,1,0:T(8,128)S(1)}, u32[]{:S(2)}, u32[]{:S(2)}) collective-permute-start(f32[8,4,8,128]{3,2,1,0:T(8,128)S(1)} %get-tuple-element.67), channel_id=1, source_target_pairs={{0,2},{1,3},{2,0},{3,1},{4,6},{5,7},{6,4},{7,5},{8,10},{9,11},{10,... | collective-permute-start | bytes 393224 | tf_op jit(solution)/shard_map/ppermute | solution.py:390
  37.2 8.1 %collective-permute-start.18 = (f32[8,4,8,128]{3,2,1,0:T(8,128)S(1)}, f32[8,4,8,128]{3,2,1,0:T(8,128)S(1)}, u32[]{:S(2)}, u32[]{:S(2)}) collective-permute-start(f32[8,4,8,128]{3,2,1,0:T(8,128)S(1)} %get-tuple-element.68), channel_id=1, source_target_pairs={{0,1},{1,0},{2,3},{3,2},{4,5},{5,4},{6,7},{7,6},{8,9},{9,8},{10,11... | collective-permute-start | bytes 393224 | tf_op jit(solution)/shard_map/ppermute | solution.py:390
  41.0 11.9 %collective-permute-start.12 = (f32[8,4,8,128]{3,2,1,0:T(8,128)S(1)}, f32[8,4,8,128]{3,2,1,0:T(8,128)S(1)}, u32[]{:S(2)}, u32[]{:S(2)}) collective-permute-start(f32[8,4,8,128]{3,2,1,0:T(8,128)S(1)} %get-tuple-element.61), channel_id=1, source_target_pairs={{0,6},{1,7},{2,4},{3,5},{4,2},{5,3},{6,0},{7,1},{8,14},{9,15},{10,... | collective-permute-start | bytes 393224 | tf_op jit(solution)/shard_map/ppermute | solution.py:390
  43.5 12.5 %collective-permute-start.13 = (f32[8,4,8,128]{3,2,1,0:T(8,128)S(1)}, f32[8,4,8,128]{3,2,1,0:T(8,128)S(1)}, u32[]{:S(2)}, u32[]{:S(2)}) collective-permute-start(f32[8,4,8,128]{3,2,1,0:T(8,128)S(1)} %get-tuple-element.62), channel_id=1, source_target_pairs={{0,7},{1,6},{2,5},{3,4},{4,3},{5,2},{6,1},{7,0},{8,15},{9,14},{10,... | collective-permute-start | bytes 393224 | tf_op jit(solution)/shard_map/ppermute | solution.py:390

commit v11 on v10

--- a/solution.py
+++ b/solution.py
@@ -473,18 +473,24 @@
                 for s in range(count)
             ],
         )
-    done, token = [], []
-    for name, orders in (("finish_far", cfg.order[:half]), ("finish_near", cfg.order[half:])):
+    done, token = {}, []
+    first_far, last_far = cfg.order[: n // 4], cfg.order[n // 4 : half]
+    for name, orders in (
+        ("finish_first", first_far),
+        ("finish_near", cfg.order[half:]),
+        ("finish_last", last_far),
+    ):
         *pieces, mark = pl.pallas_call(
             functools.partial(finish_kernel, cfg, orders),
-            out_shape=[shape(8, tiles, SUB, LANES)] * half + [shape(SUB, LANES)],
+            out_shape=[shape(8, tiles, SUB, LANES)] * len(orders) + [shape(SUB, LANES)],
             in_specs=[smem] + [vmem] * (n + 7 + len(token)),
-            out_specs=[vmem] * (half + 1),
+            out_specs=[vmem] * (len(orders) + 1),
             compiler_params=grant(2 * n),
             name=name,
         )(me, *far_second, *first[half:], mh, ml, side, taken, rows, halo, polar, *token)
-        done, token = done + pieces, [mark]
-    back = exchange(done, cfg.order)
+        done.update(zip(orders, pieces))
+        token = [mark]
+    back = exchange([done[k] for k in cfg.order], cfg.order)
     outs = ()
     for name, late in (("unpack_early", False), ("unpack_late", True)):
         orders = [k for k in cfg.order if (k in cfg.last) == late]

time: 57.2 us -> 57.1 us (level)
  waiting for transfers between devices: 22 us -> 21.4 us
    pallas_call x2 -> x3, Pallas kernels: 1.66 us -> 2.02 us  [shards(): pl.pallas_call(functools.partial(finish_kernel, cfg, orders), out_shape=[...]
  transfers between devices with their start and end apart: 19 -> 19, of which waited for: 9 -> 9; matrix products, arithmetic and copies ran while one was open for 0% -> 0% of each run, Pallas kernels for 11% -> 12%
where the time goes in v11:
time: 57.1 us; the launch traced here: 56.7 us
  starting transfers between devices  25 us (44%)
  waiting for transfers between devices  21.4 us (37%)
  Pallas kernels  9.52 us (17%)
  between operations  0.77 us (1%)
    ppermute x18, starting transfers between devices, exchange(): lax.ppermute(piece, 'phi', [(s, s ^ k) for s in range(n)])  22.9 us
    ppermute x18, waiting for transfers between devices, exchange(): lax.ppermute(piece, 'phi', [(s, s ^ k) for s in range(n)])  20.7 us
    pallas_call x2, Pallas kernels, shards(): pl.pallas_call(functools.partial(pack_kernel, cfg, late), out_shape=shape...  2.55 us
    ppermute x1, starting transfers between devices, shards(): lax.ppermute(halo, ('tile', 'phi'), [(holder(s), holder(s - cfg.split)) f...  2.09 us
    pallas_call x3, Pallas kernels, shards(): pl.pallas_call(functools.partial(finish_kernel, cfg, orders), out_shape=[...  2.02 us
    pallas_call x2, Pallas kernels, shards(): pl.pallas_call(functools.partial(unpack_kernel, cfg, orders), out_shape=[...  1.85 us
    pallas_call x1, Pallas kernels, shards(): pl.pallas_call(functools.partial(fields_kernel, cfg), out_shape=[shape(n,...  1.54 us
  transfers between devices with their start and end apart: 19, of which 9 were waited for; matrix products, arithmetic and copies ran while one was open for 0% of the time, Pallas kernels for 12%

profile of v11, /device:TPU:13, one launch (start us, length us, event | category | flops | bytes accessed | tf_op | source)
XLA Modules:
  0.0 56.7 jit_solution(5107999034175421464)
XLA Ops:
  0.6 1.2 %pack_early.1 = (f32[17,8,128]{2,1,0:T(8,128)S(1)}, f32[17,8,128]{2,1,0:T(8,128)S(1)}, f32[17,8,128]{2,1,0:T(8,128)S(1)}, f32[17,8,128]{2,1,0:T(8,128)S(1)}, f32[8,128]{1,0:T(8,128)S(1)}) custom-call(s32[1]{0:T(128)} %bitcast.me_ref, s32[8]{0:T(128)} %ids_ref.3, f32[3,32,8,128]{3,2,1,0:T(8,128)} %bitcast.15, f32[5,32,8,128]{3,2,1,0:T(8,128)} %bitcast.13), custom_call_target="tpu_custom_call" | custom-call | tf_op jit(solution)/shard_map/pack_early/pallas_call | solution.py:406
  1.8 2.4 %collective-permute-start.7 = (f32[17,8,128]{2,1,0:T(8,128)S(1)}, f32[17,8,128]{2,1,0:T(8,128)S(1)}, u32[]{:S(2)}, u32[]{:S(2)}) collective-permute-start(f32[17,8,128]{2,1,0:T(8,128)S(1)} %get-tuple-element.51), channel_id=1, source_target_pairs={{0,4},{1,5},{2,6},{3,7},{4,0},{5,1},{6,2},{7,3},{8,12},{9,13},{10,... | collective-permute-start | bytes 208904 | tf_op jit(solution)/shard_map/ppermute | solution.py:390
  4.2 0.9 %collective-permute-start.8 = (f32[17,8,128]{2,1,0:T(8,128)S(1)}, f32[17,8,128]{2,1,0:T(8,128)S(1)}, u32[]{:S(2)}, u32[]{:S(2)}) collective-permute-start(f32[17,8,128]{2,1,0:T(8,128)S(1)} %get-tuple-element.52), channel_id=1, source_target_pairs={{0,5},{1,4},{2,7},{3,6},{4,1},{5,0},{6,3},{7,2},{8,13},{9,12},{10,... | collective-permute-start | bytes 208904 | tf_op jit(solution)/shard_map/ppermute | solution.py:390
  5.1 1.4 %pack_late.1 = (f32[33,8,128]{2,1,0:T(8,128)S(1)}, f32[33,8,128]{2,1,0:T(8,128)S(1)}, f32[33,8,128]{2,1,0:T(8,128)S(1)}, f32[33,8,128]{2,1,0:T(8,128)S(1)}, f32[...) custom-call(s32[1]{0:T(128)} %bitcast.me_ref, ...), custom_call_target="tpu_custom_call" | custom-call | tf_op jit(solution)/shard_map/pack_late/pallas_call | solution.py:406
  6.7 1.3 %collective-permute-start.5 = (f32[33,8,128]{2,1,0:T(8,128)S(1)}, f32[33,8,128]{2,1,0:T(8,128)S(1)}, u32[]{:S(2)}, u32[]{:S(2)}) collective-permute-start(f32[33,8,128]{2,1,0:T(8,128)S(1)} %get-tuple-element.45), channel_id=1, source_target_pairs={{0,2},{1,3},{2,0},{3,1},{4,6},{5,7},{6,4},{7,5},{8,10},{9,11},{10,... | collective-permute-start | bytes 405512 | tf_op jit(solution)/shard_map/ppermute | solution.py:390
  8.9 1.1 %collective-permute-start.9 = (f32[17,8,128]{2,1,0:T(8,128)S(1)}, f32[17,8,128]{2,1,0:T(8,128)S(1)}, u32[]{:S(2)}, u32[]{:S(2)}) collective-permute-start(f32[17,8,128]{2,1,0:T(8,128)S(1)} %get-tuple-element.53), channel_id=1, source_target_pairs={{0,6},{1,7},{2,4},{3,5},{4,2},{5,3},{6,0},{7,1},{8,14},{9,15},{10,... | collective-permute-start | bytes 208904 | tf_op jit(solution)/shard_map/ppermute | solution.py:390
  11.3 1.1 %operators.1 = (bf16[2,2,256,256]{3,2,1,0:T(8,128)(2,1)S(1)}, bf16[2,2,256,256]{3,2,1,0:T(8,128)(2,1)S(1)}, bf16[2,3,256,256]{3,2,1,0:T(8,128)(2,1)S(1)}, bf16[2...) custom-call(s32[1]{0:T(128)} %bitcast.me_ref, ...), custom_call_target="tpu_custom_call" | custom-call | tf_op jit(solution)/shard_map/operators/pallas_call | solution.py:426
  12.3 5.3 %collective-permute-start = (f32[16,8,128]{2,1,0:T(8,128)S(1)}, f32[16,8,128]{2,1,0:T(8,128)S(1)}, u32[]{:S(2)}, u32[]{:S(2)}) collective-permute-start(f32[16,8,128]{2,1,0:T(8,128)S(1)} %get-tuple-element.40), channel_id=1, source_target_pairs={{0,4},{1,5},{2,6},{3,7},{4,0},{5,1},{6,2},{7,3},{8,12},{9,13},{10,... | collective-permute-start | bytes 196616 | tf_op jit(solution)/shard_map/ppermute | solution.py:390
  17.6 2.6 %collective-permute-start.1 = (f32[16,8,128]{2,1,0:T(8,128)S(1)}, f32[16,8,128]{2,1,0:T(8,128)S(1)}, u32[]{:S(2)}, u32[]{:S(2)}) collective-permute-start(f32[16,8,128]{2,1,0:T(8,128)S(1)} %get-tuple-element.41), channel_id=1, source_target_pairs={{0,5},{1,4},{2,7},{3,6},{4,1},{5,0},{6,3},{7,2},{8,13},{9,12},{10,... | collective-permute-start | bytes 196616 | tf_op jit(solution)/shard_map/ppermute | solution.py:390
  20.2 1.3 %collective-permute-start.2 = (f32[16,8,128]{2,1,0:T(8,128)S(1)}, f32[16,8,128]{2,1,0:T(8,128)S(1)}, u32[]{:S(2)}, u32[]{:S(2)}) collective-permute-start(f32[16,8,128]{2,1,0:T(8,128)S(1)} %get-tuple-element.42), channel_id=1, source_target_pairs={{0,6},{1,7},{2,4},{3,5},{4,2},{5,3},{6,0},{7,1},{8,14},{9,15},{10,... | collective-permute-start | bytes 196616 | tf_op jit(solution)/shard_map/ppermute | solution.py:390
  22.4 2.1 %collective-permute-start.11 = (f32[8,2,8,128]{3,2,1,0:T(8,128)S(1)}, f32[8,2,8,128]{3,2,1,0:T(8,128)S(1)}, u32[]{:S(2)}, u32[]{:S(2)}) collective-permute-start(f32[8,2,8,128]{3,2,1,0:T(8,128)S(1)} %edge.1), channel_id=1, source_target_pairs={{1,0},{2,1},{3,2},{4,3},{5,4},{6,5},{7,6},{15,7},{14,15},{13,14},{... | collective-permute-start | bytes 196616 | tf_op jit(solution)/shard_map/ppermute | solution.py:450
  24.5 1.5 %fields.1 = (f32[8,4,4,8,128]{4,3,2,1,0:T(8,128)S(1)}, bf16[2,192,192]{2,1,0:T(8,128)(2,1)S(1)}, f32[1,1,8,128]{3,2,1,0:T(8,128)S(1)}) custom-call(s32[1]{0:T(128)} %bitcast.me_ref, f32[17,8,128]{2,1,0:T(8,128)S(1)} %collective-permute-done.7.refs_0_, f32[17,8,128]{2,1,0:T(8,128)S(1)} %collective-permute-done.8.refs_1_, ...), custom_call_target="tpu_custom_call" | custom-call | tf_op jit(solution)/shard_map/fields/pallas_call | solution.py:455
  26.1 3.0 %collective-permute-done.2.refs_2_ = f32[16,8,128]{2,1,0:T(8,128)S(1)} collective-permute-done((f32[16,8,128]{2,1,0:T(8,128)S(1)}, f32[16,8,128]{2,1,0:T(8,128)S(1)}, u32[]{:S(2)}, u32[]{:S(2)}) %collective-permute-start.2) | collective-permute-done | bytes 65568 | tf_op jit(solution)/shard_map/ppermute | solution.py:390
  29.1 1.6 %collective-permute-done.3.refs_3_ = f32[16,8,128]{2,1,0:T(8,128)S(1)} collective-permute-done((f32[16,8,128]{2,1,0:T(8,128)S(1)}, f32[16,8,128]{2,1,0:T(8,128)S(1)}, u32[]{:S(2)}, u32[]{:S(2)}) %collective-permute-start.3) | collective-permute-done | bytes 65568 | tf_op jit(solution)/shard_map/ppermute | solution.py:390
  31.9 2.1 %collective-permute-start.15 = (f32[8,4,8,128]{3,2,1,0:T(8,128)S(1)}, f32[8,4,8,128]{3,2,1,0:T(8,128)S(1)}, u32[]{:S(2)}, u32[]{:S(2)}) collective-permute-start(f32[8,4,8,128]{3,2,1,0:T(8,128)S(1)} %get-tuple-element.67), channel_id=1, source_target_pairs={{0,5},{1,4},{2,7},{3,6},{4,1},{5,0},{6,3},{7,2},{8,13},{9,12},{10,... | collective-permute-start | bytes 393224 | tf_op jit(solution)/shard_map/ppermute | solution.py:390
  34.7 2.0 %collective-permute-start.17 = (f32[8,4,8,128]{3,2,1,0:T(8,128)S(1)}, f32[8,4,8,128]{3,2,1,0:T(8,128)S(1)}, u32[]{:S(2)}, u32[]{:S(2)}) collective-permute-start(f32[8,4,8,128]{3,2,1,0:T(8,128)S(1)} %get-tuple-element.69), channel_id=1, source_target_pairs={{0,2},{1,3},{2,0},{3,1},{4,6},{5,7},{6,4},{7,5},{8,10},{9,11},{10,... | collective-permute-start | bytes 393224 | tf_op jit(solution)/shard_map/ppermute | solution.py:390
  36.8 0.9 %finish_last.1 = (f32[8,4,8,128]{3,2,1,0:T(8,128)S(1)}, f32[8,4,8,128]{3,2,1,0:T(8,128)S(1)}, f32[8,128]{1,0:T(8,128)}) custom-call(s32[1]{0:T(128)} %bitcast.me_ref, f32[16,8,128]{2,1,0:T(8,128)S(1)} %collective-permute-done.refs_0_, f32[16,8,128]{2,1,0:T(8,128)S(1)} %collective-permute-done.1.refs_1_, f32[16,8,128]{2,1,0:T(8,128)S(1)} %collective-permute-done.2.refs_2_, ...), custom_call_target="tpu_custom_call" | custom-call | tf_op jit(solution)/shard_map/finish_last/pallas_call | solution.py:483
  37.7 3.1 %collective-permute-done.14.refs_0_ = f32[8,4,8,128]{3,2,1,0:T(8,128)S(1)} collective-permute-done((f32[8,4,8,128]{3,2,1,0:T(8,128)S(1)}, f32[8,4,8,128]{3,2,1,0:T(8,128)S(1)}, u32[]{:S(2)}, u32[]{:S(2)}) %collective-permute-start.14) | collective-permute-done | bytes 131104 | tf_op jit(solution)/shard_map/ppermute | solution.py:390
  40.8 2.6 %collective-permute-done.15.refs_1_ = f32[8,4,8,128]{3,2,1,0:T(8,128)S(1)} collective-permute-done((f32[8,4,8,128]{3,2,1,0:T(8,128)S(1)}, f32[8,4,8,128]{3,2,1,0:T(8,128)S(1)}, u32[]{:S(2)}, u32[]{:S(2)}) %collective-permute-start.15) | collective-permute-done | bytes 131104 | tf_op jit(solution)/shard_map/ppermute | solution.py:390
  43.4 1.7 %collective-permute-start.13 = (f32[8,4,8,128]{3,2,1,0:T(8,128)S(1)}, f32[8,4,8,128]{3,2,1,0:T(8,128)S(1)}, u32[]{:S(2)}, u32[]{:S(2)}) collective-permute-start(f32[8,4,8,128]{3,2,1,0:T(8,128)S(1)} %get-tuple-element.65), channel_id=1, source_target_pairs={{0,7},{1,6},{2,5},{3,4},{4,3},{5,2},{6,1},{7,0},{8,15},{9,14},{10,... | collective-permute-start | bytes 393224 | tf_op jit(solution)/shard_map/ppermute | solution.py:390
  45.1 1.0 %unpack_early.1 = (f32[5,32,8,128]{3,2,1,0:T(8,128)}, f32[3,32,8,128]{3,2,1,0:T(8,128)}) custom-call(s32[1]{0:T(128)} %bitcast.me_ref, f32[8,4,8,128]{3,2,1,0:T(8,128)S(1)} %collective-permute-done.14.refs_0_, f32[8,4,8,128]{3,2,1,0:T(8,128)S(1)} %collective-permute-done.15.refs_1_, f32[8,4,8,128]{3,2,1,0:T(8,128)S(1)} %collective-permute-done.16.refs_2_, ...), custom_call_target="tpu_custom_call" | custom-call | tf_op jit(solution)/shard_map/unpack_early/pallas_call | solution.py:497
  46.2 6.6 %collective-permute-done.12.refs_0_ = f32[8,4,8,128]{3,2,1,0:T(8,128)S(1)} collective-permute-done((f32[8,4,8,128]{3,2,1,0:T(8,128)S(1)}, f32[8,4,8,128]{3,2,1,0:T(8,128)S(1)}, u32[]{:S(2)}, u32[]{:S(2)}) %collective-permute-start.12) | collective-permute-done | bytes 131104 | tf_op jit(solution)/shard_map/ppermute | solution.py:390
  52.7 3.2 %collective-permute-done.13.refs_1_ = f32[8,4,8,128]{3,2,1,0:T(8,128)S(1)} collective-permute-done((f32[8,4,8,128]{3,2,1,0:T(8,128)S(1)}, f32[8,4,8,128]{3,2,1,0:T(8,128)S(1)}, u32[]{:S(2)}, u32[]{:S(2)}) %collective-permute-start.13) | collective-permute-done | bytes 131104 | tf_op jit(solution)/shard_map/ppermute | solution.py:390
  55.9 0.8 %unpack_late.1 = (f32[5,32,8,128]{3,2,1,0:T(8,128)}, f32[3,32,8,128]{3,2,1,0:T(8,128)}) custom-call(s32[1]{0:T(128)} %bitcast.me_ref, f32[8,4,8,128]{3,2,1,0:T(8,128)S(1)} %collective-permute-done.12.refs_0_, f32[8,4,8,128]{3,2,1,0:T(8,128)S(1)} %collective-permute-done.13.refs_1_, ...), custom_call_target="tpu_custom_call", output_to_operand_aliasing={{0}: (3, {}), {1}: (4, {})} | custom-call | tf_op jit(solution)/shard_map/unpack_late/pallas_call | solution.py:497
  (28 shorter events, 5.4 us)
Async XLA Ops:
  1.8 7.1 %collective-permute-start.7 = (f32[17,8,128]{2,1,0:T(8,128)S(1)}, f32[17,8,128]{2,1,0:T(8,128)S(1)}, u32[]{:S(2)}, u32[]{:S(2)}) collective-permute-start(f32[17,8,128]{2,1,0:T(8,128)S(1)} %get-tuple-element.51), channel_id=1, source_target_pairs={{0,4},{1,5},{2,6},{3,7},{4,0},{5,1},{6,2},{7,3},{8,12},{9,13},{10,... | collective-permute-start | bytes 208904 | tf_op jit(solution)/shard_map/ppermute | solution.py:390
  4.2 6.3 %collective-permute-start.8 = (f32[17,8,128]{2,1,0:T(8,128)S(1)}, f32[17,8,128]{2,1,0:T(8,128)S(1)}, u32[]{:S(2)}, u32[]{:S(2)}) collective-permute-start(f32[17,8,128]{2,1,0:T(8,128)S(1)} %get-tuple-element.52), channel_id=1, source_target_pairs={{0,5},{1,4},{2,7},{3,6},{4,1},{5,0},{6,3},{7,2},{8,13},{9,12},{10,... | collective-permute-start | bytes 208904 | tf_op jit(solution)/shard_map/ppermute | solution.py:390
  6.5 13.7 %collective-permute-start.4 = (f32[33,8,128]{2,1,0:T(8,128)S(1)}, f32[33,8,128]{2,1,0:T(8,128)S(1)}, u32[]{:S(2)}, u32[]{:S(2)}) collective-permute-start(f32[33,8,128]{2,1,0:T(8,128)S(1)} %get-tuple-element.44), channel_id=1, source_target_pairs={{0,3},{1,2},{2,1},{3,0},{4,7},{5,6},{6,5},{7,4},{8,11},{9,10},{10,... | collective-permute-start | bytes 405512 | tf_op jit(solution)/shard_map/ppermute | solution.py:390
  6.7 14.9 %collective-permute-start.5 = (f32[33,8,128]{2,1,0:T(8,128)S(1)}, f32[33,8,128]{2,1,0:T(8,128)S(1)}, u32[]{:S(2)}, u32[]{:S(2)}) collective-permute-start(f32[33,8,128]{2,1,0:T(8,128)S(1)} %get-tuple-element.45), channel_id=1, source_target_pairs={{0,2},{1,3},{2,0},{3,1},{4,6},{5,7},{6,4},{7,5},{8,10},{9,11},{10,... | collective-permute-start | bytes 405512 | tf_op jit(solution)/shard_map/ppermute | solution.py:390
  8.0 14.0 %collective-permute-start.6 = (f32[33,8,128]{2,1,0:T(8,128)S(1)}, f32[33,8,128]{2,1,0:T(8,128)S(1)}, u32[]{:S(2)}, u32[]{:S(2)}) collective-permute-start(f32[33,8,128]{2,1,0:T(8,128)S(1)} %get-tuple-element.46), channel_id=1, source_target_pairs={{0,1},{1,0},{2,3},{3,2},{4,5},{5,4},{6,7},{7,6},{8,9},{9,8},{10,11... | collective-permute-start | bytes 405512 | tf_op jit(solution)/shard_map/ppermute | solution.py:390
  8.9 2.3 %copy-start = (s32[16]{0:T(128)S(1)}, s32[16]{0:T(128)}, u32[]{:S(2)}) copy-start(s32[16]{0:T(128)} %shift_ref.1) | copy-start | bytes 196
  8.9 2.3 %copy-start.1 = (f32[16]{0:T(128)S(1)}, f32[16]{0:T(128)}, u32[]{:S(2)}) copy-start(f32[16]{0:T(128)} %frac_ref.1) | copy-start | bytes 196
  8.9 3.4 %collective-permute-start.9 = (f32[17,8,128]{2,1,0:T(8,128)S(1)}, f32[17,8,128]{2,1,0:T(8,128)S(1)}, u32[]{:S(2)}, u32[]{:S(2)}) collective-permute-start(f32[17,8,128]{2,1,0:T(8,128)S(1)} %get-tuple-element.53), channel_id=1, source_target_pairs={{0,6},{1,7},{2,4},{3,5},{4,2},{5,3},{6,0},{7,1},{8,14},{9,15},{10,... | collective-permute-start | bytes 208904 | tf_op jit(solution)/shard_map/ppermute | solution.py:390
  10.5 7.2 %collective-permute-start.10 = (f32[17,8,128]{2,1,0:T(8,128)S(1)}, f32[17,8,128]{2,1,0:T(8,128)S(1)}, u32[]{:S(2)}, u32[]{:S(2)}) collective-permute-start(f32[17,8,128]{2,1,0:T(8,128)S(1)} %get-tuple-element.54), channel_id=1, source_target_pairs={{0,7},{1,6},{2,5},{3,4},{4,3},{5,2},{6,1},{7,0},{8,15},{9,14},{10,... | collective-permute-start | bytes 208904 | tf_op jit(solution)/shard_map/ppermute | solution.py:390
  12.3 13.7 %collective-permute-start = (f32[16,8,128]{2,1,0:T(8,128)S(1)}, f32[16,8,128]{2,1,0:T(8,128)S(1)}, u32[]{:S(2)}, u32[]{:S(2)}) collective-permute-start(f32[16,8,128]{2,1,0:T(8,128)S(1)} %get-tuple-element.40), channel_id=1, source_target_pairs={{0,4},{1,5},{2,6},{3,7},{4,0},{5,1},{6,2},{7,3},{8,12},{9,13},{10,... | collective-permute-start | bytes 196616 | tf_op jit(solution)/shard_map/ppermute | solution.py:390
  17.6 8.4 %collective-permute-start.1 = (f32[16,8,128]{2,1,0:T(8,128)S(1)}, f32[16,8,128]{2,1,0:T(8,128)S(1)}, u32[]{:S(2)}, u32[]{:S(2)}) collective-permute-start(f32[16,8,128]{2,1,0:T(8,128)S(1)} %get-tuple-element.41), channel_id=1, source_target_pairs={{0,5},{1,4},{2,7},{3,6},{4,1},{5,0},{6,3},{7,2},{8,13},{9,12},{10,... | collective-permute-start | bytes 196616 | tf_op jit(solution)/shard_map/ppermute | solution.py:390
  20.2 8.9 %collective-permute-start.2 = (f32[16,8,128]{2,1,0:T(8,128)S(1)}, f32[16,8,128]{2,1,0:T(8,128)S(1)}, u32[]{:S(2)}, u32[]{:S(2)}) collective-permute-start(f32[16,8,128]{2,1,0:T(8,128)S(1)} %get-tuple-element.42), channel_id=1, source_target_pairs={{0,6},{1,7},{2,4},{3,5},{4,2},{5,3},{6,0},{7,1},{8,14},{9,15},{10,... | collective-permute-start | bytes 196616 | tf_op jit(solution)/shard_map/ppermute | solution.py:390
  21.5 9.1 %collective-permute-start.3 = (f32[16,8,128]{2,1,0:T(8,128)S(1)}, f32[16,8,128]{2,1,0:T(8,128)S(1)}, u32[]{:S(2)}, u32[]{:S(2)}) collective-permute-start(f32[16,8,128]{2,1,0:T(8,128)S(1)} %get-tuple-element.43), channel_id=1, source_target_pairs={{0,7},{1,6},{2,5},{3,4},{4,3},{5,2},{6,1},{7,0},{8,15},{9,14},{10,... | collective-permute-start | bytes 196616 | tf_op jit(solution)/shard_map/ppermute | solution.py:390
  22.4 8.9 %collective-permute-start.11 = (f32[8,2,8,128]{3,2,1,0:T(8,128)S(1)}, f32[8,2,8,128]{3,2,1,0:T(8,128)S(1)}, u32[]{:S(2)}, u32[]{:S(2)}) collective-permute-start(f32[8,2,8,128]{3,2,1,0:T(8,128)S(1)} %edge.1), channel_id=1, source_target_pairs={{1,0},{2,1},{3,2},{4,3},{5,4},{6,5},{7,6},{15,7},{14,15},{13,14},{... | collective-permute-start | bytes 196616 | tf_op jit(solution)/shard_map/ppermute | solution.py:450
  31.8 9.0 %collective-permute-start.14 = (f32[8,4,8,128]{3,2,1,0:T(8,128)S(1)}, f32[8,4,8,128]{3,2,1,0:T(8,128)S(1)}, u32[]{:S(2)}, u32[]{:S(2)}) collective-permute-start(f32[8,4,8,128]{3,2,1,0:T(8,128)S(1)} %get-tuple-element.66), channel_id=1, source_target_pairs={{0,4},{1,5},{2,6},{3,7},{4,0},{5,1},{6,2},{7,3},{8,12},{9,13},{10,... | collective-permute-start | bytes 393224 | tf_op jit(solution)/shard_map/ppermute | solution.py:390
  31.9 11.5 %collective-permute-start.15 = (f32[8,4,8,128]{3,2,1,0:T(8,128)S(1)}, f32[8,4,8,128]{3,2,1,0:T(8,128)S(1)}, u32[]{:S(2)}, u32[]{:S(2)}) collective-permute-start(f32[8,4,8,128]{3,2,1,0:T(8,128)S(1)} %get-tuple-element.67), channel_id=1, source_target_pairs={{0,5},{1,4},{2,7},{3,6},{4,1},{5,0},{6,3},{7,2},{8,13},{9,12},{10,... | collective-permute-start | bytes 393224 | tf_op jit(solution)/shard_map/ppermute | solution.py:390
  34.6 10.5 %collective-permute-start.16 = (f32[8,4,8,128]{3,2,1,0:T(8,128)S(1)}, f32[8,4,8,128]{3,2,1,0:T(8,128)S(1)}, u32[]{:S(2)}, u32[]{:S(2)}) collective-permute-start(f32[8,4,8,128]{3,2,1,0:T(8,128)S(1)} %get-tuple-element.68), channel_id=1, source_target_pairs={{0,3},{1,2},{2,1},{3,0},{4,7},{5,6},{6,5},{7,4},{8,11},{9,10},{10,... | collective-permute-start | bytes 393224 | tf_op jit(solution)/shard_map/ppermute | solution.py:390
  34.7 10.5 %collective-permute-start.17 = (f32[8,4,8,128]{3,2,1,0:T(8,128)S(1)}, f32[8,4,8,128]{3,2,1,0:T(8,128)S(1)}, u32[]{:S(2)}, u32[]{:S(2)}) collective-permute-start(f32[8,4,8,128]{3,2,1,0:T(8,128)S(1)} %get-tuple-element.69), channel_id=1, source_target_pairs={{0,2},{1,3},{2,0},{3,1},{4,6},{5,7},{6,4},{7,5},{8,10},{9,11},{10,... | collective-permute-start | bytes 393224 | tf_op jit(solution)/shard_map/ppermute | solution.py:390
  36.7 8.4 %collective-permute-start.18 = (f32[8,4,8,128]{3,2,1,0:T(8,128)S(1)}, f32[8,4,8,128]{3,2,1,0:T(8,128)S(1)}, u32[]{:S(2)}, u32[]{:S(2)}) collective-permute-start(f32[8,4,8,128]{3,2,1,0:T(8,128)S(1)} %get-tuple-element.70), channel_id=1, source_target_pairs={{0,1},{1,0},{2,3},{3,2},{4,5},{5,4},{6,7},{7,6},{8,9},{9,8},{10,11... | collective-permute-start | bytes 393224 | tf_op jit(solution)/shard_map/ppermute | solution.py:390
  40.8 11.9 %collective-permute-start.12 = (f32[8,4,8,128]{3,2,1,0:T(8,128)S(1)}, f32[8,4,8,128]{3,2,1,0:T(8,128)S(1)}, u32[]{:S(2)}, u32[]{:S(2)}) collective-permute-start(f32[8,4,8,128]{3,2,1,0:T(8,128)S(1)} %get-tuple-element.64), channel_id=1, source_target_pairs={{0,6},{1,7},{2,4},{3,5},{4,2},{5,3},{6,0},{7,1},{8,14},{9,15},{10,... | collective-permute-start | bytes 393224 | tf_op jit(solution)/shard_map/ppermute | solution.py:390
  43.4 12.5 %collective-permute-start.13 = (f32[8,4,8,128]{3,2,1,0:T(8,128)S(1)}, f32[8,4,8,128]{3,2,1,0:T(8,128)S(1)}, u32[]{:S(2)}, u32[]{:S(2)}) collective-permute-start(f32[8,4,8,128]{3,2,1,0:T(8,128)S(1)} %get-tuple-element.65), channel_id=1, source_target_pairs={{0,7},{1,6},{2,5},{3,4},{4,3},{5,2},{6,1},{7,0},{8,15},{9,14},{10,... | collective-permute-start | bytes 393224 | tf_op jit(solution)/shard_map/ppermute | solution.py:390
